TPU v7x, 32 devices: a whole 2x2x4 slice. The times are simulated.
32 devices in a mesh: seq: 4 (over y, x), grp: 8 (over z, core).
Axes of the slice: x: 2, y: 2, z: 4, core: 2. Of those that a mesh axis runs over, the one named last changes fastest.
Arguments:
- tokens: bfloat16 [16384, 768], P(('grp', 'seq')), may hold values from -6 to 6
- cotangent: bfloat16 [16384, 768], P(('grp', 'seq')), may hold values from -6 to 6
- seq_len: int32 [8], P('grp'), may hold values from 1024 to 2048, as said below
- weight_mats: bfloat16 [768, 9280], replicated
- weight_vecs: bfloat16 [768, 13], replicated
- master_mats: float32 [768, 9280], P('grp'), may hold values from -0.21875 to 0.21875
- master_vecs: float32 [768, 13], P('grp'), may hold values from -3 to 3
- moment_mats: float32 [768, 9280], P('grp'), may hold values from -384 to 384
- moment_vecs: float32 [768, 13], P('grp'), may hold values from -384 to 384
- square_mats: float32 [768, 9280], P('grp'), may hold values from 819.2 to 32768
- square_vecs: float32 [768, 13], P('grp'), may hold values from 819.2 to 32768
- average_mats: float32 [768, 9280], P('grp'), may hold values from -0.21875 to 0.21875
- average_vecs: float32 [768, 13], P('grp'), may hold values from -3 to 3
Outputs:
- block_output: bfloat16 [16384, 768], P(('grp', 'seq'))
- input_grad: bfloat16 [16384, 768], P(('grp', 'seq'))
- grad_mats: float32 [768, 9280], P('grp')
- grad_vecs: float32 [768, 13], P('grp')
- master_mats_new: float32 [768, 9280], P('grp')
- master_vecs_new: float32 [768, 13], P('grp')
- moment_mats_new: float32 [768, 9280], P('grp')
- moment_vecs_new: float32 [768, 13], P('grp')
- square_mats_new: float32 [768, 9280], P('grp')
- square_vecs_new: float32 [768, 13], P('grp')
- average_mats_new: float32 [768, 9280], P('grp')
- average_vecs_new: float32 [768, 13], P('grp')
- copy_mats: bfloat16 [768, 9280], P('grp')
- copy_vecs: bfloat16 [768, 13], P('grp')
Inputs may be any that keep to these rules, and one draw needn't show every extreme that they name: Each group's sequences all have the length seq_len of that group; both values 2 * 512 and 2048 occur in every draw.
All inputs are finite; a program needn't handle non-finite values.
Results may differ from a plain program's by a relative error of at most 0.018.
Values may be sent and summed in bfloat16 or wider, within the bound.
No kernel may reach another device: no remote copies, remote signals or barrier semaphores. Data moves between devices by JAX's collectives and lax.ppermute only.
A program may use at most 192 MiB of HBM per device.

v0:
```python
from functools import partial

import jax
import jax.numpy as jnp
from jax import lax
from jax.experimental import pallas as pl
from jax.experimental.pallas import tpu as pltpu
from jax.sharding import PartitionSpec as P

D = 768
HEADS = 12
HD = 64
FF = 3072
QUAD = 4
N_QUAD = HEADS // QUAD
AUG = 80

norm_eps = 1e-05
adam_eps = 1e-08
beta_first = 0.5
beta_second = 0.5
learn_rate = 0.01
vector_rate = 0.06
decay_rate = 0.1
average_keep = 0.9

f32 = jnp.float32
bf16 = jnp.bfloat16

S_SEQ, S_GRP, S_MASK, S_BACK = 0, 1, 4, 8

MIB = 1024 * 1024


def dot_nn(a, b):
    return lax.dot_general(a, b, (((1,), (0,)), ((), ())), preferred_element_type=f32)


def dot_nt(a, b):
    return lax.dot_general(a, b, (((1,), (1,)), ((), ())), preferred_element_type=f32)


def dot_tn(a, b):
    return lax.dot_general(a, b, (((0,), (0,)), ((), ())), preferred_element_type=f32)


def whole(shape):
    return pl.BlockSpec(tuple(shape), lambda *_: (0,) * len(shape))


def along(block, axis=0):
    return pl.BlockSpec(tuple(block), lambda i, s: tuple(i if d == axis else 0 for d in range(len(block))))


def sds(shape, dtype):
    return jax.ShapeDtypeStruct(tuple(shape), dtype)


class Line:
    def __init__(self, scal):
        self.scal = scal

    def call(self, body, args, in_specs, outs, out_specs, grid=(1,), scratch=(), flops=0, vmem=32,
             aliases=None, name=None):
        moved = sum(o.size * o.dtype.itemsize for o in outs)
        moved += sum(a.size * a.dtype.itemsize for a in args if a.size < 4 * D * D)
        got = pl.pallas_call(
            body,
            out_shape=tuple(outs),
            grid_spec=pltpu.PrefetchScalarGridSpec(
                num_scalar_prefetch=1,
                grid=grid,
                in_specs=list(in_specs),
                out_specs=tuple(out_specs),
                scratch_shapes=list(scratch),
            ),
            compiler_params=pltpu.CompilerParams(
                dimension_semantics=("arbitrary",) * len(grid), vmem_limit_bytes=vmem * MIB
            ),
            cost_estimate=pl.CostEstimate(
                flops=int(flops), bytes_accessed=int(moved), transcendentals=0
            ),
            input_output_aliases=aliases or {},
            name=name,
        )(self.scal, *args)
        self.scal, got = lax.optimization_barrier((self.scal, got))
        return got


def store_sel(refs, at, values, scal):
    if len(refs) == 1:
        refs[0][at] = values
        return
    block = D // 8
    for j in range(8):
        rel = jnp.bitwise_xor(scal[S_GRP], j)
        place = pl.multiple_of(jnp.right_shift(rel, 1) * block, block)
        odd = jnp.bitwise_and(rel, 1)
        part = values[j * block : (j + 1) * block, :]

        @pl.when(odd == 1)
        def _(part=part, place=place):
            refs[0][at, pl.ds(place, block), :] = part

        @pl.when(odd == 0)
        def _(part=part, place=place):
            refs[1][at, pl.ds(place, block), :] = part


def normalize(values):
    average = jnp.mean(values, axis=1, keepdims=True)
    centered = values - average
    variance = jnp.mean(centered * centered, axis=1, keepdims=True)
    inverse = lax.rsqrt(variance + norm_eps)
    return centered * inverse, inverse


def quad_maps(hedge_t):
    wide = QUAD * HD
    row = lax.broadcasted_iota(jnp.int32, (wide, HD), 0)
    col = lax.broadcasted_iota(jnp.int32, (wide, HD), 1)
    spread = (jnp.bitwise_and(row, HD - 1) == col).astype(bf16)
    tiled = dot_nn(spread, hedge_t)
    big_r = lax.broadcasted_iota(jnp.int32, (wide, wide), 0)
    big_c = lax.broadcasted_iota(jnp.int32, (wide, wide), 1)
    same = jnp.right_shift(big_r, 6) == jnp.right_shift(big_c, 6)
    return jnp.where(same, tiled, 0.0)


def ones_rows(count):
    return (lax.broadcasted_iota(jnp.int32, (AUG - HD, count), 0) == 0).astype(f32).astype(bf16)


def rows_up(values):
    return jnp.concatenate([values, jnp.zeros((3, values.shape[1]), f32)], axis=0).T


def pre_body(n_sel, scal, x_ref, g_ref, wq_ref, wk_ref, wv_ref, hedge_ref, vt_ref, vq_ref, *refs):
    sel = refs[:n_sel]
    qt_ref, kt_ref, fq_ref, fk_ref, vt_out, s_ref, h1_ref = refs[n_sel:]
    rows = x_ref.shape[0]

    @pl.when(pl.program_id(0) == 0)
    def _():
        normed, _ = normalize(x_ref[...].astype(f32))
        vt = vt_ref[...].astype(f32)
        h1 = (normed * vt[0:1] + vt[1:2]).astype(bf16)
        h1_ref[...] = h1
        store_sel(sel, 0, g_ref[...].T, scal)
        store_sel(sel, 1, h1.T, scal)

    h1 = h1_ref[...]
    bias = rows_up(vq_ref[...].astype(f32))
    v_t = (dot_nt(wv_ref[...], h1) + bias[:, 8:9]).astype(bf16)
    vt_out[...] = v_t
    maps = quad_maps(hedge_ref[...]).astype(bf16)
    maps2 = jnp.concatenate([maps, maps], axis=1)
    extra = ones_rows(rows)
    for which, (w_ref, save, feat) in enumerate(((wk_ref, kt_ref, fk_ref), (wq_ref, qt_ref, fq_ref))):
        pt = dot_nt(w_ref[...], h1) + bias[:, 7 - which : 8 - which]
        high = pt.astype(bf16)
        save[...] = high
        rest = (pt - high.astype(f32)).astype(bf16)
        scores = dot_nn(maps2, jnp.concatenate([high, rest], axis=0))
        for h in range(QUAD):
            s = scores[h * HD : (h + 1) * HD, :]
            top = jnp.max(s, axis=0, keepdims=True)
            bottom = jnp.min(s, axis=0, keepdims=True)
            pos = jnp.exp(s - top)
            neg = jnp.exp(bottom - s)
            pos = pos * (1.0 / jnp.sum(pos, axis=0, keepdims=True))
            neg = neg * (1.0 / jnp.sum(neg, axis=0, keepdims=True))
            both = jnp.concatenate([pos, neg], axis=0).astype(bf16)
            feat[h * 2 * HD : (h + 1) * 2 * HD, :] = both
            if which == 0:
                va = jnp.concatenate([v_t[h * HD : (h + 1) * HD, :], extra], axis=0)
                s_ref[h * AUG : (h + 1) * AUG, :] = dot_nt(va, both).astype(bf16)


def tri_mask(half):
    return lax.broadcasted_iota(jnp.int32, (half, half), 0) <= lax.broadcasted_iota(
        jnp.int32, (half, half), 1
    )


def masked_pair(left0, left1, right, keep):
    half = right.shape[1] // 2
    full = dot_tn(left0, right)
    low = dot_tn(left1, right[:, half:])
    diag0 = jnp.where(keep, full[:, :half], 0.0).astype(bf16)
    above = full[:, half:].astype(bf16)
    diag1 = jnp.where(keep, low, 0.0).astype(bf16)
    return diag0, above, diag1


def local_body(scal, fq_ref, fk_ref, vt_ref, num_ref):
    rows = fq_ref.shape[1]
    half = rows // 2
    keep = tri_mask(half)
    extra = ones_rows(rows)
    for h in range(QUAD):
        fq = fq_ref[h * 2 * HD : (h + 1) * 2 * HD, :]
        fk = fk_ref[h * 2 * HD : (h + 1) * 2 * HD, :]
        va = jnp.concatenate([vt_ref[h * HD : (h + 1) * HD, :], extra], axis=0)
        a00, a01, a11 = masked_pair(fk[:, :half], fk[:, half:], fq, keep)
        num_ref[h * AUG : (h + 1) * AUG, :half] = dot_nn(va[:, :half], a00)
        num_ref[h * AUG : (h + 1) * AUG, half:] = dot_nn(va[:, :half], a01) + dot_nn(va[:, half:], a11)


def weighted_state(scal, slot, parts):
    total = None
    for k, part in enumerate(parts):
        term = scal[slot + k].astype(f32) * part.astype(f32)
        total = term if total is None else total + term
    return total.astype(bf16)


def after_body(n_sel, n_parts, scal, *refs):
    parts = refs[:n_parts]
    num_ref, fq_ref, x_ref, w_ref, vt_ref, o_ref, den_ref, r_ref, h2_ref, sin_ref = refs[n_parts : n_parts + 10]
    sel = refs[n_parts + 10 : n_parts + 10 + n_sel]
    ob_ref = refs[-1]
    vt = vt_ref[...].astype(f32)
    state = weighted_state(scal, S_MASK, [p[...] for p in parts])
    sin_ref[...] = state
    for h in range(HEADS):
        num = num_ref[h * AUG : (h + 1) * AUG, :] + dot_nn(
            state[h * AUG : (h + 1) * AUG, :], fq_ref[h * 2 * HD : (h + 1) * 2 * HD, :]
        )
        den = num[HD : HD + 1, :]
        out = num[:HD, :] * (1.0 / den)
        o_ref[h * HD : (h + 1) * HD, :] = out
        den_ref[h : h + 1, :] = den
        ob_ref[h * HD : (h + 1) * HD, :] = out.astype(bf16)
    obt = ob_ref[...]
    store_sel(sel, 0, obt, scal)
    r = x_ref[...].astype(f32) + dot_nt(obt.T, w_ref[...]) + vt[4:5]
    r_ref[...] = r
    normed, _ = normalize(r)
    h2 = (normed * vt[2:3] + vt[3:4]).astype(bf16)
    h2_ref[...] = h2
    store_sel(sel, 1, h2.T, scal)


gelu_c = 0.7978845608028654
gelu_k = 0.044715


def mlp_body(first, scal, h2_ref, g_ref, wf_ref, wd_ref, bias_ref, *refs):
    if first:
        out_ref, dh_ref, act_ref, db_ref = refs
    else:
        out_in, dh_in, out_ref, dh_ref, act_ref, db_ref = refs
    u = dot_nt(h2_ref[...], wf_ref[...]) + bias_ref[...].astype(f32)
    de = dot_nt(g_ref[...], wd_ref[...])
    uu = u * u
    t = jnp.tanh(gelu_c * u * (1.0 + gelu_k * uu))
    half_t = 0.5 * (1.0 + t)
    e = (u * half_t).astype(bf16)
    slope = half_t + 0.5 * u * (1.0 - t * t) * (gelu_c * (1.0 + 3.0 * gelu_k * uu))
    du = (de * slope).astype(bf16)
    act_ref[0, 0] = e
    act_ref[1, 0] = du
    db_ref[...] = jnp.sum(du.astype(f32), axis=0, keepdims=True)
    add_out = dot_nn(e, wd_ref[...])
    add_dh = dot_nn(du, wf_ref[...])
    step = pl.program_id(0)

    @pl.when(step == 0)
    def _():
        if first:
            out_ref[...] = add_out
            dh_ref[...] = add_dh
        else:
            out_ref[...] = out_in[...] + add_out
            dh_ref[...] = dh_in[...] + add_dh

    @pl.when(step > 0)
    def _():
        out_ref[...] += add_out
        dh_ref[...] += add_dh


def back_body(scal, out_ref, dh_ref, r_ref, g_ref, w_ref, vt_ref, o_ref, den_ref, fq_ref, y_ref, dr_ref,
              da_ref, rho_ref, ds_ref, sums_ref, do_ref):
    vt = vt_ref[...].astype(f32)
    r = r_ref[...]
    y_ref[...] = (r + out_ref[...] + vt[5:6]).astype(bf16)
    grad_out = g_ref[...].astype(f32)
    normed, inverse = normalize(r)
    up = dh_ref[...]
    dn = up * vt[2:3]
    dr = grad_out + inverse * (
        dn - jnp.mean(dn, axis=1, keepdims=True) - normed * jnp.mean(dn * normed, axis=1, keepdims=True)
    )
    dr_ref[...] = dr
    da = dr.astype(bf16)
    da_ref[...] = da
    sums_ref[...] = jnp.concatenate(
        [
            jnp.sum(up * normed, axis=0, keepdims=True),
            jnp.sum(up, axis=0, keepdims=True),
            jnp.sum(da.astype(f32), axis=0, keepdims=True),
            jnp.sum(grad_out, axis=0, keepdims=True),
        ],
        axis=0,
    )
    do_ref[...] = dot_nn(da, w_ref[...]).astype(bf16).T
    rows = r.shape[0]
    zero_row = lax.broadcasted_iota(jnp.int32, (AUG - HD, rows), 0) == 0
    for h in range(HEADS):
        dout = do_ref[h * HD : (h + 1) * HD, :].astype(f32)
        inv = 1.0 / den_ref[h : h + 1, :]
        rho = (dout * inv).astype(bf16)
        c = -jnp.sum(dout * o_ref[h * HD : (h + 1) * HD, :], axis=0, keepdims=True) * inv
        extra = jnp.where(zero_row, jnp.broadcast_to(c, (AUG - HD, rows)), 0.0).astype(bf16)
        ra = jnp.concatenate([rho, extra], axis=0)
        rho_ref[h * AUG : (h + 1) * AUG, :] = ra
        ds_ref[h * AUG : (h + 1) * AUG, :] = dot_nt(ra, fq_ref[h * 2 * HD : (h + 1) * 2 * HD, :]).astype(bf16)


def feature_back(feat, upstream):
    pos, neg = feat[:HD].astype(f32), feat[HD:].astype(f32)
    up_pos, up_neg = upstream[:HD], upstream[HD:]
    return pos * (up_pos - jnp.sum(pos * up_pos, axis=0, keepdims=True)) - neg * (
        up_neg - jnp.sum(neg * up_neg, axis=0, keepdims=True)
    )


def attend_back_body(n_parts, scal, *refs):
    parts = refs[:n_parts]
    (fq_ref, fk_ref, vt_ref, rho_ref, sin_ref, qt_ref, kt_ref, hedge_ref, dp_ref, dm_ref,
     db_ref) = refs[n_parts:]
    rows = fq_ref.shape[1]
    half = rows // 2
    keep = tri_mask(half)
    extra = ones_rows(rows)
    back_state = weighted_state(scal, S_BACK, [p[...] for p in parts])
    ds_q, ds_k = [], []
    for h in range(QUAD):
        fq = fq_ref[h * 2 * HD : (h + 1) * 2 * HD, :]
        fk = fk_ref[h * 2 * HD : (h + 1) * 2 * HD, :]
        head = slice(h * HD, (h + 1) * HD)
        aug = slice(h * AUG, (h + 1) * AUG)
        va = jnp.concatenate([vt_ref[head, :], extra], axis=0)
        ra = rho_ref[aug, :]
        state, back = sin_ref[aug, :], back_state[aug, :]
        a00, a01, a11 = masked_pair(fk[:, :half], fk[:, half:], fq, keep)
        g00, g01, g11 = masked_pair(va[:, :half], va[:, half:], ra, keep)
        far = dot_tn(state, ra)
        left = far[:, :half] + dot_nn(fk[:, :half], g00)
        right = far[:, half:] + dot_nn(fk[:, :half], g01) + dot_nn(fk[:, half:], g11)
        dfq = jnp.concatenate([left, right], axis=1)
        far_k = dot_tn(back, va)
        left = far_k[:, :half] + dot_nt(fq[:, :half], g00) + dot_nt(fq[:, half:], g01)
        right = far_k[:, half:] + dot_nt(fq[:, half:], g11)
        dfk = jnp.concatenate([left, right], axis=1)
        far_v = dot_nn(back, fk)[:HD]
        rv = ra[:HD]
        left = far_v[:, :half] + dot_nt(rv[:, :half], a00) + dot_nt(rv[:, half:], a01)
        right = far_v[:, half:] + dot_nt(rv[:, half:], a11)
        dp_ref[2, head, :] = jnp.concatenate([left, right], axis=1).astype(bf16)
        dsq = feature_back(fq, dfq).astype(bf16)
        dsk = feature_back(fk, dfk).astype(bf16)
        ds_q.append(dsq)
        ds_k.append(dsk)
        dm_ref[head, :] = dot_nt(qt_ref[head, :], dsq) + dot_nt(kt_ref[head, :], dsk)
    maps = quad_maps(hedge_ref[...]).T.astype(bf16)
    dq = dot_nn(maps, jnp.concatenate(ds_q, axis=0)).astype(bf16)
    dk = dot_nn(maps, jnp.concatenate(ds_k, axis=0)).astype(bf16)
    dp_ref[0] = dq
    dp_ref[1] = dk
    db_ref[...] = jnp.concatenate(
        [jnp.sum(v.astype(f32), axis=1, keepdims=True) for v in (dq, dk, dp_ref[2])], axis=1
    )


def input_body(fast, scal, dp_ref, w_ref, x_ref, dr_ref, vt_ref, sums_ref, dbfc_ref, db_ref, dm_ref, *refs):
    gin_ref, *small_refs, acc_ref = refs
    step = pl.program_id(0)
    part = dot_tn(dp_ref[0], w_ref[...])

    @pl.when(step == 0)
    def _():
        acc_ref[...] = part

    @pl.when(step == 1)
    def _():
        acc_ref[...] += part

    @pl.when(step == 2)
    def _():
        vt = vt_ref[...].astype(f32)
        up = acc_ref[...] + part
        normed, inverse = normalize(x_ref[...].astype(f32))
        dn = up * vt[0:1]
        gin = dr_ref[...] + inverse * (
            dn - jnp.mean(dn, axis=1, keepdims=True) - normed * jnp.mean(dn * normed, axis=1, keepdims=True)
        )
        gin_ref[...] = gin.astype(bf16)
        rows16 = jnp.concatenate(
            [
                jnp.sum(up * normed, axis=0, keepdims=True),
                jnp.sum(up, axis=0, keepdims=True),
                sums_ref[...],
                jnp.zeros((3, D), f32),
                dbfc_ref[...],
                jnp.zeros((3, D), f32),
            ],
            axis=0,
        )
        cols = rows16.T
        lane = lax.broadcasted_iota(jnp.int32, (D, HD), 1)
        tail = jnp.concatenate([cols, jnp.zeros((D, HD - 16), f32)], axis=1)
        for k in range(3):
            tail = jnp.where(lane == 6 + k, db_ref[:, k : k + 1], tail)
        small = jnp.concatenate([dm_ref[...], tail], axis=1)
        store_sel(small_refs, 0, small, scal)


def order_a(i):
    return jnp.where(i < 2, 2 * i + 1, 2 * i - 4)


def order_b(i):
    return jnp.where(i < 2, i + 2, i - 2)


def put(send, keep, value):
    step = pl.program_id(0)

    @pl.when(step < 2)
    def _():
        send[...] = value[None]

    @pl.when(step >= 2)
    def _():
        keep[...] = value[None]


def mlp_grads_body(n_src, scal, *refs):
    sels, acts_a, acts_b = refs[:n_src], refs[n_src : 2 * n_src], refs[2 * n_src : 3 * n_src]
    sels_h = refs[3 * n_src : 4 * n_src]
    send_a, keep_a, send_b, keep_b = refs[4 * n_src :]

    def total(lefts, rights):
        acc = dot_nn(lefts[0][0], rights[0][0, 0])
        for left, right in zip(lefts[1:], rights[1:]):
            acc += dot_nn(left[0], right[0, 0])
        return acc.astype(bf16)

    put(send_a, keep_a, total(sels, acts_a))
    put(send_b, keep_b, total(sels_h, acts_b))


def split_specs(depth, wq):
    send = pl.BlockSpec((1, depth, wq), lambda i, s: (jnp.minimum(i, 1), 0, 0))
    keep = pl.BlockSpec((1, depth, wq), lambda i, s: (jnp.maximum(i - 2, 0), 0, 0))
    return [sds((2, depth, wq), bf16)] * 4, [send, keep, send, keep]


def mlp_grads(line, sel_first, sel_second, acts):
    n_src = len(acts)
    _, depth, rows = sel_first[0].shape
    wq = acts[0].shape[3]
    outs, out_specs = split_specs(depth, wq)
    return line.call(
        partial(mlp_grads_body, n_src),
        [*sel_first, *acts, *acts, *sel_second],
        [pl.BlockSpec((1, depth, rows), lambda i, s: (0, 0, 0))] * n_src
        + [pl.BlockSpec((1, 1, rows, wq), lambda i, s: (0, order_a(i), 0, 0))] * n_src
        + [pl.BlockSpec((1, 1, rows, wq), lambda i, s: (1, order_b(i), 0, 0))] * n_src
        + [pl.BlockSpec((1, depth, rows), lambda i, s: (1, 0, 0))] * n_src,
        outs,
        out_specs,
        grid=(4,),
        flops=2 * 2 * n_src * depth * rows * wq * 4,
        vmem=24,
        name="mlp_grads",
    )


def tail_grads_body(n_src, scal, *refs):
    it = iter(refs)

    def take():
        return [next(it) for _ in range(n_src)]

    h1, ob, dqk, dv, da = take(), take(), take(), take(), take()
    send_a, keep_a, send_b, keep_b = it
    qb = jnp.bitwise_xor(order_b(pl.program_id(0)), scal[S_SEQ])

    def total(lefts, rights):
        acc = dot_nt(lefts[0][0], rights[0][0])
        for left, right in zip(lefts[1:], rights[1:]):
            acc += dot_nt(left[0], right[0])
        return acc.astype(bf16)

    put(send_a, keep_a, total(h1, dqk))

    @pl.when(qb < 2)
    def _():
        put(send_b, keep_b, total(h1, dv))

    @pl.when(qb >= 2)
    def _():
        acc = dot_nn(ob[0][0], da[0][...])
        for left, right in zip(ob[1:], da[1:]):
            acc += dot_nn(left[0], right[...])
        put(send_b, keep_b, acc.astype(bf16))


def tail_grads(line, sel_first, sel_second, dp, da):
    n_src = len(dp)
    _, depth, rows = sel_first[0].shape
    wq = D // 2
    dp = [v.reshape(6, wq, rows) for v in dp]
    outs, out_specs = split_specs(depth, wq)
    return line.call(
        partial(tail_grads_body, n_src),
        [*sel_first, *sel_second, *dp, *dp, *da],
        [pl.BlockSpec((1, depth, rows), lambda i, s: (1, 0, 0))] * n_src
        + [pl.BlockSpec((1, depth, rows), lambda i, s: (0, 0, 0))] * n_src
        + [pl.BlockSpec((1, wq, rows), lambda i, s: (jnp.bitwise_xor(order_a(i), s[S_SEQ]), 0, 0))] * n_src
        + [pl.BlockSpec((1, wq, rows), lambda i, s: (
            4 + jnp.minimum(jnp.bitwise_xor(order_b(i), s[S_SEQ]), 1), 0, 0))] * n_src
        + [pl.BlockSpec((rows, wq), lambda i, s: (
            0, jnp.maximum(jnp.bitwise_xor(order_b(i), s[S_SEQ]) - 2, 0)))] * n_src,
        outs,
        out_specs,
        grid=(4,),
        flops=2 * 2 * n_src * depth * rows * wq * 4,
        vmem=24,
        name="tail_grads",
    )


def swap(value, axis, size, bit):
    return lax.ppermute(value, axis, [(i, i ^ bit) for i in range(size)])


def add_one_body(scal, keep_a, recv_a, keep_b, recv_b, send_a, send_b):
    send_a[...] = (keep_a[0].astype(f32) + recv_a[0].astype(f32)).astype(bf16)
    send_b[...] = (keep_b[0].astype(f32) + recv_b[0].astype(f32)).astype(bf16)


def add_two_body(scal, keep_a, recv_a, keep_b, recv_b, far_a, far_b, own_ref, *out_refs):
    block = own_ref.shape[1]
    for path, (keep, recv, far) in enumerate(((keep_a, recv_a, far_a), (keep_b, recv_b, far_b))):
        total = keep[0].astype(f32) + recv[0].astype(f32) + far[...].astype(f32)
        own_ref[path] = total[:block]
        for k, ref in enumerate(out_refs):
            ref[path] = total[(k + 1) * block : (k + 2) * block].astype(bf16)


def add_three_body(scal, own, *refs):
    total = own[...]
    for ref in refs[:-1]:
        total = total + ref[...].astype(f32)
    refs[-1][...] = total.astype(refs[-1].dtype)


class Piece:
    def __init__(self, line, send_a, keep_a, send_b, keep_b):
        self.line = line
        self.keep_a, self.keep_b = keep_a, keep_b
        self.recv_a, self.recv_b = swap(send_a, "seq", 4, 1), swap(send_b, "seq", 4, 2)

    def one(self):
        _, depth, wq = self.keep_a.shape
        second = pl.BlockSpec((1, depth, wq), lambda i, s: (1, 0, 0))
        next_a, next_b = self.line.call(
            add_one_body, [self.keep_a, self.recv_a, self.keep_b, self.recv_b], [second] * 4,
            [sds((depth, wq), bf16)] * 2, [whole((depth, wq))] * 2, flops=2 * depth * wq, vmem=8,
            name="add_one",
        )
        self.far_a, self.far_b = swap(next_a, "seq", 4, 2), swap(next_b, "seq", 4, 1)

    def two(self):
        _, depth, wq = self.keep_a.shape
        zero = pl.BlockSpec((1, depth, wq), lambda i, s: (0, 0, 0))
        shard = (2, depth // 4, wq)
        self.own, *sends = self.line.call(
            add_two_body,
            [self.keep_a, self.recv_a, self.keep_b, self.recv_b, self.far_a, self.far_b],
            [zero] * 4 + [whole((depth, wq))] * 2,
            [sds(shard, f32)] + [sds(shard, bf16)] * 3, [whole(shard)] * 4, flops=4 * depth * wq, vmem=10,
            name="add_two",
        )
        self.got = [swap(v, "grp", 8, 2 * (k + 1)) for k, v in enumerate(sends)]

    def three(self):
        shard = self.own.shape
        (mine,) = self.line.call(
            add_three_body, [self.own, *self.got], [whole(shard)] * 4, [sds(shard, bf16)], [whole(shard)],
            flops=6 * shard[1] * shard[2], vmem=6, name="add_three",
        )
        self.parts = [mine] + [swap(mine, "seq", 4, k) for k in (1, 2, 3)]


def adam_math(grad, master, first, second, average, rate):
    new_first = beta_first * first + (1.0 - beta_first) * grad
    new_second = beta_second * second + (1.0 - beta_second) * grad * grad
    new_master = master - rate * (
        new_first / (jnp.sqrt(new_second) + adam_eps) + decay_rate * master
    )
    new_average = average_keep * average + (1.0 - average_keep) * new_master
    return new_master, new_first, new_second, new_average


def adam_body(n_alias, has_small, scal, *refs):
    parts, refs = refs[:4], refs[4:]
    if has_small:
        small, vec_in, refs = refs[0], refs[1:5], refs[5:]
    states, refs = refs[:4], refs[4 + n_alias :]
    outs, vec_outs = refs[:6], refs[6:]
    grad_ref = outs[0]
    wq = parts[0].shape[2]
    step = pl.program_id(0)
    path, half = jnp.right_shift(step, 1), jnp.bitwise_and(step, 1)
    for k, ref in enumerate(parts):
        quarter = jnp.bitwise_xor(scal[S_SEQ], k)

        @pl.when((jnp.right_shift(quarter, 1) == half) & (step < 4))
        def _(ref=ref, quarter=quarter):
            at = pl.multiple_of(jnp.bitwise_and(quarter, 1) * wq, 128)
            grad_ref[:, pl.ds(at, wq)] = ref[jnp.minimum(path, 1)].astype(f32)

    if has_small:

        @pl.when(step == 4)
        def _():
            grad_ref[...] = jnp.zeros_like(grad_ref)
            grad_ref[:, : 2 * HD] = small[...]
            grad = small[...].T[HD : HD + vec_in[0].shape[0]]
            results = adam_math(grad, *[v[...] for v in vec_in], vector_rate)
            for ref, value in zip(vec_outs, (grad, *results, results[0])):
                ref[...] = value.astype(ref.dtype)

    results = adam_math(grad_ref[...], *[v[...] for v in states], learn_rate)
    for ref, value in zip(outs[1:], (*results, results[0])):
        ref[...] = value.astype(ref.dtype)


def adam_piece(line, parts, states, outs, block_of, small=(), vecs=()):
    _, block, _ = parts[0].shape
    rows, wide = states[0].shape
    spec = pl.BlockSpec((block, D), lambda i, s: (0, block_of(i)))
    anywhere = pl.BlockSpec(memory_space=pl.ANY)
    n_alias = 0 if outs is None else 6
    shapes = [sds((rows, wide), f32)] * 5 + [sds((rows, wide), bf16)]
    args = [*parts, *small, *vecs, *states]
    n_before = len(args)
    out_specs = [spec] * 6
    if vecs:
        shapes += [sds(vecs[0].shape, f32)] * 5 + [sds(vecs[0].shape, bf16)]
        out_specs += [whole(vecs[0].shape)] * 6
    return line.call(
        partial(adam_body, n_alias, bool(vecs)),
        [*args, *(outs or [])],
        [whole(v.shape) for v in [*parts, *small, *vecs]] + [spec] * 4 + [anywhere] * n_alias,
        shapes,
        out_specs,
        grid=(5,) if vecs else (4,),
        flops=20 * 4 * block * D,
        aliases={1 + n_before + i: i for i in range(n_alias)},
        vmem=16,
        name="adam",
    )


def on_device(
    n_seq,
    n_grp,
    tokens,
    cotangent,
    seq_len,
    weight_mats,
    weight_vecs,
    master_mats,
    master_vecs,
    moment_mats,
    moment_vecs,
    square_mats,
    square_vecs,
    average_mats,
    average_vecs,
):
    rows = tokens.shape[0]
    fast = n_seq == 4 and n_grp == 8
    seq_at = lax.axis_index("seq")
    grp_at = lax.axis_index("grp")
    slot = jnp.arange(16, dtype=jnp.int32)
    seq_length = seq_len[0]
    peer = jnp.bitwise_xor(seq_at, jnp.bitwise_and(slot, 3) + 1)
    same = (peer * rows) // seq_length == (seq_at * rows) // seq_length
    before = (same & (peer < seq_at)).astype(jnp.int32)
    after = (same & (peer > seq_at)).astype(jnp.int32)
    scal = jnp.where(slot < 8, before, after)
    scal = jnp.where(slot == S_SEQ, seq_at if fast else 0, scal)
    scal = jnp.where(slot == S_GRP, grp_at, scal)
    line = Line(scal)

    w_t = weight_mats.T
    v_t13 = weight_vecs.T
    n_vec = v_t13.shape[0]
    bias_fc = v_t13[9:].reshape(1, FF)
    wide = QUAD * HD
    n_peer = n_seq - 1
    sel_rows = [D // 2, D // 2] if fast else [D]
    n_sel = len(sel_rows)
    sel_shapes = [sds((2, r, rows), bf16) for r in sel_rows]
    sel_specs = [whole(s.shape) for s in sel_shapes]

    def both(value):
        return [value, swap(value, "grp", 8, 1)] if fast else [value]

    def pair(sel):
        return [sel[1], swap(sel[0], "grp", 8, 1)] if fast else list(sel)

    def w_rows(count, at):
        return pl.BlockSpec((count, D), lambda i, s: (at(i, s), 0))

    hedge_spec = pl.BlockSpec((HD, wide), lambda i, s: ((4 * D + 2 * FF) // HD, i))
    vec_whole = whole(v_t13.shape)
    head_spec, feat_spec = along((wide, rows)), along((2 * wide, rows))
    aug_spec, quad_state = along((QUAD * AUG, rows)), along((QUAD * AUG, 2 * HD))
    st_shape = (HEADS * AUG, 2 * HD)
    got = line.call(
        partial(pre_body, n_sel),
        [tokens, cotangent, w_t, w_t, w_t, w_t, v_t13, v_t13],
        [
            whole((rows, D)),
            whole((rows, D)),
            w_rows(wide, lambda i, s: i),
            w_rows(wide, lambda i, s: N_QUAD + i),
            w_rows(wide, lambda i, s: 2 * N_QUAD + i),
            hedge_spec,
            vec_whole,
            pl.BlockSpec((n_vec, wide), lambda i, s: (0, i)),
        ],
        sel_shapes
        + [
            sds((D, rows), bf16),
            sds((D, rows), bf16),
            sds((2 * D, rows), bf16),
            sds((2 * D, rows), bf16),
            sds((D, rows), bf16),
            sds(st_shape, bf16),
        ],
        sel_specs + [head_spec, head_spec, feat_spec, feat_spec, head_spec, quad_state],
        grid=(N_QUAD,),
        scratch=[pltpu.VMEM((rows, D), bf16)],
        flops=2 * rows * D * 3 * D,
        vmem=32,
        name="pre",
    )
    sel_first = got[:n_sel]
    qt, kt, fq, fk, v_t, s_own = got[n_sel:]
    states = [swap(s_own, "seq", n_seq, k + 1) for k in range(n_peer)]
    sel_first = pair(sel_first)

    (num,) = line.call(
        local_body,
        [fq, fk, v_t],
        [feat_spec, feat_spec, head_spec],
        [sds((HEADS * AUG, rows), f32)],
        [aug_spec],
        grid=(N_QUAD,),
        flops=HEADS * 2 * rows * rows * 256,
        vmem=24,
        name="local",
    )
    got = line.call(
        partial(after_body, n_sel, n_peer),
        [*states, num, fq, tokens, w_t, v_t13],
        [whole(st_shape)] * n_peer
        + [whole(num.shape), whole(fq.shape), whole((rows, D)), w_rows(D, lambda i, s: 3), vec_whole],
        [
            sds((D, rows), f32),
            sds((16, rows), f32),
            sds((rows, D), f32),
            sds((rows, D), bf16),
            sds(st_shape, bf16),
        ]
        + sel_shapes,
        [whole((D, rows)), whole((16, rows)), whole((rows, D)), whole((rows, D)), whole(st_shape)] + sel_specs,
        scratch=[pltpu.VMEM((D, rows), bf16)],
        flops=2 * rows * D * D,
        vmem=32,
        name="after",
    )
    o_t, den, resid, h2, s_in = got[:5]
    sel_second = pair(got[5:])

    n_piece = 2
    piece = FF // n_piece
    wq = piece // 4
    acc, acts, db_fc = [], [], []
    for j in range(n_piece):
        q_of = lambda i, s, j=j: 4 * j + jnp.bitwise_xor(i, s[S_SEQ])
        out_y, out_dh, act, db = line.call(
            partial(mlp_body, j == 0),
            [h2, cotangent, w_t, w_t, bias_fc, *acc],
            [
                whole((rows, D)),
                whole((rows, D)),
                w_rows(wq, lambda i, s: 4 * D // wq + q_of(i, s)),
                w_rows(wq, lambda i, s: (4 * D + FF) // wq + q_of(i, s)),
                pl.BlockSpec((1, wq), lambda i, s: (0, q_of(i, s))),
            ]
            + [whole((rows, D))] * len(acc),
            [sds((rows, D), f32), sds((rows, D), f32), sds((2, 4, rows, wq), bf16), sds((1, piece), f32)],
            [
                whole((rows, D)),
                whole((rows, D)),
                pl.BlockSpec((2, 1, rows, wq), lambda i, s: (0, i, 0, 0)),
                pl.BlockSpec((1, wq), lambda i, s: (0, jnp.bitwise_xor(i, s[S_SEQ]))),
            ],
            grid=(4,),
            flops=4 * 2 * rows * D * piece,
            vmem=32,
            name="mlp",
        )
        acc = [out_y, out_dh]
        db_fc.append(db)
        acts.append(both(act))

    grads = [mlp_grads(line, sel_first, sel_second, acts[0])]
    if fast:
        first = Piece(line, *grads[0])
    block_output, d_resid, d_attn, rho, ds_own, sums = line.call(
        back_body,
        [*acc, resid, cotangent, w_t, v_t13, o_t, den, fq],
        [whole((rows, D))] * 4
        + [w_rows(D, lambda i, s: 3), vec_whole, whole((D, rows)), whole((16, rows)), whole((2 * D, rows))],
        [
            sds((rows, D), bf16),
            sds((rows, D), f32),
            sds((rows, D), bf16),
            sds((HEADS * AUG, rows), bf16),
            sds(st_shape, bf16),
            sds((4, D), f32),
        ],
        [whole((rows, D))] * 3 + [whole((HEADS * AUG, rows)), whole(st_shape), whole((4, D))],
        scratch=[pltpu.VMEM((D, rows), bf16)],
        flops=2 * rows * D * D,
        vmem=32,
        name="back",
    )
    back_states = [swap(ds_own, "seq", n_seq, k + 1) for k in range(n_peer)]
    da = both(d_attn)
    grads.append(mlp_grads(line, sel_first, sel_second, acts[1]))
    if fast:
        second = Piece(line, *grads[1])
        first.one()

    dp, dm, db_qkv = line.call(
        partial(attend_back_body, n_peer),
        [*back_states, fq, fk, v_t, rho, s_in, qt, kt, w_t],
        [quad_state] * n_peer
        + [feat_spec, feat_spec, head_spec, aug_spec, quad_state, head_spec, head_spec, hedge_spec],
        [sds((3, D, rows), bf16), sds((D, HD), f32), sds((D, 3), f32)],
        [along((3, wide, rows), 1), along((wide, HD)), along((wide, 3))],
        grid=(N_QUAD,),
        flops=HEADS * 2 * rows * rows * 768,
        vmem=32,
        name="attend_back",
    )
    dp_both = both(dp)
    if fast:
        second.one()
        first.two()
    db_fc_rows = jnp.concatenate(db_fc, axis=1).reshape(FF // D, D)
    input_grad, *small = line.call(
        partial(input_body, fast),
        [dp, w_t, tokens, d_resid, v_t13, sums, db_fc_rows, db_qkv, dm],
        [
            along((1, D, rows)),
            w_rows(D, lambda i, s: i),
            whole((rows, D)),
            whole((rows, D)),
            vec_whole,
            whole((4, D)),
            whole((FF // D, D)),
            whole((D, 3)),
            whole((D, HD)),
        ],
        [sds((rows, D), bf16)] + [sds((1, r, 2 * HD), f32) for r in sel_rows],
        [whole((rows, D))] + [whole((1, r, 2 * HD)) for r in sel_rows],
        grid=(3,),
        scratch=[pltpu.VMEM((rows, D), f32)],
        flops=2 * rows * D * 3 * D,
        vmem=32,
        name="input",
    )
    tail = tail_grads(line, sel_first, sel_second, dp_both, da)

    states_m = [master_mats, moment_mats, square_mats, average_mats]
    states_v = [v.T for v in (master_vecs, moment_vecs, square_vecs, average_vecs)]
    if fast:
        last = Piece(line, *tail)
        theirs, mine = small
        total = mine[0] + swap(theirs[0].astype(bf16), "grp", 8, 1).astype(f32)
        for bit in (1, 2):
            total = total + swap(total.astype(bf16), "seq", 4, bit).astype(f32)
        total = total.reshape(4, D // 8, 2 * HD)
        low = total.astype(bf16)
        small_own = total[0]
        for k in (1, 2, 3):
            small_own = small_own + swap(low[k], "grp", 8, 2 * k).astype(f32)

        def at_piece(j):
            return lambda i: jnp.where(i < 2, (4 * D + FF) // D + 2 * j + i, 4 + 2 * j + i - 2)

        second.two()
        first.three()
        last.one()
        second.three()
        outs = adam_piece(line, first.parts, states_m, None, at_piece(0))
        last.two()
        outs = adam_piece(line, second.parts, states_m, outs, at_piece(1))
        last.three()
        outs = adam_piece(
            line, last.parts, states_m, outs, lambda i: jnp.where(i < 4, i, (4 * D + 2 * FF) // D),
            small=[small_own], vecs=states_v,
        )
        mats, vecs = outs[:6], [v.T for v in outs[6:]]
    else:

        def joined(send, keep, order):
            parts = {**dict(zip(order[:2], send)), **dict(zip(order[2:], keep))}
            return [parts[q] for q in range(4)]

        fc, dn = [], []
        for send_a, keep_a, send_b, keep_b in grads:
            dn += joined(send_a, keep_a, (1, 3, 0, 2))
            fc += joined(send_b, keep_b, (2, 3, 0, 1))
        send_a, keep_a, send_b, keep_b = tail
        qkvo = joined(send_a, keep_a, (1, 3, 0, 2)) + joined(send_b, keep_b, (2, 3, 0, 1))
        small = small[0][0]
        grad = jnp.concatenate([*qkvo, *fc, *dn, small[:, :HD].astype(bf16)], axis=1)
        own = lax.psum_scatter(grad, "grp", scatter_dimension=0, tiled=True)
        own = lax.psum(own, "seq").astype(f32)
        own_v = lax.psum(lax.psum_scatter(small, "grp", scatter_dimension=0, tiled=True), "seq")
        own_v = own_v[:, HD : HD + n_vec]
        results = adam_math(own, *states_m, learn_rate)
        mats = [own, *results, results[0].astype(bf16)]
        results = adam_math(own_v.T, *states_v, vector_rate)
        vecs = [own_v, *[v.T for v in (*results, results[0].astype(bf16))]]
    flat = [x for pair_ in zip(mats, vecs) for x in pair_]
    return (block_output, input_grad, *flat)


def solution(mesh):
    tok = P(("grp", "seq"), None)
    own = P("grp", None)
    in_specs = (tok, tok, P("grp"), P(), P()) + (own,) * 8
    out_specs = (tok, tok) + (own,) * 12
    body = partial(on_device, mesh.shape["seq"], mesh.shape["grp"])
    return jax.shard_map(body, mesh=mesh, in_specs=in_specs, out_specs=out_specs, check_vma=False)
```

profile of v0, /device:TPU:0, one launch (start us, length us, event | category | flops | bytes accessed | tf_op | source)
XLA Modules:
  0.0 252.5 jit_solution(8417106455435302831)
XLA Ops:
  1.5 1.1 copy-done.6
  2.6 1.1 copy-done.8
  4.5 9.4 %pre.1 = (bf16[2,384,512]{2,1,0:T(8,128)(2,1)S(1)}, bf16[2,384,512]{2,1,0:T(8,128)(2,1)S(1)}, bf16[768,512]{1,0:T(8,128)(2,1)S(1)}, bf16[768,512]{1,0:T(8,128)(2...) custom-call(s32[16]{0:T(128)S(1)} %compare_select_fusion.2.scal, ...), custom_call_target="tpu_custom_call" | custom-call | flops 1811939328 | bytes 8936448 | tf_op jit(solution)/shard_map/pre/pallas_call | solution.py:67
  15.6 4.0 %collective-permute-start.2 = (bf16[960,128]{1,0:T(8,128)(2,1)S(1)}, bf16[960,128]{1,0:T(8,128)(2,1)S(1)}, u32[]{:S(2)}, u32[]{:S(2)}) collective-permute-start(bf16[960,128]{1,0:T(8,128)(2,1)S(1)} %get-tuple-element.231), channel_id=1, source_target_pairs={{0,24},{8,16},{16,8},{24,0},{1,25},{9,17},{17,9},{25,1},{2,26},{10... | collective-permute-start | bytes 737288 | tf_op jit(solution)/shard_map/ppermute | solution.py:539
  20.3 4.0 %local.1.refs_3_ = f32[960,512]{1,0:T(8,128)S(1)} custom-call(s32[16]{0:T(128)S(1)} %compare_select_fusion.2.scal, bf16[1536,512]{1,0:T(8,128)(2,1)S(1)} %get-tuple-element.227.fq_ref.refs_4_.refs_3_, bf16[1536,512]{1,0:T(8,128)(2,1)S(1)} %get-tuple-element.228.fk_ref.refs_4_, bf16[768,512]{1,0:T(8,128)(2,1)S(1)} %get-tuple-element.229.vt_ref.refs_5_), custom_call_target="tpu_custom_call" | custom-call | flops 1610612736 | bytes 5898240 | tf_op jit(solution)/shard_map/local/pallas_call | solution.py:67
  24.3 2.2 collective-permute-done.2.refs_2_
  26.4 4.4 %collective-permute-done.1.refs_1_ = bf16[960,128]{1,0:T(8,128)(2,1)S(1)} collective-permute-done((bf16[960,128]{1,0:T(8,128)(2,1)S(1)}, bf16[960,128]{1,0:T(8,128)(2,1)S(1)}, u32[]{:S(2)}, u32[]{:S(2)}) %collective-permute-start.1) | collective-permute-done | bytes 245792 | tf_op jit(solution)/shard_map/ppermute | solution.py:539
  31.1 4.3 %after.1 = (f32[768,512]{1,0:T(8,128)S(1)}, f32[16,512]{1,0:T(8,128)S(1)}, f32[512,768]{1,0:T(8,128)S(1)}, bf16[512,768]{1,0:T(8,128)(2,1)S(1)}, bf16[960,128]{1...) custom-call(s32[16]{0:T(128)S(1)} %compare_select_fusion.2.scal, ...), custom_call_target="tpu_custom_call" | custom-call | flops 603979776 | bytes 10866176 | tf_op jit(solution)/shard_map/after/pallas_call | solution.py:67
  36.3 5.3 %copy-done = bf16[768,9280]{0,1:T(8,128)(2,1)S(1)} copy-done((bf16[768,9280]{0,1:T(8,128)(2,1)S(1)}, bf16[768,9280]{0,1:T(8,128)(2,1)}, u32[]{:S(2)}) %copy-start) | copy-done | bytes 14254104
  41.6 9.8 %mlp.2 = (f32[512,768]{1,0:T(8,128)S(1)}, f32[512,768]{1,0:T(8,128)S(1)}, bf16[2,4,512,384]{3,2,1,0:T(8,128)(2,1)S(1)}, f32[1,1536]{1,0:T(1,128)S(1)}) custom-call(s32[16]{0:T(128)S(1)} %compare_select_fusion.2.scal, bf16[512,768]{1,0:T(8,128)(2,1)S(1)} %get-tuple-element.241.h2_ref, bf16[512,768]{1,0:T(8,128)(2,1)S(1)} %copy-done.7, ...), custom_call_target="tpu_custom_call" | custom-call | flops 4831838208 | bytes 7876608 | tf_op jit(solution)/shard_map/mlp/pallas_call | solution.py:67
  51.5 11.2 %mlp.3 = (f32[512,768]{1,0:T(8,128)S(1)}, f32[512,768]{1,0:T(8,128)S(1)}, bf16[2,4,512,384]{3,2,1,0:T(8,128)(2,1)S(1)}, f32[1,1536]{1,0:T(1,128)S(1)}) custom-call(s32[16]{0:T(128)S(1)} %compare_select_fusion.2.scal, bf16[512,768]{1,0:T(8,128)(2,1)S(1)} %get-tuple-element.241.h2_ref, bf16[512,768]{1,0:T(8,128)(2,1)S(1)} %copy-done.7, ...), custom_call_target="tpu_custom_call" | custom-call | flops 4831838208 | bytes 11022336 | tf_op jit(solution)/shard_map/mlp/pallas_call | solution.py:67
  63.8 5.9 %collective-permute-done.3.refs_1_ = bf16[2,384,512]{2,1,0:T(8,128)(2,1)S(1)} collective-permute-done((bf16[2,384,512]{2,1,0:T(8,128)(2,1)S(1)}, bf16[2,384,512]{2,1,0:T(8,128)(2,1)S(1)}, u32[]{:S(2)}, u32[]{:S(2)}) %collective-permute-start.3) | collective-permute-done | bytes 786464 | tf_op jit(solution)/shard_map/ppermute | solution.py:539
  69.7 1.1 collective-permute-done.5.refs_7_.refs_3_
  70.8 6.3 %mlp_grads.2 = (bf16[2,384,384]{2,1,0:T(8,128)(2,1)}, bf16[2,384,384]{2,1,0:T(8,128)(2,1)S(1)}, bf16[2,384,384]{2,1,0:T(8,128)(2,1)}, bf16[2,384,384]{2,1,0:T(8,128)(2,1)S(1)}) custom-call(s32[16]{0:T(128)S(1)} %compare_select_fusion.2.scal, bf16[2,384,512]{2,1,0:T(8,128)(2,1)S(1)} %get-tuple-element.254.refs_0_, ...), custom_call_target="tpu_custom_call" | custom-call | flops 2415919104 | bytes 18087936 | tf_op jit(solution)/shard_map/mlp_grads/pallas_call | solution.py:67
  77.1 1.5 collective-permute-start.7
  79.2 4.3 %back.1 = (bf16[512,768]{1,0:T(8,128)(2,1)}, f32[512,768]{1,0:T(8,128)S(1)}, bf16[512,768]{1,0:T(8,128)(2,1)}, bf16[960,512]{1,0:T(8,128)(2,1)S(1)}, bf16[960,128]{1,0:T(8,128)(2,1)S(1)}, /*index=5*/f32[4,768]{1,0:T(4,128)S(1)}) custom-call(s32[16]{0:T(128)S(1)} %compare_select_fusion.2.scal, f32[512,768]{1,0:T(8,128)S(1)} %get-tuple-element.264.out_ref, ...), custom_call_target="tpu_custom_call" | custom-call | flops 603979776 | bytes 13090304 | tf_op jit(solution)/shard_map/back/pallas_call | solution.py:67
  83.6 1.1 copy-done.35
  84.7 1.4 collective-permute-start.11
  86.1 1.4 collective-permute-start.10
  88.2 6.2 %mlp_grads.3 = (bf16[2,384,384]{2,1,0:T(8,128)(2,1)S(1)}, bf16[2,384,384]{2,1,0:T(8,128)(2,1)S(1)}, bf16[2,384,384]{2,1,0:T(8,128)(2,1)}, bf16[2,384,384]{2,1,0:T(8,128)(2,1)S(1)}) custom-call(s32[16]{0:T(128)S(1)} %compare_select_fusion.2.scal, bf16[2,384,512]{2,1,0:T(8,128)(2,1)S(1)} %get-tuple-element.254.refs_0_, ...), custom_call_target="tpu_custom_call" | custom-call | flops 2415919104 | bytes 18087936 | tf_op jit(solution)/shard_map/mlp_grads/pallas_call | solution.py:67
  94.4 5.9 %collective-permute-done.8.recv_b = bf16[2,384,384]{2,1,0:T(8,128)(2,1)S(1)} collective-permute-done((bf16[2,384,384]{2,1,0:T(8,128)(2,1)}, bf16[2,384,384]{2,1,0:T(8,128)(2,1)S(1)}, u32[]{:S(2)}, u32[]{:S(2)}) %collective-permute-start.8) | collective-permute-done | bytes 589856 | tf_op jit(solution)/shard_map/ppermute | solution.py:539
  100.3 1.4 add_one.3
  101.7 2.9 %collective-permute-done.10.refs_1_ = bf16[960,128]{1,0:T(8,128)(2,1)S(1)} collective-permute-done((bf16[960,128]{1,0:T(8,128)(2,1)S(1)}, bf16[960,128]{1,0:T(8,128)(2,1)S(1)}, u32[]{:S(2)}, u32[]{:S(2)}) %collective-permute-start.10) | collective-permute-done | bytes 245792 | tf_op jit(solution)/shard_map/ppermute | solution.py:539
  104.7 12.8 %attend_back.1 = (bf16[3,768,512]{2,1,0:T(8,128)(2,1)S(1)}, f32[768,64]{1,0:T(8,128)S(1)}, f32[768,3]{1,0:T(8,128)S(1)}) custom-call(s32[16]{0:T(128)S(1)} %compare_select_fusion.2.scal, bf16[960,128]{1,0:T(8,128)(2,1)S(1)} %collective-permute-done.9.refs_0_, bf16[960,128]{1,0:T(8,128)(2,1)S(1)} %collective-permute-done.10.refs_1_, ...), custom_call_target="tpu_custom_call" | custom-call | flops 4831838208 | bytes 10036224 | tf_op jit(solution)/shard_map/attend_back/pallas_call | solution.py:67
  119.8 1.4 collective-permute-start.13
  121.9 12.9 %collective-permute-done.12.recv_a = bf16[2,384,384]{2,1,0:T(8,128)(2,1)S(1)} collective-permute-done((bf16[2,384,384]{2,1,0:T(8,128)(2,1)S(1)}, bf16[2,384,384]{2,1,0:T(8,128)(2,1)S(1)}, u32[]{:S(2)}, u32[]{:S(2)}) %collective-permute-start.12) | collective-permute-done | bytes 589856 | tf_op jit(solution)/shard_map/ppermute | solution.py:539
  136.3 1.1 copy-done.19
  137.4 1.1 copy-done.22
  138.5 1.1 copy-done.29
  139.5 1.6 add_one.4
  141.2 1.5 collective-permute-start.18
  143.4 1.4 collective-permute-done.15.far_b
  144.8 1.1 copy-done.25
  145.8 1.1 copy-done.27
  146.9 1.1 copy-done.32
  148.0 1.1 copy-done.34
  149.0 1.7 add_two.3
  150.8 5.0 %copy-done.1 = bf16[768,9280]{0,1:T(8,128)(2,1)S(1)} copy-done((bf16[768,9280]{0,1:T(8,128)(2,1)S(1)}, bf16[768,9280]{0,1:T(8,128)(2,1)}, u32[]{:S(2)}) %copy-start.1) | copy-done | bytes 14254104
  157.8 6.1 %input.1 = (bf16[512,768]{1,0:T(8,128)(2,1)}, f32[1,384,128]{2,1,0:T(8,128)S(1)}, f32[1,384,128]{2,1,0:T(8,128)S(1)}) custom-call(s32[16]{0:T(128)S(1)} %compare_select_fusion.2.scal, bf16[3,768,512]{2,1,0:T(8,128)(2,1)S(1)} %get-tuple-element.313.dp_ref, bf16[9280,768]{1,0:T(8,128)(2,1)S(1)} %bitcast.45, bf16[512,768]{1,0:T(8,128)(2,1)S(1)} %copy-done.9, ...), custom_call_target="tpu_custom_call" | custom-call | flops 1811939328 | bytes 6148608 | tf_op jit(solution)/shard_map/input/pallas_call | solution.py:67
  164.0 7.4 %tail_grads.1 = (bf16[2,384,384]{2,1,0:T(8,128)(2,1)S(1)}, bf16[2,384,384]{2,1,0:T(8,128)(2,1)S(1)}, bf16[2,384,384]{2,1,0:T(8,128)(2,1)S(1)}, bf16[2,384,384]{2,1,0:T(8,128)(2,1)S(1)}) custom-call(s32[16]{0:T(128)S(1)} %compare_select_fusion.2.scal, bf16[2,384,512]{2,1,0:T(8,128)(2,1)S(1)} %copy-done.11, bf16[2,384,512]{2,1,0:T(8,128)(2,1)S(1)} %copy-done.15, ...), custom_call_target="tpu_custom_call" | custom-call | flops 2415919104 | bytes 16515072 | tf_op jit(solution)/shard_map/tail_grads/pallas_call | solution.py:67
  172.0 1.5 collective-permute-start.24
  173.5 1.6 collective-permute-start.20
  175.1 2.6 %collective-permute-start.21 = (bf16[2,96,384]{2,1,0:T(8,128)(2,1)S(1)}, bf16[2,96,384]{2,1,0:T(8,128)(2,1)S(1)}, u32[]{:S(2)}, u32[]{:S(2)}) collective-permute-start(bf16[2,96,384]{2,1,0:T(8,128)(2,1)S(1)} %get-tuple-element.340), channel_id=1, source_target_pairs={{0,4},{1,5},{2,6},{3,7},{4,0},{5,1},{6,2},{7,3},{8,12},{9,13},{10,... | collective-permute-start | bytes 442376 | tf_op jit(solution)/shard_map/ppermute | solution.py:539
  178.0 3.9 %collective-permute-done.20.refs_0_ = bf16[2,96,384]{2,1,0:T(8,128)(2,1)S(1)} collective-permute-done((bf16[2,96,384]{2,1,0:T(8,128)(2,1)S(1)}, bf16[2,96,384]{2,1,0:T(8,128)(2,1)S(1)}, u32[]{:S(2)}, u32[]{:S(2)}) %collective-permute-start.20) | collective-permute-done | bytes 147488 | tf_op jit(solution)/shard_map/ppermute | solution.py:539
  182.5 1.7 add_two.4
  184.2 4.9 %collective-permute-done.21.refs_1_ = bf16[2,96,384]{2,1,0:T(8,128)(2,1)S(1)} collective-permute-done((bf16[2,96,384]{2,1,0:T(8,128)(2,1)S(1)}, bf16[2,96,384]{2,1,0:T(8,128)(2,1)S(1)}, u32[]{:S(2)}, u32[]{:S(2)}) %collective-permute-start.21) | collective-permute-done | bytes 147488 | tf_op jit(solution)/shard_map/ppermute | solution.py:539
  189.7 1.6 collective-permute-start.30
  191.3 2.7 %collective-permute-start.25 = (bf16[2,96,384]{2,1,0:T(8,128)(2,1)S(1)}, bf16[2,96,384]{2,1,0:T(8,128)(2,1)S(1)}, u32[]{:S(2)}, u32[]{:S(2)}) collective-permute-start(bf16[2,96,384]{2,1,0:T(8,128)(2,1)S(1)} %get-tuple-element.351), channel_id=1, source_target_pairs={{0,2},{1,3},{2,0},{3,1},{4,6},{5,7},{6,4},{7,5},{8,10},{9,11},{10,... | collective-permute-start | bytes 442376 | tf_op jit(solution)/shard_map/ppermute | solution.py:539
  195.0 1.5 collective-permute-start.27
  199.5 7.6 %collective-permute-done.26.refs_1_ = bf16[2,96,384]{2,1,0:T(8,128)(2,1)S(1)} collective-permute-done((bf16[2,96,384]{2,1,0:T(8,128)(2,1)S(1)}, bf16[2,96,384]{2,1,0:T(8,128)(2,1)S(1)}, u32[]{:S(2)}, u32[]{:S(2)}) %collective-permute-start.26) | collective-permute-done | bytes 147488 | tf_op jit(solution)/shard_map/ppermute | solution.py:539
  207.6 1.5 collective-permute-start.29
  210.5 1.3 collective-permute-start.35
  211.8 1.9 collective-permute-done.29.refs_2_
  214.6 2.4 collective-permute-done.28.refs_1_
  217.5 4.7 %adam.3 = (f32[96,9280]{1,0:T(8,128)}, f32[96,9280]{1,0:T(8,128)}, f32[96,9280]{1,0:T(8,128)}, f32[96,9280]{1,0:T(8,128)}, f32[96,9280]{1,0:T(8,128)}, /*index=5*/bf16[96,9280]{1,0:T(8,128)(2,1)}) custom-call(s32[16]{0:T(128)S(1)} %compare_select_fusion.2.scal, bf16[2,96,384]{2,1,0:T(8,128)(2,1)S(1)} %add_three.3.refs_0_, ...), custom_call_target="tpu_custom_call" | custom-call | flops 5898240 | bytes 34443264 | tf_op jit(solution)/shard_map/adam/pallas_call | solution.py:67
  222.9 1.3 collective-permute-start.36
  224.2 4.5 %collective-permute-start.37 = (bf16[2,96,384]{2,1,0:T(8,128)(2,1)S(1)}, bf16[2,96,384]{2,1,0:T(8,128)(2,1)S(1)}, u32[]{:S(2)}, u32[]{:S(2)}) collective-permute-start(bf16[2,96,384]{2,1,0:T(8,128)(2,1)S(1)} %get-tuple-element.386), channel_id=1, source_target_pairs={{0,4},{1,5},{2,6},{3,7},{4,0},{5,1},{6,2},{7,3},{8,12},{9,13},{10,... | collective-permute-start | bytes 442376 | tf_op jit(solution)/shard_map/ppermute | solution.py:539
  229.4 3.3 %collective-permute-start.47 = (bf16[96,128]{1,0:T(8,128)(2,1)S(1)}, bf16[96,128]{1,0:T(8,128)(2,1)S(1)}, u32[]{:S(2)}, u32[]{:S(2)}) collective-permute-start(bf16[96,128]{1,0:T(8,128)(2,1)S(1)} %get-tuple-element.425), channel_id=1, source_target_pairs={{0,6},{1,7},{2,4},{3,5},{4,2},{5,3},{6,0},{7,1},{8,14},{9,15},{10,... | collective-permute-start | bytes 73736 | tf_op jit(solution)/shard_map/ppermute | solution.py:539
  233.3 4.7 %adam.4 = (f32[96,9280]{1,0:T(8,128)}, f32[96,9280]{1,0:T(8,128)}, f32[96,9280]{1,0:T(8,128)}, f32[96,9280]{1,0:T(8,128)}, f32[96,9280]{1,0:T(8,128)}, /*index=5*/bf16[96,9280]{1,0:T(8,128)(2,1)}) custom-call(s32[16]{0:T(128)S(1)} %compare_select_fusion.2.scal, ...), custom_call_target="tpu_custom_call", output_to_operand_aliasing={{0}: (9, {}), {1}: (10, {}), {2}: (11, {}), {3}: (12, {}), ... | custom-call | flops 5898240 | bytes 54042624 | tf_op jit(solution)/shard_map/adam/pallas_call | solution.py:67
  238.6 1.7 collective-permute-start.41
  240.4 1.4 collective-permute-start.40
  242.2 2.6 %collective-permute-done.41.refs_3_ = bf16[2,96,384]{2,1,0:T(8,128)(2,1)S(1)} collective-permute-done((bf16[2,96,384]{2,1,0:T(8,128)(2,1)S(1)}, bf16[2,96,384]{2,1,0:T(8,128)(2,1)S(1)}, u32[]{:S(2)}, u32[]{:S(2)}) %collective-permute-start.41) | collective-permute-done | bytes 147488 | tf_op jit(solution)/shard_map/ppermute | solution.py:539
  244.8 1.5 collective-permute-done.40.refs_2_
  246.9 5.3 %adam.5 = (f32[96,9280]{1,0:T(8,128)}, f32[96,9280]{1,0:T(8,128)}, f32[96,9280]{1,0:T(8,128)}, f32[96,9280]{1,0:T(8,128)}, f32[96,9280]{1,0:T(8,128)}, /*index=5...) custom-call(s32[16]{0:T(128)S(1)} %compare_select_fusion.2.scal, ...), custom_call_target="tpu_custom_call", output_to_operand_aliasing={{0}: (14, {}), {1}: (15, {}), {2}: (16, {}), {3}: (17, {}),... | custom-call | flops 5898240 | bytes 54139200 | tf_op jit(solution)/shard_map/adam/pallas_call | solution.py:67
  (180 shorter events, 27.0 us)
Async XLA Ops:
  15.6 72.6 %copy-start.10 = (bf16[2,384,512]{2,1,0:T(8,128)(2,1)}, bf16[2,384,512]{2,1,0:T(8,128)(2,1)S(1)}, u32[]{:S(2)}) copy-start(bf16[2,384,512]{2,1,0:T(8,128)(2,1)S(1)} %get-tuple-element.254.refs_0_) | copy-start | bytes 2359300
  15.6 10.8 %collective-permute-start.2 = (bf16[960,128]{1,0:T(8,128)(2,1)S(1)}, bf16[960,128]{1,0:T(8,128)(2,1)S(1)}, u32[]{:S(2)}, u32[]{:S(2)}) collective-permute-start(bf16[960,128]{1,0:T(8,128)(2,1)S(1)} %get-tuple-element.231), channel_id=1, source_target_pairs={{0,24},{8,16},{16,8},{24,0},{1,25},{9,17},{17,9},{25,1},{2,26},{10... | collective-permute-start | bytes 737288 | tf_op jit(solution)/shard_map/ppermute | solution.py:539
  19.6 11.2 %collective-permute-start.1 = (bf16[960,128]{1,0:T(8,128)(2,1)S(1)}, bf16[960,128]{1,0:T(8,128)(2,1)S(1)}, u32[]{:S(2)}, u32[]{:S(2)}) collective-permute-start(bf16[960,128]{1,0:T(8,128)(2,1)S(1)} %get-tuple-element.231), channel_id=1, source_target_pairs={{0,16},{8,24},{16,0},{24,8},{1,17},{9,25},{17,1},{25,9},{2,18},{10... | collective-permute-start | bytes 737288 | tf_op jit(solution)/shard_map/ppermute | solution.py:539
  20.1 11.0 %collective-permute-start = (bf16[960,128]{1,0:T(8,128)(2,1)S(1)}, bf16[960,128]{1,0:T(8,128)(2,1)S(1)}, u32[]{:S(2)}, u32[]{:S(2)}) collective-permute-start(bf16[960,128]{1,0:T(8,128)(2,1)S(1)} %get-tuple-element.231), channel_id=1, source_target_pairs={{0,8},{8,0},{16,24},{24,16},{1,9},{9,1},{17,25},{25,17},{2,10},{10... | collective-permute-start | bytes 737288 | tf_op jit(solution)/shard_map/ppermute | solution.py:539
  36.3 51.9 %copy-start.12 = (bf16[2,384,512]{2,1,0:T(8,128)(2,1)}, bf16[2,384,512]{2,1,0:T(8,128)(2,1)S(1)}, u32[]{:S(2)}) copy-start(bf16[2,384,512]{2,1,0:T(8,128)(2,1)S(1)} %get-tuple-element.257.refs_6_.refs_2_) | copy-start | bytes 2359300
  51.4 19.4 %collective-permute-start.4 = (bf16[2,4,512,384]{3,2,1,0:T(8,128)(2,1)S(1)}, bf16[2,4,512,384]{3,2,1,0:T(8,128)(2,1)S(1)}, u32[]{:S(2)}, u32[]{:S(2)}) collective-permute-start(bf16[2,4,512,384]{3,2,1,0:T(8,128)(2,1)S(1)} %get-tuple-element.256.refs_2_.refs_4_), channel_id=1, source_target_pairs={{0,1},{1,0},{2,3},{3,2},{4,5},{5,4},{6,7},{7,6},{8,9},{9,8},{10,11... | collective-permute-start | bytes 9437192 | tf_op jit(solution)/shard_map/ppermute | solution.py:539
  62.7 24.8 %collective-permute-start.6 = (bf16[2,4,512,384]{3,2,1,0:T(8,128)(2,1)S(1)}, bf16[2,4,512,384]{3,2,1,0:T(8,128)(2,1)S(1)}, u32[]{:S(2)}, u32[]{:S(2)}) collective-permute-start(bf16[2,4,512,384]{3,2,1,0:T(8,128)(2,1)S(1)} %get-tuple-element.277.refs_2_.refs_4_), channel_id=1, source_target_pairs={{0,1},{1,0},{2,3},{3,2},{4,5},{5,4},{6,7},{7,6},{8,9},{9,8},{10,11... | collective-permute-start | bytes 9437192 | tf_op jit(solution)/shard_map/ppermute | solution.py:539
  63.3 6.4 %collective-permute-start.3 = (bf16[2,384,512]{2,1,0:T(8,128)(2,1)S(1)}, bf16[2,384,512]{2,1,0:T(8,128)(2,1)S(1)}, u32[]{:S(2)}, u32[]{:S(2)}) collective-permute-start(bf16[2,384,512]{2,1,0:T(8,128)(2,1)S(1)} %copy-done.54), channel_id=1, source_target_pairs={{0,1},{1,0},{2,3},{3,2},{4,5},{5,4},{6,7},{7,6},{8,9},{9,8},{10,11... | collective-permute-start | bytes 2359304 | tf_op jit(solution)/shard_map/ppermute | solution.py:539
  63.4 7.4 %collective-permute-start.5 = (bf16[2,384,512]{2,1,0:T(8,128)(2,1)S(1)}, bf16[2,384,512]{2,1,0:T(8,128)(2,1)S(1)}, u32[]{:S(2)}, u32[]{:S(2)}) collective-permute-start(bf16[2,384,512]{2,1,0:T(8,128)(2,1)S(1)} %copy-done.56), channel_id=1, source_target_pairs={{0,1},{1,0},{2,3},{3,2},{4,5},{5,4},{6,7},{7,6},{8,9},{9,8},{10,11... | collective-permute-start | bytes 2359304 | tf_op jit(solution)/shard_map/ppermute | solution.py:539
  77.1 23.2 %copy-start.24 = (bf16[2,384,384]{2,1,0:T(8,128)(2,1)}, bf16[2,384,384]{2,1,0:T(8,128)(2,1)S(1)}, u32[]{:S(2)}) copy-start(bf16[2,384,384]{2,1,0:T(8,128)(2,1)S(1)} %get-tuple-element.283.keep_a) | copy-start | bytes 1769476
  77.1 23.2 %copy-start.26 = (bf16[2,384,384]{2,1,0:T(8,128)(2,1)}, bf16[2,384,384]{2,1,0:T(8,128)(2,1)S(1)}, u32[]{:S(2)}) copy-start(bf16[2,384,384]{2,1,0:T(8,128)(2,1)S(1)} %get-tuple-element.285.keep_b) | copy-start | bytes 1769476
  77.1 17.3 %collective-permute-start.7 = (bf16[2,384,384]{2,1,0:T(8,128)(2,1)}, bf16[2,384,384]{2,1,0:T(8,128)(2,1)S(1)}, u32[]{:S(2)}, u32[]{:S(2)}) collective-permute-start(bf16[2,384,384]{2,1,0:T(8,128)(2,1)} %get-tuple-element.284), channel_id=1, source_target_pairs={{0,8},{8,0},{16,24},{24,16},{1,9},{9,1},{17,25},{25,17},{2,10},{10... | collective-permute-start | bytes 1769480 | tf_op jit(solution)/shard_map/ppermute | solution.py:539
  78.6 21.7 %collective-permute-start.8 = (bf16[2,384,384]{2,1,0:T(8,128)(2,1)}, bf16[2,384,384]{2,1,0:T(8,128)(2,1)S(1)}, u32[]{:S(2)}, u32[]{:S(2)}) collective-permute-start(bf16[2,384,384]{2,1,0:T(8,128)(2,1)} %get-tuple-element.286), channel_id=1, source_target_pairs={{0,16},{8,24},{16,0},{24,8},{1,17},{9,25},{17,1},{25,9},{2,18},{10... | collective-permute-start | bytes 1769480 | tf_op jit(solution)/shard_map/ppermute | solution.py:539
  84.7 20.0 %copy-start.38 = (bf16[768,512]{1,0:T(8,128)(2,1)S(1)}, bf16[768,512]{1,0:T(8,128)(2,1)}, u32[]{:S(2)}) copy-start(bf16[768,512]{1,0:T(8,128)(2,1)} %copy-done.37) | copy-start | bytes 2359300
  84.7 20.0 %copy-start.40 = (bf16[768,512]{1,0:T(8,128)(2,1)S(1)}, bf16[768,512]{1,0:T(8,128)(2,1)}, u32[]{:S(2)}) copy-start(bf16[768,512]{1,0:T(8,128)(2,1)} %copy-done.39) | copy-start | bytes 2359300
  84.7 20.0 %copy-start.42 = (bf16[768,512]{1,0:T(8,128)(2,1)S(1)}, bf16[768,512]{1,0:T(8,128)(2,1)}, u32[]{:S(2)}) copy-start(bf16[768,512]{1,0:T(8,128)(2,1)} %copy-done.41) | copy-start | bytes 2359300
  84.7 17.0 %collective-permute-start.11 = (bf16[960,128]{1,0:T(8,128)(2,1)S(1)}, bf16[960,128]{1,0:T(8,128)(2,1)S(1)}, u32[]{:S(2)}, u32[]{:S(2)}) collective-permute-start(bf16[960,128]{1,0:T(8,128)(2,1)S(1)} %get-tuple-element.290), channel_id=1, source_target_pairs={{0,24},{8,16},{16,8},{24,0},{1,25},{9,17},{17,9},{25,1},{2,26},{10... | collective-permute-start | bytes 737288 | tf_op jit(solution)/shard_map/ppermute | solution.py:539
  86.1 18.6 %collective-permute-start.10 = (bf16[960,128]{1,0:T(8,128)(2,1)S(1)}, bf16[960,128]{1,0:T(8,128)(2,1)S(1)}, u32[]{:S(2)}, u32[]{:S(2)}) collective-permute-start(bf16[960,128]{1,0:T(8,128)(2,1)S(1)} %get-tuple-element.290), channel_id=1, source_target_pairs={{0,16},{8,24},{16,0},{24,8},{1,17},{9,25},{17,1},{25,9},{2,18},{10... | collective-permute-start | bytes 737288 | tf_op jit(solution)/shard_map/ppermute | solution.py:539
  87.5 17.1 %collective-permute-start.9 = (bf16[960,128]{1,0:T(8,128)(2,1)S(1)}, bf16[960,128]{1,0:T(8,128)(2,1)S(1)}, u32[]{:S(2)}, u32[]{:S(2)}) collective-permute-start(bf16[960,128]{1,0:T(8,128)(2,1)S(1)} %get-tuple-element.290), channel_id=1, source_target_pairs={{0,8},{8,0},{16,24},{24,16},{1,9},{9,1},{17,25},{25,17},{2,10},{10... | collective-permute-start | bytes 737288 | tf_op jit(solution)/shard_map/ppermute | solution.py:539
  94.4 23.2 %copy-start.18 = (bf16[2,384,384]{2,1,0:T(8,128)(2,1)}, bf16[2,384,384]{2,1,0:T(8,128)(2,1)S(1)}, u32[]{:S(2)}) copy-start(bf16[2,384,384]{2,1,0:T(8,128)(2,1)S(1)} %get-tuple-element.299.keep_a) | copy-start | bytes 1769476
  94.4 23.2 %copy-start.21 = (bf16[2,384,384]{2,1,0:T(8,128)(2,1)}, bf16[2,384,384]{2,1,0:T(8,128)(2,1)S(1)}, u32[]{:S(2)}) copy-start(bf16[2,384,384]{2,1,0:T(8,128)(2,1)S(1)} %get-tuple-element.301.keep_b) | copy-start | bytes 1769476
  94.4 23.2 %copy-start.31 = (bf16[2,384,384]{2,1,0:T(8,128)(2,1)}, bf16[2,384,384]{2,1,0:T(8,128)(2,1)S(1)}, u32[]{:S(2)}) copy-start(bf16[2,384,384]{2,1,0:T(8,128)(2,1)S(1)} %collective-permute-done.7.recv_a) | copy-start | bytes 1769476
  119.1 31.7 %copy-start.9 = (bf16[512,768]{1,0:T(8,128)(2,1)S(1)}, bf16[512,768]{1,0:T(8,128)(2,1)}, u32[]{:S(2)}) copy-start(bf16[512,768]{1,0:T(8,128)(2,1)} %x_ref.3) | copy-start | bytes 2359300
  119.1 44.8 %collective-permute-start.16 = (bf16[3,768,512]{2,1,0:T(8,128)(2,1)S(1)}, bf16[3,768,512]{2,1,0:T(8,128)(2,1)}, u32[]{:S(2)}, u32[]{:S(2)}) collective-permute-start(bf16[3,768,512]{2,1,0:T(8,128)(2,1)S(1)} %get-tuple-element.313.dp_ref), channel_id=1, source_target_pairs={{0,1},{1,0},{2,3},{3,2},{4,5},{5,4},{6,7},{7,6},{8,9},{9,8},{10,11... | collective-permute-start | bytes 7077896 | tf_op jit(solution)/shard_map/ppermute | solution.py:539
  119.1 15.7 %collective-permute-start.12 = (bf16[2,384,384]{2,1,0:T(8,128)(2,1)S(1)}, bf16[2,384,384]{2,1,0:T(8,128)(2,1)S(1)}, u32[]{:S(2)}, u32[]{:S(2)}) collective-permute-start(bf16[2,384,384]{2,1,0:T(8,128)(2,1)S(1)} %get-tuple-element.300), channel_id=1, source_target_pairs={{0,8},{8,0},{16,24},{24,16},{1,9},{9,1},{17,25},{25,17},{2,10},{10... | collective-permute-start | bytes 1769480 | tf_op jit(solution)/shard_map/ppermute | solution.py:539
  119.6 44.3 %collective-permute-start.17 = (bf16[512,768]{1,0:T(8,128)(2,1)}, bf16[512,768]{1,0:T(8,128)(2,1)}, u32[]{:S(2)}, u32[]{:S(2)}) collective-permute-start(bf16[512,768]{1,0:T(8,128)(2,1)} %get-tuple-element.325.refs_8_), channel_id=1, source_target_pairs={{0,1},{1,0},{2,3},{3,2},{4,5},{5,4},{6,7},{7,6},{8,9},{9,8},{10,11... | collective-permute-start | bytes 2359304 | tf_op jit(solution)/shard_map/ppermute | solution.py:539
  119.8 16.5 %collective-permute-start.13 = (bf16[2,384,384]{2,1,0:T(8,128)(2,1)}, bf16[2,384,384]{2,1,0:T(8,128)(2,1)}, u32[]{:S(2)}, u32[]{:S(2)}) collective-permute-start(bf16[2,384,384]{2,1,0:T(8,128)(2,1)} %get-tuple-element.302), channel_id=1, source_target_pairs={{0,16},{8,24},{16,0},{24,8},{1,17},{9,25},{17,1},{25,9},{2,18},{10... | collective-permute-start | bytes 1769480 | tf_op jit(solution)/shard_map/ppermute | solution.py:539
  121.3 21.4 %collective-permute-start.14 = (bf16[384,384]{1,0:T(8,128)(2,1)}, bf16[384,384]{1,0:T(8,128)(2,1)S(1)}, u32[]{:S(2)}, u32[]{:S(2)}) collective-permute-start(bf16[384,384]{1,0:T(8,128)(2,1)} %get-tuple-element.306), channel_id=1, source_target_pairs={{0,16},{8,24},{16,0},{24,8},{1,17},{9,25},{17,1},{25,9},{2,18},{10... | collective-permute-start | bytes 884744 | tf_op jit(solution)/shard_map/ppermute | solution.py:539
  135.6 9.1 %collective-permute-start.15 = (bf16[384,384]{1,0:T(8,128)(2,1)}, bf16[384,384]{1,0:T(8,128)(2,1)}, u32[]{:S(2)}, u32[]{:S(2)}) collective-permute-start(bf16[384,384]{1,0:T(8,128)(2,1)} %get-tuple-element.307), channel_id=1, source_target_pairs={{0,8},{8,0},{16,24},{24,16},{1,9},{9,1},{17,25},{25,17},{2,10},{10... | collective-permute-start | bytes 884744 | tf_op jit(solution)/shard_map/ppermute | solution.py:539
  141.2 32.4 %collective-permute-start.18 = (bf16[384,384]{1,0:T(8,128)(2,1)S(1)}, bf16[384,384]{1,0:T(8,128)(2,1)S(1)}, u32[]{:S(2)}, u32[]{:S(2)}) collective-permute-start(bf16[384,384]{1,0:T(8,128)(2,1)S(1)} %get-tuple-element.331), channel_id=1, source_target_pairs={{0,16},{8,24},{16,0},{24,8},{1,17},{9,25},{17,1},{25,9},{2,18},{10... | collective-permute-start | bytes 884744 | tf_op jit(solution)/shard_map/ppermute | solution.py:539
  142.7 32.4 %collective-permute-start.19 = (bf16[384,384]{1,0:T(8,128)(2,1)S(1)}, bf16[384,384]{1,0:T(8,128)(2,1)S(1)}, u32[]{:S(2)}, u32[]{:S(2)}) collective-permute-start(bf16[384,384]{1,0:T(8,128)(2,1)S(1)} %get-tuple-element.332), channel_id=1, source_target_pairs={{0,8},{8,0},{16,24},{24,16},{1,9},{9,1},{17,25},{25,17},{2,10},{10... | collective-permute-start | bytes 884744 | tf_op jit(solution)/shard_map/ppermute | solution.py:539
  163.9 18.5 %copy-start.20 = (bf16[2,384,384]{2,1,0:T(8,128)(2,1)S(1)}, bf16[2,384,384]{2,1,0:T(8,128)(2,1)}, u32[]{:S(2)}) copy-start(bf16[2,384,384]{2,1,0:T(8,128)(2,1)} %copy-done.18) | copy-start | bytes 1769476
  164.0 53.5 %copy-start.4 = (f32[96,9280]{1,0:T(8,128)S(1)}, f32[96,9280]{1,0:T(8,128)}, u32[]{:S(2)}) copy-start(f32[96,9280]{1,0:T(8,128)} %refs_11_.1) | copy-start | bytes 10690564
  164.0 53.5 %copy-start.5 = (f32[96,9280]{1,0:T(8,128)S(1)}, f32[96,9280]{1,0:T(8,128)}, u32[]{:S(2)}) copy-start(f32[96,9280]{1,0:T(8,128)} %refs_12_.1) | copy-start | bytes 10690564
  171.4 23.6 %collective-permute-start.23 = (bf16[2,384,384]{2,1,0:T(8,128)(2,1)S(1)}, bf16[2,384,384]{2,1,0:T(8,128)(2,1)S(1)}, u32[]{:S(2)}, u32[]{:S(2)}) collective-permute-start(bf16[2,384,384]{2,1,0:T(8,128)(2,1)S(1)} %get-tuple-element.344), channel_id=1, source_target_pairs={{0,8},{8,0},{16,24},{24,16},{1,9},{9,1},{17,25},{25,17},{2,10},{10... | collective-permute-start | bytes 1769480 | tf_op jit(solution)/shard_map/ppermute | solution.py:539
  171.9 5.8 %collective-permute-start.42 = (bf16[384,128]{1,0:T(8,128)(2,1)S(1)}, bf16[384,128]{1,0:T(8,128)(2,1)S(1)}, u32[]{:S(2)}, u32[]{:S(2)}) collective-permute-start(bf16[384,128]{1,0:T(8,128)(2,1)S(1)} %convert_bitcast_fusion), channel_id=1, source_target_pairs={{0,1},{1,0},{2,3},{3,2},{4,5},{5,4},{6,7},{7,6},{8,9},{9,8},{10,11... | collective-permute-start | bytes 294920 | tf_op jit(solution)/shard_map/ppermute | solution.py:539
  172.0 24.6 %collective-permute-start.24 = (bf16[2,384,384]{2,1,0:T(8,128)(2,1)S(1)}, bf16[2,384,384]{2,1,0:T(8,128)(2,1)S(1)}, u32[]{:S(2)}, u32[]{:S(2)}) collective-permute-start(bf16[2,384,384]{2,1,0:T(8,128)(2,1)S(1)} %get-tuple-element.346), channel_id=1, source_target_pairs={{0,16},{8,24},{16,0},{24,8},{1,17},{9,25},{17,1},{25,9},{2,18},{10... | collective-permute-start | bytes 1769480 | tf_op jit(solution)/shard_map/ppermute | solution.py:539
  173.5 8.4 %collective-permute-start.20 = (bf16[2,96,384]{2,1,0:T(8,128)(2,1)S(1)}, bf16[2,96,384]{2,1,0:T(8,128)(2,1)S(1)}, u32[]{:S(2)}, u32[]{:S(2)}) collective-permute-start(bf16[2,96,384]{2,1,0:T(8,128)(2,1)S(1)} %get-tuple-element.339), channel_id=1, source_target_pairs={{0,2},{1,3},{2,0},{3,1},{4,6},{5,7},{6,4},{7,5},{8,10},{9,11},{10,... | collective-permute-start | bytes 442376 | tf_op jit(solution)/shard_map/ppermute | solution.py:539
  175.1 13.9 %collective-permute-start.21 = (bf16[2,96,384]{2,1,0:T(8,128)(2,1)S(1)}, bf16[2,96,384]{2,1,0:T(8,128)(2,1)S(1)}, u32[]{:S(2)}, u32[]{:S(2)}) collective-permute-start(bf16[2,96,384]{2,1,0:T(8,128)(2,1)S(1)} %get-tuple-element.340), channel_id=1, source_target_pairs={{0,4},{1,5},{2,6},{3,7},{4,0},{5,1},{6,2},{7,3},{8,12},{9,13},{10,... | collective-permute-start | bytes 442376 | tf_op jit(solution)/shard_map/ppermute | solution.py:539
  177.7 11.4 %collective-permute-start.22 = (bf16[2,96,384]{2,1,0:T(8,128)(2,1)S(1)}, bf16[2,96,384]{2,1,0:T(8,128)(2,1)S(1)}, u32[]{:S(2)}, u32[]{:S(2)}) collective-permute-start(bf16[2,96,384]{2,1,0:T(8,128)(2,1)S(1)} %get-tuple-element.341), channel_id=1, source_target_pairs={{0,6},{1,7},{2,4},{3,5},{4,2},{5,3},{6,0},{7,1},{8,14},{9,15},{10,... | collective-permute-start | bytes 442376 | tf_op jit(solution)/shard_map/ppermute | solution.py:539
  178.0 39.5 %copy-start.2 = (f32[96,9280]{1,0:T(8,128)S(1)}, f32[96,9280]{1,0:T(8,128)}, u32[]{:S(2)}) copy-start(f32[96,9280]{1,0:T(8,128)} %refs_9_.1) | copy-start | bytes 10690564
  178.0 39.5 %copy-start.3 = (f32[96,9280]{1,0:T(8,128)S(1)}, f32[96,9280]{1,0:T(8,128)}, u32[]{:S(2)}) copy-start(f32[96,9280]{1,0:T(8,128)} %refs_10_.1) | copy-start | bytes 10690564
  181.9 12.1 %collective-permute-start.43 = (bf16[384,128]{1,0:T(8,128)(2,1)S(1)}, bf16[384,128]{1,0:T(8,128)(2,1)S(1)}, u32[]{:S(2)}, u32[]{:S(2)}) collective-permute-start(bf16[384,128]{1,0:T(8,128)(2,1)S(1)} %fusion.1), channel_id=1, source_target_pairs={{0,8},{8,0},{16,24},{24,16},{1,9},{9,1},{17,25},{25,17},{2,10},{10... | collective-permute-start | bytes 294920 | tf_op jit(solution)/shard_map/ppermute | solution.py:539
  189.7 20.8 %collective-permute-start.30 = (bf16[2,96,384]{2,1,0:T(8,128)(2,1)S(1)}, bf16[2,96,384]{2,1,0:T(8,128)(2,1)S(1)}, u32[]{:S(2)}, u32[]{:S(2)}) collective-permute-start(bf16[2,96,384]{2,1,0:T(8,128)(2,1)S(1)} %add_three.3.refs_0_), channel_id=1, source_target_pairs={{0,24},{8,16},{16,8},{24,0},{1,25},{9,17},{17,9},{25,1},{2,26},{10... | collective-permute-start | bytes 442376 | tf_op jit(solution)/shard_map/ppermute | solution.py:539
  191.3 7.4 %collective-permute-start.25 = (bf16[2,96,384]{2,1,0:T(8,128)(2,1)S(1)}, bf16[2,96,384]{2,1,0:T(8,128)(2,1)S(1)}, u32[]{:S(2)}, u32[]{:S(2)}) collective-permute-start(bf16[2,96,384]{2,1,0:T(8,128)(2,1)S(1)} %get-tuple-element.351), channel_id=1, source_target_pairs={{0,2},{1,3},{2,0},{3,1},{4,6},{5,7},{6,4},{7,5},{8,10},{9,11},{10,... | collective-permute-start | bytes 442376 | tf_op jit(solution)/shard_map/ppermute | solution.py:539
  194.0 13.1 %collective-permute-start.26 = (bf16[2,96,384]{2,1,0:T(8,128)(2,1)S(1)}, bf16[2,96,384]{2,1,0:T(8,128)(2,1)S(1)}, u32[]{:S(2)}, u32[]{:S(2)}) collective-permute-start(bf16[2,96,384]{2,1,0:T(8,128)(2,1)S(1)} %get-tuple-element.352), channel_id=1, source_target_pairs={{0,4},{1,5},{2,6},{3,7},{4,0},{5,1},{6,2},{7,3},{8,12},{9,13},{10,... | collective-permute-start | bytes 442376 | tf_op jit(solution)/shard_map/ppermute | solution.py:539
  195.0 12.5 %collective-permute-start.27 = (bf16[2,96,384]{2,1,0:T(8,128)(2,1)S(1)}, bf16[2,96,384]{2,1,0:T(8,128)(2,1)S(1)}, u32[]{:S(2)}, u32[]{:S(2)}) collective-permute-start(bf16[2,96,384]{2,1,0:T(8,128)(2,1)S(1)} %get-tuple-element.353), channel_id=1, source_target_pairs={{0,6},{1,7},{2,4},{3,5},{4,2},{5,3},{6,0},{7,1},{8,14},{9,15},{10,... | collective-permute-start | bytes 442376 | tf_op jit(solution)/shard_map/ppermute | solution.py:539
  196.6 13.0 %collective-permute-start.44 = (bf16[384,128]{1,0:T(8,128)(2,1)S(1)}, bf16[384,128]{1,0:T(8,128)(2,1)S(1)}, u32[]{:S(2)}, u32[]{:S(2)}) collective-permute-start(bf16[384,128]{1,0:T(8,128)(2,1)S(1)} %fusion), channel_id=1, source_target_pairs={{0,16},{8,24},{16,0},{24,8},{1,17},{9,25},{17,1},{25,9},{2,18},{10... | collective-permute-start | bytes 294920 | tf_op jit(solution)/shard_map/ppermute | solution.py:539
  198.7 23.4 %collective-permute-start.31 = (bf16[384,384]{1,0:T(8,128)(2,1)S(1)}, bf16[384,384]{1,0:T(8,128)(2,1)S(1)}, u32[]{:S(2)}, u32[]{:S(2)}) collective-permute-start(bf16[384,384]{1,0:T(8,128)(2,1)S(1)} %get-tuple-element.363), channel_id=1, source_target_pairs={{0,16},{8,24},{16,0},{24,8},{1,17},{9,25},{17,1},{25,9},{2,18},{10... | collective-permute-start | bytes 884744 | tf_op jit(solution)/shard_map/ppermute | solution.py:539
  207.1 15.1 %collective-permute-start.32 = (bf16[384,384]{1,0:T(8,128)(2,1)S(1)}, bf16[384,384]{1,0:T(8,128)(2,1)S(1)}, u32[]{:S(2)}, u32[]{:S(2)}) collective-permute-start(bf16[384,384]{1,0:T(8,128)(2,1)S(1)} %get-tuple-element.364), channel_id=1, source_target_pairs={{0,8},{8,0},{16,24},{24,16},{1,9},{9,1},{17,25},{25,17},{2,10},{10... | collective-permute-start | bytes 884744 | tf_op jit(solution)/shard_map/ppermute | solution.py:539
  207.6 6.1 %collective-permute-start.29 = (bf16[2,96,384]{2,1,0:T(8,128)(2,1)S(1)}, bf16[2,96,384]{2,1,0:T(8,128)(2,1)S(1)}, u32[]{:S(2)}, u32[]{:S(2)}) collective-permute-start(bf16[2,96,384]{2,1,0:T(8,128)(2,1)S(1)} %add_three.3.refs_0_), channel_id=1, source_target_pairs={{0,16},{8,24},{16,0},{24,8},{1,17},{9,25},{17,1},{25,9},{2,18},{10... | collective-permute-start | bytes 442376 | tf_op jit(solution)/shard_map/ppermute | solution.py:539
  209.7 7.3 %collective-permute-start.28 = (bf16[2,96,384]{2,1,0:T(8,128)(2,1)S(1)}, bf16[2,96,384]{2,1,0:T(8,128)(2,1)S(1)}, u32[]{:S(2)}, u32[]{:S(2)}) collective-permute-start(bf16[2,96,384]{2,1,0:T(8,128)(2,1)S(1)} %add_three.3.refs_0_), channel_id=1, source_target_pairs={{0,8},{8,0},{16,24},{24,16},{1,9},{9,1},{17,25},{25,17},{2,10},{10... | collective-permute-start | bytes 442376 | tf_op jit(solution)/shard_map/ppermute | solution.py:539
  210.5 18.2 %collective-permute-start.35 = (bf16[2,96,384]{2,1,0:T(8,128)(2,1)S(1)}, bf16[2,96,384]{2,1,0:T(8,128)(2,1)S(1)}, u32[]{:S(2)}, u32[]{:S(2)}) collective-permute-start(bf16[2,96,384]{2,1,0:T(8,128)(2,1)S(1)} %add_three.4.refs_0_), channel_id=1, source_target_pairs={{0,24},{8,16},{16,8},{24,0},{1,25},{9,17},{17,9},{25,1},{2,26},{10... | collective-permute-start | bytes 442376 | tf_op jit(solution)/shard_map/ppermute | solution.py:539
  213.7 15.1 %collective-permute-start.34 = (bf16[2,96,384]{2,1,0:T(8,128)(2,1)S(1)}, bf16[2,96,384]{2,1,0:T(8,128)(2,1)S(1)}, u32[]{:S(2)}, u32[]{:S(2)}) collective-permute-start(bf16[2,96,384]{2,1,0:T(8,128)(2,1)S(1)} %add_three.4.refs_0_), channel_id=1, source_target_pairs={{0,16},{8,24},{16,0},{24,8},{1,17},{9,25},{17,1},{25,9},{2,18},{10... | collective-permute-start | bytes 442376 | tf_op jit(solution)/shard_map/ppermute | solution.py:539
  217.0 12.4 %collective-permute-start.33 = (bf16[2,96,384]{2,1,0:T(8,128)(2,1)S(1)}, bf16[2,96,384]{2,1,0:T(8,128)(2,1)S(1)}, u32[]{:S(2)}, u32[]{:S(2)}) collective-permute-start(bf16[2,96,384]{2,1,0:T(8,128)(2,1)S(1)} %add_three.4.refs_0_), channel_id=1, source_target_pairs={{0,8},{8,0},{16,24},{24,16},{1,9},{9,1},{17,25},{25,17},{2,10},{10... | collective-permute-start | bytes 442376 | tf_op jit(solution)/shard_map/ppermute | solution.py:539
  222.9 9.8 %collective-permute-start.36 = (bf16[2,96,384]{2,1,0:T(8,128)(2,1)S(1)}, bf16[2,96,384]{2,1,0:T(8,128)(2,1)S(1)}, u32[]{:S(2)}, u32[]{:S(2)}) collective-permute-start(bf16[2,96,384]{2,1,0:T(8,128)(2,1)S(1)} %get-tuple-element.385), channel_id=1, source_target_pairs={{0,2},{1,3},{2,0},{3,1},{4,6},{5,7},{6,4},{7,5},{8,10},{9,11},{10,... | collective-permute-start | bytes 442376 | tf_op jit(solution)/shard_map/ppermute | solution.py:539
  224.2 13.8 %collective-permute-start.37 = (bf16[2,96,384]{2,1,0:T(8,128)(2,1)S(1)}, bf16[2,96,384]{2,1,0:T(8,128)(2,1)S(1)}, u32[]{:S(2)}, u32[]{:S(2)}) collective-permute-start(bf16[2,96,384]{2,1,0:T(8,128)(2,1)S(1)} %get-tuple-element.386), channel_id=1, source_target_pairs={{0,4},{1,5},{2,6},{3,7},{4,0},{5,1},{6,2},{7,3},{8,12},{9,13},{10,... | collective-permute-start | bytes 442376 | tf_op jit(solution)/shard_map/ppermute | solution.py:539
  228.8 9.3 %collective-permute-start.38 = (bf16[2,96,384]{2,1,0:T(8,128)(2,1)S(1)}, bf16[2,96,384]{2,1,0:T(8,128)(2,1)S(1)}, u32[]{:S(2)}, u32[]{:S(2)}) collective-permute-start(bf16[2,96,384]{2,1,0:T(8,128)(2,1)S(1)} %get-tuple-element.387), channel_id=1, source_target_pairs={{0,6},{1,7},{2,4},{3,5},{4,2},{5,3},{6,0},{7,1},{8,14},{9,15},{10,... | collective-permute-start | bytes 442376 | tf_op jit(solution)/shard_map/ppermute | solution.py:539
  228.8 13.0 %collective-permute-start.45 = (bf16[96,128]{1,0:T(8,128)(2,1)S(1)}, bf16[96,128]{1,0:T(8,128)(2,1)S(1)}, u32[]{:S(2)}, u32[]{:S(2)}) collective-permute-start(bf16[96,128]{1,0:T(8,128)(2,1)S(1)} %get-tuple-element.424), channel_id=1, source_target_pairs={{0,2},{1,3},{2,0},{3,1},{4,6},{5,7},{6,4},{7,5},{8,10},{9,11},{10,... | collective-permute-start | bytes 73736 | tf_op jit(solution)/shard_map/ppermute | solution.py:539
  229.4 12.8 %collective-permute-start.47 = (bf16[96,128]{1,0:T(8,128)(2,1)S(1)}, bf16[96,128]{1,0:T(8,128)(2,1)S(1)}, u32[]{:S(2)}, u32[]{:S(2)}) collective-permute-start(bf16[96,128]{1,0:T(8,128)(2,1)S(1)} %get-tuple-element.425), channel_id=1, source_target_pairs={{0,6},{1,7},{2,4},{3,5},{4,2},{5,3},{6,0},{7,1},{8,14},{9,15},{10,... | collective-permute-start | bytes 73736 | tf_op jit(solution)/shard_map/ppermute | solution.py:539
  232.8 9.4 %collective-permute-start.46 = (bf16[96,128]{1,0:T(8,128)(2,1)S(1)}, bf16[96,128]{1,0:T(8,128)(2,1)S(1)}, u32[]{:S(2)}, u32[]{:S(2)}) collective-permute-start(bf16[96,128]{1,0:T(8,128)(2,1)S(1)} %get-tuple-element.426), channel_id=1, source_target_pairs={{0,4},{1,5},{2,6},{3,7},{4,0},{5,1},{6,2},{7,3},{8,12},{9,13},{10,... | collective-permute-start | bytes 73736 | tf_op jit(solution)/shard_map/ppermute | solution.py:539
  238.6 6.2 %collective-permute-start.41 = (bf16[2,96,384]{2,1,0:T(8,128)(2,1)S(1)}, bf16[2,96,384]{2,1,0:T(8,128)(2,1)S(1)}, u32[]{:S(2)}, u32[]{:S(2)}) collective-permute-start(bf16[2,96,384]{2,1,0:T(8,128)(2,1)S(1)} %add_three.5.refs_0_), channel_id=1, source_target_pairs={{0,24},{8,16},{16,8},{24,0},{1,25},{9,17},{17,9},{25,1},{2,26},{10... | collective-permute-start | bytes 442376 | tf_op jit(solution)/shard_map/ppermute | solution.py:539
  240.4 6.0 %collective-permute-start.40 = (bf16[2,96,384]{2,1,0:T(8,128)(2,1)S(1)}, bf16[2,96,384]{2,1,0:T(8,128)(2,1)S(1)}, u32[]{:S(2)}, u32[]{:S(2)}) collective-permute-start(bf16[2,96,384]{2,1,0:T(8,128)(2,1)S(1)} %add_three.5.refs_0_), channel_id=1, source_target_pairs={{0,16},{8,24},{16,0},{24,8},{1,17},{9,25},{17,1},{25,9},{2,18},{10... | collective-permute-start | bytes 442376 | tf_op jit(solution)/shard_map/ppermute | solution.py:539
  241.7 5.1 %collective-permute-start.39 = (bf16[2,96,384]{2,1,0:T(8,128)(2,1)S(1)}, bf16[2,96,384]{2,1,0:T(8,128)(2,1)S(1)}, u32[]{:S(2)}, u32[]{:S(2)}) collective-permute-start(bf16[2,96,384]{2,1,0:T(8,128)(2,1)S(1)} %add_three.5.refs_0_), channel_id=1, source_target_pairs={{0,8},{8,0},{16,24},{24,16},{1,9},{9,1},{17,25},{25,17},{2,10},{10... | collective-permute-start | bytes 442376 | tf_op jit(solution)/shard_map/ppermute | solution.py:539
  (41 other events, 293.1 us)
where the time goes:
time: 253 us; the launch traced here: 252 us
  Pallas kernels  106 us (42%)
  waiting for transfers between devices  63.2 us (25%)
  starting transfers between devices  51.6 us (20%)
  local copies, waits for them, and re-layouts  29.1 us (12%)
    pallas_call x23, Pallas kernels, call(): pl.pallas_call(body, out_shape=tuple(outs), grid_spec=pltpu.PrefetchScala...  106 us
    ppermute x48, waiting for transfers between devices, swap(): return lax.ppermute(value, axis, [(i, i ^ bit) for i in range(size)])  63.2 us
    ppermute x48, starting transfers between devices, swap(): return lax.ppermute(value, axis, [(i, i ^ bit) for i in range(size)])  51.6 us
    unnamed x116, local copies, waits for them, and re-layouts  29.1 us
  transfers between devices with their start and end apart: 48, of which 19 were waited for; matrix products, arithmetic and copies ran while one was open for 0% of the time, Pallas kernels for 26%

commit v1 on v0

--- a/solution.py
+++ b/solution.py
@@ -59,11 +59,15 @@
 class Line:
     def __init__(self, scal):
         self.scal = scal
-
-    def call(self, body, args, in_specs, outs, out_specs, grid=(1,), scratch=(), flops=0, vmem=32,
-             aliases=None, name=None):
-        moved = sum(o.size * o.dtype.itemsize for o in outs)
-        moved += sum(a.size * a.dtype.itemsize for a in args if a.size < 4 * D * D)
+        self.stay = set()
+
+    def wait(self, *values):
+        self.scal, values = lax.optimization_barrier((self.scal, values))
+        return values
+
+    def call(self, body, args, in_specs, outs, out_specs, grid=(1,), scratch=(), vmem=32,
+             hold=0, aliases=None, name=None):
+        args = [pltpu.with_memory_space_constraint(a, pltpu.HBM) if id(a) in self.stay else a for a in args]
         got = pl.pallas_call(
             body,
             out_shape=tuple(outs),
@@ -78,7 +82,7 @@
                 dimension_semantics=("arbitrary",) * len(grid), vmem_limit_bytes=vmem * MIB
             ),
             cost_estimate=pl.CostEstimate(
-                flops=int(flops), bytes_accessed=int(moved), transcendentals=0
+                flops=hold * 10**9, bytes_accessed=1024, transcendentals=0
             ),
             input_output_aliases=aliases or {},
             name=name,
@@ -217,8 +221,9 @@
 
 def after_body(n_sel, n_parts, scal, *refs):
     parts = refs[:n_parts]
-    num_ref, fq_ref, x_ref, w_ref, vt_ref, o_ref, den_ref, r_ref, h2_ref, sin_ref = refs[n_parts : n_parts + 10]
-    sel = refs[n_parts + 10 : n_parts + 10 + n_sel]
+    num_ref, fq_ref, x_ref, w_ref, vt_ref = refs[n_parts : n_parts + 5]
+    o_ref, den_ref, r_ref, h2_ref, sin_ref = refs[n_parts + 5 + n_sel : n_parts + 10 + n_sel]
+    sel = refs[-1 - n_sel : -1]
     ob_ref = refs[-1]
     vt = vt_ref[...].astype(f32)
     state = weighted_state(scal, S_MASK, [p[...] for p in parts])
@@ -295,7 +300,7 @@
     )
     dr_ref[...] = dr
     da = dr.astype(bf16)
-    da_ref[...] = da
+    da_ref[...] = da.T
     sums_ref[...] = jnp.concatenate(
         [
             jnp.sum(up * normed, axis=0, keepdims=True),
@@ -329,8 +334,9 @@
 
 def attend_back_body(n_parts, scal, *refs):
     parts = refs[:n_parts]
-    (fq_ref, fk_ref, vt_ref, rho_ref, sin_ref, qt_ref, kt_ref, hedge_ref, dp_ref, dm_ref,
+    (fq_ref, fk_ref, vt_ref, rho_ref, sin_ref, qt_ref, kt_ref, hedge_ref, da_ref, dp_ref, dm_ref,
      db_ref) = refs[n_parts:]
+    dp_ref[3] = da_ref[...]
     rows = fq_ref.shape[1]
     half = rows // 2
     keep = tri_mask(half)
@@ -418,6 +424,80 @@
         store_sel(small_refs, 0, small, scal)
 
 
+def mlp_grads_body(by_z, scal, *refs):
+    sels, acts_a, acts_b, sels_h = refs[0:2], refs[2:4], refs[4:6], refs[6:8]
+    send, keep = refs[8:]
+    block = D // 8
+
+    def total(lefts, rights):
+        return (dot_nn(lefts[0][0], rights[0][0, 0]) + dot_nn(lefts[1][0], rights[1][0, 0])).astype(bf16)
+
+    for path, value in enumerate((total(sels, acts_a), total(sels_h, acts_b))):
+        rows = slice(path * block, (path + 1) * block)
+
+        def part(z, value=value):
+            return value[z * block : (z + 1) * block]
+
+        if by_z:
+            for at, z in enumerate((3, 1)):
+                send[at, rows, :] = part(z)
+            for at, z in enumerate((2, 0)):
+                keep[at, rows, :] = part(z)
+        else:
+
+            @pl.when(pl.program_id(0) < 2)
+            def _(part=part, rows=rows):
+                for at, z in enumerate((3, 1, 2, 0)):
+                    send[at, rows, :] = part(z)
+
+            @pl.when(pl.program_id(0) >= 2)
+            def _(part=part, rows=rows):
+                for at, z in enumerate((3, 1, 2, 0)):
+                    keep[at, rows, :] = part(z)
+
+
+def mlp_grads(line, by_z, sels, acts):
+    _, depth, rows = sels[0].shape
+    wq = acts[0].shape[3]
+    half = sds((8, 2 * (D // 8), wq), bf16)
+
+    def quarter(i):
+        high, low = 1 - i // 2, 1 - lax.rem(i, 2)
+        return high + 2 * low if by_z else 2 * high + low
+
+    def act(path):
+        return pl.BlockSpec((1, 1, rows, wq), lambda i, s: (path, quarter(i), 0, 0))
+
+    def sel(slot):
+        return pl.BlockSpec((1, depth, rows), lambda i, s: (slot, 0, 0))
+
+    if by_z:
+        out_specs = [along((2,) + half.shape[1:])] * 2
+    else:
+        out_specs = [
+            pl.BlockSpec((4,) + half.shape[1:], lambda i, s: (jnp.minimum(i, 1), 0, 0)),
+            pl.BlockSpec((4,) + half.shape[1:], lambda i, s: (jnp.maximum(i - 2, 0), 0, 0)),
+        ]
+    return line.call(
+        partial(mlp_grads_body, by_z),
+        [*sels, *acts, *acts, *sels],
+        [sel(0)] * 2 + [act(0)] * 2 + [act(1)] * 2 + [sel(3)] * 2,
+        [half] * 2,
+        out_specs,
+        grid=(4,),
+        vmem=20,
+        name="mlp_grads",
+    )
+
+
+def pack_rows(values, count):
+    return jnp.concatenate([values[b * count : (b + 1) * count] for b in range(3)], axis=1)
+
+
+def unpack_rows(values):
+    return jnp.concatenate([values[:, b * 128 : (b + 1) * 128] for b in range(3)], axis=0)
+
+
 def order_a(i):
     return jnp.where(i < 2, 2 * i + 1, 2 * i - 4)
 
@@ -426,111 +506,67 @@
     return jnp.where(i < 2, i + 2, i - 2)
 
 
-def put(send, keep, value):
+def tail_grads_body(scal, *refs):
+    h1, ob, dqk, dvo = refs[0:2], refs[2:4], refs[4:6], refs[6:8]
+    small_own, small_other, send_a, keep_a, send_b, keep_b, small_ref = refs[8:]
     step = pl.program_id(0)
-
-    @pl.when(step < 2)
-    def _():
-        send[...] = value[None]
-
-    @pl.when(step >= 2)
-    def _():
-        keep[...] = value[None]
-
-
-def mlp_grads_body(n_src, scal, *refs):
-    sels, acts_a, acts_b = refs[:n_src], refs[n_src : 2 * n_src], refs[2 * n_src : 3 * n_src]
-    sels_h = refs[3 * n_src : 4 * n_src]
-    send_a, keep_a, send_b, keep_b = refs[4 * n_src :]
+    wq = send_a.shape[1]
+    qb = jnp.bitwise_xor(order_b(step), scal[S_SEQ])
+    at = pl.multiple_of(jnp.bitwise_and(step, 1) * wq, wq)
 
     def total(lefts, rights):
-        acc = dot_nn(lefts[0][0], rights[0][0, 0])
-        for left, right in zip(lefts[1:], rights[1:]):
-            acc += dot_nn(left[0], right[0, 0])
-        return acc.astype(bf16)
-
-    put(send_a, keep_a, total(sels, acts_a))
-    put(send_b, keep_b, total(sels_h, acts_b))
-
-
-def split_specs(depth, wq):
-    send = pl.BlockSpec((1, depth, wq), lambda i, s: (jnp.minimum(i, 1), 0, 0))
-    keep = pl.BlockSpec((1, depth, wq), lambda i, s: (jnp.maximum(i - 2, 0), 0, 0))
-    return [sds((2, depth, wq), bf16)] * 4, [send, keep, send, keep]
-
-
-def mlp_grads(line, sel_first, sel_second, acts):
-    n_src = len(acts)
-    _, depth, rows = sel_first[0].shape
-    wq = acts[0].shape[3]
-    outs, out_specs = split_specs(depth, wq)
-    return line.call(
-        partial(mlp_grads_body, n_src),
-        [*sel_first, *acts, *acts, *sel_second],
-        [pl.BlockSpec((1, depth, rows), lambda i, s: (0, 0, 0))] * n_src
-        + [pl.BlockSpec((1, 1, rows, wq), lambda i, s: (0, order_a(i), 0, 0))] * n_src
-        + [pl.BlockSpec((1, 1, rows, wq), lambda i, s: (1, order_b(i), 0, 0))] * n_src
-        + [pl.BlockSpec((1, depth, rows), lambda i, s: (1, 0, 0))] * n_src,
-        outs,
-        out_specs,
-        grid=(4,),
-        flops=2 * 2 * n_src * depth * rows * wq * 4,
-        vmem=24,
-        name="mlp_grads",
-    )
-
-
-def tail_grads_body(n_src, scal, *refs):
-    it = iter(refs)
-
-    def take():
-        return [next(it) for _ in range(n_src)]
-
-    h1, ob, dqk, dv, da = take(), take(), take(), take(), take()
-    send_a, keep_a, send_b, keep_b = it
-    qb = jnp.bitwise_xor(order_b(pl.program_id(0)), scal[S_SEQ])
-
-    def total(lefts, rights):
-        acc = dot_nt(lefts[0][0], rights[0][0])
-        for left, right in zip(lefts[1:], rights[1:]):
-            acc += dot_nt(left[0], right[0])
-        return acc.astype(bf16)
+        return (dot_nt(lefts[0][0], rights[0][0]) + dot_nt(lefts[1][0], rights[1][0])).astype(bf16)
+
+    def put(send, keep, value):
+        @pl.when(step < 2)
+        def _():
+            send[pl.ds(at, wq), :] = value
+
+        @pl.when(step >= 2)
+        def _():
+            keep[pl.ds(at, wq), :] = value
 
     put(send_a, keep_a, total(h1, dqk))
 
     @pl.when(qb < 2)
     def _():
-        put(send_b, keep_b, total(h1, dv))
+        put(send_b, keep_b, total(h1, dvo))
 
     @pl.when(qb >= 2)
     def _():
-        acc = dot_nn(ob[0][0], da[0][...])
-        for left, right in zip(ob[1:], da[1:]):
-            acc += dot_nn(left[0], right[...])
-        put(send_b, keep_b, acc.astype(bf16))
-
-
-def tail_grads(line, sel_first, sel_second, dp, da):
-    n_src = len(dp)
-    _, depth, rows = sel_first[0].shape
+        put(send_b, keep_b, total(ob, dvo))
+
+    @pl.when(step == 0)
+    def _():
+        small = pack_rows(small_own[0] + small_other[0].astype(f32), 128)
+        small_ref[...] = small
+        send_a[2 * wq :, :] = small.astype(bf16)
+
+
+def tail_grads(line, sels, dp, small):
+    _, depth, rows = sels[0].shape
     wq = D // 2
-    dp = [v.reshape(6, wq, rows) for v in dp]
-    outs, out_specs = split_specs(depth, wq)
+    dp = [v.reshape(8, wq, rows) for v in dp]
+
+    def sel(slot):
+        return pl.BlockSpec((1, depth, rows), lambda i, s: (slot, 0, 0))
+
+    outs = [
+        sds((2 * wq + 128, wq), bf16), sds((2 * wq, wq), bf16),
+        sds((2 * wq, wq), bf16), sds((2 * wq, wq), bf16), sds((128, wq), f32),
+    ]
     return line.call(
-        partial(tail_grads_body, n_src),
-        [*sel_first, *sel_second, *dp, *dp, *da],
-        [pl.BlockSpec((1, depth, rows), lambda i, s: (1, 0, 0))] * n_src
-        + [pl.BlockSpec((1, depth, rows), lambda i, s: (0, 0, 0))] * n_src
-        + [pl.BlockSpec((1, wq, rows), lambda i, s: (jnp.bitwise_xor(order_a(i), s[S_SEQ]), 0, 0))] * n_src
-        + [pl.BlockSpec((1, wq, rows), lambda i, s: (
-            4 + jnp.minimum(jnp.bitwise_xor(order_b(i), s[S_SEQ]), 1), 0, 0))] * n_src
-        + [pl.BlockSpec((rows, wq), lambda i, s: (
-            0, jnp.maximum(jnp.bitwise_xor(order_b(i), s[S_SEQ]) - 2, 0)))] * n_src,
+        tail_grads_body,
+        [*sels, *sels, *dp, *dp, *small],
+        [sel(1)] * 2
+        + [sel(2)] * 2
+        + [pl.BlockSpec((1, wq, rows), lambda i, s: (jnp.bitwise_xor(order_a(i), s[S_SEQ]), 0, 0))] * 2
+        + [pl.BlockSpec((1, wq, rows), lambda i, s: (4 + jnp.bitwise_xor(order_b(i), s[S_SEQ]), 0, 0))] * 2
+        + [whole(small[0].shape)] * 2,
         outs,
-        out_specs,
+        [whole(o.shape) for o in outs],
         grid=(4,),
-        flops=2 * 2 * n_src * depth * rows * wq * 4,
-        vmem=24,
+        vmem=20,
         name="tail_grads",
     )
 
@@ -539,63 +575,109 @@
     return lax.ppermute(value, axis, [(i, i ^ bit) for i in range(size)])
 
 
-def add_one_body(scal, keep_a, recv_a, keep_b, recv_b, send_a, send_b):
-    send_a[...] = (keep_a[0].astype(f32) + recv_a[0].astype(f32)).astype(bf16)
-    send_b[...] = (keep_b[0].astype(f32) + recv_b[0].astype(f32)).astype(bf16)
-
-
-def add_two_body(scal, keep_a, recv_a, keep_b, recv_b, far_a, far_b, own_ref, *out_refs):
-    block = own_ref.shape[1]
-    for path, (keep, recv, far) in enumerate(((keep_a, recv_a, far_a), (keep_b, recv_b, far_b))):
-        total = keep[0].astype(f32) + recv[0].astype(f32) + far[...].astype(f32)
-        own_ref[path] = total[:block]
-        for k, ref in enumerate(out_refs):
-            ref[path] = total[(k + 1) * block : (k + 2) * block].astype(bf16)
-
-
-def add_three_body(scal, own, *refs):
-    total = own[...]
-    for ref in refs[:-1]:
-        total = total + ref[...].astype(f32)
-    refs[-1][...] = total.astype(refs[-1].dtype)
-
-
-class Piece:
-    def __init__(self, line, send_a, keep_a, send_b, keep_b):
-        self.line = line
-        self.keep_a, self.keep_b = keep_a, keep_b
-        self.recv_a, self.recv_b = swap(send_a, "seq", 4, 1), swap(send_b, "seq", 4, 2)
-
-    def one(self):
-        _, depth, wq = self.keep_a.shape
-        second = pl.BlockSpec((1, depth, wq), lambda i, s: (1, 0, 0))
-        next_a, next_b = self.line.call(
-            add_one_body, [self.keep_a, self.recv_a, self.keep_b, self.recv_b], [second] * 4,
-            [sds((depth, wq), bf16)] * 2, [whole((depth, wq))] * 2, flops=2 * depth * wq, vmem=8,
-            name="add_one",
+def halve_body(scal, keep_ref, recv_ref, send_ref, left_ref):
+    half = send_ref.shape[0]
+    send_ref[...] = (keep_ref[:half].astype(f32) + recv_ref[:half].astype(f32)).astype(bf16)
+    left_ref[...] = (keep_ref[half:].astype(f32) + recv_ref[half:].astype(f32)).astype(left_ref.dtype)
+
+
+class Halves:
+    def __init__(self, line, send, keep, stages):
+        self.line, self.keep, self.stages = line, keep, list(stages)
+        self.recv = swap(send, *self.stages.pop(0))
+
+    def step(self, hold=0):
+        count, rows, wq = self.keep.shape
+        shape = (count // 2, rows, wq)
+        send, self.keep = self.line.call(
+            halve_body, [self.keep, self.recv], [whole(self.keep.shape)] * 2,
+            [sds(shape, bf16), sds(shape, self.keep.dtype)], [whole(shape)] * 2,
+            vmem=2 + count * rows * wq * 12 // MIB, hold=hold, name="halve",
         )
-        self.far_a, self.far_b = swap(next_a, "seq", 4, 2), swap(next_b, "seq", 4, 1)
-
-    def two(self):
-        _, depth, wq = self.keep_a.shape
-        zero = pl.BlockSpec((1, depth, wq), lambda i, s: (0, 0, 0))
-        shard = (2, depth // 4, wq)
-        self.own, *sends = self.line.call(
-            add_two_body,
-            [self.keep_a, self.recv_a, self.keep_b, self.recv_b, self.far_a, self.far_b],
-            [zero] * 4 + [whole((depth, wq))] * 2,
-            [sds(shard, f32)] + [sds(shard, bf16)] * 3, [whole(shard)] * 4, flops=4 * depth * wq, vmem=10,
-            name="add_two",
+        self.recv = swap(send, *self.stages.pop(0))
+
+
+def final_body(scal, *refs):
+    out = refs[-1]
+    for j in range(2):
+        out[j] = (refs[2 * j][0].astype(f32) + refs[2 * j + 1][0].astype(f32)).astype(bf16)
+
+
+def final_both(line, pieces):
+    shape = (2,) + pieces[0].keep.shape[1:]
+    (mine,) = line.call(
+        final_body, [v for p in pieces for v in (p.keep, p.recv)], [whole((1,) + shape[1:])] * 4,
+        [sds(shape, bf16)], [whole(shape)], vmem=4, name="final",
+    )
+    return mine.reshape(4, D // 8, shape[2])
+
+
+def tail_one_body(scal, keep_a, recv_a, keep_b, recv_b, small_ref, send_a, send_b):
+    wq = send_b.shape[0]
+    send_a[:wq, :] = (keep_a[wq : 2 * wq].astype(f32) + recv_a[wq : 2 * wq].astype(f32)).astype(bf16)
+    send_a[wq:, :] = (small_ref[...] + recv_a[2 * wq :].astype(f32)).astype(bf16)
+    send_b[...] = (keep_b[wq:].astype(f32) + recv_b[wq:].astype(f32)).astype(bf16)
+
+
+def tail_two_body(scal, keep_a, recv_a, keep_b, recv_b, small_ref, far_a, far_b, send_ref, left_ref):
+    wq = far_b.shape[0]
+    block = D // 8
+    small = small_ref[...] + recv_a[2 * wq :].astype(f32) + far_a[wq:].astype(f32)
+    small = unpack_rows(small)
+    first = keep_a[:wq].astype(f32) + recv_a[:wq].astype(f32) + far_a[:wq].astype(f32)
+    second = keep_b[:wq].astype(f32) + recv_b[:wq].astype(f32) + far_b[...].astype(f32)
+    for ref, order in ((send_ref, (3, 1)), (left_ref, (2, 0))):
+        for at, z in enumerate(order):
+            rows = slice(z * block, (z + 1) * block)
+            ref[at, :block, :] = first[rows].astype(ref.dtype)
+            ref[at, block : 2 * block, :] = second[rows].astype(ref.dtype)
+            ref[at, 2 * block :, :] = pack_rows(small[rows], block // 3).astype(ref.dtype)
+
+
+def tail_final_body(scal, keep_ref, recv_ref, mine_ref, small_ref):
+    block = mine_ref.shape[1]
+    total = keep_ref[0] + recv_ref[0].astype(f32)
+    mine_ref[0] = total[:block].astype(bf16)
+    mine_ref[1] = total[block : 2 * block].astype(bf16)
+    small_ref[...] = unpack_rows(total[2 * block :])
+
+
+def tail_one(line, tail):
+    send_a, keep_a, send_b, keep_b, small = tail
+    wq = D // 2
+    recv_a, recv_b = swap(send_a, "seq", 4, 1), swap(send_b, "seq", 4, 2)
+    shapes = [sds((wq + 128, wq), bf16), sds((wq, wq), bf16)]
+
+    def first():
+        args = [keep_a, recv_a, keep_b, recv_b, small]
+        next_a, next_b = line.call(
+            tail_one_body, args, [whole(v.shape) for v in args], shapes, [whole(v.shape) for v in shapes],            vmem=12, name="tail_one",
         )
-        self.got = [swap(v, "grp", 8, 2 * (k + 1)) for k, v in enumerate(sends)]
-
-    def three(self):
-        shard = self.own.shape
-        (mine,) = self.line.call(
-            add_three_body, [self.own, *self.got], [whole(shard)] * 4, [sds(shard, bf16)], [whole(shard)],
-            flops=6 * shard[1] * shard[2], vmem=6, name="add_three",
+        return swap(next_a, "seq", 4, 2), swap(next_b, "seq", 4, 1)
+
+    def second(far_a, far_b):
+        args = [keep_a, recv_a, keep_b, recv_b, small, far_a, far_b]
+        shape = (2, 2 * (D // 8) + D // 24, wq)
+        send, keep = line.call(
+            tail_two_body, args, [whole(v.shape) for v in args], [sds(shape, bf16), sds(shape, f32)],
+            [whole(shape)] * 2, vmem=16, name="tail_two",
         )
-        self.parts = [mine] + [swap(mine, "seq", 4, k) for k in (1, 2, 3)]
+        return Halves(line, send, keep, [("grp", 8, 2), ("grp", 8, 4)])
+
+    return first, second
+
+
+def tail_final(line, piece):
+    wq = piece.keep.shape[2]
+    shapes = [sds((2, D // 8, wq), bf16), sds((D // 8, 2 * HD), f32)]
+    return line.call(
+        tail_final_body, [piece.keep, piece.recv], [whole(piece.keep.shape)] * 2, shapes,
+        [whole(v.shape) for v in shapes], vmem=4, name="tail_final",
+    )
+
+
+def gather_parts(mine):
+    return [mine] + [swap(mine, "seq", 4, k) for k in (1, 2, 3)]
 
 
 def adam_math(grad, master, first, second, average, rate):
@@ -615,20 +697,20 @@
     states, refs = refs[:4], refs[4 + n_alias :]
     outs, vec_outs = refs[:6], refs[6:]
     grad_ref = outs[0]
-    wq = parts[0].shape[2]
+    count, _, wq = parts[0].shape
     step = pl.program_id(0)
     path, half = jnp.right_shift(step, 1), jnp.bitwise_and(step, 1)
     for k, ref in enumerate(parts):
         quarter = jnp.bitwise_xor(scal[S_SEQ], k)
 
-        @pl.when((jnp.right_shift(quarter, 1) == half) & (step < 4))
+        @pl.when((jnp.right_shift(quarter, 1) == half) & (step < 2 * count))
         def _(ref=ref, quarter=quarter):
             at = pl.multiple_of(jnp.bitwise_and(quarter, 1) * wq, 128)
-            grad_ref[:, pl.ds(at, wq)] = ref[jnp.minimum(path, 1)].astype(f32)
+            grad_ref[:, pl.ds(at, wq)] = ref[jnp.minimum(path, count - 1)].astype(f32)
 
     if has_small:
 
-        @pl.when(step == 4)
+        @pl.when(step == 2 * count)
         def _():
             grad_ref[...] = jnp.zeros_like(grad_ref)
             grad_ref[:, : 2 * HD] = small[...]
@@ -643,7 +725,7 @@
 
 
 def adam_piece(line, parts, states, outs, block_of, small=(), vecs=()):
-    _, block, _ = parts[0].shape
+    count, block, _ = parts[0].shape
     rows, wide = states[0].shape
     spec = pl.BlockSpec((block, D), lambda i, s: (0, block_of(i)))
     anywhere = pl.BlockSpec(memory_space=pl.ANY)
@@ -661,8 +743,7 @@
         [whole(v.shape) for v in [*parts, *small, *vecs]] + [spec] * 4 + [anywhere] * n_alias,
         shapes,
         out_specs,
-        grid=(5,) if vecs else (4,),
-        flops=20 * 4 * block * D,
+        grid=(2 * count + (1 if vecs else 0),),
         aliases={1 + n_before + i: i for i in range(n_alias)},
         vmem=16,
         name="adam",
@@ -702,6 +783,7 @@
     line = Line(scal)
 
     w_t = weight_mats.T
+    line.stay = {id(w_t), id(tokens), id(cotangent)}
     v_t13 = weight_vecs.T
     n_vec = v_t13.shape[0]
     bias_fc = v_t13[9:].reshape(1, FF)
@@ -709,14 +791,12 @@
     n_peer = n_seq - 1
     sel_rows = [D // 2, D // 2] if fast else [D]
     n_sel = len(sel_rows)
-    sel_shapes = [sds((2, r, rows), bf16) for r in sel_rows]
-    sel_specs = [whole(s.shape) for s in sel_shapes]
+    sel_shapes = [sds((4, r, rows), bf16) for r in sel_rows]
+    sel_low = [whole((2, r, rows)) for r in sel_rows]
+    sel_high = [pl.BlockSpec((2, r, rows), lambda i, s: (1, 0, 0)) for r in sel_rows]
 
     def both(value):
         return [value, swap(value, "grp", 8, 1)] if fast else [value]
-
-    def pair(sel):
-        return [sel[1], swap(sel[0], "grp", 8, 1)] if fast else list(sel)
 
     def w_rows(count, at):
         return pl.BlockSpec((count, D), lambda i, s: (at(i, s), 0))
@@ -748,17 +828,15 @@
             sds((D, rows), bf16),
             sds(st_shape, bf16),
         ],
-        sel_specs + [head_spec, head_spec, feat_spec, feat_spec, head_spec, quad_state],
+        sel_low + [head_spec, head_spec, feat_spec, feat_spec, head_spec, quad_state],
         grid=(N_QUAD,),
         scratch=[pltpu.VMEM((rows, D), bf16)],
-        flops=2 * rows * D * 3 * D,
         vmem=32,
         name="pre",
     )
-    sel_first = got[:n_sel]
+    sels = got[:n_sel]
     qt, kt, fq, fk, v_t, s_own = got[n_sel:]
     states = [swap(s_own, "seq", n_seq, k + 1) for k in range(n_peer)]
-    sel_first = pair(sel_first)
 
     (num,) = line.call(
         local_body,
@@ -767,15 +845,15 @@
         [sds((HEADS * AUG, rows), f32)],
         [aug_spec],
         grid=(N_QUAD,),
-        flops=HEADS * 2 * rows * rows * 256,
         vmem=24,
         name="local",
     )
     got = line.call(
         partial(after_body, n_sel, n_peer),
-        [*states, num, fq, tokens, w_t, v_t13],
+        [*states, num, fq, tokens, w_t, v_t13, *sels],
         [whole(st_shape)] * n_peer
-        + [whole(num.shape), whole(fq.shape), whole((rows, D)), w_rows(D, lambda i, s: 3), vec_whole],
+        + [whole(num.shape), whole(fq.shape), whole((rows, D)), w_rows(D, lambda i, s: 3), vec_whole]
+        + [pl.BlockSpec(memory_space=pl.ANY)] * n_sel,
         [
             sds((D, rows), f32),
             sds((16, rows), f32),
@@ -784,20 +862,24 @@
             sds(st_shape, bf16),
         ]
         + sel_shapes,
-        [whole((D, rows)), whole((16, rows)), whole((rows, D)), whole((rows, D)), whole(st_shape)] + sel_specs,
+        [whole((D, rows)), whole((16, rows)), whole((rows, D)), whole((rows, D)), whole(st_shape)] + sel_high,
+        aliases={n_peer + 6 + i: 5 + i for i in range(n_sel)},
         scratch=[pltpu.VMEM((D, rows), bf16)],
-        flops=2 * rows * D * D,
         vmem=32,
         name="after",
     )
     o_t, den, resid, h2, s_in = got[:5]
-    sel_second = pair(got[5:])
+    sels = got[5:]
+    if fast:
+        sels = [sels[1], swap(sels[0], "grp", 8, 1)]
 
     n_piece = 2
     piece = FF // n_piece
     wq = piece // 4
     acc, acts, db_fc = [], [], []
     for j in range(n_piece):
+        if j == 1:
+            (sels,) = line.wait(sels)
         q_of = lambda i, s, j=j: 4 * j + jnp.bitwise_xor(i, s[S_SEQ])
         out_y, out_dh, act, db = line.call(
             partial(mlp_body, j == 0),
@@ -818,7 +900,6 @@
                 pl.BlockSpec((1, wq), lambda i, s: (0, jnp.bitwise_xor(i, s[S_SEQ]))),
             ],
             grid=(4,),
-            flops=4 * 2 * rows * D * piece,
             vmem=32,
             name="mlp",
         )
@@ -826,9 +907,8 @@
         db_fc.append(db)
         acts.append(both(act))
 
-    grads = [mlp_grads(line, sel_first, sel_second, acts[0])]
     if fast:
-        first = Piece(line, *grads[0])
+        (acts[0],) = line.wait(acts[0])
     block_output, d_resid, d_attn, rho, ds_own, sums = line.call(
         back_body,
         [*acc, resid, cotangent, w_t, v_t13, o_t, den, fq],
@@ -837,40 +917,45 @@
         [
             sds((rows, D), bf16),
             sds((rows, D), f32),
-            sds((rows, D), bf16),
+            sds((D, rows), bf16),
             sds((HEADS * AUG, rows), bf16),
             sds(st_shape, bf16),
             sds((4, D), f32),
         ],
-        [whole((rows, D))] * 3 + [whole((HEADS * AUG, rows)), whole(st_shape), whole((4, D))],
+        [whole((rows, D))] * 2
+        + [whole((D, rows)), whole((HEADS * AUG, rows)), whole(st_shape), whole((4, D))],
         scratch=[pltpu.VMEM((D, rows), bf16)],
-        flops=2 * rows * D * D,
         vmem=32,
         name="back",
     )
     back_states = [swap(ds_own, "seq", n_seq, k + 1) for k in range(n_peer)]
-    da = both(d_attn)
-    grads.append(mlp_grads(line, sel_first, sel_second, acts[1]))
     if fast:
-        second = Piece(line, *grads[1])
-        first.one()
+        first = Halves(
+            line, *mlp_grads(line, True, sels, acts[0]),
+            [("grp", 8, 2), ("seq", 4, 1), ("seq", 4, 2), ("grp", 8, 4)],
+        )
+        (acts[1],) = line.wait(acts[1])
+        second = mlp_grads(line, False, sels, acts[1])
+        (back_states,) = line.wait(back_states)
+        second = Halves(
+            line, *second, [("seq", 4, 2), ("seq", 4, 1), ("grp", 8, 2), ("grp", 8, 4)]
+        )
 
     dp, dm, db_qkv = line.call(
         partial(attend_back_body, n_peer),
-        [*back_states, fq, fk, v_t, rho, s_in, qt, kt, w_t],
+        [*back_states, fq, fk, v_t, rho, s_in, qt, kt, w_t, d_attn],
         [quad_state] * n_peer
-        + [feat_spec, feat_spec, head_spec, aug_spec, quad_state, head_spec, head_spec, hedge_spec],
-        [sds((3, D, rows), bf16), sds((D, HD), f32), sds((D, 3), f32)],
-        [along((3, wide, rows), 1), along((wide, HD)), along((wide, 3))],
+        + [feat_spec, feat_spec, head_spec, aug_spec, quad_state, head_spec, head_spec, hedge_spec, head_spec],
+        [sds((4, D, rows), bf16), sds((D, HD), f32), sds((D, 3), f32)],
+        [along((4, wide, rows), 1), along((wide, HD)), along((wide, 3))],
         grid=(N_QUAD,),
-        flops=HEADS * 2 * rows * rows * 768,
         vmem=32,
+        hold=12,
         name="attend_back",
     )
     dp_both = both(dp)
     if fast:
-        second.one()
-        first.two()
+        first.step()
     db_fc_rows = jnp.concatenate(db_fc, axis=1).reshape(FF // D, D)
     input_grad, *small = line.call(
         partial(input_body, fast),
@@ -890,56 +975,45 @@
         [whole((rows, D))] + [whole((1, r, 2 * HD)) for r in sel_rows],
         grid=(3,),
         scratch=[pltpu.VMEM((rows, D), f32)],
-        flops=2 * rows * D * 3 * D,
         vmem=32,
+        hold=12,
         name="input",
     )
-    tail = tail_grads(line, sel_first, sel_second, dp_both, da)
-
     states_m = [master_mats, moment_mats, square_mats, average_mats]
     states_v = [v.T for v in (master_vecs, moment_vecs, square_vecs, average_vecs)]
     if fast:
-        last = Piece(line, *tail)
         theirs, mine = small
-        total = mine[0] + swap(theirs[0].astype(bf16), "grp", 8, 1).astype(f32)
-        for bit in (1, 2):
-            total = total + swap(total.astype(bf16), "seq", 4, bit).astype(f32)
-        total = total.reshape(4, D // 8, 2 * HD)
-        low = total.astype(bf16)
-        small_own = total[0]
-        for k in (1, 2, 3):
-            small_own = small_own + swap(low[k], "grp", 8, 2 * k).astype(f32)
-
-        def at_piece(j):
-            return lambda i: jnp.where(i < 2, (4 * D + FF) // D + 2 * j + i, 4 + 2 * j + i - 2)
-
-        second.two()
-        first.three()
-        last.one()
-        second.three()
-        outs = adam_piece(line, first.parts, states_m, None, at_piece(0))
-        last.two()
-        outs = adam_piece(line, second.parts, states_m, outs, at_piece(1))
-        last.three()
+        small = [mine, swap(theirs, "grp", 8, 1)]
+        second.step(hold=60)
+        tail = tail_grads(line, sels, dp_both, small)
+        tail_first, tail_second = tail_one(line, tail)
+        first.step()
+        far = tail_first()
+        first.step()
+        second.step()
+        last = tail_second(*far)
+        second.step()
+        both_mine = gather_parts(final_both(line, [first, second]))
+        last.step()
+        last_mine, small_own = tail_final(line, last)
         outs = adam_piece(
-            line, last.parts, states_m, outs, lambda i: jnp.where(i < 4, i, (4 * D + 2 * FF) // D),
+            line, both_mine, states_m, None,
+            lambda i: jnp.where(jnp.bitwise_and(i, 2) == 0, 8, 4) + 2 * (i // 4) + jnp.bitwise_and(i, 1),
+        )
+        last_parts = gather_parts(last_mine)
+        outs = adam_piece(
+            line, last_parts, states_m, outs, lambda i: jnp.where(i < 4, i, (4 * D + 2 * FF) // D),
             small=[small_own], vecs=states_v,
         )
         mats, vecs = outs[:6], [v.T for v in outs[6:]]
     else:
-
-        def joined(send, keep, order):
-            parts = {**dict(zip(order[:2], send)), **dict(zip(order[2:], keep))}
-            return [parts[q] for q in range(4)]
-
-        fc, dn = [], []
-        for send_a, keep_a, send_b, keep_b in grads:
-            dn += joined(send_a, keep_a, (1, 3, 0, 2))
-            fc += joined(send_b, keep_b, (2, 3, 0, 1))
-        send_a, keep_a, send_b, keep_b = tail
-        qkvo = joined(send_a, keep_a, (1, 3, 0, 2)) + joined(send_b, keep_b, (2, 3, 0, 1))
+        h1t, obt, h2t = sels[0][1], sels[0][2], sels[0][3]
+        joined = [jnp.transpose(a[0], (0, 2, 1, 3)).reshape(2, rows, piece) for a in acts]
+        dn = [dot_tn(cotangent, v[0]) for v in joined]
+        fc = [dot_nn(h2t, v[1]) for v in joined]
+        qkvo = [dot_nt(h1t, dp[k]) for k in range(3)] + [dot_nt(obt, dp[3])]
         small = small[0][0]
-        grad = jnp.concatenate([*qkvo, *fc, *dn, small[:, :HD].astype(bf16)], axis=1)
+        grad = jnp.concatenate([*qkvo, *fc, *dn, small[:, :HD]], axis=1).astype(bf16)
         own = lax.psum_scatter(grad, "grp", scatter_dimension=0, tiled=True)
         own = lax.psum(own, "seq").astype(f32)
         own_v = lax.psum(lax.psum_scatter(small, "grp", scatter_dimension=0, tiled=True), "seq")

time: 253 us -> 206 us (0.81)
  local copies, waits for them, and re-layouts: 29.1 us -> 1.91 us
  starting transfers between devices: 51.6 us -> 37.2 us
  waiting for transfers between devices: 63.2 us -> 56.5 us
    unnamed x116 -> x58, local copies, waits for them, and re-layouts: 29.1 us -> 1.9 us
    ppermute x48 -> x31, starting transfers between devices: 51.6 us -> 37.2 us  [swap(): return lax.ppermute(value, axis, [(i, i ^ bit) for i in range(size)])]
    ppermute x48 -> x31, waiting for transfers between devices: 63.2 us -> 56.5 us  [swap(): return lax.ppermute(value, axis, [(i, i ^ bit) for i in range(size)])]
    pallas_call x23 -> x24, Pallas kernels: 106 us -> 108 us  [call(): pl.pallas_call(body, out_shape=tuple(outs), grid_spec=pltpu.PrefetchScala...]
  transfers between devices with their start and end apart: 48 -> 31, of which waited for: 19 -> 13; matrix products, arithmetic and copies ran while one was open for 0% -> 0% of each run, Pallas kernels for 26% -> 43%
where the time goes in v1:
time: 206 us
  Pallas kernels  108 us (52%)
  waiting for transfers between devices  56.5 us (27%)
  starting transfers between devices  37.2 us (18%)
  between operations  2.07 us (1%)
    pallas_call x24, Pallas kernels, call(): pl.pallas_call(body, out_shape=tuple(outs), grid_spec=pltpu.PrefetchScala...  108 us
    ppermute x31, waiting for transfers between devices, swap(): return lax.ppermute(value, axis, [(i, i ^ bit) for i in range(size)])  56.5 us
    ppermute x31, starting transfers between devices, swap(): return lax.ppermute(value, axis, [(i, i ^ bit) for i in range(size)])  37.2 us
  transfers between devices with their start and end apart: 31, of which 13 were waited for; matrix products, arithmetic and copies ran while one was open for 0% of the time, Pallas kernels for 43%

profile of v1, /device:TPU:0, one launch (start us, length us, event | category | flops | bytes accessed | tf_op | source)
XLA Modules:
  0.0 205.6 jit_solution(6747015507694096137)
XLA Ops:
  1.5 0.7 copy-done.12
  2.2 9.9 %pre.1 = (bf16[4,384,512]{2,1,0:T(8,128)(2,1)S(1)}, bf16[4,384,512]{2,1,0:T(8,128)(2,1)S(1)}, bf16[768,512]{1,0:T(8,128)(2,1)S(1)}, bf16[768,512]{1,0:T(8,128)(2...) custom-call(s32[16]{0:T(128)S(1)} %compare_select_fusion.2.scal, ...), custom_call_target="tpu_custom_call" | custom-call | bytes 1024 | tf_op jit(solution)/shard_map/pre/pallas_call | solution.py:71
  12.2 4.0 %collective-permute-start.2 = (bf16[960,128]{1,0:T(8,128)(2,1)S(1)}, bf16[960,128]{1,0:T(8,128)(2,1)S(1)}, u32[]{:S(2)}, u32[]{:S(2)}) collective-permute-start(bf16[960,128]{1,0:T(8,128)(2,1)S(1)} %get-tuple-element.229), channel_id=1, source_target_pairs={{0,24},{8,16},{16,8},{24,0},{1,25},{9,17},{17,9},{25,1},{2,26},{10... | collective-permute-start | bytes 737288 | tf_op jit(solution)/shard_map/ppermute | solution.py:575
  16.1 0.5 collective-permute-start.1
  16.8 4.0 %local.1.refs_3_ = f32[960,512]{1,0:T(8,128)S(1)} custom-call(s32[16]{0:T(128)S(1)} %compare_select_fusion.2.scal, bf16[1536,512]{1,0:T(8,128)(2,1)S(1)} %get-tuple-element.225.fq_ref.refs_4_.refs_3_, bf16[1536,512]{1,0:T(8,128)(2,1)S(1)} %get-tuple-element.226.fk_ref.refs_4_, bf16[768,512]{1,0:T(8,128)(2,1)S(1)} %get-tuple-element.227.vt_ref.refs_5_), custom_call_target="tpu_custom_call" | custom-call | bytes 1024 | tf_op jit(solution)/shard_map/local/pallas_call | solution.py:71
  20.8 2.1 %collective-permute-done.2.refs_2_ = bf16[960,128]{1,0:T(8,128)(2,1)S(1)} collective-permute-done((bf16[960,128]{1,0:T(8,128)(2,1)S(1)}, bf16[960,128]{1,0:T(8,128)(2,1)S(1)}, u32[]{:S(2)}, u32[]{:S(2)}) %collective-permute-start.2) | collective-permute-done | bytes 245792 | tf_op jit(solution)/shard_map/ppermute | solution.py:575
  23.0 4.4 %collective-permute-done.1.refs_1_ = bf16[960,128]{1,0:T(8,128)(2,1)S(1)} collective-permute-done((bf16[960,128]{1,0:T(8,128)(2,1)S(1)}, bf16[960,128]{1,0:T(8,128)(2,1)S(1)}, u32[]{:S(2)}, u32[]{:S(2)}) %collective-permute-start.1) | collective-permute-done | bytes 245792 | tf_op jit(solution)/shard_map/ppermute | solution.py:575
  27.6 4.5 %after.1 = (f32[768,512]{1,0:T(8,128)S(1)}, f32[16,512]{1,0:T(8,128)S(1)}, f32[512,768]{1,0:T(8,128)S(1)}, bf16[512,768]{1,0:T(8,128)(2,1)S(1)}, bf16[960,128]{1...) custom-call(s32[16]{0:T(128)S(1)} %compare_select_fusion.2.scal, ...), custom_call_target="tpu_custom_call", output_to_operand_aliasing={{5}: (9, {}), {6}: (10, {})} | custom-call | bytes 1024 | tf_op jit(solution)/shard_map/after/pallas_call | solution.py:71
  32.3 11.3 %mlp.2 = (f32[512,768]{1,0:T(8,128)S(1)}, f32[512,768]{1,0:T(8,128)S(1)}, bf16[2,4,512,384]{3,2,1,0:T(8,128)(2,1)S(1)}, f32[1,1536]{1,0:T(1,128)S(1)}) custom-call(s32[16]{0:T(128)S(1)} %compare_select_fusion.2.scal, bf16[512,768]{1,0:T(8,128)(2,1)S(1)} %get-tuple-element.241.h2_ref, bf16[512,768]{1,0:T(8,128)(2,1)} %g_ref.7, bf16[9280,768]{1,0:T(8,128)(2,1)} %bitcast.49, ...), custom_call_target="tpu_custom_call" | custom-call | bytes 1024 | tf_op jit(solution)/shard_map/mlp/pallas_call | solution.py:71
  43.6 0.6 collective-permute-start.4
  44.1 12.0 %mlp.3 = (f32[512,768]{1,0:T(8,128)S(1)}, f32[512,768]{1,0:T(8,128)S(1)}, bf16[2,4,512,384]{3,2,1,0:T(8,128)(2,1)}, f32[1,1536]{1,0:T(1,128)S(1)}) custom-call(s32[16]{0:T(128)S(1)} %compare_select_fusion.2.scal, bf16[512,768]{1,0:T(8,128)(2,1)S(1)} %get-tuple-element.241.h2_ref, bf16[512,768]{1,0:T(8,128)(2,1)} %g_ref.7, bf16[9280,768]{1,0:T(8,128)(2,1)} %bitcast.51, ...), custom_call_target="tpu_custom_call" | custom-call | bytes 1024 | tf_op jit(solution)/shard_map/mlp/pallas_call | solution.py:71
  56.1 5.2 %back.1 = (bf16[512,768]{1,0:T(8,128)(2,1)}, f32[512,768]{1,0:T(8,128)S(1)}, bf16[768,512]{1,0:T(8,128)(2,1)S(1)}, bf16[960,512]{1,0:T(8,128)(2,1)S(1)}, bf16[960,128]{1,0:T(8,128)(2,1)}, /*index=5*/f32[4,768]{1,0:T(4,128)S(1)}) custom-call(s32[16]{0:T(128)S(1)} %compare_select_fusion.2.scal, f32[512,768]{1,0:T(8,128)S(1)} %get-tuple-element.259.out_ref, ...), custom_call_target="tpu_custom_call" | custom-call | bytes 1024 | tf_op jit(solution)/shard_map/back/pallas_call | solution.py:71
  61.4 1.6 collective-permute-start.8
  63.0 1.4 collective-permute-start.7
  64.4 0.5 collective-permute-start.6
  64.9 5.3 %mlp_grads.2 = (bf16[8,192,384]{2,1,0:T(8,128)(2,1)}, bf16[8,192,384]{2,1,0:T(8,128)(2,1)S(1)}) custom-call(s32[16]{0:T(128)S(1)} %compare_select_fusion.2.scal, bf16[4,384,512]{2,1,0:T(8,128)(2,1)S(1)} %get-tuple-element.272.refs_0_.refs_6_.refs_2_, bf16[4,384,512]{2,1,0:T(8,128)(2,1)S(1)} %collective-permute-done.3.refs_1_.refs_7_.refs_3_, ...), custom_call_target="tpu_custom_call" | custom-call | bytes 1024 | tf_op jit(solution)/shard_map/mlp_grads/pallas_call | solution.py:71
  70.2 1.0 copy-done.8
  71.2 1.6 collective-permute-start.9
  73.0 6.9 %mlp_grads.3 = (bf16[8,192,384]{2,1,0:T(8,128)(2,1)S(1)}, bf16[8,192,384]{2,1,0:T(8,128)(2,1)S(1)}) custom-call(s32[16]{0:T(128)S(1)} %compare_select_fusion.2.scal, bf16[4,384,512]{2,1,0:T(8,128)(2,1)S(1)} %get-tuple-element.272.refs_0_.refs_6_.refs_2_, bf16[4,384,512]{2,1,0:T(8,128)(2,1)S(1)} %collective-permute-done.3.refs_1_.refs_7_.refs_3_, ...), custom_call_target="tpu_custom_call" | custom-call | bytes 1024 | tf_op jit(solution)/shard_map/mlp_grads/pallas_call | solution.py:71
  79.9 1.5 collective-permute-start.10
  81.4 13.1 %attend_back.1 = (bf16[4,768,512]{2,1,0:T(8,128)(2,1)S(1)}, f32[768,64]{1,0:T(8,128)S(1)}, f32[768,3]{1,0:T(8,128)S(1)}) custom-call(s32[16]{0:T(128)S(1)} %compare_select_fusion.2.scal, bf16[960,128]{1,0:T(8,128)(2,1)} %collective-permute-done.6.refs_0_, bf16[960,128]{1,0:T(8,128)(2,1)} %collective-permute-done.7.refs_1_, ...), custom_call_target="tpu_custom_call" | custom-call | flops 12000000000 | bytes 1024 | tf_op jit(solution)/shard_map/attend_back/pallas_call | solution.py:71
  94.5 4.5 %collective-permute-done.9.recv_ref = bf16[8,192,384]{2,1,0:T(8,128)(2,1)} collective-permute-done((bf16[8,192,384]{2,1,0:T(8,128)(2,1)}, bf16[8,192,384]{2,1,0:T(8,128)(2,1)}, u32[]{:S(2)}, u32[]{:S(2)}) %collective-permute-start.9) | collective-permute-done | bytes 1179680 | tf_op jit(solution)/shard_map/ppermute | solution.py:575
  99.1 2.1 %halve.7 = (bf16[4,192,384]{2,1,0:T(8,128)(2,1)S(1)}, bf16[4,192,384]{2,1,0:T(8,128)(2,1)S(1)}) custom-call(s32[16]{0:T(128)S(1)} %compare_select_fusion.2.scal, bf16[8,192,384]{2,1,0:T(8,128)(2,1)S(1)} %copy-done.9, bf16[8,192,384]{2,1,0:T(8,128)(2,1)} %collective-permute-done.9.recv_ref), custom_call_target="tpu_custom_call" | custom-call | bytes 1024 | tf_op jit(solution)/shard_map/halve/pallas_call | solution.py:71
  101.3 7.8 %input.1 = (bf16[512,768]{1,0:T(8,128)(2,1)}, f32[1,384,128]{2,1,0:T(8,128)S(1)}, f32[1,384,128]{2,1,0:T(8,128)S(1)}) custom-call(s32[16]{0:T(128)S(1)} %compare_select_fusion.2.scal, bf16[4,768,512]{2,1,0:T(8,128)(2,1)S(1)} %get-tuple-element.305.dp_ref, bf16[9280,768]{1,0:T(8,128)(2,1)} %bitcast.55, bf16[512,768]{1,0:T(8,128)(2,1)} %x_ref.3, ...), custom_call_target="tpu_custom_call" | custom-call | flops 12000000000 | bytes 1024 | tf_op jit(solution)/shard_map/input/pallas_call | solution.py:71
  109.1 0.5 collective-permute-start.12
  109.6 1.5 collective-permute-start.13
  111.1 0.8 halve.8
  112.0 5.6 %tail_grads.1 = (bf16[896,384]{1,0:T(8,128)(2,1)S(1)}, bf16[768,384]{1,0:T(8,128)(2,1)S(1)}, bf16[768,384]{1,0:T(8,128)(2,1)S(1)}, bf16[768,384]{1,0:T(8,128)(2,1)S(1)}, f32[128,384]{1,0:T(8,128)S(1)}) custom-call(s32[16]{0:T(128)S(1)} %compare_select_fusion.2.scal, bf16[4,384,512]{2,1,0:T(8,128)(2,1)S(1)} %get-tuple-element.272.refs_0_.refs_6_.refs_2_, ...), custom_call_target="tpu_custom_call" | custom-call | bytes 1024 | tf_op jit(solution)/shard_map/tail_grads/pallas_call | solution.py:71
  117.6 0.6 collective-permute-start.14
  118.2 1.4 collective-permute-start.15
  119.6 0.7 collective-permute-start.17
  120.3 5.5 %collective-permute-done.13.recv_ref = bf16[4,192,384]{2,1,0:T(8,128)(2,1)S(1)} collective-permute-done((bf16[4,192,384]{2,1,0:T(8,128)(2,1)S(1)}, bf16[4,192,384]{2,1,0:T(8,128)(2,1)S(1)}, u32[]{:S(2)}, u32[]{:S(2)}) %collective-permute-start.13) | collective-permute-done | bytes 589856 | tf_op jit(solution)/shard_map/ppermute | solution.py:575
  125.8 0.7 halve.9
  126.5 1.5 collective-permute-start.16
  128.0 6.5 %collective-permute-done.15.recv_b = bf16[768,384]{1,0:T(8,128)(2,1)S(1)} collective-permute-done((bf16[768,384]{1,0:T(8,128)(2,1)S(1)}, bf16[768,384]{1,0:T(8,128)(2,1)S(1)}, u32[]{:S(2)}, u32[]{:S(2)}) %collective-permute-start.15) | collective-permute-done | bytes 589856 | tf_op jit(solution)/shard_map/ppermute | solution.py:575
  134.4 6.1 %collective-permute-done.14.recv_a = bf16[896,384]{1,0:T(8,128)(2,1)S(1)} collective-permute-done((bf16[896,384]{1,0:T(8,128)(2,1)S(1)}, bf16[896,384]{1,0:T(8,128)(2,1)S(1)}, u32[]{:S(2)}, u32[]{:S(2)}) %collective-permute-start.14) | collective-permute-done | bytes 688160 | tf_op jit(solution)/shard_map/ppermute | solution.py:575
  140.5 0.7 tail_one.1
  141.2 1.5 collective-permute-start.18
  142.7 0.7 collective-permute-start.19
  143.4 0.6 halve.10
  144.0 9.1 %collective-permute-done.17.recv_ref = bf16[4,192,384]{2,1,0:T(8,128)(2,1)S(1)} collective-permute-done((bf16[4,192,384]{2,1,0:T(8,128)(2,1)S(1)}, bf16[4,192,384]{2,1,0:T(8,128)(2,1)S(1)}, u32[]{:S(2)}, u32[]{:S(2)}) %collective-permute-start.17) | collective-permute-done | bytes 589856 | tf_op jit(solution)/shard_map/ppermute | solution.py:575
  153.2 0.7 halve.11
  153.9 1.7 collective-permute-start.20
  155.5 3.1 %collective-permute-done.19.far_b = bf16[384,384]{1,0:T(8,128)(2,1)S(1)} collective-permute-done((bf16[384,384]{1,0:T(8,128)(2,1)S(1)}, bf16[384,384]{1,0:T(8,128)(2,1)S(1)}, u32[]{:S(2)}, u32[]{:S(2)}) %collective-permute-start.19) | collective-permute-done | bytes 294944 | tf_op jit(solution)/shard_map/ppermute | solution.py:575
  158.6 0.8 tail_two.1
  159.4 1.7 collective-permute-start.23
  161.0 2.6 %collective-permute-start.21 = (bf16[1,192,384]{2,1,0:T(8,128)(2,1)S(1)}, bf16[1,192,384]{2,1,0:T(8,128)(2,1)S(1)}, u32[]{:S(2)}, u32[]{:S(2)}) collective-permute-start(bf16[1,192,384]{2,1,0:T(8,128)(2,1)S(1)} %get-tuple-element.364), channel_id=1, source_target_pairs={{0,4},{1,5},{2,6},{3,7},{4,0},{5,1},{6,2},{7,3},{8,12},{9,13},{10,... | collective-permute-start | bytes 442376 | tf_op jit(solution)/shard_map/ppermute | solution.py:575
  163.6 0.6 halve.12
  164.6 7.8 %collective-permute-done.21.refs_1_ = bf16[1,192,384]{2,1,0:T(8,128)(2,1)S(1)} collective-permute-done((bf16[1,192,384]{2,1,0:T(8,128)(2,1)S(1)}, bf16[1,192,384]{2,1,0:T(8,128)(2,1)S(1)}, u32[]{:S(2)}, u32[]{:S(2)}) %collective-permute-start.21) | collective-permute-done | bytes 147488 | tf_op jit(solution)/shard_map/ppermute | solution.py:575
  172.5 1.6 collective-permute-done.22.refs_3_
  174.1 0.6 final.1
  174.7 1.7 collective-permute-start.27
  176.4 0.6 halve.13
  177.0 3.5 %collective-permute-start.24 = (bf16[1,224,384]{2,1,0:T(8,128)(2,1)S(1)}, bf16[1,224,384]{2,1,0:T(8,128)(2,1)S(1)}, u32[]{:S(2)}, u32[]{:S(2)}) collective-permute-start(bf16[1,224,384]{2,1,0:T(8,128)(2,1)S(1)} %get-tuple-element.374), channel_id=1, source_target_pairs={{0,4},{1,5},{2,6},{3,7},{4,0},{5,1},{6,2},{7,3},{8,12},{9,13},{10,... | collective-permute-start | bytes 516104 | tf_op jit(solution)/shard_map/ppermute | solution.py:575
  180.5 1.3 collective-permute-start.26
  181.8 0.5 collective-permute-start.25
  182.3 4.6 %collective-permute-done.24.recv_ref = bf16[1,224,384]{2,1,0:T(8,128)(2,1)S(1)} collective-permute-done((bf16[1,224,384]{2,1,0:T(8,128)(2,1)S(1)}, bf16[1,224,384]{2,1,0:T(8,128)(2,1)S(1)}, u32[]{:S(2)}, u32[]{:S(2)}) %collective-permute-start.24) | collective-permute-done | bytes 172064 | tf_op jit(solution)/shard_map/ppermute | solution.py:575
  186.9 0.6 tail_final.1
  187.6 1.4 collective-permute-start.30
  188.9 1.4 collective-permute-start.29
  190.3 0.8 collective-permute-start.28
  191.1 0.9 collective-permute-done.26.refs_2_
  192.0 8.0 %adam.2 = (f32[96,9280]{1,0:T(8,128)}, f32[96,9280]{1,0:T(8,128)}, f32[96,9280]{1,0:T(8,128)}, f32[96,9280]{1,0:T(8,128)}, f32[96,9280]{1,0:T(8,128)}, /*index=5*/bf16[96,9280]{1,0:T(8,128)(2,1)}) custom-call(s32[16]{0:T(128)S(1)} %compare_select_fusion.2.scal, bf16[4,96,384]{2,1,0:T(8,128)(2,1)S(1)} %bitcast.31, ...), custom_call_target="tpu_custom_call" | custom-call | bytes 1024 | tf_op jit(solution)/shard_map/adam/pallas_call | solution.py:71
  200.1 5.3 %adam.3 = (f32[96,9280]{1,0:T(8,128)}, f32[96,9280]{1,0:T(8,128)}, f32[96,9280]{1,0:T(8,128)}, f32[96,9280]{1,0:T(8,128)}, f32[96,9280]{1,0:T(8,128)}, /*index=5...) custom-call(s32[16]{0:T(128)S(1)} %compare_select_fusion.2.scal, ...), custom_call_target="tpu_custom_call", output_to_operand_aliasing={{0}: (14, {}), {1}: (15, {}), {2}: (16, {}), {3}: (17, {}),... | custom-call | bytes 1024 | tf_op jit(solution)/shard_map/adam/pallas_call | solution.py:71
  (83 shorter events, 1.4 us)
Async XLA Ops:
  1.5 0.7 copy-start.12
  12.1 8.7 %copy-start.6 = (bf16[1536,512]{1,0:T(8,128)(2,1)}, bf16[1536,512]{1,0:T(8,128)(2,1)S(1)}, u32[]{:S(2)}) copy-start(bf16[1536,512]{1,0:T(8,128)(2,1)S(1)} %get-tuple-element.226.fk_ref.refs_4_) | copy-start | bytes 4718596
  12.1 8.7 %copy-start.10 = (bf16[768,512]{1,0:T(8,128)(2,1)}, bf16[768,512]{1,0:T(8,128)(2,1)S(1)}, u32[]{:S(2)}) copy-start(bf16[768,512]{1,0:T(8,128)(2,1)S(1)} %get-tuple-element.227.vt_ref.refs_5_) | copy-start | bytes 2359300
  12.1 8.7 %copy-start.22 = (bf16[768,512]{1,0:T(8,128)(2,1)}, bf16[768,512]{1,0:T(8,128)(2,1)S(1)}, u32[]{:S(2)}) copy-start(bf16[768,512]{1,0:T(8,128)(2,1)S(1)} %get-tuple-element.293.refs_8_) | copy-start | bytes 2359300
  12.2 8.7 %copy-start.24 = (bf16[768,512]{1,0:T(8,128)(2,1)}, bf16[768,512]{1,0:T(8,128)(2,1)S(1)}, u32[]{:S(2)}) copy-start(bf16[768,512]{1,0:T(8,128)(2,1)S(1)} %get-tuple-element.294.refs_9_) | copy-start | bytes 2359300
  12.2 44.0 %copy-start.4 = (bf16[1536,512]{1,0:T(8,128)(2,1)}, bf16[1536,512]{1,0:T(8,128)(2,1)S(1)}, u32[]{:S(2)}) copy-start(bf16[1536,512]{1,0:T(8,128)(2,1)S(1)} %get-tuple-element.225.fq_ref.refs_4_.refs_3_) | copy-start | bytes 4718596
  12.2 10.8 %collective-permute-start.2 = (bf16[960,128]{1,0:T(8,128)(2,1)S(1)}, bf16[960,128]{1,0:T(8,128)(2,1)S(1)}, u32[]{:S(2)}, u32[]{:S(2)}) collective-permute-start(bf16[960,128]{1,0:T(8,128)(2,1)S(1)} %get-tuple-element.229), channel_id=1, source_target_pairs={{0,24},{8,16},{16,8},{24,0},{1,25},{9,17},{17,9},{25,1},{2,26},{10... | collective-permute-start | bytes 737288 | tf_op jit(solution)/shard_map/ppermute | solution.py:575
  16.1 11.2 %collective-permute-start.1 = (bf16[960,128]{1,0:T(8,128)(2,1)S(1)}, bf16[960,128]{1,0:T(8,128)(2,1)S(1)}, u32[]{:S(2)}, u32[]{:S(2)}) collective-permute-start(bf16[960,128]{1,0:T(8,128)(2,1)S(1)} %get-tuple-element.229), channel_id=1, source_target_pairs={{0,16},{8,24},{16,0},{24,8},{1,17},{9,25},{17,1},{25,9},{2,18},{10... | collective-permute-start | bytes 737288 | tf_op jit(solution)/shard_map/ppermute | solution.py:575
  16.6 11.0 %collective-permute-start = (bf16[960,128]{1,0:T(8,128)(2,1)S(1)}, bf16[960,128]{1,0:T(8,128)(2,1)S(1)}, u32[]{:S(2)}, u32[]{:S(2)}) collective-permute-start(bf16[960,128]{1,0:T(8,128)(2,1)S(1)} %get-tuple-element.229), channel_id=1, source_target_pairs={{0,8},{8,0},{16,24},{24,16},{1,9},{9,1},{17,25},{25,17},{2,10},{10... | collective-permute-start | bytes 737288 | tf_op jit(solution)/shard_map/ppermute | solution.py:575
  32.2 12.0 %collective-permute-start.3 = (bf16[4,384,512]{2,1,0:T(8,128)(2,1)S(1)}, bf16[4,384,512]{2,1,0:T(8,128)(2,1)S(1)}, u32[]{:S(2)}, u32[]{:S(2)}) collective-permute-start(bf16[4,384,512]{2,1,0:T(8,128)(2,1)S(1)} %get-tuple-element.248), channel_id=1, source_target_pairs={{0,1},{1,0},{2,3},{3,2},{4,5},{5,4},{6,7},{7,6},{8,9},{9,8},{10,11... | collective-permute-start | bytes 4718600 | tf_op jit(solution)/shard_map/ppermute | solution.py:575
  43.6 12.6 %collective-permute-start.4 = (bf16[2,4,512,384]{3,2,1,0:T(8,128)(2,1)S(1)}, bf16[2,4,512,384]{3,2,1,0:T(8,128)(2,1)S(1)}, u32[]{:S(2)}, u32[]{:S(2)}) collective-permute-start(bf16[2,4,512,384]{3,2,1,0:T(8,128)(2,1)S(1)} %get-tuple-element.274.refs_2_.refs_4_), channel_id=1, source_target_pairs={{0,1},{1,0},{2,3},{3,2},{4,5},{5,4},{6,7},{7,6},{8,9},{9,8},{10,11... | collective-permute-start | bytes 9437192 | tf_op jit(solution)/shard_map/ppermute | solution.py:575
  56.1 16.9 %collective-permute-start.5 = (bf16[2,4,512,384]{3,2,1,0:T(8,128)(2,1)}, bf16[2,4,512,384]{3,2,1,0:T(8,128)(2,1)}, u32[]{:S(2)}, u32[]{:S(2)}) collective-permute-start(bf16[2,4,512,384]{3,2,1,0:T(8,128)(2,1)} %get-tuple-element.281.refs_2_.refs_4_), channel_id=1, source_target_pairs={{0,1},{1,0},{2,3},{3,2},{4,5},{5,4},{6,7},{7,6},{8,9},{9,8},{10,11... | collective-permute-start | bytes 9437192 | tf_op jit(solution)/shard_map/ppermute | solution.py:575
  61.4 8.8 %copy-start.18 = (f32[512,768]{1,0:T(8,128)}, f32[512,768]{1,0:T(8,128)S(1)}, u32[]{:S(2)}) copy-start(f32[512,768]{1,0:T(8,128)S(1)} %get-tuple-element.306.dr_ref) | copy-start | bytes 4718596
  61.4 8.8 %copy-start.20 = (bf16[960,512]{1,0:T(8,128)(2,1)}, bf16[960,512]{1,0:T(8,128)(2,1)S(1)}, u32[]{:S(2)}) copy-start(bf16[960,512]{1,0:T(8,128)(2,1)S(1)} %get-tuple-element.291.refs_6_) | copy-start | bytes 2949124
  61.4 8.8 %copy-start.26 = (bf16[768,512]{1,0:T(8,128)(2,1)}, bf16[768,512]{1,0:T(8,128)(2,1)S(1)}, u32[]{:S(2)}) copy-start(bf16[768,512]{1,0:T(8,128)(2,1)S(1)} %get-tuple-element.295.refs_11_) | copy-start | bytes 2359300
  61.4 18.5 %collective-permute-start.8 = (bf16[960,128]{1,0:T(8,128)(2,1)}, bf16[960,128]{1,0:T(8,128)(2,1)}, u32[]{:S(2)}, u32[]{:S(2)}) collective-permute-start(bf16[960,128]{1,0:T(8,128)(2,1)} %get-tuple-element.286), channel_id=1, source_target_pairs={{0,24},{8,16},{16,8},{24,0},{1,25},{9,17},{17,9},{25,1},{2,26},{10... | collective-permute-start | bytes 737288 | tf_op jit(solution)/shard_map/ppermute | solution.py:575
  63.0 16.9 %collective-permute-start.7 = (bf16[960,128]{1,0:T(8,128)(2,1)}, bf16[960,128]{1,0:T(8,128)(2,1)}, u32[]{:S(2)}, u32[]{:S(2)}) collective-permute-start(bf16[960,128]{1,0:T(8,128)(2,1)} %get-tuple-element.286), channel_id=1, source_target_pairs={{0,16},{8,24},{16,0},{24,8},{1,17},{9,25},{17,1},{25,9},{2,18},{10... | collective-permute-start | bytes 737288 | tf_op jit(solution)/shard_map/ppermute | solution.py:575
  64.4 15.5 %collective-permute-start.6 = (bf16[960,128]{1,0:T(8,128)(2,1)}, bf16[960,128]{1,0:T(8,128)(2,1)}, u32[]{:S(2)}, u32[]{:S(2)}) collective-permute-start(bf16[960,128]{1,0:T(8,128)(2,1)} %get-tuple-element.286), channel_id=1, source_target_pairs={{0,8},{8,0},{16,24},{24,16},{1,9},{9,1},{17,25},{25,17},{2,10},{10... | collective-permute-start | bytes 737288 | tf_op jit(solution)/shard_map/ppermute | solution.py:575
  70.2 1.0 copy-start.8
  71.2 27.8 %collective-permute-start.9 = (bf16[8,192,384]{2,1,0:T(8,128)(2,1)}, bf16[8,192,384]{2,1,0:T(8,128)(2,1)}, u32[]{:S(2)}, u32[]{:S(2)}) collective-permute-start(bf16[8,192,384]{2,1,0:T(8,128)(2,1)} %get-tuple-element.301), channel_id=1, source_target_pairs={{0,2},{1,3},{2,0},{3,1},{4,6},{5,7},{6,4},{7,5},{8,10},{9,11},{10,... | collective-permute-start | bytes 3538952 | tf_op jit(solution)/shard_map/ppermute | solution.py:575
  72.9 8.5 %copy-start.5 = (bf16[1536,512]{1,0:T(8,128)(2,1)S(1)}, bf16[1536,512]{1,0:T(8,128)(2,1)}, u32[]{:S(2)}) copy-start(bf16[1536,512]{1,0:T(8,128)(2,1)} %copy-done.4) | copy-start | bytes 4718596
  72.9 8.5 %copy-start.7 = (bf16[1536,512]{1,0:T(8,128)(2,1)S(1)}, bf16[1536,512]{1,0:T(8,128)(2,1)}, u32[]{:S(2)}) copy-start(bf16[1536,512]{1,0:T(8,128)(2,1)} %copy-done.6) | copy-start | bytes 4718596
  72.9 8.5 %copy-start.11 = (bf16[768,512]{1,0:T(8,128)(2,1)S(1)}, bf16[768,512]{1,0:T(8,128)(2,1)}, u32[]{:S(2)}) copy-start(bf16[768,512]{1,0:T(8,128)(2,1)} %copy-done.10) | copy-start | bytes 2359300
  72.9 8.5 %copy-start.21 = (bf16[960,512]{1,0:T(8,128)(2,1)S(1)}, bf16[960,512]{1,0:T(8,128)(2,1)}, u32[]{:S(2)}) copy-start(bf16[960,512]{1,0:T(8,128)(2,1)} %copy-done.20) | copy-start | bytes 2949124
  72.9 8.5 %copy-start.23 = (bf16[768,512]{1,0:T(8,128)(2,1)S(1)}, bf16[768,512]{1,0:T(8,128)(2,1)}, u32[]{:S(2)}) copy-start(bf16[768,512]{1,0:T(8,128)(2,1)} %copy-done.22) | copy-start | bytes 2359300
  72.9 8.5 %copy-start.25 = (bf16[768,512]{1,0:T(8,128)(2,1)S(1)}, bf16[768,512]{1,0:T(8,128)(2,1)}, u32[]{:S(2)}) copy-start(bf16[768,512]{1,0:T(8,128)(2,1)} %copy-done.24) | copy-start | bytes 2359300
  72.9 8.5 %copy-start.27 = (bf16[768,512]{1,0:T(8,128)(2,1)S(1)}, bf16[768,512]{1,0:T(8,128)(2,1)}, u32[]{:S(2)}) copy-start(bf16[768,512]{1,0:T(8,128)(2,1)} %copy-done.26) | copy-start | bytes 2359300
  79.8 19.2 %copy-start.9 = (bf16[8,192,384]{2,1,0:T(8,128)(2,1)S(1)}, bf16[8,192,384]{2,1,0:T(8,128)(2,1)}, u32[]{:S(2)}) copy-start(bf16[8,192,384]{2,1,0:T(8,128)(2,1)} %copy-done.8) | copy-start | bytes 3538948
  79.9 31.2 %collective-permute-start.10 = (bf16[8,192,384]{2,1,0:T(8,128)(2,1)S(1)}, bf16[8,192,384]{2,1,0:T(8,128)(2,1)S(1)}, u32[]{:S(2)}, u32[]{:S(2)}) collective-permute-start(bf16[8,192,384]{2,1,0:T(8,128)(2,1)S(1)} %get-tuple-element.318), channel_id=1, source_target_pairs={{0,16},{8,24},{16,0},{24,8},{1,17},{9,25},{17,1},{25,9},{2,18},{10... | collective-permute-start | bytes 3538952 | tf_op jit(solution)/shard_map/ppermute | solution.py:575
  94.5 6.7 %copy-start.13 = (bf16[768,13]{0,1:T(8,128)(2,1)S(1)}, bf16[768,13]{0,1:T(8,128)(2,1)}, u32[]{:S(2)}) copy-start(bf16[768,13]{0,1:T(8,128)(2,1)} %param.17) | copy-start | bytes 59908
  94.5 6.7 %copy-start.19 = (f32[512,768]{1,0:T(8,128)S(1)}, f32[512,768]{1,0:T(8,128)}, u32[]{:S(2)}) copy-start(f32[512,768]{1,0:T(8,128)} %copy-done.18) | copy-start | bytes 4718596
  101.2 10.8 %collective-permute-start.11 = (bf16[4,768,512]{2,1,0:T(8,128)(2,1)S(1)}, bf16[4,768,512]{2,1,0:T(8,128)(2,1)S(1)}, u32[]{:S(2)}, u32[]{:S(2)}) collective-permute-start(bf16[4,768,512]{2,1,0:T(8,128)(2,1)S(1)} %get-tuple-element.305.dp_ref), channel_id=1, source_target_pairs={{0,1},{1,0},{2,3},{3,2},{4,5},{5,4},{6,7},{7,6},{8,9},{9,8},{10,11... | collective-permute-start | bytes 9437192 | tf_op jit(solution)/shard_map/ppermute | solution.py:575
  109.1 2.8 %collective-permute-start.12 = (f32[1,384,128]{2,1,0:T(8,128)S(1)}, f32[1,384,128]{2,1,0:T(8,128)S(1)}, u32[]{:S(2)}, u32[]{:S(2)}) collective-permute-start(f32[1,384,128]{2,1,0:T(8,128)S(1)} %get-tuple-element.323), channel_id=1, source_target_pairs={{0,1},{1,0},{2,3},{3,2},{4,5},{5,4},{6,7},{7,6},{8,9},{9,8},{10,11... | collective-permute-start | bytes 589832 | tf_op jit(solution)/shard_map/ppermute | solution.py:575
  109.6 16.2 %collective-permute-start.13 = (bf16[4,192,384]{2,1,0:T(8,128)(2,1)S(1)}, bf16[4,192,384]{2,1,0:T(8,128)(2,1)S(1)}, u32[]{:S(2)}, u32[]{:S(2)}) collective-permute-start(bf16[4,192,384]{2,1,0:T(8,128)(2,1)S(1)} %get-tuple-element.331), channel_id=1, source_target_pairs={{0,8},{8,0},{16,24},{24,16},{1,9},{9,1},{17,25},{25,17},{2,10},{10... | collective-permute-start | bytes 1769480 | tf_op jit(solution)/shard_map/ppermute | solution.py:575
  112.0 80.1 %copy-start.3 = (f32[96,9280]{1,0:T(8,128)S(1)}, f32[96,9280]{1,0:T(8,128)}, u32[]{:S(2)}) copy-start(f32[96,9280]{1,0:T(8,128)} %refs_12_.1) | copy-start | bytes 10690564
  117.6 22.9 %collective-permute-start.14 = (bf16[896,384]{1,0:T(8,128)(2,1)S(1)}, bf16[896,384]{1,0:T(8,128)(2,1)S(1)}, u32[]{:S(2)}, u32[]{:S(2)}) collective-permute-start(bf16[896,384]{1,0:T(8,128)(2,1)S(1)} %get-tuple-element.336), channel_id=1, source_target_pairs={{0,8},{8,0},{16,24},{24,16},{1,9},{9,1},{17,25},{25,17},{2,10},{10... | collective-permute-start | bytes 2064392 | tf_op jit(solution)/shard_map/ppermute | solution.py:575
  118.2 16.2 %collective-permute-start.15 = (bf16[768,384]{1,0:T(8,128)(2,1)S(1)}, bf16[768,384]{1,0:T(8,128)(2,1)S(1)}, u32[]{:S(2)}, u32[]{:S(2)}) collective-permute-start(bf16[768,384]{1,0:T(8,128)(2,1)S(1)} %get-tuple-element.338), channel_id=1, source_target_pairs={{0,16},{8,24},{16,0},{24,8},{1,17},{9,25},{17,1},{25,9},{2,18},{10... | collective-permute-start | bytes 1769480 | tf_op jit(solution)/shard_map/ppermute | solution.py:575
  119.6 33.5 %collective-permute-start.17 = (bf16[4,192,384]{2,1,0:T(8,128)(2,1)S(1)}, bf16[4,192,384]{2,1,0:T(8,128)(2,1)S(1)}, u32[]{:S(2)}, u32[]{:S(2)}) collective-permute-start(bf16[4,192,384]{2,1,0:T(8,128)(2,1)S(1)} %get-tuple-element.349), channel_id=1, source_target_pairs={{0,8},{8,0},{16,24},{24,16},{1,9},{9,1},{17,25},{25,17},{2,10},{10... | collective-permute-start | bytes 1769480 | tf_op jit(solution)/shard_map/ppermute | solution.py:575
  126.5 16.9 %collective-permute-start.16 = (bf16[2,192,384]{2,1,0:T(8,128)(2,1)S(1)}, bf16[2,192,384]{2,1,0:T(8,128)(2,1)S(1)}, u32[]{:S(2)}, u32[]{:S(2)}) collective-permute-start(bf16[2,192,384]{2,1,0:T(8,128)(2,1)S(1)} %get-tuple-element.344), channel_id=1, source_target_pairs={{0,16},{8,24},{16,0},{24,8},{1,17},{9,25},{17,1},{25,9},{2,18},{10... | collective-permute-start | bytes 884744 | tf_op jit(solution)/shard_map/ppermute | solution.py:575
  140.5 51.5 %copy-start.2 = (f32[96,9280]{1,0:T(8,128)S(1)}, f32[96,9280]{1,0:T(8,128)}, u32[]{:S(2)}) copy-start(f32[96,9280]{1,0:T(8,128)} %refs_11_.1) | copy-start | bytes 10690564
  141.2 17.3 %collective-permute-start.18 = (bf16[512,384]{1,0:T(8,128)(2,1)S(1)}, bf16[512,384]{1,0:T(8,128)(2,1)S(1)}, u32[]{:S(2)}, u32[]{:S(2)}) collective-permute-start(bf16[512,384]{1,0:T(8,128)(2,1)S(1)} %get-tuple-element.353), channel_id=1, source_target_pairs={{0,16},{8,24},{16,0},{24,8},{1,17},{9,25},{17,1},{25,9},{2,18},{10... | collective-permute-start | bytes 1179656 | tf_op jit(solution)/shard_map/ppermute | solution.py:575
  142.7 15.8 %collective-permute-start.19 = (bf16[384,384]{1,0:T(8,128)(2,1)S(1)}, bf16[384,384]{1,0:T(8,128)(2,1)S(1)}, u32[]{:S(2)}, u32[]{:S(2)}) collective-permute-start(bf16[384,384]{1,0:T(8,128)(2,1)S(1)} %get-tuple-element.354), channel_id=1, source_target_pairs={{0,8},{8,0},{16,24},{24,16},{1,9},{9,1},{17,25},{25,17},{2,10},{10... | collective-permute-start | bytes 884744 | tf_op jit(solution)/shard_map/ppermute | solution.py:575
  153.2 38.8 %copy-start.1 = (f32[96,9280]{1,0:T(8,128)S(1)}, f32[96,9280]{1,0:T(8,128)}, u32[]{:S(2)}) copy-start(f32[96,9280]{1,0:T(8,128)} %refs_10_.1) | copy-start | bytes 10690564
  153.9 9.7 %collective-permute-start.20 = (bf16[2,192,384]{2,1,0:T(8,128)(2,1)S(1)}, bf16[2,192,384]{2,1,0:T(8,128)(2,1)S(1)}, u32[]{:S(2)}, u32[]{:S(2)}) collective-permute-start(bf16[2,192,384]{2,1,0:T(8,128)(2,1)S(1)} %get-tuple-element.359), channel_id=1, source_target_pairs={{0,2},{1,3},{2,0},{3,1},{4,6},{5,7},{6,4},{7,5},{8,10},{9,11},{10,... | collective-permute-start | bytes 884744 | tf_op jit(solution)/shard_map/ppermute | solution.py:575
  158.6 33.4 %copy-start = (f32[96,9280]{1,0:T(8,128)S(1)}, f32[96,9280]{1,0:T(8,128)}, u32[]{:S(2)}) copy-start(f32[96,9280]{1,0:T(8,128)} %refs_9_.1) | copy-start | bytes 10690564
  159.4 17.0 %collective-permute-start.23 = (bf16[2,224,384]{2,1,0:T(8,128)(2,1)S(1)}, bf16[2,224,384]{2,1,0:T(8,128)(2,1)S(1)}, u32[]{:S(2)}, u32[]{:S(2)}) collective-permute-start(bf16[2,224,384]{2,1,0:T(8,128)(2,1)S(1)} %get-tuple-element.369), channel_id=1, source_target_pairs={{0,2},{1,3},{2,0},{3,1},{4,6},{5,7},{6,4},{7,5},{8,10},{9,11},{10,... | collective-permute-start | bytes 1032200 | tf_op jit(solution)/shard_map/ppermute | solution.py:575
  161.0 11.5 %collective-permute-start.21 = (bf16[1,192,384]{2,1,0:T(8,128)(2,1)S(1)}, bf16[1,192,384]{2,1,0:T(8,128)(2,1)S(1)}, u32[]{:S(2)}, u32[]{:S(2)}) collective-permute-start(bf16[1,192,384]{2,1,0:T(8,128)(2,1)S(1)} %get-tuple-element.364), channel_id=1, source_target_pairs={{0,4},{1,5},{2,6},{3,7},{4,0},{5,1},{6,2},{7,3},{8,12},{9,13},{10,... | collective-permute-start | bytes 442376 | tf_op jit(solution)/shard_map/ppermute | solution.py:575
  164.2 9.8 %collective-permute-start.22 = (bf16[1,192,384]{2,1,0:T(8,128)(2,1)S(1)}, bf16[1,192,384]{2,1,0:T(8,128)(2,1)S(1)}, u32[]{:S(2)}, u32[]{:S(2)}) collective-permute-start(bf16[1,192,384]{2,1,0:T(8,128)(2,1)S(1)} %get-tuple-element.366), channel_id=1, source_target_pairs={{0,4},{1,5},{2,6},{3,7},{4,0},{5,1},{6,2},{7,3},{8,12},{9,13},{10,... | collective-permute-start | bytes 442376 | tf_op jit(solution)/shard_map/ppermute | solution.py:575
  174.7 15.7 %collective-permute-start.27 = (bf16[4,96,384]{2,1,0:T(8,128)(2,1)S(1)}, bf16[4,96,384]{2,1,0:T(8,128)(2,1)S(1)}, u32[]{:S(2)}, u32[]{:S(2)}) collective-permute-start(bf16[4,96,384]{2,1,0:T(8,128)(2,1)S(1)} %bitcast.28), channel_id=1, source_target_pairs={{0,24},{8,16},{16,8},{24,0},{1,25},{9,17},{17,9},{25,1},{2,26},{10... | collective-permute-start | bytes 884744 | tf_op jit(solution)/shard_map/ppermute | solution.py:575
  177.0 10.0 %collective-permute-start.24 = (bf16[1,224,384]{2,1,0:T(8,128)(2,1)S(1)}, bf16[1,224,384]{2,1,0:T(8,128)(2,1)S(1)}, u32[]{:S(2)}, u32[]{:S(2)}) collective-permute-start(bf16[1,224,384]{2,1,0:T(8,128)(2,1)S(1)} %get-tuple-element.374), channel_id=1, source_target_pairs={{0,4},{1,5},{2,6},{3,7},{4,0},{5,1},{6,2},{7,3},{8,12},{9,13},{10,... | collective-permute-start | bytes 516104 | tf_op jit(solution)/shard_map/ppermute | solution.py:575
  180.5 11.5 %collective-permute-start.26 = (bf16[4,96,384]{2,1,0:T(8,128)(2,1)S(1)}, bf16[4,96,384]{2,1,0:T(8,128)(2,1)S(1)}, u32[]{:S(2)}, u32[]{:S(2)}) collective-permute-start(bf16[4,96,384]{2,1,0:T(8,128)(2,1)S(1)} %bitcast.29), channel_id=1, source_target_pairs={{0,16},{8,24},{16,0},{24,8},{1,17},{9,25},{17,1},{25,9},{2,18},{10... | collective-permute-start | bytes 884744 | tf_op jit(solution)/shard_map/ppermute | solution.py:575
  181.8 10.2 %collective-permute-start.25 = (bf16[4,96,384]{2,1,0:T(8,128)(2,1)S(1)}, bf16[4,96,384]{2,1,0:T(8,128)(2,1)S(1)}, u32[]{:S(2)}, u32[]{:S(2)}) collective-permute-start(bf16[4,96,384]{2,1,0:T(8,128)(2,1)S(1)} %bitcast.30), channel_id=1, source_target_pairs={{0,8},{8,0},{16,24},{24,16},{1,9},{9,1},{17,25},{25,17},{2,10},{10... | collective-permute-start | bytes 884744 | tf_op jit(solution)/shard_map/ppermute | solution.py:575
  187.5 12.6 %copy-start.14 = (f32[96,13]{0,1:T(8,128)S(1)}, f32[96,13]{0,1:T(8,128)}, u32[]{:S(2)}) copy-start(f32[96,13]{0,1:T(8,128)} %param.19) | copy-start | bytes 14980
  187.5 12.6 %copy-start.15 = (f32[96,13]{0,1:T(8,128)S(1)}, f32[96,13]{0,1:T(8,128)}, u32[]{:S(2)}) copy-start(f32[96,13]{0,1:T(8,128)} %param.21) | copy-start | bytes 14980
  187.5 12.6 %copy-start.16 = (f32[96,13]{0,1:T(8,128)S(1)}, f32[96,13]{0,1:T(8,128)}, u32[]{:S(2)}) copy-start(f32[96,13]{0,1:T(8,128)} %param.23) | copy-start | bytes 14980
  187.5 12.5 %copy-start.17 = (f32[96,13]{0,1:T(8,128)S(1)}, f32[96,13]{0,1:T(8,128)}, u32[]{:S(2)}) copy-start(f32[96,13]{0,1:T(8,128)} %param.25) | copy-start | bytes 14980
  187.6 12.5 %collective-permute-start.30 = (bf16[2,96,384]{2,1,0:T(8,128)(2,1)S(1)}, bf16[2,96,384]{2,1,0:T(8,128)(2,1)S(1)}, u32[]{:S(2)}, u32[]{:S(2)}) collective-permute-start(bf16[2,96,384]{2,1,0:T(8,128)(2,1)S(1)} %get-tuple-element.386.refs_0_), channel_id=1, source_target_pairs={{0,24},{8,16},{16,8},{24,0},{1,25},{9,17},{17,9},{25,1},{2,26},{10... | collective-permute-start | bytes 442376 | tf_op jit(solution)/shard_map/ppermute | solution.py:575
  188.9 11.1 %collective-permute-start.29 = (bf16[2,96,384]{2,1,0:T(8,128)(2,1)S(1)}, bf16[2,96,384]{2,1,0:T(8,128)(2,1)S(1)}, u32[]{:S(2)}, u32[]{:S(2)}) collective-permute-start(bf16[2,96,384]{2,1,0:T(8,128)(2,1)S(1)} %get-tuple-element.386.refs_0_), channel_id=1, source_target_pairs={{0,16},{8,24},{16,0},{24,8},{1,17},{9,25},{17,1},{25,9},{2,18},{10... | collective-permute-start | bytes 442376 | tf_op jit(solution)/shard_map/ppermute | solution.py:575
  190.3 9.7 %collective-permute-start.28 = (bf16[2,96,384]{2,1,0:T(8,128)(2,1)S(1)}, bf16[2,96,384]{2,1,0:T(8,128)(2,1)S(1)}, u32[]{:S(2)}, u32[]{:S(2)}) collective-permute-start(bf16[2,96,384]{2,1,0:T(8,128)(2,1)S(1)} %get-tuple-element.386.refs_0_), channel_id=1, source_target_pairs={{0,8},{8,0},{16,24},{24,16},{1,9},{9,1},{17,25},{25,17},{2,10},{10... | collective-permute-start | bytes 442376 | tf_op jit(solution)/shard_map/ppermute | solution.py:575

commit v2 on v1

--- a/solution.py
+++ b/solution.py
@@ -66,8 +66,11 @@
         return values
 
     def call(self, body, args, in_specs, outs, out_specs, grid=(1,), scratch=(), vmem=32,
-             hold=0, aliases=None, name=None):
-        args = [pltpu.with_memory_space_constraint(a, pltpu.HBM) if id(a) in self.stay else a for a in args]
+             hold=0, far=(), aliases=None, name=None):
+        args = [
+            pltpu.with_memory_space_constraint(a, pltpu.HBM) if id(a) in self.stay or k in far else a
+            for k, a in enumerate(args)
+        ]
         got = pl.pallas_call(
             body,
             out_shape=tuple(outs),
@@ -139,46 +142,60 @@
     return jnp.concatenate([values, jnp.zeros((3, values.shape[1]), f32)], axis=0).T
 
 
-def pre_body(n_sel, scal, x_ref, g_ref, wq_ref, wk_ref, wv_ref, hedge_ref, vt_ref, vq_ref, *refs):
-    sel = refs[:n_sel]
-    qt_ref, kt_ref, fq_ref, fk_ref, vt_out, s_ref, h1_ref = refs[n_sel:]
+def features(pt, maps):
+    high = pt.astype(bf16)
+    rest = (pt - high.astype(f32)).astype(bf16)
+    scores = dot_nn(jnp.concatenate([maps, maps], axis=1), jnp.concatenate([high, rest], axis=0))
+    heads = []
+    for h in range(QUAD):
+        s = scores[h * HD : (h + 1) * HD, :]
+        top = jnp.max(s, axis=0, keepdims=True)
+        bottom = jnp.min(s, axis=0, keepdims=True)
+        pos = jnp.exp(s - top)
+        neg = jnp.exp(bottom - s)
+        pos = pos * (1.0 / jnp.sum(pos, axis=0, keepdims=True))
+        neg = neg * (1.0 / jnp.sum(neg, axis=0, keepdims=True))
+        heads.append(jnp.concatenate([pos, neg], axis=0).astype(bf16))
+    return high, heads
+
+
+def keys_body(scal, x_ref, wk_ref, wv_ref, hedge_ref, vt_ref, vq_ref, h1_ref, kt_ref, fk_ref, vt_out, s_ref):
     rows = x_ref.shape[0]
 
     @pl.when(pl.program_id(0) == 0)
     def _():
         normed, _ = normalize(x_ref[...].astype(f32))
         vt = vt_ref[...].astype(f32)
-        h1 = (normed * vt[0:1] + vt[1:2]).astype(bf16)
-        h1_ref[...] = h1
-        store_sel(sel, 0, g_ref[...].T, scal)
-        store_sel(sel, 1, h1.T, scal)
+        h1_ref[...] = (normed * vt[0:1] + vt[1:2]).astype(bf16)
 
     h1 = h1_ref[...]
     bias = rows_up(vq_ref[...].astype(f32))
     v_t = (dot_nt(wv_ref[...], h1) + bias[:, 8:9]).astype(bf16)
     vt_out[...] = v_t
-    maps = quad_maps(hedge_ref[...]).astype(bf16)
-    maps2 = jnp.concatenate([maps, maps], axis=1)
+    pt = dot_nt(wk_ref[...], h1) + bias[:, 7:8]
+    kt_ref[...], heads = features(pt, quad_maps(hedge_ref[...]).astype(bf16))
     extra = ones_rows(rows)
-    for which, (w_ref, save, feat) in enumerate(((wk_ref, kt_ref, fk_ref), (wq_ref, qt_ref, fq_ref))):
-        pt = dot_nt(w_ref[...], h1) + bias[:, 7 - which : 8 - which]
-        high = pt.astype(bf16)
-        save[...] = high
-        rest = (pt - high.astype(f32)).astype(bf16)
-        scores = dot_nn(maps2, jnp.concatenate([high, rest], axis=0))
-        for h in range(QUAD):
-            s = scores[h * HD : (h + 1) * HD, :]
-            top = jnp.max(s, axis=0, keepdims=True)
-            bottom = jnp.min(s, axis=0, keepdims=True)
-            pos = jnp.exp(s - top)
-            neg = jnp.exp(bottom - s)
-            pos = pos * (1.0 / jnp.sum(pos, axis=0, keepdims=True))
-            neg = neg * (1.0 / jnp.sum(neg, axis=0, keepdims=True))
-            both = jnp.concatenate([pos, neg], axis=0).astype(bf16)
-            feat[h * 2 * HD : (h + 1) * 2 * HD, :] = both
-            if which == 0:
-                va = jnp.concatenate([v_t[h * HD : (h + 1) * HD, :], extra], axis=0)
-                s_ref[h * AUG : (h + 1) * AUG, :] = dot_nt(va, both).astype(bf16)
+    for h, both in enumerate(heads):
+        fk_ref[h * 2 * HD : (h + 1) * 2 * HD, :] = both
+        va = jnp.concatenate([v_t[h * HD : (h + 1) * HD, :], extra], axis=0)
+        s_ref[h * AUG : (h + 1) * AUG, :] = dot_nt(va, both).astype(bf16)
+
+
+def queries_body(n_sel, scal, h1_ref, g_ref, wq_ref, hedge_ref, vq_ref, *refs):
+    sel = refs[:n_sel]
+    qt_ref, fq_ref = refs[n_sel:]
+    h1 = h1_ref[...]
+
+    @pl.when(pl.program_id(0) == 0)
+    def _():
+        store_sel(sel, 0, g_ref[...].T, scal)
+        store_sel(sel, 1, h1.T, scal)
+
+    bias = rows_up(vq_ref[...].astype(f32))
+    pt = dot_nt(wq_ref[...], h1) + bias[:, 6:7]
+    qt_ref[...], heads = features(pt, quad_maps(hedge_ref[...]).astype(bf16))
+    for h, both in enumerate(heads):
+        fq_ref[h * 2 * HD : (h + 1) * 2 * HD, :] = both
 
 
 def tri_mask(half):
@@ -334,8 +351,8 @@
 
 def attend_back_body(n_parts, scal, *refs):
     parts = refs[:n_parts]
-    (fq_ref, fk_ref, vt_ref, rho_ref, sin_ref, qt_ref, kt_ref, hedge_ref, da_ref, dp_ref, dm_ref,
-     db_ref) = refs[n_parts:]
+    (fq_ref, fk_ref, vt_ref, rho_ref, sin_ref, qt_ref, kt_ref, hedge_ref, da_ref) = refs[n_parts : n_parts + 9]
+    dp_ref, dm_ref, db_ref = refs[-3:]
     dp_ref[3] = da_ref[...]
     rows = fq_ref.shape[1]
     half = rows // 2
@@ -424,68 +441,57 @@
         store_sel(small_refs, 0, small, scal)
 
 
-def mlp_grads_body(by_z, scal, *refs):
+def mlp_grads_body(by_y, scal, *refs):
     sels, acts_a, acts_b, sels_h = refs[0:2], refs[2:4], refs[4:6], refs[6:8]
     send, keep = refs[8:]
     block = D // 8
+    wq = send.shape[2]
+    y_last = 1 - pl.program_id(0)
 
     def total(lefts, rights):
         return (dot_nn(lefts[0][0], rights[0][0, 0]) + dot_nn(lefts[1][0], rights[1][0, 0])).astype(bf16)
 
     for path, value in enumerate((total(sels, acts_a), total(sels_h, acts_b))):
         rows = slice(path * block, (path + 1) * block)
-
-        def part(z, value=value):
-            return value[z * block : (z + 1) * block]
-
-        if by_z:
-            for at, z in enumerate((3, 1)):
-                send[at, rows, :] = part(z)
-            for at, z in enumerate((2, 0)):
-                keep[at, rows, :] = part(z)
-        else:
-
-            @pl.when(pl.program_id(0) < 2)
-            def _(part=part, rows=rows):
-                for at, z in enumerate((3, 1, 2, 0)):
-                    send[at, rows, :] = part(z)
-
-            @pl.when(pl.program_id(0) >= 2)
-            def _(part=part, rows=rows):
-                for at, z in enumerate((3, 1, 2, 0)):
-                    keep[at, rows, :] = part(z)
-
-
-def mlp_grads(line, by_z, sels, acts):
+        for half in range(2):
+            x_last = 1 - jnp.bitwise_xor(half, jnp.bitwise_and(scal[S_SEQ], 1))
+            cols = slice(half * wq, (half + 1) * wq)
+
+            def part(z, value=value, cols=cols):
+                return value[z * block : (z + 1) * block, cols]
+
+            if by_y:
+                for bit, ref in ((0, send), (1, keep)):
+
+                    @pl.when(y_last == bit)
+                    def _(ref=ref, part=part, rows=rows, x_last=x_last):
+                        for at, z in enumerate((3, 1, 2, 0)):
+                            ref[4 * (at // 2) + 2 * x_last + at % 2, rows, :] = part(z)
+            else:
+                base = y_last + 4 * x_last
+                for ref, order in ((send, (3, 1)), (keep, (2, 0))):
+                    for at, z in enumerate(order):
+                        ref[2 * at + base, rows, :] = part(z)
+
+
+def mlp_grads(line, by_y, sels, acts):
     _, depth, rows = sels[0].shape
-    wq = acts[0].shape[3]
-    half = sds((8, 2 * (D // 8), wq), bf16)
-
-    def quarter(i):
-        high, low = 1 - i // 2, 1 - lax.rem(i, 2)
-        return high + 2 * low if by_z else 2 * high + low
+    half = sds((8, 2 * (D // 8), D // 2), bf16)
 
     def act(path):
-        return pl.BlockSpec((1, 1, rows, wq), lambda i, s: (path, quarter(i), 0, 0))
+        return pl.BlockSpec((1, 1, rows, D), lambda i, s: (path, i, 0, 0))
 
     def sel(slot):
         return pl.BlockSpec((1, depth, rows), lambda i, s: (slot, 0, 0))
 
-    if by_z:
-        out_specs = [along((2,) + half.shape[1:])] * 2
-    else:
-        out_specs = [
-            pl.BlockSpec((4,) + half.shape[1:], lambda i, s: (jnp.minimum(i, 1), 0, 0)),
-            pl.BlockSpec((4,) + half.shape[1:], lambda i, s: (jnp.maximum(i - 2, 0), 0, 0)),
-        ]
     return line.call(
-        partial(mlp_grads_body, by_z),
+        partial(mlp_grads_body, by_y),
         [*sels, *acts, *acts, *sels],
         [sel(0)] * 2 + [act(0)] * 2 + [act(1)] * 2 + [sel(3)] * 2,
         [half] * 2,
-        out_specs,
-        grid=(4,),
-        vmem=20,
+        [whole(half.shape)] * 2,
+        grid=(2,),
+        vmem=10,
         name="mlp_grads",
     )
 
@@ -566,7 +572,7 @@
         outs,
         [whole(o.shape) for o in outs],
         grid=(4,),
-        vmem=20,
+        vmem=10,
         name="tail_grads",
     )
 
@@ -592,7 +598,7 @@
         send, self.keep = self.line.call(
             halve_body, [self.keep, self.recv], [whole(self.keep.shape)] * 2,
             [sds(shape, bf16), sds(shape, self.keep.dtype)], [whole(shape)] * 2,
-            vmem=2 + count * rows * wq * 12 // MIB, hold=hold, name="halve",
+            vmem=8, hold=hold, name="halve",
         )
         self.recv = swap(send, *self.stages.pop(0))
 
@@ -619,24 +625,26 @@
     send_b[...] = (keep_b[wq:].astype(f32) + recv_b[wq:].astype(f32)).astype(bf16)
 
 
-def tail_two_body(scal, keep_a, recv_a, keep_b, recv_b, small_ref, far_a, far_b, send_ref, left_ref):
+def tail_two_body(scal, keep_a, recv_a, keep_b, recv_b, small_ref, far_a, far_b, own_ref, *out_refs):
     wq = far_b.shape[0]
     block = D // 8
     small = small_ref[...] + recv_a[2 * wq :].astype(f32) + far_a[wq:].astype(f32)
     small = unpack_rows(small)
     first = keep_a[:wq].astype(f32) + recv_a[:wq].astype(f32) + far_a[:wq].astype(f32)
     second = keep_b[:wq].astype(f32) + recv_b[:wq].astype(f32) + far_b[...].astype(f32)
-    for ref, order in ((send_ref, (3, 1)), (left_ref, (2, 0))):
-        for at, z in enumerate(order):
-            rows = slice(z * block, (z + 1) * block)
-            ref[at, :block, :] = first[rows].astype(ref.dtype)
-            ref[at, block : 2 * block, :] = second[rows].astype(ref.dtype)
-            ref[at, 2 * block :, :] = pack_rows(small[rows], block // 3).astype(ref.dtype)
-
-
-def tail_final_body(scal, keep_ref, recv_ref, mine_ref, small_ref):
+    for z, ref in enumerate((own_ref, *out_refs)):
+        rows = slice(z * block, (z + 1) * block)
+        ref[:block, :] = first[rows].astype(ref.dtype)
+        ref[block : 2 * block, :] = second[rows].astype(ref.dtype)
+        ref[2 * block :, :] = pack_rows(small[rows], block // 3).astype(ref.dtype)
+
+
+def tail_final_body(scal, *refs):
+    mine_ref, small_ref = refs[-2:]
     block = mine_ref.shape[1]
-    total = keep_ref[0] + recv_ref[0].astype(f32)
+    total = refs[0][...]
+    for ref in refs[1:-2]:
+        total = total + ref[...].astype(f32)
     mine_ref[0] = total[:block].astype(bf16)
     mine_ref[1] = total[block : 2 * block].astype(bf16)
     small_ref[...] = unpack_rows(total[2 * block :])
@@ -651,28 +659,29 @@
     def first():
         args = [keep_a, recv_a, keep_b, recv_b, small]
         next_a, next_b = line.call(
-            tail_one_body, args, [whole(v.shape) for v in args], shapes, [whole(v.shape) for v in shapes],            vmem=12, name="tail_one",
+            tail_one_body, args, [whole(v.shape) for v in args], shapes, [whole(v.shape) for v in shapes],
+            vmem=12, name="tail_one",
         )
         return swap(next_a, "seq", 4, 2), swap(next_b, "seq", 4, 1)
 
     def second(far_a, far_b):
         args = [keep_a, recv_a, keep_b, recv_b, small, far_a, far_b]
-        shape = (2, 2 * (D // 8) + D // 24, wq)
-        send, keep = line.call(
-            tail_two_body, args, [whole(v.shape) for v in args], [sds(shape, bf16), sds(shape, f32)],
-            [whole(shape)] * 2, vmem=16, name="tail_two",
-        )
-        return Halves(line, send, keep, [("grp", 8, 2), ("grp", 8, 4)])
+        shape = (2 * (D // 8) + D // 24, wq)
+        own, *sends = line.call(
+            tail_two_body, args, [whole(v.shape) for v in args], [sds(shape, f32)] + [sds(shape, bf16)] * 3,
+            [whole(shape)] * 4, vmem=10, hold=5, name="tail_two",
+        )
+        return [own, *(swap(v, "grp", 8, 2 * (k + 1)) for k, v in enumerate(sends))]
 
     return first, second
 
 
-def tail_final(line, piece):
-    wq = piece.keep.shape[2]
+def tail_final(line, args):
+    wq = D // 2
     shapes = [sds((2, D // 8, wq), bf16), sds((D // 8, 2 * HD), f32)]
     return line.call(
-        tail_final_body, [piece.keep, piece.recv], [whole(piece.keep.shape)] * 2, shapes,
-        [whole(v.shape) for v in shapes], vmem=4, name="tail_final",
+        tail_final_body, args, [whole(v.shape) for v in args], shapes, [whole(v.shape) for v in shapes],
+        vmem=6, hold=5, name="tail_final",
     )
 
 
@@ -783,7 +792,8 @@
     line = Line(scal)
 
     w_t = weight_mats.T
-    line.stay = {id(w_t), id(tokens), id(cotangent)}
+    states_m = [master_mats, moment_mats, square_mats, average_mats]
+    line.stay = {id(v) for v in (w_t, tokens, cotangent)}
     v_t13 = weight_vecs.T
     n_vec = v_t13.shape[0]
     bias_fc = v_t13[9:].reshape(1, FF)
@@ -806,37 +816,43 @@
     head_spec, feat_spec = along((wide, rows)), along((2 * wide, rows))
     aug_spec, quad_state = along((QUAD * AUG, rows)), along((QUAD * AUG, 2 * HD))
     st_shape = (HEADS * AUG, 2 * HD)
-    got = line.call(
-        partial(pre_body, n_sel),
-        [tokens, cotangent, w_t, w_t, w_t, w_t, v_t13, v_t13],
+    vec_quad = pl.BlockSpec((n_vec, wide), lambda i, s: (0, i))
+    h1, kt, fk, v_t, s_own = line.call(
+        keys_body,
+        [tokens, w_t, w_t, w_t, v_t13, v_t13],
         [
             whole((rows, D)),
-            whole((rows, D)),
-            w_rows(wide, lambda i, s: i),
             w_rows(wide, lambda i, s: N_QUAD + i),
             w_rows(wide, lambda i, s: 2 * N_QUAD + i),
             hedge_spec,
             vec_whole,
-            pl.BlockSpec((n_vec, wide), lambda i, s: (0, i)),
+            vec_quad,
         ],
-        sel_shapes
-        + [
+        [
+            sds((rows, D), bf16),
             sds((D, rows), bf16),
-            sds((D, rows), bf16),
-            sds((2 * D, rows), bf16),
             sds((2 * D, rows), bf16),
             sds((D, rows), bf16),
             sds(st_shape, bf16),
         ],
-        sel_low + [head_spec, head_spec, feat_spec, feat_spec, head_spec, quad_state],
+        [whole((rows, D)), head_spec, feat_spec, head_spec, quad_state],
         grid=(N_QUAD,),
-        scratch=[pltpu.VMEM((rows, D), bf16)],
-        vmem=32,
-        name="pre",
-    )
-    sels = got[:n_sel]
-    qt, kt, fq, fk, v_t, s_own = got[n_sel:]
+        vmem=12,
+        name="keys",
+    )
+    n_peer = n_seq - 1
     states = [swap(s_own, "seq", n_seq, k + 1) for k in range(n_peer)]
+    got = line.call(
+        partial(queries_body, n_sel),
+        [h1, cotangent, w_t, w_t, v_t13],
+        [whole((rows, D)), whole((rows, D)), w_rows(wide, lambda i, s: i), hedge_spec, vec_quad],
+        sel_shapes + [sds((D, rows), bf16), sds((2 * D, rows), bf16)],
+        sel_low + [head_spec, feat_spec],
+        grid=(N_QUAD,),
+        vmem=12,
+        name="queries",
+    )
+    sels, (qt, fq) = got[:n_sel], got[n_sel:]
 
     (num,) = line.call(
         local_body,
@@ -845,7 +861,7 @@
         [sds((HEADS * AUG, rows), f32)],
         [aug_spec],
         grid=(N_QUAD,),
-        vmem=24,
+        vmem=10,
         name="local",
     )
     got = line.call(
@@ -865,7 +881,7 @@
         [whole((D, rows)), whole((16, rows)), whole((rows, D)), whole((rows, D)), whole(st_shape)] + sel_high,
         aliases={n_peer + 6 + i: 5 + i for i in range(n_sel)},
         scratch=[pltpu.VMEM((D, rows), bf16)],
-        vmem=32,
+        vmem=10,
         name="after",
     )
     o_t, den, resid, h2, s_in = got[:5]
@@ -875,32 +891,31 @@
 
     n_piece = 2
     piece = FF // n_piece
-    wq = piece // 4
     acc, acts, db_fc = [], [], []
     for j in range(n_piece):
         if j == 1:
             (sels,) = line.wait(sels)
-        q_of = lambda i, s, j=j: 4 * j + jnp.bitwise_xor(i, s[S_SEQ])
+        pair_of = lambda i, s, j=j: 2 * j + jnp.bitwise_xor(i, jnp.right_shift(s[S_SEQ], 1))
         out_y, out_dh, act, db = line.call(
             partial(mlp_body, j == 0),
             [h2, cotangent, w_t, w_t, bias_fc, *acc],
             [
                 whole((rows, D)),
                 whole((rows, D)),
-                w_rows(wq, lambda i, s: 4 * D // wq + q_of(i, s)),
-                w_rows(wq, lambda i, s: (4 * D + FF) // wq + q_of(i, s)),
-                pl.BlockSpec((1, wq), lambda i, s: (0, q_of(i, s))),
+                w_rows(D, lambda i, s: 4 + pair_of(i, s)),
+                w_rows(D, lambda i, s: 8 + pair_of(i, s)),
+                pl.BlockSpec((1, D), lambda i, s: (0, pair_of(i, s))),
             ]
             + [whole((rows, D))] * len(acc),
-            [sds((rows, D), f32), sds((rows, D), f32), sds((2, 4, rows, wq), bf16), sds((1, piece), f32)],
+            [sds((rows, D), f32), sds((rows, D), f32), sds((2, 2, rows, D), bf16), sds((1, piece), f32)],
             [
                 whole((rows, D)),
                 whole((rows, D)),
-                pl.BlockSpec((2, 1, rows, wq), lambda i, s: (0, i, 0, 0)),
-                pl.BlockSpec((1, wq), lambda i, s: (0, jnp.bitwise_xor(i, s[S_SEQ]))),
+                pl.BlockSpec((2, 1, rows, D), lambda i, s: (0, i, 0, 0)),
+                pl.BlockSpec((1, D), lambda i, s: (0, jnp.bitwise_xor(i, jnp.right_shift(s[S_SEQ], 1)))),
             ],
-            grid=(4,),
-            vmem=32,
+            grid=(2,),
+            vmem=14,
             name="mlp",
         )
         acc = [out_y, out_dh]
@@ -908,7 +923,11 @@
         acts.append(both(act))
 
     if fast:
-        (acts[0],) = line.wait(acts[0])
+        first = Halves(
+            line, *mlp_grads(line, False, sels, acts[0]),
+            [("grp", 8, 2), ("seq", 4, 1), ("grp", 8, 4), ("seq", 4, 2)],
+        )
+        (acts[1],) = line.wait(acts[1])
     block_output, d_resid, d_attn, rho, ds_own, sums = line.call(
         back_body,
         [*acc, resid, cotangent, w_t, v_t13, o_t, den, fq],
@@ -925,37 +944,46 @@
         [whole((rows, D))] * 2
         + [whole((D, rows)), whole((HEADS * AUG, rows)), whole(st_shape), whole((4, D))],
         scratch=[pltpu.VMEM((D, rows), bf16)],
-        vmem=32,
+        vmem=10,
         name="back",
     )
     back_states = [swap(ds_own, "seq", n_seq, k + 1) for k in range(n_peer)]
     if fast:
-        first = Halves(
-            line, *mlp_grads(line, True, sels, acts[0]),
-            [("grp", 8, 2), ("seq", 4, 1), ("seq", 4, 2), ("grp", 8, 4)],
-        )
-        (acts[1],) = line.wait(acts[1])
-        second = mlp_grads(line, False, sels, acts[1])
+        second = mlp_grads(line, True, sels, acts[1])
         (back_states,) = line.wait(back_states)
         second = Halves(
-            line, *second, [("seq", 4, 2), ("seq", 4, 1), ("grp", 8, 2), ("grp", 8, 4)]
-        )
-
-    dp, dm, db_qkv = line.call(
-        partial(attend_back_body, n_peer),
-        [*back_states, fq, fk, v_t, rho, s_in, qt, kt, w_t, d_attn],
-        [quad_state] * n_peer
-        + [feat_spec, feat_spec, head_spec, aug_spec, quad_state, head_spec, head_spec, hedge_spec, head_spec],
-        [sds((4, D, rows), bf16), sds((D, HD), f32), sds((D, 3), f32)],
-        [along((4, wide, rows), 1), along((wide, HD)), along((wide, 3))],
-        grid=(N_QUAD,),
-        vmem=32,
-        hold=12,
-        name="attend_back",
-    )
+            line, *second, [("seq", 4, 2), ("grp", 8, 2), ("seq", 4, 1), ("grp", 8, 4)]
+        )
+
+    grads = [sds((4, D, rows), bf16), sds((D, HD), f32), sds((D, 3), f32)]
+    got = []
+    for start, count in ((0, N_QUAD),):
+
+        def at(block, axis=0, start=start):
+            return pl.BlockSpec(
+                tuple(block), lambda i, s: tuple(start + i if d == axis else 0 for d in range(len(block)))
+            )
+
+        feat, head = at((2 * wide, rows)), at((wide, rows))
+        state = at((QUAD * AUG, 2 * HD))
+        args = [*back_states, fq, fk, v_t, rho, s_in, qt, kt, w_t, d_attn]
+        got = line.call(
+            partial(attend_back_body, n_peer),
+            [*args, *got],
+            [state] * n_peer
+            + [feat, feat, head, at((QUAD * AUG, rows)), state, head, head]
+            + [pl.BlockSpec((HD, wide), lambda i, s, start=start: ((4 * D + 2 * FF) // HD, start + i)), head]
+            + [pl.BlockSpec(memory_space=pl.ANY)] * len(got),
+            grads,
+            [at((4, wide, rows), 1), at((wide, HD)), at((wide, 3))],
+            grid=(count,),
+            aliases={1 + len(args) + k: k for k in range(len(got))},
+            hold=1,
+            vmem=12,
+            name="attend_back",
+        )
+    dp, dm, db_qkv = got
     dp_both = both(dp)
-    if fast:
-        first.step()
     db_fc_rows = jnp.concatenate(db_fc, axis=1).reshape(FF // D, D)
     input_grad, *small = line.call(
         partial(input_body, fast),
@@ -975,26 +1003,26 @@
         [whole((rows, D))] + [whole((1, r, 2 * HD)) for r in sel_rows],
         grid=(3,),
         scratch=[pltpu.VMEM((rows, D), f32)],
-        vmem=32,
-        hold=12,
+        vmem=14,
         name="input",
     )
-    states_m = [master_mats, moment_mats, square_mats, average_mats]
     states_v = [v.T for v in (master_vecs, moment_vecs, square_vecs, average_vecs)]
     if fast:
         theirs, mine = small
         small = [mine, swap(theirs, "grp", 8, 1)]
+        first.step(hold=14)
         second.step(hold=60)
         tail = tail_grads(line, sels, dp_both, small)
         tail_first, tail_second = tail_one(line, tail)
         first.step()
+        second.step(hold=4)
         far = tail_first()
         first.step()
         second.step()
+        mine = final_both(line, [first, second])
+        part_x, part_y = swap(mine, "seq", 4, 1), swap(mine, "seq", 4, 2)
+        both_mine = [mine, part_x, part_y, swap(part_x, "seq", 4, 2)]
         last = tail_second(*far)
-        second.step()
-        both_mine = gather_parts(final_both(line, [first, second]))
-        last.step()
         last_mine, small_own = tail_final(line, last)
         outs = adam_piece(
             line, both_mine, states_m, None,

time: 206 us -> 189 us (0.917)
  waiting for transfers between devices: 56.5 us -> 37.6 us
  Pallas kernels: 108 us -> 101 us
  local copies, waits for them, and re-layouts: 1.91 us -> 8.66 us
    ppermute x31 -> x32, waiting for transfers between devices: 56.5 us -> 37.6 us  [swap(): return lax.ppermute(value, axis, [(i, i ^ bit) for i in range(size)])]
    pallas_call x24, Pallas kernels: 108 us -> 101 us  [call(): pl.pallas_call(body, out_shape=tuple(outs), grid_spec=pltpu.PrefetchScala...]
    unnamed x58 -> x66, local copies, waits for them, and re-layouts: 1.9 us -> 8.64 us
    ppermute x31 -> x32, starting transfers between devices: 37.2 us -> 38.9 us  [swap(): return lax.ppermute(value, axis, [(i, i ^ bit) for i in range(size)])]
  transfers between devices with their start and end apart: 31 -> 32, of which waited for: 13 -> 14; matrix products, arithmetic and copies ran while one was open for 0% -> 0% of each run, Pallas kernels for 43% -> 45%
where the time goes in v2:
time: 189 us; the launch traced here: 188 us
  Pallas kernels  101 us (53%)
  starting transfers between devices  38.9 us (21%)
  waiting for transfers between devices  37.6 us (20%)
  local copies, waits for them, and re-layouts  8.66 us (5%)
  between operations  2.03 us (1%)
    pallas_call x24, Pallas kernels, call(): pl.pallas_call(body, out_shape=tuple(outs), grid_spec=pltpu.PrefetchScala...  101 us
    ppermute x32, starting transfers between devices, swap(): return lax.ppermute(value, axis, [(i, i ^ bit) for i in range(size)])  38.9 us
    ppermute x32, waiting for transfers between devices, swap(): return lax.ppermute(value, axis, [(i, i ^ bit) for i in range(size)])  37.6 us
    unnamed x66, local copies, waits for them, and re-layouts  8.64 us
  transfers between devices with their start and end apart: 32, of which 14 were waited for; matrix products, arithmetic and copies ran while one was open for 0% of the time, Pallas kernels for 45%

profile of v2, /device:TPU:0, one launch (start us, length us, event | category | flops | bytes accessed | tf_op | source)
XLA Modules:
  0.0 188.2 jit_solution(18143751170996769702)
XLA Ops:
  1.5 0.7 copy-done.18
  2.2 6.6 %keys.1 = (bf16[512,768]{1,0:T(8,128)(2,1)S(1)}, bf16[768,512]{1,0:T(8,128)(2,1)S(1)}, bf16[1536,512]{1,0:T(8,128)(2,1)S(1)}, bf16[768,512]{1,0:T(8,128)(2,1)S(1)}, bf16[960,128]{1,0:T(8,128)(2,1)S(1)}) custom-call(s32[16]{0:T(128)S(1)} %compare_select_fusion.2.scal, bf16[512,768]{1,0:T(8,128)(2,1)} %x_ref.3, bf16[9280,768]{1,0:T(8,128)(2,1)} %bitcast.44, ...), custom_call_target="tpu_custom_call" | custom-call | bytes 1024 | tf_op jit(solution)/shard_map/keys/pallas_call | solution.py:74
  8.8 4.0 %collective-permute-start.2 = (bf16[960,128]{1,0:T(8,128)(2,1)S(1)}, bf16[960,128]{1,0:T(8,128)(2,1)S(1)}, u32[]{:S(2)}, u32[]{:S(2)}) collective-permute-start(bf16[960,128]{1,0:T(8,128)(2,1)S(1)} %get-tuple-element.231), channel_id=1, source_target_pairs={{0,24},{8,16},{16,8},{24,0},{1,25},{9,17},{17,9},{25,1},{2,26},{10... | collective-permute-start | bytes 737288 | tf_op jit(solution)/shard_map/ppermute | solution.py:581
  13.5 5.7 %queries.1 = (bf16[4,384,512]{2,1,0:T(8,128)(2,1)S(1)}, bf16[4,384,512]{2,1,0:T(8,128)(2,1)S(1)}, bf16[768,512]{1,0:T(8,128)(2,1)S(1)}, bf16[1536,512]{1,0:T(8,128)(2,1)S(1)}) custom-call(s32[16]{0:T(128)S(1)} %compare_select_fusion.2.scal, bf16[512,768]{1,0:T(8,128)(2,1)S(1)} %get-tuple-element.221.h1_ref, bf16[512,768]{1,0:T(8,128)(2,1)} %g_ref.7, ...), custom_call_target="tpu_custom_call" | custom-call | bytes 1024 | tf_op jit(solution)/shard_map/queries/pallas_call | solution.py:74
  19.2 4.0 %local.1.refs_3_ = f32[960,512]{1,0:T(8,128)S(1)} custom-call(s32[16]{0:T(128)S(1)} %compare_select_fusion.2.scal, bf16[1536,512]{1,0:T(8,128)(2,1)S(1)} %get-tuple-element.227.fq_ref.refs_4_.refs_3_, bf16[1536,512]{1,0:T(8,128)(2,1)S(1)} %get-tuple-element.228.fk_ref.refs_4_, bf16[768,512]{1,0:T(8,128)(2,1)S(1)} %get-tuple-element.229.vt_ref.refs_5_), custom_call_target="tpu_custom_call" | custom-call | bytes 1024 | tf_op jit(solution)/shard_map/local/pallas_call | solution.py:74
  23.2 0.8 collective-permute-done.1.refs_1_
  24.3 4.4 %after.1 = (f32[768,512]{1,0:T(8,128)S(1)}, f32[16,512]{1,0:T(8,128)S(1)}, f32[512,768]{1,0:T(8,128)S(1)}, bf16[512,768]{1,0:T(8,128)(2,1)S(1)}, bf16[960,128]{1...) custom-call(s32[16]{0:T(128)S(1)} %compare_select_fusion.2.scal, ...), custom_call_target="tpu_custom_call", output_to_operand_aliasing={{5}: (9, {}), {6}: (10, {})} | custom-call | bytes 1024 | tf_op jit(solution)/shard_map/after/pallas_call | solution.py:74
  28.8 9.1 %mlp.2 = (f32[512,768]{1,0:T(8,128)S(1)}, f32[512,768]{1,0:T(8,128)S(1)}, bf16[2,2,512,768]{3,2,1,0:T(8,128)(2,1)S(1)}, f32[1,1536]{1,0:T(1,128)S(1)}) custom-call(s32[16]{0:T(128)S(1)} %compare_select_fusion.2.scal, bf16[512,768]{1,0:T(8,128)(2,1)S(1)} %get-tuple-element.243.h2_ref, bf16[512,768]{1,0:T(8,128)(2,1)} %g_ref.7, bf16[9280,768]{1,0:T(8,128)(2,1)} %bitcast.50, ...), custom_call_target="tpu_custom_call" | custom-call | bytes 1024 | tf_op jit(solution)/shard_map/mlp/pallas_call | solution.py:74
  38.5 9.1 %mlp.3 = (f32[512,768]{1,0:T(8,128)S(1)}, f32[512,768]{1,0:T(8,128)S(1)}, bf16[2,2,512,768]{3,2,1,0:T(8,128)(2,1)S(1)}, f32[1,1536]{1,0:T(1,128)S(1)}) custom-call(s32[16]{0:T(128)S(1)} %compare_select_fusion.2.scal, bf16[512,768]{1,0:T(8,128)(2,1)S(1)} %get-tuple-element.243.h2_ref, bf16[512,768]{1,0:T(8,128)(2,1)} %g_ref.7, bf16[9280,768]{1,0:T(8,128)(2,1)} %bitcast.52, ...), custom_call_target="tpu_custom_call" | custom-call | bytes 1024 | tf_op jit(solution)/shard_map/mlp/pallas_call | solution.py:74
  47.7 4.4 %mlp_grads.2 = (bf16[8,192,384]{2,1,0:T(8,128)(2,1)}, bf16[8,192,384]{2,1,0:T(8,128)(2,1)S(1)}) custom-call(s32[16]{0:T(128)S(1)} %compare_select_fusion.2.scal, bf16[4,384,512]{2,1,0:T(8,128)(2,1)S(1)} %get-tuple-element.259.refs_0_.refs_6_.refs_2_, bf16[4,384,512]{2,1,0:T(8,128)(2,1)S(1)} %collective-permute-done.3.refs_1_.refs_7_.refs_3_, ...), custom_call_target="tpu_custom_call" | custom-call | bytes 1024 | tf_op jit(solution)/shard_map/mlp_grads/pallas_call | solution.py:74
  52.1 1.0 copy-done.30
  53.1 1.6 collective-permute-start.9
  54.7 5.8 %back.1 = (bf16[512,768]{1,0:T(8,128)(2,1)}, f32[512,768]{1,0:T(8,128)S(1)}, bf16[768,512]{1,0:T(8,128)(2,1)S(1)}, bf16[960,512]{1,0:T(8,128)(2,1)S(1)}, bf16[960,128]{1,0:T(8,128)(2,1)}, /*index=5*/f32[4,768]{1,0:T(4,128)S(1)}) custom-call(s32[16]{0:T(128)S(1)} %compare_select_fusion.2.scal, f32[512,768]{1,0:T(8,128)S(1)} %get-tuple-element.267.out_ref, ...), custom_call_target="tpu_custom_call" | custom-call | bytes 1024 | tf_op jit(solution)/shard_map/back/pallas_call | solution.py:74
  60.5 1.1 copy-done.14
  61.7 0.9 copy-done.16
  62.6 0.9 copy-done.24
  63.5 1.8 collective-permute-start.8
  65.2 1.2 collective-permute-start.7
  67.0 1.9 copy-done.7
  68.9 1.9 %copy-done.9 = bf16[2,2,512,768]{3,2,1,0:T(8,128)(2,1)S(1)} copy-done((bf16[2,2,512,768]{3,2,1,0:T(8,128)(2,1)S(1)}, bf16[2,2,512,768]{3,2,1,0:T(8,128)(2,1)}, u32[]{:S(2)}) %copy-start.9) | copy-done | bytes 3145752
  70.9 3.6 %mlp_grads.3 = (bf16[8,192,384]{2,1,0:T(8,128)(2,1)S(1)}, bf16[8,192,384]{2,1,0:T(8,128)(2,1)S(1)}) custom-call(s32[16]{0:T(128)S(1)} %compare_select_fusion.2.scal, bf16[4,384,512]{2,1,0:T(8,128)(2,1)S(1)} %get-tuple-element.259.refs_0_.refs_6_.refs_2_, bf16[4,384,512]{2,1,0:T(8,128)(2,1)S(1)} %collective-permute-done.3.refs_1_.refs_7_.refs_3_, ...), custom_call_target="tpu_custom_call" | custom-call | bytes 1024 | tf_op jit(solution)/shard_map/mlp_grads/pallas_call | solution.py:74
  74.5 1.5 collective-permute-start.10
  76.0 2.1 %collective-permute-done.7.refs_1_ = bf16[960,128]{1,0:T(8,128)(2,1)} collective-permute-done((bf16[960,128]{1,0:T(8,128)(2,1)}, bf16[960,128]{1,0:T(8,128)(2,1)}, u32[]{:S(2)}, u32[]{:S(2)}) %collective-permute-start.7) | collective-permute-done | bytes 245792 | tf_op jit(solution)/shard_map/ppermute | solution.py:581
  78.2 13.1 %attend_back.1 = (bf16[4,768,512]{2,1,0:T(8,128)(2,1)S(1)}, f32[768,64]{1,0:T(8,128)S(1)}, f32[768,3]{1,0:T(8,128)S(1)}) custom-call(s32[16]{0:T(128)S(1)} %compare_select_fusion.2.scal, bf16[960,128]{1,0:T(8,128)(2,1)} %collective-permute-done.6.refs_0_, bf16[960,128]{1,0:T(8,128)(2,1)} %collective-permute-done.7.refs_1_, ...), custom_call_target="tpu_custom_call" | custom-call | flops 1000000000 | bytes 1024 | tf_op jit(solution)/shard_map/attend_back/pallas_call | solution.py:74
  91.4 7.8 %input.1 = (bf16[512,768]{1,0:T(8,128)(2,1)}, f32[1,384,128]{2,1,0:T(8,128)S(1)}, f32[1,384,128]{2,1,0:T(8,128)S(1)}) custom-call(s32[16]{0:T(128)S(1)} %compare_select_fusion.2.scal, bf16[4,768,512]{2,1,0:T(8,128)(2,1)S(1)} %get-tuple-element.299.dp_ref, bf16[9280,768]{1,0:T(8,128)(2,1)} %bitcast.56, bf16[512,768]{1,0:T(8,128)(2,1)} %x_ref.3, ...), custom_call_target="tpu_custom_call" | custom-call | bytes 1024 | tf_op jit(solution)/shard_map/input/pallas_call | solution.py:74
  99.2 2.1 %halve.6 = (bf16[4,192,384]{2,1,0:T(8,128)(2,1)S(1)}, bf16[4,192,384]{2,1,0:T(8,128)(2,1)S(1)}) custom-call(s32[16]{0:T(128)S(1)} %compare_select_fusion.2.scal, bf16[8,192,384]{2,1,0:T(8,128)(2,1)S(1)} %copy-done.31, bf16[8,192,384]{2,1,0:T(8,128)(2,1)} %collective-permute-done.9.recv_ref), custom_call_target="tpu_custom_call" | custom-call | flops 14000000000 | bytes 1024 | tf_op jit(solution)/shard_map/halve/pallas_call | solution.py:74
  101.3 1.6 collective-permute-start.13
  103.2 0.8 halve.7
  104.6 1.4 collective-permute-done.12.refs_9_
  106.0 5.7 %tail_grads.1 = (bf16[896,384]{1,0:T(8,128)(2,1)S(1)}, bf16[768,384]{1,0:T(8,128)(2,1)S(1)}, bf16[768,384]{1,0:T(8,128)(2,1)S(1)}, bf16[768,384]{1,0:T(8,128)(2,1)S(1)}, f32[128,384]{1,0:T(8,128)S(1)}) custom-call(s32[16]{0:T(128)S(1)} %compare_select_fusion.2.scal, bf16[4,384,512]{2,1,0:T(8,128)(2,1)S(1)} %get-tuple-element.259.refs_0_.refs_6_.refs_2_, ...), custom_call_target="tpu_custom_call" | custom-call | bytes 1024 | tf_op jit(solution)/shard_map/tail_grads/pallas_call | solution.py:74
  111.7 1.6 collective-permute-start.15
  113.2 0.8 collective-permute-start.16
  114.0 3.5 %collective-permute-done.13.recv_ref = bf16[4,192,384]{2,1,0:T(8,128)(2,1)S(1)} collective-permute-done((bf16[4,192,384]{2,1,0:T(8,128)(2,1)S(1)}, bf16[4,192,384]{2,1,0:T(8,128)(2,1)S(1)}, u32[]{:S(2)}, u32[]{:S(2)}) %collective-permute-start.13) | collective-permute-done | bytes 589856 | tf_op jit(solution)/shard_map/ppermute | solution.py:581
  117.5 0.7 halve.8
  118.2 2.7 %collective-permute-start.17 = (bf16[2,192,384]{2,1,0:T(8,128)(2,1)S(1)}, bf16[2,192,384]{2,1,0:T(8,128)(2,1)S(1)}, u32[]{:S(2)}, u32[]{:S(2)}) collective-permute-start(bf16[2,192,384]{2,1,0:T(8,128)(2,1)S(1)} %get-tuple-element.348), channel_id=1, source_target_pairs={{0,4},{1,5},{2,6},{3,7},{4,0},{5,1},{6,2},{7,3},{8,12},{9,13},{10,... | collective-permute-start | bytes 884744 | tf_op jit(solution)/shard_map/ppermute | solution.py:581
  120.9 0.7 halve.9
  121.6 1.6 collective-permute-start.18
  123.1 5.2 %collective-permute-done.16.recv_b = bf16[768,384]{1,0:T(8,128)(2,1)S(1)} collective-permute-done((bf16[768,384]{1,0:T(8,128)(2,1)S(1)}, bf16[768,384]{1,0:T(8,128)(2,1)S(1)}, u32[]{:S(2)}, u32[]{:S(2)}) %collective-permute-start.16) | collective-permute-done | bytes 589856 | tf_op jit(solution)/shard_map/ppermute | solution.py:581
  128.3 3.9 %collective-permute-done.15.recv_a = bf16[896,384]{1,0:T(8,128)(2,1)S(1)} collective-permute-done((bf16[896,384]{1,0:T(8,128)(2,1)S(1)}, bf16[896,384]{1,0:T(8,128)(2,1)S(1)}, u32[]{:S(2)}, u32[]{:S(2)}) %collective-permute-start.15) | collective-permute-done | bytes 688160 | tf_op jit(solution)/shard_map/ppermute | solution.py:581
  132.3 0.7 tail_one.1
  133.0 1.5 collective-permute-start.21
  134.5 0.9 collective-permute-start.22
  135.4 0.6 halve.10
  136.0 2.6 %collective-permute-done.18.recv_ref = bf16[2,192,384]{2,1,0:T(8,128)(2,1)S(1)} collective-permute-done((bf16[2,192,384]{2,1,0:T(8,128)(2,1)S(1)}, bf16[2,192,384]{2,1,0:T(8,128)(2,1)S(1)}, u32[]{:S(2)}, u32[]{:S(2)}) %collective-permute-start.18) | collective-permute-done | bytes 294944 | tf_op jit(solution)/shard_map/ppermute | solution.py:581
  138.6 0.6 halve.11
  139.2 2.7 %collective-permute-start.20 = (bf16[1,192,384]{2,1,0:T(8,128)(2,1)S(1)}, bf16[1,192,384]{2,1,0:T(8,128)(2,1)S(1)}, u32[]{:S(2)}, u32[]{:S(2)}) collective-permute-start(bf16[1,192,384]{2,1,0:T(8,128)(2,1)S(1)} %get-tuple-element.360), channel_id=1, source_target_pairs={{0,4},{1,5},{2,6},{3,7},{4,0},{5,1},{6,2},{7,3},{8,12},{9,13},{10,... | collective-permute-start | bytes 442376 | tf_op jit(solution)/shard_map/ppermute | solution.py:581
  141.9 1.4 collective-permute-start.19
  143.3 5.0 %collective-permute-done.20.refs_3_ = bf16[1,192,384]{2,1,0:T(8,128)(2,1)S(1)} collective-permute-done((bf16[1,192,384]{2,1,0:T(8,128)(2,1)S(1)}, bf16[1,192,384]{2,1,0:T(8,128)(2,1)S(1)}, u32[]{:S(2)}, u32[]{:S(2)}) %collective-permute-start.20) | collective-permute-done | bytes 147488 | tf_op jit(solution)/shard_map/ppermute | solution.py:581
  148.3 0.6 final.1
  148.9 1.6 collective-permute-start.26
  150.5 0.8 tail_two.1
  151.4 3.1 %collective-permute-start.24 = (bf16[224,384]{1,0:T(8,128)(2,1)S(1)}, bf16[224,384]{1,0:T(8,128)(2,1)S(1)}, u32[]{:S(2)}, u32[]{:S(2)}) collective-permute-start(bf16[224,384]{1,0:T(8,128)(2,1)S(1)} %get-tuple-element.371), channel_id=1, source_target_pairs={{0,4},{1,5},{2,6},{3,7},{4,0},{5,1},{6,2},{7,3},{8,12},{9,13},{10,... | collective-permute-start | bytes 516104 | tf_op jit(solution)/shard_map/ppermute | solution.py:581
  154.5 1.2 collective-permute-start.25
  155.7 0.8 collective-permute-start.27
  156.6 1.3 collective-permute-done.26.refs_1_
  157.9 1.4 collective-permute-start.28
  159.3 1.0 collective-permute-done.23.refs_1_
  160.3 6.7 %collective-permute-done.24.refs_2_ = bf16[224,384]{1,0:T(8,128)(2,1)S(1)} collective-permute-done((bf16[224,384]{1,0:T(8,128)(2,1)S(1)}, bf16[224,384]{1,0:T(8,128)(2,1)S(1)}, u32[]{:S(2)}, u32[]{:S(2)}) %collective-permute-start.24) | collective-permute-done | bytes 172064 | tf_op jit(solution)/shard_map/ppermute | solution.py:581
  167.0 0.6 tail_final.1
  167.7 1.5 collective-permute-start.31
  169.8 1.5 collective-permute-start.29
  171.3 3.3 %collective-permute-done.28.refs_3_ = bf16[4,96,384]{2,1,0:T(8,128)(2,1)S(1)} collective-permute-done((bf16[4,96,384]{2,1,0:T(8,128)(2,1)S(1)}, bf16[4,96,384]{2,1,0:T(8,128)(2,1)S(1)}, u32[]{:S(2)}, u32[]{:S(2)}) %collective-permute-start.28) | collective-permute-done | bytes 294944 | tf_op jit(solution)/shard_map/ppermute | solution.py:581
  174.6 8.0 %adam.2 = (f32[96,9280]{1,0:T(8,128)}, f32[96,9280]{1,0:T(8,128)}, f32[96,9280]{1,0:T(8,128)}, f32[96,9280]{1,0:T(8,128)}, f32[96,9280]{1,0:T(8,128)}, /*index=5*/bf16[96,9280]{1,0:T(8,128)(2,1)}) custom-call(s32[16]{0:T(128)S(1)} %compare_select_fusion.2.scal, bf16[4,96,384]{2,1,0:T(8,128)(2,1)S(1)} %bitcast.30, ...), custom_call_target="tpu_custom_call" | custom-call | bytes 1024 | tf_op jit(solution)/shard_map/adam/pallas_call | solution.py:74
  182.7 5.3 %adam.3 = (f32[96,9280]{1,0:T(8,128)}, f32[96,9280]{1,0:T(8,128)}, f32[96,9280]{1,0:T(8,128)}, f32[96,9280]{1,0:T(8,128)}, f32[96,9280]{1,0:T(8,128)}, /*index=5...) custom-call(s32[16]{0:T(128)S(1)} %compare_select_fusion.2.scal, ...), custom_call_target="tpu_custom_call", output_to_operand_aliasing={{0}: (14, {}), {1}: (15, {}), {2}: (16, {}), {3}: (17, {}),... | custom-call | bytes 1024 | tf_op jit(solution)/shard_map/adam/pallas_call | solution.py:74
  (93 shorter events, 4.2 us)
Async XLA Ops:
  1.5 0.7 copy-start.18
  8.8 10.3 %copy-start.20 = (bf16[768,512]{1,0:T(8,128)(2,1)}, bf16[768,512]{1,0:T(8,128)(2,1)S(1)}, u32[]{:S(2)}) copy-start(bf16[768,512]{1,0:T(8,128)(2,1)S(1)} %get-tuple-element.293.refs_9_) | copy-start | bytes 2359300
  8.8 10.3 %copy-start.10 = (bf16[1536,512]{1,0:T(8,128)(2,1)}, bf16[1536,512]{1,0:T(8,128)(2,1)S(1)}, u32[]{:S(2)}) copy-start(bf16[1536,512]{1,0:T(8,128)(2,1)S(1)} %get-tuple-element.228.fk_ref.refs_4_) | copy-start | bytes 4718596
  8.8 10.3 %copy-start.12 = (bf16[768,512]{1,0:T(8,128)(2,1)}, bf16[768,512]{1,0:T(8,128)(2,1)S(1)}, u32[]{:S(2)}) copy-start(bf16[768,512]{1,0:T(8,128)(2,1)S(1)} %get-tuple-element.229.vt_ref.refs_5_) | copy-start | bytes 2359300
  8.8 14.4 %collective-permute-start.2 = (bf16[960,128]{1,0:T(8,128)(2,1)S(1)}, bf16[960,128]{1,0:T(8,128)(2,1)S(1)}, u32[]{:S(2)}, u32[]{:S(2)}) collective-permute-start(bf16[960,128]{1,0:T(8,128)(2,1)S(1)} %get-tuple-element.231), channel_id=1, source_target_pairs={{0,24},{8,16},{16,8},{24,0},{1,25},{9,17},{17,9},{25,1},{2,26},{10... | collective-permute-start | bytes 737288 | tf_op jit(solution)/shard_map/ppermute | solution.py:581
  12.8 11.2 %collective-permute-start.1 = (bf16[960,128]{1,0:T(8,128)(2,1)S(1)}, bf16[960,128]{1,0:T(8,128)(2,1)S(1)}, u32[]{:S(2)}, u32[]{:S(2)}) collective-permute-start(bf16[960,128]{1,0:T(8,128)(2,1)S(1)} %get-tuple-element.231), channel_id=1, source_target_pairs={{0,16},{8,24},{16,0},{24,8},{1,17},{9,25},{17,1},{25,9},{2,18},{10... | collective-permute-start | bytes 737288 | tf_op jit(solution)/shard_map/ppermute | solution.py:581
  13.3 11.0 %collective-permute-start = (bf16[960,128]{1,0:T(8,128)(2,1)S(1)}, bf16[960,128]{1,0:T(8,128)(2,1)S(1)}, u32[]{:S(2)}, u32[]{:S(2)}) collective-permute-start(bf16[960,128]{1,0:T(8,128)(2,1)S(1)} %get-tuple-element.231), channel_id=1, source_target_pairs={{0,8},{8,0},{16,24},{24,16},{1,9},{9,1},{17,25},{25,17},{2,10},{10... | collective-permute-start | bytes 737288 | tf_op jit(solution)/shard_map/ppermute | solution.py:581
  19.1 4.1 %copy-start.22 = (bf16[768,512]{1,0:T(8,128)(2,1)}, bf16[768,512]{1,0:T(8,128)(2,1)S(1)}, u32[]{:S(2)}) copy-start(bf16[768,512]{1,0:T(8,128)(2,1)S(1)} %get-tuple-element.292.refs_8_) | copy-start | bytes 2359300
  19.1 35.5 %copy-start = (bf16[1536,512]{1,0:T(8,128)(2,1)}, bf16[1536,512]{1,0:T(8,128)(2,1)S(1)}, u32[]{:S(2)}) copy-start(bf16[1536,512]{1,0:T(8,128)(2,1)S(1)} %get-tuple-element.227.fq_ref.refs_4_.refs_3_) | copy-start | bytes 4718596
  28.7 9.8 %collective-permute-start.3 = (bf16[4,384,512]{2,1,0:T(8,128)(2,1)S(1)}, bf16[4,384,512]{2,1,0:T(8,128)(2,1)S(1)}, u32[]{:S(2)}, u32[]{:S(2)}) collective-permute-start(bf16[4,384,512]{2,1,0:T(8,128)(2,1)S(1)} %get-tuple-element.250), channel_id=1, source_target_pairs={{0,1},{1,0},{2,3},{3,2},{4,5},{5,4},{6,7},{7,6},{8,9},{9,8},{10,11... | collective-permute-start | bytes 4718600 | tf_op jit(solution)/shard_map/ppermute | solution.py:581
  37.9 9.8 %collective-permute-start.4 = (bf16[2,2,512,768]{3,2,1,0:T(8,128)(2,1)S(1)}, bf16[2,2,512,768]{3,2,1,0:T(8,128)(2,1)S(1)}, u32[]{:S(2)}, u32[]{:S(2)}) collective-permute-start(bf16[2,2,512,768]{3,2,1,0:T(8,128)(2,1)S(1)} %get-tuple-element.261.refs_2_.refs_4_), channel_id=1, source_target_pairs={{0,1},{1,0},{2,3},{3,2},{4,5},{5,4},{6,7},{7,6},{8,9},{9,8},{10,11... | collective-permute-start | bytes 9437192 | tf_op jit(solution)/shard_map/ppermute | solution.py:581
  47.6 4.5 %copy-start.6 = (bf16[2,2,512,768]{3,2,1,0:T(8,128)(2,1)}, bf16[2,2,512,768]{3,2,1,0:T(8,128)(2,1)S(1)}, u32[]{:S(2)}) copy-start(bf16[2,2,512,768]{3,2,1,0:T(8,128)(2,1)S(1)} %get-tuple-element.280.refs_2_.refs_4_) | copy-start | bytes 9437188
  47.6 7.1 %copy-start.19 = (bf16[768,13]{0,1:T(8,128)(2,1)S(1)}, bf16[768,13]{0,1:T(8,128)(2,1)}, u32[]{:S(2)}) copy-start(bf16[768,13]{0,1:T(8,128)(2,1)} %param.17) | copy-start | bytes 59908
  47.6 7.1 %collective-permute-start.5 = (bf16[2,2,512,768]{3,2,1,0:T(8,128)(2,1)S(1)}, bf16[2,2,512,768]{3,2,1,0:T(8,128)(2,1)S(1)}, u32[]{:S(2)}, u32[]{:S(2)}) collective-permute-start(bf16[2,2,512,768]{3,2,1,0:T(8,128)(2,1)S(1)} %get-tuple-element.280.refs_2_.refs_4_), channel_id=1, source_target_pairs={{0,1},{1,0},{2,3},{3,2},{4,5},{5,4},{6,7},{7,6},{8,9},{9,8},{10,11... | collective-permute-start | bytes 9437192 | tf_op jit(solution)/shard_map/ppermute | solution.py:581
  52.1 1.0 copy-start.30
  53.1 46.1 %collective-permute-start.9 = (bf16[8,192,384]{2,1,0:T(8,128)(2,1)}, bf16[8,192,384]{2,1,0:T(8,128)(2,1)}, u32[]{:S(2)}, u32[]{:S(2)}) collective-permute-start(bf16[8,192,384]{2,1,0:T(8,128)(2,1)} %get-tuple-element.312), channel_id=1, source_target_pairs={{0,2},{1,3},{2,0},{3,1},{4,6},{5,7},{6,4},{7,5},{8,10},{9,11},{10,... | collective-permute-start | bytes 3538952 | tf_op jit(solution)/shard_map/ppermute | solution.py:581
  54.7 5.8 %copy-start.8 = (bf16[2,2,512,768]{3,2,1,0:T(8,128)(2,1)}, bf16[2,2,512,768]{3,2,1,0:T(8,128)(2,1)S(1)}, u32[]{:S(2)}) copy-start(bf16[2,2,512,768]{3,2,1,0:T(8,128)(2,1)S(1)} %collective-permute-done.5.refs_3_.refs_5_) | copy-start | bytes 9437188
  60.5 1.1 copy-start.14
  61.7 0.9 copy-start.16
  62.6 0.9 copy-start.24
  63.5 12.5 %collective-permute-start.8 = (bf16[960,128]{1,0:T(8,128)(2,1)}, bf16[960,128]{1,0:T(8,128)(2,1)}, u32[]{:S(2)}, u32[]{:S(2)}) collective-permute-start(bf16[960,128]{1,0:T(8,128)(2,1)} %get-tuple-element.285), channel_id=1, source_target_pairs={{0,24},{8,16},{16,8},{24,0},{1,25},{9,17},{17,9},{25,1},{2,26},{10... | collective-permute-start | bytes 737288 | tf_op jit(solution)/shard_map/ppermute | solution.py:581
  65.2 12.9 %collective-permute-start.7 = (bf16[960,128]{1,0:T(8,128)(2,1)}, bf16[960,128]{1,0:T(8,128)(2,1)}, u32[]{:S(2)}, u32[]{:S(2)}) collective-permute-start(bf16[960,128]{1,0:T(8,128)(2,1)} %get-tuple-element.285), channel_id=1, source_target_pairs={{0,16},{8,24},{16,0},{24,8},{1,17},{9,25},{17,1},{25,9},{2,18},{10... | collective-permute-start | bytes 737288 | tf_op jit(solution)/shard_map/ppermute | solution.py:581
  66.4 11.7 %collective-permute-start.6 = (bf16[960,128]{1,0:T(8,128)(2,1)}, bf16[960,128]{1,0:T(8,128)(2,1)}, u32[]{:S(2)}, u32[]{:S(2)}) collective-permute-start(bf16[960,128]{1,0:T(8,128)(2,1)} %get-tuple-element.285), channel_id=1, source_target_pairs={{0,8},{8,0},{16,24},{24,16},{1,9},{9,1},{17,25},{25,17},{2,10},{10... | collective-permute-start | bytes 737288 | tf_op jit(solution)/shard_map/ppermute | solution.py:581
  67.0 1.9 %copy-start.7 = (bf16[2,2,512,768]{3,2,1,0:T(8,128)(2,1)S(1)}, bf16[2,2,512,768]{3,2,1,0:T(8,128)(2,1)}, u32[]{:S(2)}) copy-start(bf16[2,2,512,768]{3,2,1,0:T(8,128)(2,1)} %copy-done.6) | copy-start | bytes 9437188
  68.9 1.9 %copy-start.9 = (bf16[2,2,512,768]{3,2,1,0:T(8,128)(2,1)S(1)}, bf16[2,2,512,768]{3,2,1,0:T(8,128)(2,1)}, u32[]{:S(2)}) copy-start(bf16[2,2,512,768]{3,2,1,0:T(8,128)(2,1)} %copy-done.8) | copy-start | bytes 9437188
  70.8 7.3 %copy-start.1 = (bf16[1536,512]{1,0:T(8,128)(2,1)S(1)}, bf16[1536,512]{1,0:T(8,128)(2,1)}, u32[]{:S(2)}) copy-start(bf16[1536,512]{1,0:T(8,128)(2,1)} %copy-done) | copy-start | bytes 4718596
  70.8 7.3 %copy-start.11 = (bf16[1536,512]{1,0:T(8,128)(2,1)S(1)}, bf16[1536,512]{1,0:T(8,128)(2,1)}, u32[]{:S(2)}) copy-start(bf16[1536,512]{1,0:T(8,128)(2,1)} %copy-done.10) | copy-start | bytes 4718596
  70.8 7.3 %copy-start.13 = (bf16[768,512]{1,0:T(8,128)(2,1)S(1)}, bf16[768,512]{1,0:T(8,128)(2,1)}, u32[]{:S(2)}) copy-start(bf16[768,512]{1,0:T(8,128)(2,1)} %copy-done.12) | copy-start | bytes 2359300
  70.8 7.3 %copy-start.17 = (bf16[960,512]{1,0:T(8,128)(2,1)S(1)}, bf16[960,512]{1,0:T(8,128)(2,1)}, u32[]{:S(2)}) copy-start(bf16[960,512]{1,0:T(8,128)(2,1)} %copy-done.16) | copy-start | bytes 2949124
  70.8 7.3 %copy-start.21 = (bf16[768,512]{1,0:T(8,128)(2,1)S(1)}, bf16[768,512]{1,0:T(8,128)(2,1)}, u32[]{:S(2)}) copy-start(bf16[768,512]{1,0:T(8,128)(2,1)} %copy-done.20) | copy-start | bytes 2359300
  70.8 7.3 %copy-start.23 = (bf16[768,512]{1,0:T(8,128)(2,1)S(1)}, bf16[768,512]{1,0:T(8,128)(2,1)}, u32[]{:S(2)}) copy-start(bf16[768,512]{1,0:T(8,128)(2,1)} %copy-done.22) | copy-start | bytes 2359300
  70.8 7.3 %copy-start.25 = (bf16[768,512]{1,0:T(8,128)(2,1)S(1)}, bf16[768,512]{1,0:T(8,128)(2,1)}, u32[]{:S(2)}) copy-start(bf16[768,512]{1,0:T(8,128)(2,1)} %copy-done.24) | copy-start | bytes 2359300
  74.5 16.9 %copy-start.15 = (f32[512,768]{1,0:T(8,128)S(1)}, f32[512,768]{1,0:T(8,128)}, u32[]{:S(2)}) copy-start(f32[512,768]{1,0:T(8,128)} %copy-done.14) | copy-start | bytes 4718596
  74.5 28.7 %collective-permute-start.10 = (bf16[8,192,384]{2,1,0:T(8,128)(2,1)S(1)}, bf16[8,192,384]{2,1,0:T(8,128)(2,1)S(1)}, u32[]{:S(2)}, u32[]{:S(2)}) collective-permute-start(bf16[8,192,384]{2,1,0:T(8,128)(2,1)S(1)} %get-tuple-element.317), channel_id=1, source_target_pairs={{0,16},{8,24},{16,0},{24,8},{1,17},{9,25},{17,1},{25,9},{2,18},{10... | collective-permute-start | bytes 3538952 | tf_op jit(solution)/shard_map/ppermute | solution.py:581
  91.3 7.9 %copy-start.31 = (bf16[8,192,384]{2,1,0:T(8,128)(2,1)S(1)}, bf16[8,192,384]{2,1,0:T(8,128)(2,1)}, u32[]{:S(2)}) copy-start(bf16[8,192,384]{2,1,0:T(8,128)(2,1)} %copy-done.30) | copy-start | bytes 3538948
  91.3 14.7 %collective-permute-start.11 = (bf16[4,768,512]{2,1,0:T(8,128)(2,1)S(1)}, bf16[4,768,512]{2,1,0:T(8,128)(2,1)S(1)}, u32[]{:S(2)}, u32[]{:S(2)}) collective-permute-start(bf16[4,768,512]{2,1,0:T(8,128)(2,1)S(1)} %get-tuple-element.299.dp_ref), channel_id=1, source_target_pairs={{0,1},{1,0},{2,3},{3,2},{4,5},{5,4},{6,7},{7,6},{8,9},{9,8},{10,11... | collective-permute-start | bytes 9437192 | tf_op jit(solution)/shard_map/ppermute | solution.py:581
  101.3 16.2 %collective-permute-start.13 = (bf16[4,192,384]{2,1,0:T(8,128)(2,1)S(1)}, bf16[4,192,384]{2,1,0:T(8,128)(2,1)S(1)}, u32[]{:S(2)}, u32[]{:S(2)}) collective-permute-start(bf16[4,192,384]{2,1,0:T(8,128)(2,1)S(1)} %get-tuple-element.330), channel_id=1, source_target_pairs={{0,8},{8,0},{16,24},{24,16},{1,9},{9,1},{17,25},{25,17},{2,10},{10... | collective-permute-start | bytes 1769480 | tf_op jit(solution)/shard_map/ppermute | solution.py:581
  104.0 16.8 %collective-permute-start.14 = (bf16[4,192,384]{2,1,0:T(8,128)(2,1)S(1)}, bf16[4,192,384]{2,1,0:T(8,128)(2,1)S(1)}, u32[]{:S(2)}, u32[]{:S(2)}) collective-permute-start(bf16[4,192,384]{2,1,0:T(8,128)(2,1)S(1)} %get-tuple-element.335), channel_id=1, source_target_pairs={{0,2},{1,3},{2,0},{3,1},{4,6},{5,7},{6,4},{7,5},{8,10},{9,11},{10,... | collective-permute-start | bytes 1769480 | tf_op jit(solution)/shard_map/ppermute | solution.py:581
  104.6 1.4 collective-permute-start.12
  111.7 20.6 %collective-permute-start.15 = (bf16[896,384]{1,0:T(8,128)(2,1)S(1)}, bf16[896,384]{1,0:T(8,128)(2,1)S(1)}, u32[]{:S(2)}, u32[]{:S(2)}) collective-permute-start(bf16[896,384]{1,0:T(8,128)(2,1)S(1)} %get-tuple-element.340), channel_id=1, source_target_pairs={{0,8},{8,0},{16,24},{24,16},{1,9},{9,1},{17,25},{25,17},{2,10},{10... | collective-permute-start | bytes 2064392 | tf_op jit(solution)/shard_map/ppermute | solution.py:581
  113.2 15.1 %collective-permute-start.16 = (bf16[768,384]{1,0:T(8,128)(2,1)S(1)}, bf16[768,384]{1,0:T(8,128)(2,1)S(1)}, u32[]{:S(2)}, u32[]{:S(2)}) collective-permute-start(bf16[768,384]{1,0:T(8,128)(2,1)S(1)} %get-tuple-element.342), channel_id=1, source_target_pairs={{0,16},{8,24},{16,0},{24,8},{1,17},{9,25},{17,1},{25,9},{2,18},{10... | collective-permute-start | bytes 1769480 | tf_op jit(solution)/shard_map/ppermute | solution.py:581
  118.2 17.2 %collective-permute-start.17 = (bf16[2,192,384]{2,1,0:T(8,128)(2,1)S(1)}, bf16[2,192,384]{2,1,0:T(8,128)(2,1)S(1)}, u32[]{:S(2)}, u32[]{:S(2)}) collective-permute-start(bf16[2,192,384]{2,1,0:T(8,128)(2,1)S(1)} %get-tuple-element.348), channel_id=1, source_target_pairs={{0,4},{1,5},{2,6},{3,7},{4,0},{5,1},{6,2},{7,3},{8,12},{9,13},{10,... | collective-permute-start | bytes 884744 | tf_op jit(solution)/shard_map/ppermute | solution.py:581
  121.6 17.0 %collective-permute-start.18 = (bf16[2,192,384]{2,1,0:T(8,128)(2,1)S(1)}, bf16[2,192,384]{2,1,0:T(8,128)(2,1)S(1)}, u32[]{:S(2)}, u32[]{:S(2)}) collective-permute-start(bf16[2,192,384]{2,1,0:T(8,128)(2,1)S(1)} %get-tuple-element.353), channel_id=1, source_target_pairs={{0,8},{8,0},{16,24},{24,16},{1,9},{9,1},{17,25},{25,17},{2,10},{10... | collective-permute-start | bytes 884744 | tf_op jit(solution)/shard_map/ppermute | solution.py:581
  133.0 17.5 %collective-permute-start.21 = (bf16[512,384]{1,0:T(8,128)(2,1)S(1)}, bf16[512,384]{1,0:T(8,128)(2,1)S(1)}, u32[]{:S(2)}, u32[]{:S(2)}) collective-permute-start(bf16[512,384]{1,0:T(8,128)(2,1)S(1)} %get-tuple-element.362), channel_id=1, source_target_pairs={{0,16},{8,24},{16,0},{24,8},{1,17},{9,25},{17,1},{25,9},{2,18},{10... | collective-permute-start | bytes 1179656 | tf_op jit(solution)/shard_map/ppermute | solution.py:581
  134.5 16.0 %collective-permute-start.22 = (bf16[384,384]{1,0:T(8,128)(2,1)S(1)}, bf16[384,384]{1,0:T(8,128)(2,1)S(1)}, u32[]{:S(2)}, u32[]{:S(2)}) collective-permute-start(bf16[384,384]{1,0:T(8,128)(2,1)S(1)} %get-tuple-element.363), channel_id=1, source_target_pairs={{0,8},{8,0},{16,24},{24,16},{1,9},{9,1},{17,25},{25,17},{2,10},{10... | collective-permute-start | bytes 884744 | tf_op jit(solution)/shard_map/ppermute | solution.py:581
  139.2 9.1 %collective-permute-start.20 = (bf16[1,192,384]{2,1,0:T(8,128)(2,1)S(1)}, bf16[1,192,384]{2,1,0:T(8,128)(2,1)S(1)}, u32[]{:S(2)}, u32[]{:S(2)}) collective-permute-start(bf16[1,192,384]{2,1,0:T(8,128)(2,1)S(1)} %get-tuple-element.360), channel_id=1, source_target_pairs={{0,4},{1,5},{2,6},{3,7},{4,0},{5,1},{6,2},{7,3},{8,12},{9,13},{10,... | collective-permute-start | bytes 442376 | tf_op jit(solution)/shard_map/ppermute | solution.py:581
  141.9 6.4 %collective-permute-start.19 = (bf16[1,192,384]{2,1,0:T(8,128)(2,1)S(1)}, bf16[1,192,384]{2,1,0:T(8,128)(2,1)S(1)}, u32[]{:S(2)}, u32[]{:S(2)}) collective-permute-start(bf16[1,192,384]{2,1,0:T(8,128)(2,1)S(1)} %get-tuple-element.358), channel_id=1, source_target_pairs={{0,16},{8,24},{16,0},{24,8},{1,17},{9,25},{17,1},{25,9},{2,18},{10... | collective-permute-start | bytes 442376 | tf_op jit(solution)/shard_map/ppermute | solution.py:581
  148.9 9.0 %collective-permute-start.26 = (bf16[4,96,384]{2,1,0:T(8,128)(2,1)S(1)}, bf16[4,96,384]{2,1,0:T(8,128)(2,1)S(1)}, u32[]{:S(2)}, u32[]{:S(2)}) collective-permute-start(bf16[4,96,384]{2,1,0:T(8,128)(2,1)S(1)} %bitcast.28), channel_id=1, source_target_pairs={{0,8},{8,0},{16,24},{24,16},{1,9},{9,1},{17,25},{25,17},{2,10},{10... | collective-permute-start | bytes 884744 | tf_op jit(solution)/shard_map/ppermute | solution.py:581
  151.3 9.1 %collective-permute-start.23 = (bf16[224,384]{1,0:T(8,128)(2,1)S(1)}, bf16[224,384]{1,0:T(8,128)(2,1)S(1)}, u32[]{:S(2)}, u32[]{:S(2)}) collective-permute-start(bf16[224,384]{1,0:T(8,128)(2,1)S(1)} %get-tuple-element.370), channel_id=1, source_target_pairs={{0,2},{1,3},{2,0},{3,1},{4,6},{5,7},{6,4},{7,5},{8,10},{9,11},{10,... | collective-permute-start | bytes 516104 | tf_op jit(solution)/shard_map/ppermute | solution.py:581
  151.4 15.6 %collective-permute-start.24 = (bf16[224,384]{1,0:T(8,128)(2,1)S(1)}, bf16[224,384]{1,0:T(8,128)(2,1)S(1)}, u32[]{:S(2)}, u32[]{:S(2)}) collective-permute-start(bf16[224,384]{1,0:T(8,128)(2,1)S(1)} %get-tuple-element.371), channel_id=1, source_target_pairs={{0,4},{1,5},{2,6},{3,7},{4,0},{5,1},{6,2},{7,3},{8,12},{9,13},{10,... | collective-permute-start | bytes 516104 | tf_op jit(solution)/shard_map/ppermute | solution.py:581
  154.5 12.5 %collective-permute-start.25 = (bf16[224,384]{1,0:T(8,128)(2,1)S(1)}, bf16[224,384]{1,0:T(8,128)(2,1)S(1)}, u32[]{:S(2)}, u32[]{:S(2)}) collective-permute-start(bf16[224,384]{1,0:T(8,128)(2,1)S(1)} %get-tuple-element.372), channel_id=1, source_target_pairs={{0,6},{1,7},{2,4},{3,5},{4,2},{5,3},{6,0},{7,1},{8,14},{9,15},{10,... | collective-permute-start | bytes 516104 | tf_op jit(solution)/shard_map/ppermute | solution.py:581
  155.7 15.5 %collective-permute-start.27 = (bf16[4,96,384]{2,1,0:T(8,128)(2,1)S(1)}, bf16[4,96,384]{2,1,0:T(8,128)(2,1)S(1)}, u32[]{:S(2)}, u32[]{:S(2)}) collective-permute-start(bf16[4,96,384]{2,1,0:T(8,128)(2,1)S(1)} %bitcast.29), channel_id=1, source_target_pairs={{0,16},{8,24},{16,0},{24,8},{1,17},{9,25},{17,1},{25,9},{2,18},{10... | collective-permute-start | bytes 884744 | tf_op jit(solution)/shard_map/ppermute | solution.py:581
  157.9 16.7 %collective-permute-start.28 = (bf16[4,96,384]{2,1,0:T(8,128)(2,1)S(1)}, bf16[4,96,384]{2,1,0:T(8,128)(2,1)S(1)}, u32[]{:S(2)}, u32[]{:S(2)}) collective-permute-start(bf16[4,96,384]{2,1,0:T(8,128)(2,1)S(1)} %collective-permute-done.26.refs_1_), channel_id=1, source_target_pairs={{0,16},{8,24},{16,0},{24,8},{1,17},{9,25},{17,1},{25,9},{2,18},{10... | collective-permute-start | bytes 884744 | tf_op jit(solution)/shard_map/ppermute | solution.py:581
  167.0 7.6 %copy-start.2 = (f32[96,9280]{1,0:T(8,128)S(1)}, f32[96,9280]{1,0:T(8,128)}, u32[]{:S(2)}) copy-start(f32[96,9280]{1,0:T(8,128)} %refs_9_.1) | copy-start | bytes 10690564
  167.0 7.6 %copy-start.3 = (f32[96,9280]{1,0:T(8,128)S(1)}, f32[96,9280]{1,0:T(8,128)}, u32[]{:S(2)}) copy-start(f32[96,9280]{1,0:T(8,128)} %refs_10_.1) | copy-start | bytes 10690564
  167.0 7.6 %copy-start.4 = (f32[96,9280]{1,0:T(8,128)S(1)}, f32[96,9280]{1,0:T(8,128)}, u32[]{:S(2)}) copy-start(f32[96,9280]{1,0:T(8,128)} %refs_11_.1) | copy-start | bytes 10690564
  167.0 7.6 %copy-start.5 = (f32[96,9280]{1,0:T(8,128)S(1)}, f32[96,9280]{1,0:T(8,128)}, u32[]{:S(2)}) copy-start(f32[96,9280]{1,0:T(8,128)} %refs_12_.1) | copy-start | bytes 10690564
  167.7 15.0 %copy-start.26 = (f32[96,13]{0,1:T(8,128)S(1)}, f32[96,13]{0,1:T(8,128)}, u32[]{:S(2)}) copy-start(f32[96,13]{0,1:T(8,128)} %param.19) | copy-start | bytes 14980
  167.7 15.0 %copy-start.27 = (f32[96,13]{0,1:T(8,128)S(1)}, f32[96,13]{0,1:T(8,128)}, u32[]{:S(2)}) copy-start(f32[96,13]{0,1:T(8,128)} %param.21) | copy-start | bytes 14980
  167.7 15.0 %copy-start.28 = (f32[96,13]{0,1:T(8,128)S(1)}, f32[96,13]{0,1:T(8,128)}, u32[]{:S(2)}) copy-start(f32[96,13]{0,1:T(8,128)} %param.23) | copy-start | bytes 14980
  167.7 15.0 %copy-start.29 = (f32[96,13]{0,1:T(8,128)S(1)}, f32[96,13]{0,1:T(8,128)}, u32[]{:S(2)}) copy-start(f32[96,13]{0,1:T(8,128)} %param.25) | copy-start | bytes 14980
  167.7 14.9 %collective-permute-start.31 = (bf16[2,96,384]{2,1,0:T(8,128)(2,1)S(1)}, bf16[2,96,384]{2,1,0:T(8,128)(2,1)S(1)}, u32[]{:S(2)}, u32[]{:S(2)}) collective-permute-start(bf16[2,96,384]{2,1,0:T(8,128)(2,1)S(1)} %get-tuple-element.384.refs_0_), channel_id=1, source_target_pairs={{0,24},{8,16},{16,8},{24,0},{1,25},{9,17},{17,9},{25,1},{2,26},{10... | collective-permute-start | bytes 442376 | tf_op jit(solution)/shard_map/ppermute | solution.py:581
  169.2 13.5 %collective-permute-start.30 = (bf16[2,96,384]{2,1,0:T(8,128)(2,1)S(1)}, bf16[2,96,384]{2,1,0:T(8,128)(2,1)S(1)}, u32[]{:S(2)}, u32[]{:S(2)}) collective-permute-start(bf16[2,96,384]{2,1,0:T(8,128)(2,1)S(1)} %get-tuple-element.384.refs_0_), channel_id=1, source_target_pairs={{0,16},{8,24},{16,0},{24,8},{1,17},{9,25},{17,1},{25,9},{2,18},{10... | collective-permute-start | bytes 442376 | tf_op jit(solution)/shard_map/ppermute | solution.py:581
  169.8 12.9 %collective-permute-start.29 = (bf16[2,96,384]{2,1,0:T(8,128)(2,1)S(1)}, bf16[2,96,384]{2,1,0:T(8,128)(2,1)S(1)}, u32[]{:S(2)}, u32[]{:S(2)}) collective-permute-start(bf16[2,96,384]{2,1,0:T(8,128)(2,1)S(1)} %get-tuple-element.384.refs_0_), channel_id=1, source_target_pairs={{0,8},{8,0},{16,24},{24,16},{1,9},{9,1},{17,25},{25,17},{2,10},{10... | collective-permute-start | bytes 442376 | tf_op jit(solution)/shard_map/ppermute | solution.py:581

commit v3 on v2

--- a/solution.py
+++ b/solution.py
@@ -66,14 +66,14 @@
         return values
 
     def call(self, body, args, in_specs, outs, out_specs, grid=(1,), scratch=(), vmem=32,
-             hold=0, far=(), aliases=None, name=None):
+             hold=0, far=(), out_far=(), aliases=None, name=None):
         args = [
             pltpu.with_memory_space_constraint(a, pltpu.HBM) if id(a) in self.stay or k in far else a
             for k, a in enumerate(args)
         ]
         got = pl.pallas_call(
             body,
-            out_shape=tuple(outs),
+            out_shape=tuple(pltpu.HBM(o.shape, o.dtype) if k in out_far else o for k, o in enumerate(outs)),
             grid_spec=pltpu.PrefetchScalarGridSpec(
                 num_scalar_prefetch=1,
                 grid=grid,
@@ -474,7 +474,7 @@
                         ref[2 * at + base, rows, :] = part(z)
 
 
-def mlp_grads(line, by_y, sels, acts):
+def mlp_grads(line, by_y, sels, acts, far=(), out_far=()):
     _, depth, rows = sels[0].shape
     half = sds((8, 2 * (D // 8), D // 2), bf16)
 
@@ -491,7 +491,9 @@
         [half] * 2,
         [whole(half.shape)] * 2,
         grid=(2,),
-        vmem=10,
+        vmem=24,
+        far=far,
+        out_far=out_far,
         name="mlp_grads",
     )
 
@@ -573,6 +575,7 @@
         [whole(o.shape) for o in outs],
         grid=(4,),
         vmem=10,
+        hold=4,
         name="tail_grads",
     )
 
@@ -924,7 +927,7 @@
 
     if fast:
         first = Halves(
-            line, *mlp_grads(line, False, sels, acts[0]),
+            line, *mlp_grads(line, False, sels, acts[0], out_far=(1,)),
             [("grp", 8, 2), ("seq", 4, 1), ("grp", 8, 4), ("seq", 4, 2)],
         )
         (acts[1],) = line.wait(acts[1])
@@ -945,11 +948,12 @@
         + [whole((D, rows)), whole((HEADS * AUG, rows)), whole(st_shape), whole((4, D))],
         scratch=[pltpu.VMEM((D, rows), bf16)],
         vmem=10,
+        out_far=(1, 2, 3),
         name="back",
     )
     back_states = [swap(ds_own, "seq", n_seq, k + 1) for k in range(n_peer)]
     if fast:
-        second = mlp_grads(line, True, sels, acts[1])
+        second = mlp_grads(line, True, sels, acts[1], far=range(2, 6))
         (back_states,) = line.wait(back_states)
         second = Halves(
             line, *second, [("seq", 4, 2), ("grp", 8, 2), ("seq", 4, 1), ("grp", 8, 4)]
@@ -979,7 +983,8 @@
             grid=(count,),
             aliases={1 + len(args) + k: k for k in range(len(got))},
             hold=1,
-            vmem=12,
+            far=(n_peer + 3, n_peer + 8),
+            vmem=16,
             name="attend_back",
         )
     dp, dm, db_qkv = got

time: 189 us -> 183 us (0.968)
  local copies, waits for them, and re-layouts: 8.66 us -> 1.01 us
  Pallas kernels: 101 us -> 105 us
  waiting for transfers between devices: 37.6 us -> 35.7 us
    unnamed x66 -> x50, local copies, waits for them, and re-layouts: 8.64 us -> 1 us
    pallas_call x24, Pallas kernels: 101 us -> 105 us  [call(): pl.pallas_call(body, out_shape=tuple((pltpu.HBM(o.shape, o.dtype) if k in...]
    ppermute x32, waiting for transfers between devices: 37.6 us -> 35.7 us  [swap(): return lax.ppermute(value, axis, [(i, i ^ bit) for i in range(size)])]
  transfers between devices with their start and end apart: 32 -> 32, of which waited for: 14 -> 12; matrix products, arithmetic and copies ran while one was open for 0% -> 0% of each run, Pallas kernels for 45% -> 48%
where the time goes in v3:
time: 183 us
  Pallas kernels  105 us (57%)
  starting transfers between devices  39.3 us (21%)
  waiting for transfers between devices  35.7 us (20%)
  between operations  2 us (1%)
    pallas_call x24, Pallas kernels, call(): pl.pallas_call(body, out_shape=tuple((pltpu.HBM(o.shape, o.dtype) if k in...  105 us
    ppermute x32, starting transfers between devices, swap(): return lax.ppermute(value, axis, [(i, i ^ bit) for i in range(size)])  39.3 us
    ppermute x32, waiting for transfers between devices, swap(): return lax.ppermute(value, axis, [(i, i ^ bit) for i in range(size)])  35.7 us
  transfers between devices with their start and end apart: 32, of which 12 were waited for; matrix products, arithmetic and copies ran while one was open for 0% of the time, Pallas kernels for 48%

profile of v3, /device:TPU:0, one launch (start us, length us, event | category | flops | bytes accessed | tf_op | source)
XLA Modules:
  0.0 182.8 jit_solution(7763323740171805809)
XLA Ops:
  1.5 0.7 copy-done.12
  2.2 6.6 %keys.1 = (bf16[512,768]{1,0:T(8,128)(2,1)S(1)}, bf16[768,512]{1,0:T(8,128)(2,1)S(1)}, bf16[1536,512]{1,0:T(8,128)(2,1)S(1)}, bf16[768,512]{1,0:T(8,128)(2,1)S(1)}, bf16[960,128]{1,0:T(8,128)(2,1)S(1)}) custom-call(s32[16]{0:T(128)S(1)} %compare_select_fusion.2.scal, bf16[512,768]{1,0:T(8,128)(2,1)} %x_ref.3, bf16[9280,768]{1,0:T(8,128)(2,1)} %bitcast.44, ...), custom_call_target="tpu_custom_call" | custom-call | bytes 1024 | tf_op jit(solution)/shard_map/keys/pallas_call | solution.py:74
  8.8 4.0 %collective-permute-start.2 = (bf16[960,128]{1,0:T(8,128)(2,1)S(1)}, bf16[960,128]{1,0:T(8,128)(2,1)S(1)}, u32[]{:S(2)}, u32[]{:S(2)}) collective-permute-start(bf16[960,128]{1,0:T(8,128)(2,1)S(1)} %get-tuple-element.231), channel_id=1, source_target_pairs={{0,24},{8,16},{16,8},{24,0},{1,25},{9,17},{17,9},{25,1},{2,26},{10... | collective-permute-start | bytes 737288 | tf_op jit(solution)/shard_map/ppermute | solution.py:584
  12.8 0.5 collective-permute-start.1
  13.5 5.7 %queries.1 = (bf16[4,384,512]{2,1,0:T(8,128)(2,1)S(1)}, bf16[4,384,512]{2,1,0:T(8,128)(2,1)S(1)}, bf16[768,512]{1,0:T(8,128)(2,1)S(1)}, bf16[1536,512]{1,0:T(8,128)(2,1)S(1)}) custom-call(s32[16]{0:T(128)S(1)} %compare_select_fusion.2.scal, bf16[512,768]{1,0:T(8,128)(2,1)S(1)} %get-tuple-element.221.h1_ref, bf16[512,768]{1,0:T(8,128)(2,1)} %g_ref.7, ...), custom_call_target="tpu_custom_call" | custom-call | bytes 1024 | tf_op jit(solution)/shard_map/queries/pallas_call | solution.py:74
  19.2 4.0 %local.1.refs_3_ = f32[960,512]{1,0:T(8,128)S(1)} custom-call(s32[16]{0:T(128)S(1)} %compare_select_fusion.2.scal, bf16[1536,512]{1,0:T(8,128)(2,1)S(1)} %get-tuple-element.227.fq_ref.refs_4_.refs_3_, bf16[1536,512]{1,0:T(8,128)(2,1)S(1)} %get-tuple-element.228.fk_ref.refs_4_, bf16[768,512]{1,0:T(8,128)(2,1)S(1)} %get-tuple-element.229.vt_ref.refs_5_), custom_call_target="tpu_custom_call" | custom-call | bytes 1024 | tf_op jit(solution)/shard_map/local/pallas_call | solution.py:74
  23.2 0.8 collective-permute-done.1.refs_1_
  24.0 0.3 collective-permute-done.refs_0_
  24.3 4.3 %after.1 = (f32[768,512]{1,0:T(8,128)S(1)}, f32[16,512]{1,0:T(8,128)S(1)}, f32[512,768]{1,0:T(8,128)S(1)}, bf16[512,768]{1,0:T(8,128)(2,1)S(1)}, bf16[960,128]{1...) custom-call(s32[16]{0:T(128)S(1)} %compare_select_fusion.2.scal, ...), custom_call_target="tpu_custom_call", output_to_operand_aliasing={{5}: (9, {}), {6}: (10, {})} | custom-call | bytes 1024 | tf_op jit(solution)/shard_map/after/pallas_call | solution.py:74
  28.8 9.1 %mlp.2 = (f32[512,768]{1,0:T(8,128)S(1)}, f32[512,768]{1,0:T(8,128)S(1)}, bf16[2,2,512,768]{3,2,1,0:T(8,128)(2,1)S(1)}, f32[1,1536]{1,0:T(1,128)S(1)}) custom-call(s32[16]{0:T(128)S(1)} %compare_select_fusion.2.scal, bf16[512,768]{1,0:T(8,128)(2,1)S(1)} %get-tuple-element.243.h2_ref, bf16[512,768]{1,0:T(8,128)(2,1)} %g_ref.7, bf16[9280,768]{1,0:T(8,128)(2,1)} %bitcast.50, ...), custom_call_target="tpu_custom_call" | custom-call | bytes 1024 | tf_op jit(solution)/shard_map/mlp/pallas_call | solution.py:74
  37.9 0.6 collective-permute-start.4
  38.4 9.1 %mlp.3 = (f32[512,768]{1,0:T(8,128)S(1)}, f32[512,768]{1,0:T(8,128)S(1)}, bf16[2,2,512,768]{3,2,1,0:T(8,128)(2,1)S(1)}, f32[1,1536]{1,0:T(1,128)S(1)}) custom-call(s32[16]{0:T(128)S(1)} %compare_select_fusion.2.scal, bf16[512,768]{1,0:T(8,128)(2,1)S(1)} %get-tuple-element.243.h2_ref, bf16[512,768]{1,0:T(8,128)(2,1)} %g_ref.7, bf16[9280,768]{1,0:T(8,128)(2,1)} %bitcast.52, ...), custom_call_target="tpu_custom_call" | custom-call | bytes 1024 | tf_op jit(solution)/shard_map/mlp/pallas_call | solution.py:74
  47.7 4.7 %mlp_grads.2 = (bf16[8,192,384]{2,1,0:T(8,128)(2,1)}, bf16[8,192,384]{2,1,0:T(8,128)(2,1)}) custom-call(s32[16]{0:T(128)S(1)} %compare_select_fusion.2.scal, bf16[4,384,512]{2,1,0:T(8,128)(2,1)S(1)} %get-tuple-element.259.refs_0_.refs_6_.refs_2_, bf16[4,384,512]{2,1,0:T(8,128)(2,1)S(1)} %collective-permute-done.3.refs_1_.refs_7_.refs_3_, ...), custom_call_target="tpu_custom_call" | custom-call | bytes 1024 | tf_op jit(solution)/shard_map/mlp_grads/pallas_call | solution.py:74
  52.4 1.6 collective-permute-start.9
  54.0 6.7 %back.1 = (bf16[512,768]{1,0:T(8,128)(2,1)}, f32[512,768]{1,0:T(8,128)}, bf16[768,512]{1,0:T(8,128)(2,1)}, bf16[960,512]{1,0:T(8,128)(2,1)}, bf16[960,128]{1,0:T(8,128)(2,1)}, /*index=5*/f32[4,768]{1,0:T(4,128)S(1)}) custom-call(s32[16]{0:T(128)S(1)} %compare_select_fusion.2.scal, f32[512,768]{1,0:T(8,128)S(1)} %get-tuple-element.267.out_ref, ...), custom_call_target="tpu_custom_call" | custom-call | bytes 1024 | tf_op jit(solution)/shard_map/back/pallas_call | solution.py:74
  60.8 1.8 collective-permute-start.8
  62.5 1.2 collective-permute-start.7
  63.7 0.5 collective-permute-start.6
  64.4 5.8 %mlp_grads.3 = (bf16[8,192,384]{2,1,0:T(8,128)(2,1)S(1)}, bf16[8,192,384]{2,1,0:T(8,128)(2,1)S(1)}) custom-call(s32[16]{0:T(128)S(1)} %compare_select_fusion.2.scal, bf16[4,384,512]{2,1,0:T(8,128)(2,1)S(1)} %get-tuple-element.259.refs_0_.refs_6_.refs_2_, bf16[4,384,512]{2,1,0:T(8,128)(2,1)S(1)} %collective-permute-done.3.refs_1_.refs_7_.refs_3_, ...), custom_call_target="tpu_custom_call" | custom-call | bytes 1024 | tf_op jit(solution)/shard_map/mlp_grads/pallas_call | solution.py:74
  70.2 1.5 collective-permute-start.10
  71.7 3.7 %collective-permute-done.7.refs_1_ = bf16[960,128]{1,0:T(8,128)(2,1)} collective-permute-done((bf16[960,128]{1,0:T(8,128)(2,1)}, bf16[960,128]{1,0:T(8,128)(2,1)}, u32[]{:S(2)}, u32[]{:S(2)}) %collective-permute-start.7) | collective-permute-done | bytes 245792 | tf_op jit(solution)/shard_map/ppermute | solution.py:584
  75.4 13.4 %attend_back.1 = (bf16[4,768,512]{2,1,0:T(8,128)(2,1)S(1)}, f32[768,64]{1,0:T(8,128)S(1)}, f32[768,3]{1,0:T(8,128)S(1)}) custom-call(s32[16]{0:T(128)S(1)} %compare_select_fusion.2.scal, bf16[960,128]{1,0:T(8,128)(2,1)} %collective-permute-done.6.refs_0_, bf16[960,128]{1,0:T(8,128)(2,1)} %collective-permute-done.7.refs_1_, ...), custom_call_target="tpu_custom_call" | custom-call | flops 1000000000 | bytes 1024 | tf_op jit(solution)/shard_map/attend_back/pallas_call | solution.py:74
  88.9 7.8 %input.1 = (bf16[512,768]{1,0:T(8,128)(2,1)}, f32[1,384,128]{2,1,0:T(8,128)S(1)}, f32[1,384,128]{2,1,0:T(8,128)S(1)}) custom-call(s32[16]{0:T(128)S(1)} %compare_select_fusion.2.scal, bf16[4,768,512]{2,1,0:T(8,128)(2,1)S(1)} %get-tuple-element.299.dp_ref, bf16[9280,768]{1,0:T(8,128)(2,1)} %bitcast.56, bf16[512,768]{1,0:T(8,128)(2,1)} %x_ref.3, ...), custom_call_target="tpu_custom_call" | custom-call | bytes 1024 | tf_op jit(solution)/shard_map/input/pallas_call | solution.py:74
  96.8 0.5 collective-permute-start.12
  97.3 2.1 %halve.6 = (bf16[4,192,384]{2,1,0:T(8,128)(2,1)S(1)}, bf16[4,192,384]{2,1,0:T(8,128)(2,1)S(1)}) custom-call(s32[16]{0:T(128)S(1)} %compare_select_fusion.2.scal, bf16[8,192,384]{2,1,0:T(8,128)(2,1)S(1)} %copy-done.22, bf16[8,192,384]{2,1,0:T(8,128)(2,1)} %collective-permute-done.9.recv_ref), custom_call_target="tpu_custom_call" | custom-call | flops 14000000000 | bytes 1024 | tf_op jit(solution)/shard_map/halve/pallas_call | solution.py:74
  99.4 1.6 collective-permute-start.13
  100.9 0.8 halve.7
  101.8 0.9 collective-permute-start.14
  102.6 5.7 %tail_grads.1 = (bf16[896,384]{1,0:T(8,128)(2,1)S(1)}, bf16[768,384]{1,0:T(8,128)(2,1)S(1)}, bf16[768,384]{1,0:T(8,128)(2,1)S(1)}, bf16[768,384]{1,0:T(8,128)(2,1)S(1)}, f32[128,384]{1,0:T(8,128)S(1)}) custom-call(s32[16]{0:T(128)S(1)} %compare_select_fusion.2.scal, bf16[4,384,512]{2,1,0:T(8,128)(2,1)S(1)} %get-tuple-element.259.refs_0_.refs_6_.refs_2_, ...), custom_call_target="tpu_custom_call" | custom-call | flops 4000000000 | bytes 1024 | tf_op jit(solution)/shard_map/tail_grads/pallas_call | solution.py:74
  108.3 1.1 collective-permute-start.15
  109.4 0.9 collective-permute-start.16
  110.3 5.3 %collective-permute-done.13.recv_ref = bf16[4,192,384]{2,1,0:T(8,128)(2,1)S(1)} collective-permute-done((bf16[4,192,384]{2,1,0:T(8,128)(2,1)S(1)}, bf16[4,192,384]{2,1,0:T(8,128)(2,1)S(1)}, u32[]{:S(2)}, u32[]{:S(2)}) %collective-permute-start.13) | collective-permute-done | bytes 589856 | tf_op jit(solution)/shard_map/ppermute | solution.py:584
  115.6 0.7 halve.8
  116.3 2.6 %collective-permute-start.17 = (bf16[2,192,384]{2,1,0:T(8,128)(2,1)S(1)}, bf16[2,192,384]{2,1,0:T(8,128)(2,1)S(1)}, u32[]{:S(2)}, u32[]{:S(2)}) collective-permute-start(bf16[2,192,384]{2,1,0:T(8,128)(2,1)S(1)} %get-tuple-element.348), channel_id=1, source_target_pairs={{0,4},{1,5},{2,6},{3,7},{4,0},{5,1},{6,2},{7,3},{8,12},{9,13},{10,... | collective-permute-start | bytes 884744 | tf_op jit(solution)/shard_map/ppermute | solution.py:584
  118.9 0.7 halve.9
  119.6 1.6 collective-permute-start.18
  121.2 2.9 %collective-permute-done.16.recv_b = bf16[768,384]{1,0:T(8,128)(2,1)S(1)} collective-permute-done((bf16[768,384]{1,0:T(8,128)(2,1)S(1)}, bf16[768,384]{1,0:T(8,128)(2,1)S(1)}, u32[]{:S(2)}, u32[]{:S(2)}) %collective-permute-start.16) | collective-permute-done | bytes 589856 | tf_op jit(solution)/shard_map/ppermute | solution.py:584
  124.1 6.2 %collective-permute-done.15.recv_a = bf16[896,384]{1,0:T(8,128)(2,1)S(1)} collective-permute-done((bf16[896,384]{1,0:T(8,128)(2,1)S(1)}, bf16[896,384]{1,0:T(8,128)(2,1)S(1)}, u32[]{:S(2)}, u32[]{:S(2)}) %collective-permute-start.15) | collective-permute-done | bytes 688160 | tf_op jit(solution)/shard_map/ppermute | solution.py:584
  130.4 0.7 tail_one.1
  131.1 1.5 collective-permute-start.21
  132.5 0.9 collective-permute-start.22
  133.4 0.6 halve.10
  134.1 2.6 %collective-permute-done.18.recv_ref = bf16[2,192,384]{2,1,0:T(8,128)(2,1)S(1)} collective-permute-done((bf16[2,192,384]{2,1,0:T(8,128)(2,1)S(1)}, bf16[2,192,384]{2,1,0:T(8,128)(2,1)S(1)}, u32[]{:S(2)}, u32[]{:S(2)}) %collective-permute-start.18) | collective-permute-done | bytes 294944 | tf_op jit(solution)/shard_map/ppermute | solution.py:584
  136.7 0.6 halve.11
  137.3 2.6 %collective-permute-start.20 = (bf16[1,192,384]{2,1,0:T(8,128)(2,1)S(1)}, bf16[1,192,384]{2,1,0:T(8,128)(2,1)S(1)}, u32[]{:S(2)}, u32[]{:S(2)}) collective-permute-start(bf16[1,192,384]{2,1,0:T(8,128)(2,1)S(1)} %get-tuple-element.360), channel_id=1, source_target_pairs={{0,4},{1,5},{2,6},{3,7},{4,0},{5,1},{6,2},{7,3},{8,12},{9,13},{10,... | collective-permute-start | bytes 442376 | tf_op jit(solution)/shard_map/ppermute | solution.py:584
  139.9 1.4 collective-permute-start.19
  141.4 4.1 %collective-permute-done.20.refs_3_ = bf16[1,192,384]{2,1,0:T(8,128)(2,1)S(1)} collective-permute-done((bf16[1,192,384]{2,1,0:T(8,128)(2,1)S(1)}, bf16[1,192,384]{2,1,0:T(8,128)(2,1)S(1)}, u32[]{:S(2)}, u32[]{:S(2)}) %collective-permute-start.20) | collective-permute-done | bytes 147488 | tf_op jit(solution)/shard_map/ppermute | solution.py:584
  145.4 0.6 final.1
  146.0 1.6 collective-permute-start.26
  147.6 0.8 tail_two.1
  148.4 0.5 collective-permute-start.23
  149.0 2.9 %collective-permute-start.24 = (bf16[224,384]{1,0:T(8,128)(2,1)S(1)}, bf16[224,384]{1,0:T(8,128)(2,1)S(1)}, u32[]{:S(2)}, u32[]{:S(2)}) collective-permute-start(bf16[224,384]{1,0:T(8,128)(2,1)S(1)} %get-tuple-element.371), channel_id=1, source_target_pairs={{0,4},{1,5},{2,6},{3,7},{4,0},{5,1},{6,2},{7,3},{8,12},{9,13},{10,... | collective-permute-start | bytes 516104 | tf_op jit(solution)/shard_map/ppermute | solution.py:584
  151.9 1.0 collective-permute-start.25
  152.9 0.8 collective-permute-start.27
  153.9 1.4 collective-permute-start.28
  155.3 0.4 collective-permute-done.23.refs_1_
  155.8 8.2 %collective-permute-done.24.refs_2_ = bf16[224,384]{1,0:T(8,128)(2,1)S(1)} collective-permute-done((bf16[224,384]{1,0:T(8,128)(2,1)S(1)}, bf16[224,384]{1,0:T(8,128)(2,1)S(1)}, u32[]{:S(2)}, u32[]{:S(2)}) %collective-permute-start.24) | collective-permute-done | bytes 172064 | tf_op jit(solution)/shard_map/ppermute | solution.py:584
  164.1 0.6 tail_final.1
  164.7 1.4 collective-permute-start.31
  166.2 0.6 collective-permute-start.30
  166.8 1.5 collective-permute-start.29
  168.3 0.7 collective-permute-done.28.refs_3_
  169.2 8.0 %adam.2 = (f32[96,9280]{1,0:T(8,128)}, f32[96,9280]{1,0:T(8,128)}, f32[96,9280]{1,0:T(8,128)}, f32[96,9280]{1,0:T(8,128)}, f32[96,9280]{1,0:T(8,128)}, /*index=5*/bf16[96,9280]{1,0:T(8,128)(2,1)}) custom-call(s32[16]{0:T(128)S(1)} %compare_select_fusion.2.scal, bf16[4,96,384]{2,1,0:T(8,128)(2,1)S(1)} %bitcast.30, ...), custom_call_target="tpu_custom_call" | custom-call | bytes 1024 | tf_op jit(solution)/shard_map/adam/pallas_call | solution.py:74
  177.2 5.3 %adam.3 = (f32[96,9280]{1,0:T(8,128)}, f32[96,9280]{1,0:T(8,128)}, f32[96,9280]{1,0:T(8,128)}, f32[96,9280]{1,0:T(8,128)}, f32[96,9280]{1,0:T(8,128)}, /*index=5...) custom-call(s32[16]{0:T(128)S(1)} %compare_select_fusion.2.scal, ...), custom_call_target="tpu_custom_call", output_to_operand_aliasing={{0}: (14, {}), {1}: (15, {}), {2}: (16, {}), {3}: (17, {}),... | custom-call | bytes 1024 | tf_op jit(solution)/shard_map/adam/pallas_call | solution.py:74
  (77 shorter events, 1.1 us)
Async XLA Ops:
  1.5 0.7 copy-start.12
  8.8 10.3 %copy-start.14 = (bf16[768,512]{1,0:T(8,128)(2,1)}, bf16[768,512]{1,0:T(8,128)(2,1)S(1)}, u32[]{:S(2)}) copy-start(bf16[768,512]{1,0:T(8,128)(2,1)S(1)} %get-tuple-element.293.refs_9_) | copy-start | bytes 2359300
  8.8 10.3 %copy-start.7 = (bf16[1536,512]{1,0:T(8,128)(2,1)}, bf16[1536,512]{1,0:T(8,128)(2,1)S(1)}, u32[]{:S(2)}) copy-start(bf16[1536,512]{1,0:T(8,128)(2,1)S(1)} %get-tuple-element.228.fk_ref.refs_4_) | copy-start | bytes 4718596
  8.8 10.3 %copy-start.9 = (bf16[768,512]{1,0:T(8,128)(2,1)}, bf16[768,512]{1,0:T(8,128)(2,1)S(1)}, u32[]{:S(2)}) copy-start(bf16[768,512]{1,0:T(8,128)(2,1)S(1)} %get-tuple-element.229.vt_ref.refs_5_) | copy-start | bytes 2359300
  8.8 14.3 %collective-permute-start.2 = (bf16[960,128]{1,0:T(8,128)(2,1)S(1)}, bf16[960,128]{1,0:T(8,128)(2,1)S(1)}, u32[]{:S(2)}, u32[]{:S(2)}) collective-permute-start(bf16[960,128]{1,0:T(8,128)(2,1)S(1)} %get-tuple-element.231), channel_id=1, source_target_pairs={{0,24},{8,16},{16,8},{24,0},{1,25},{9,17},{17,9},{25,1},{2,26},{10... | collective-permute-start | bytes 737288 | tf_op jit(solution)/shard_map/ppermute | solution.py:584
  12.8 11.2 %collective-permute-start.1 = (bf16[960,128]{1,0:T(8,128)(2,1)S(1)}, bf16[960,128]{1,0:T(8,128)(2,1)S(1)}, u32[]{:S(2)}, u32[]{:S(2)}) collective-permute-start(bf16[960,128]{1,0:T(8,128)(2,1)S(1)} %get-tuple-element.231), channel_id=1, source_target_pairs={{0,16},{8,24},{16,0},{24,8},{1,17},{9,25},{17,1},{25,9},{2,18},{10... | collective-permute-start | bytes 737288 | tf_op jit(solution)/shard_map/ppermute | solution.py:584
  13.3 11.0 %collective-permute-start = (bf16[960,128]{1,0:T(8,128)(2,1)S(1)}, bf16[960,128]{1,0:T(8,128)(2,1)S(1)}, u32[]{:S(2)}, u32[]{:S(2)}) collective-permute-start(bf16[960,128]{1,0:T(8,128)(2,1)S(1)} %get-tuple-element.231), channel_id=1, source_target_pairs={{0,8},{8,0},{16,24},{24,16},{1,9},{9,1},{17,25},{25,17},{2,10},{10... | collective-permute-start | bytes 737288 | tf_op jit(solution)/shard_map/ppermute | solution.py:584
  19.1 4.1 %copy-start.16 = (bf16[768,512]{1,0:T(8,128)(2,1)}, bf16[768,512]{1,0:T(8,128)(2,1)S(1)}, u32[]{:S(2)}) copy-start(bf16[768,512]{1,0:T(8,128)(2,1)S(1)} %get-tuple-element.292.refs_8_) | copy-start | bytes 2359300
  19.1 34.9 %copy-start = (bf16[1536,512]{1,0:T(8,128)(2,1)}, bf16[1536,512]{1,0:T(8,128)(2,1)S(1)}, u32[]{:S(2)}) copy-start(bf16[1536,512]{1,0:T(8,128)(2,1)S(1)} %get-tuple-element.227.fq_ref.refs_4_.refs_3_) | copy-start | bytes 4718596
  28.7 9.8 %collective-permute-start.3 = (bf16[4,384,512]{2,1,0:T(8,128)(2,1)S(1)}, bf16[4,384,512]{2,1,0:T(8,128)(2,1)S(1)}, u32[]{:S(2)}, u32[]{:S(2)}) collective-permute-start(bf16[4,384,512]{2,1,0:T(8,128)(2,1)S(1)} %get-tuple-element.250), channel_id=1, source_target_pairs={{0,1},{1,0},{2,3},{3,2},{4,5},{5,4},{6,7},{7,6},{8,9},{9,8},{10,11... | collective-permute-start | bytes 4718600 | tf_op jit(solution)/shard_map/ppermute | solution.py:584
  37.9 9.8 %collective-permute-start.4 = (bf16[2,2,512,768]{3,2,1,0:T(8,128)(2,1)S(1)}, bf16[2,2,512,768]{3,2,1,0:T(8,128)(2,1)S(1)}, u32[]{:S(2)}, u32[]{:S(2)}) collective-permute-start(bf16[2,2,512,768]{3,2,1,0:T(8,128)(2,1)S(1)} %get-tuple-element.261.refs_2_.refs_4_), channel_id=1, source_target_pairs={{0,1},{1,0},{2,3},{3,2},{4,5},{5,4},{6,7},{7,6},{8,9},{9,8},{10,11... | collective-permute-start | bytes 9437192 | tf_op jit(solution)/shard_map/ppermute | solution.py:584
  47.5 4.9 %copy-start.6 = (bf16[2,2,512,768]{3,2,1,0:T(8,128)(2,1)}, bf16[2,2,512,768]{3,2,1,0:T(8,128)(2,1)S(1)}, u32[]{:S(2)}) copy-start(bf16[2,2,512,768]{3,2,1,0:T(8,128)(2,1)S(1)} %get-tuple-element.280.refs_2_.refs_4_) | copy-start | bytes 9437188
  47.6 6.5 %copy-start.13 = (bf16[768,13]{0,1:T(8,128)(2,1)S(1)}, bf16[768,13]{0,1:T(8,128)(2,1)}, u32[]{:S(2)}) copy-start(bf16[768,13]{0,1:T(8,128)(2,1)} %param.17) | copy-start | bytes 59908
  47.6 6.4 %collective-permute-start.5 = (bf16[2,2,512,768]{3,2,1,0:T(8,128)(2,1)S(1)}, bf16[2,2,512,768]{3,2,1,0:T(8,128)(2,1)S(1)}, u32[]{:S(2)}, u32[]{:S(2)}) collective-permute-start(bf16[2,2,512,768]{3,2,1,0:T(8,128)(2,1)S(1)} %get-tuple-element.280.refs_2_.refs_4_), channel_id=1, source_target_pairs={{0,1},{1,0},{2,3},{3,2},{4,5},{5,4},{6,7},{7,6},{8,9},{9,8},{10,11... | collective-permute-start | bytes 9437192 | tf_op jit(solution)/shard_map/ppermute | solution.py:584
  52.4 44.8 %collective-permute-start.9 = (bf16[8,192,384]{2,1,0:T(8,128)(2,1)}, bf16[8,192,384]{2,1,0:T(8,128)(2,1)}, u32[]{:S(2)}, u32[]{:S(2)}) collective-permute-start(bf16[8,192,384]{2,1,0:T(8,128)(2,1)} %get-tuple-element.312), channel_id=1, source_target_pairs={{0,2},{1,3},{2,0},{3,1},{4,6},{5,7},{6,4},{7,5},{8,10},{9,11},{10,... | collective-permute-start | bytes 3538952 | tf_op jit(solution)/shard_map/ppermute | solution.py:584
  54.0 6.7 %copy-start.23 = (bf16[2,2,512,768]{3,2,1,0:T(8,128)(2,1)}, bf16[2,2,512,768]{3,2,1,0:T(8,128)(2,1)S(1)}, u32[]{:S(2)}) copy-start(bf16[2,2,512,768]{3,2,1,0:T(8,128)(2,1)S(1)} %collective-permute-done.5.refs_3_.refs_5_) | copy-start | bytes 9437188
  60.8 10.9 %collective-permute-start.8 = (bf16[960,128]{1,0:T(8,128)(2,1)}, bf16[960,128]{1,0:T(8,128)(2,1)}, u32[]{:S(2)}, u32[]{:S(2)}) collective-permute-start(bf16[960,128]{1,0:T(8,128)(2,1)} %get-tuple-element.285), channel_id=1, source_target_pairs={{0,24},{8,16},{16,8},{24,0},{1,25},{9,17},{17,9},{25,1},{2,26},{10... | collective-permute-start | bytes 737288 | tf_op jit(solution)/shard_map/ppermute | solution.py:584
  62.5 12.9 %collective-permute-start.7 = (bf16[960,128]{1,0:T(8,128)(2,1)}, bf16[960,128]{1,0:T(8,128)(2,1)}, u32[]{:S(2)}, u32[]{:S(2)}) collective-permute-start(bf16[960,128]{1,0:T(8,128)(2,1)} %get-tuple-element.285), channel_id=1, source_target_pairs={{0,16},{8,24},{16,0},{24,8},{1,17},{9,25},{17,1},{25,9},{2,18},{10... | collective-permute-start | bytes 737288 | tf_op jit(solution)/shard_map/ppermute | solution.py:584
  63.7 11.7 %collective-permute-start.6 = (bf16[960,128]{1,0:T(8,128)(2,1)}, bf16[960,128]{1,0:T(8,128)(2,1)}, u32[]{:S(2)}, u32[]{:S(2)}) collective-permute-start(bf16[960,128]{1,0:T(8,128)(2,1)} %get-tuple-element.285), channel_id=1, source_target_pairs={{0,8},{8,0},{16,24},{24,16},{1,9},{9,1},{17,25},{25,17},{2,10},{10... | collective-permute-start | bytes 737288 | tf_op jit(solution)/shard_map/ppermute | solution.py:584
  64.3 11.1 %copy-start.1 = (bf16[1536,512]{1,0:T(8,128)(2,1)S(1)}, bf16[1536,512]{1,0:T(8,128)(2,1)}, u32[]{:S(2)}) copy-start(bf16[1536,512]{1,0:T(8,128)(2,1)} %copy-done) | copy-start | bytes 4718596
  64.3 11.1 %copy-start.8 = (bf16[1536,512]{1,0:T(8,128)(2,1)S(1)}, bf16[1536,512]{1,0:T(8,128)(2,1)}, u32[]{:S(2)}) copy-start(bf16[1536,512]{1,0:T(8,128)(2,1)} %copy-done.7) | copy-start | bytes 4718596
  64.3 11.1 %copy-start.10 = (bf16[768,512]{1,0:T(8,128)(2,1)S(1)}, bf16[768,512]{1,0:T(8,128)(2,1)}, u32[]{:S(2)}) copy-start(bf16[768,512]{1,0:T(8,128)(2,1)} %copy-done.9) | copy-start | bytes 2359300
  64.3 11.1 %copy-start.15 = (bf16[768,512]{1,0:T(8,128)(2,1)S(1)}, bf16[768,512]{1,0:T(8,128)(2,1)}, u32[]{:S(2)}) copy-start(bf16[768,512]{1,0:T(8,128)(2,1)} %copy-done.14) | copy-start | bytes 2359300
  64.3 11.1 %copy-start.17 = (bf16[768,512]{1,0:T(8,128)(2,1)S(1)}, bf16[768,512]{1,0:T(8,128)(2,1)}, u32[]{:S(2)}) copy-start(bf16[768,512]{1,0:T(8,128)(2,1)} %copy-done.16) | copy-start | bytes 2359300
  70.2 18.8 %copy-start.11 = (f32[512,768]{1,0:T(8,128)S(1)}, f32[512,768]{1,0:T(8,128)}, u32[]{:S(2)}) copy-start(f32[512,768]{1,0:T(8,128)} %get-tuple-element.300.dr_ref) | copy-start | bytes 4718596
  70.2 30.7 %collective-permute-start.10 = (bf16[8,192,384]{2,1,0:T(8,128)(2,1)S(1)}, bf16[8,192,384]{2,1,0:T(8,128)(2,1)S(1)}, u32[]{:S(2)}, u32[]{:S(2)}) collective-permute-start(bf16[8,192,384]{2,1,0:T(8,128)(2,1)S(1)} %get-tuple-element.317), channel_id=1, source_target_pairs={{0,16},{8,24},{16,0},{24,8},{1,17},{9,25},{17,1},{25,9},{2,18},{10... | collective-permute-start | bytes 3538952 | tf_op jit(solution)/shard_map/ppermute | solution.py:584
  88.8 8.4 %copy-start.22 = (bf16[8,192,384]{2,1,0:T(8,128)(2,1)S(1)}, bf16[8,192,384]{2,1,0:T(8,128)(2,1)}, u32[]{:S(2)}) copy-start(bf16[8,192,384]{2,1,0:T(8,128)(2,1)} %get-tuple-element.311.keep_ref) | copy-start | bytes 3538948
  88.9 13.8 %collective-permute-start.11 = (bf16[4,768,512]{2,1,0:T(8,128)(2,1)S(1)}, bf16[4,768,512]{2,1,0:T(8,128)(2,1)S(1)}, u32[]{:S(2)}, u32[]{:S(2)}) collective-permute-start(bf16[4,768,512]{2,1,0:T(8,128)(2,1)S(1)} %get-tuple-element.299.dp_ref), channel_id=1, source_target_pairs={{0,1},{1,0},{2,3},{3,2},{4,5},{5,4},{6,7},{7,6},{8,9},{9,8},{10,11... | collective-permute-start | bytes 9437192 | tf_op jit(solution)/shard_map/ppermute | solution.py:584
  96.8 5.9 %collective-permute-start.12 = (f32[1,384,128]{2,1,0:T(8,128)S(1)}, f32[1,384,128]{2,1,0:T(8,128)S(1)}, u32[]{:S(2)}, u32[]{:S(2)}) collective-permute-start(f32[1,384,128]{2,1,0:T(8,128)S(1)} %get-tuple-element.322), channel_id=1, source_target_pairs={{0,1},{1,0},{2,3},{3,2},{4,5},{5,4},{6,7},{7,6},{8,9},{9,8},{10,11... | collective-permute-start | bytes 589832 | tf_op jit(solution)/shard_map/ppermute | solution.py:584
  99.4 16.3 %collective-permute-start.13 = (bf16[4,192,384]{2,1,0:T(8,128)(2,1)S(1)}, bf16[4,192,384]{2,1,0:T(8,128)(2,1)S(1)}, u32[]{:S(2)}, u32[]{:S(2)}) collective-permute-start(bf16[4,192,384]{2,1,0:T(8,128)(2,1)S(1)} %get-tuple-element.330), channel_id=1, source_target_pairs={{0,8},{8,0},{16,24},{24,16},{1,9},{9,1},{17,25},{25,17},{2,10},{10... | collective-permute-start | bytes 1769480 | tf_op jit(solution)/shard_map/ppermute | solution.py:584
  101.8 17.2 %collective-permute-start.14 = (bf16[4,192,384]{2,1,0:T(8,128)(2,1)S(1)}, bf16[4,192,384]{2,1,0:T(8,128)(2,1)S(1)}, u32[]{:S(2)}, u32[]{:S(2)}) collective-permute-start(bf16[4,192,384]{2,1,0:T(8,128)(2,1)S(1)} %get-tuple-element.335), channel_id=1, source_target_pairs={{0,2},{1,3},{2,0},{3,1},{4,6},{5,7},{6,4},{7,5},{8,10},{9,11},{10,... | collective-permute-start | bytes 1769480 | tf_op jit(solution)/shard_map/ppermute | solution.py:584
  108.3 22.1 %collective-permute-start.15 = (bf16[896,384]{1,0:T(8,128)(2,1)S(1)}, bf16[896,384]{1,0:T(8,128)(2,1)S(1)}, u32[]{:S(2)}, u32[]{:S(2)}) collective-permute-start(bf16[896,384]{1,0:T(8,128)(2,1)S(1)} %get-tuple-element.340), channel_id=1, source_target_pairs={{0,8},{8,0},{16,24},{24,16},{1,9},{9,1},{17,25},{25,17},{2,10},{10... | collective-permute-start | bytes 2064392 | tf_op jit(solution)/shard_map/ppermute | solution.py:584
  109.4 14.7 %collective-permute-start.16 = (bf16[768,384]{1,0:T(8,128)(2,1)S(1)}, bf16[768,384]{1,0:T(8,128)(2,1)S(1)}, u32[]{:S(2)}, u32[]{:S(2)}) collective-permute-start(bf16[768,384]{1,0:T(8,128)(2,1)S(1)} %get-tuple-element.342), channel_id=1, source_target_pairs={{0,16},{8,24},{16,0},{24,8},{1,17},{9,25},{17,1},{25,9},{2,18},{10... | collective-permute-start | bytes 1769480 | tf_op jit(solution)/shard_map/ppermute | solution.py:584
  116.3 17.1 %collective-permute-start.17 = (bf16[2,192,384]{2,1,0:T(8,128)(2,1)S(1)}, bf16[2,192,384]{2,1,0:T(8,128)(2,1)S(1)}, u32[]{:S(2)}, u32[]{:S(2)}) collective-permute-start(bf16[2,192,384]{2,1,0:T(8,128)(2,1)S(1)} %get-tuple-element.348), channel_id=1, source_target_pairs={{0,4},{1,5},{2,6},{3,7},{4,0},{5,1},{6,2},{7,3},{8,12},{9,13},{10,... | collective-permute-start | bytes 884744 | tf_op jit(solution)/shard_map/ppermute | solution.py:584
  119.6 17.0 %collective-permute-start.18 = (bf16[2,192,384]{2,1,0:T(8,128)(2,1)S(1)}, bf16[2,192,384]{2,1,0:T(8,128)(2,1)S(1)}, u32[]{:S(2)}, u32[]{:S(2)}) collective-permute-start(bf16[2,192,384]{2,1,0:T(8,128)(2,1)S(1)} %get-tuple-element.353), channel_id=1, source_target_pairs={{0,8},{8,0},{16,24},{24,16},{1,9},{9,1},{17,25},{25,17},{2,10},{10... | collective-permute-start | bytes 884744 | tf_op jit(solution)/shard_map/ppermute | solution.py:584
  131.1 16.5 %collective-permute-start.21 = (bf16[512,384]{1,0:T(8,128)(2,1)S(1)}, bf16[512,384]{1,0:T(8,128)(2,1)S(1)}, u32[]{:S(2)}, u32[]{:S(2)}) collective-permute-start(bf16[512,384]{1,0:T(8,128)(2,1)S(1)} %get-tuple-element.362), channel_id=1, source_target_pairs={{0,16},{8,24},{16,0},{24,8},{1,17},{9,25},{17,1},{25,9},{2,18},{10... | collective-permute-start | bytes 1179656 | tf_op jit(solution)/shard_map/ppermute | solution.py:584
  132.5 15.1 %collective-permute-start.22 = (bf16[384,384]{1,0:T(8,128)(2,1)S(1)}, bf16[384,384]{1,0:T(8,128)(2,1)S(1)}, u32[]{:S(2)}, u32[]{:S(2)}) collective-permute-start(bf16[384,384]{1,0:T(8,128)(2,1)S(1)} %get-tuple-element.363), channel_id=1, source_target_pairs={{0,8},{8,0},{16,24},{24,16},{1,9},{9,1},{17,25},{25,17},{2,10},{10... | collective-permute-start | bytes 884744 | tf_op jit(solution)/shard_map/ppermute | solution.py:584
  137.3 8.1 %collective-permute-start.20 = (bf16[1,192,384]{2,1,0:T(8,128)(2,1)S(1)}, bf16[1,192,384]{2,1,0:T(8,128)(2,1)S(1)}, u32[]{:S(2)}, u32[]{:S(2)}) collective-permute-start(bf16[1,192,384]{2,1,0:T(8,128)(2,1)S(1)} %get-tuple-element.360), channel_id=1, source_target_pairs={{0,4},{1,5},{2,6},{3,7},{4,0},{5,1},{6,2},{7,3},{8,12},{9,13},{10,... | collective-permute-start | bytes 442376 | tf_op jit(solution)/shard_map/ppermute | solution.py:584
  139.9 5.5 %collective-permute-start.19 = (bf16[1,192,384]{2,1,0:T(8,128)(2,1)S(1)}, bf16[1,192,384]{2,1,0:T(8,128)(2,1)S(1)}, u32[]{:S(2)}, u32[]{:S(2)}) collective-permute-start(bf16[1,192,384]{2,1,0:T(8,128)(2,1)S(1)} %get-tuple-element.358), channel_id=1, source_target_pairs={{0,16},{8,24},{16,0},{24,8},{1,17},{9,25},{17,1},{25,9},{2,18},{10... | collective-permute-start | bytes 442376 | tf_op jit(solution)/shard_map/ppermute | solution.py:584
  146.0 7.9 %collective-permute-start.26 = (bf16[4,96,384]{2,1,0:T(8,128)(2,1)S(1)}, bf16[4,96,384]{2,1,0:T(8,128)(2,1)S(1)}, u32[]{:S(2)}, u32[]{:S(2)}) collective-permute-start(bf16[4,96,384]{2,1,0:T(8,128)(2,1)S(1)} %bitcast.28), channel_id=1, source_target_pairs={{0,8},{8,0},{16,24},{24,16},{1,9},{9,1},{17,25},{25,17},{2,10},{10... | collective-permute-start | bytes 884744 | tf_op jit(solution)/shard_map/ppermute | solution.py:584
  148.4 7.4 %collective-permute-start.23 = (bf16[224,384]{1,0:T(8,128)(2,1)S(1)}, bf16[224,384]{1,0:T(8,128)(2,1)S(1)}, u32[]{:S(2)}, u32[]{:S(2)}) collective-permute-start(bf16[224,384]{1,0:T(8,128)(2,1)S(1)} %get-tuple-element.370), channel_id=1, source_target_pairs={{0,2},{1,3},{2,0},{3,1},{4,6},{5,7},{6,4},{7,5},{8,10},{9,11},{10,... | collective-permute-start | bytes 516104 | tf_op jit(solution)/shard_map/ppermute | solution.py:584
  149.0 15.1 %collective-permute-start.24 = (bf16[224,384]{1,0:T(8,128)(2,1)S(1)}, bf16[224,384]{1,0:T(8,128)(2,1)S(1)}, u32[]{:S(2)}, u32[]{:S(2)}) collective-permute-start(bf16[224,384]{1,0:T(8,128)(2,1)S(1)} %get-tuple-element.371), channel_id=1, source_target_pairs={{0,4},{1,5},{2,6},{3,7},{4,0},{5,1},{6,2},{7,3},{8,12},{9,13},{10,... | collective-permute-start | bytes 516104 | tf_op jit(solution)/shard_map/ppermute | solution.py:584
  151.9 12.1 %collective-permute-start.25 = (bf16[224,384]{1,0:T(8,128)(2,1)S(1)}, bf16[224,384]{1,0:T(8,128)(2,1)S(1)}, u32[]{:S(2)}, u32[]{:S(2)}) collective-permute-start(bf16[224,384]{1,0:T(8,128)(2,1)S(1)} %get-tuple-element.372), channel_id=1, source_target_pairs={{0,6},{1,7},{2,4},{3,5},{4,2},{5,3},{6,0},{7,1},{8,14},{9,15},{10,... | collective-permute-start | bytes 516104 | tf_op jit(solution)/shard_map/ppermute | solution.py:584
  152.9 15.4 %collective-permute-start.27 = (bf16[4,96,384]{2,1,0:T(8,128)(2,1)S(1)}, bf16[4,96,384]{2,1,0:T(8,128)(2,1)S(1)}, u32[]{:S(2)}, u32[]{:S(2)}) collective-permute-start(bf16[4,96,384]{2,1,0:T(8,128)(2,1)S(1)} %bitcast.29), channel_id=1, source_target_pairs={{0,16},{8,24},{16,0},{24,8},{1,17},{9,25},{17,1},{25,9},{2,18},{10... | collective-permute-start | bytes 884744 | tf_op jit(solution)/shard_map/ppermute | solution.py:584
  153.9 15.1 %collective-permute-start.28 = (bf16[4,96,384]{2,1,0:T(8,128)(2,1)S(1)}, bf16[4,96,384]{2,1,0:T(8,128)(2,1)S(1)}, u32[]{:S(2)}, u32[]{:S(2)}) collective-permute-start(bf16[4,96,384]{2,1,0:T(8,128)(2,1)S(1)} %collective-permute-done.26.refs_1_), channel_id=1, source_target_pairs={{0,16},{8,24},{16,0},{24,8},{1,17},{9,25},{17,1},{25,9},{2,18},{10... | collective-permute-start | bytes 884744 | tf_op jit(solution)/shard_map/ppermute | solution.py:584
  164.0 5.0 %copy-start.2 = (f32[96,9280]{1,0:T(8,128)S(1)}, f32[96,9280]{1,0:T(8,128)}, u32[]{:S(2)}) copy-start(f32[96,9280]{1,0:T(8,128)} %refs_9_.1) | copy-start | bytes 10690564
  164.0 5.0 %copy-start.3 = (f32[96,9280]{1,0:T(8,128)S(1)}, f32[96,9280]{1,0:T(8,128)}, u32[]{:S(2)}) copy-start(f32[96,9280]{1,0:T(8,128)} %refs_10_.1) | copy-start | bytes 10690564
  164.0 5.0 %copy-start.4 = (f32[96,9280]{1,0:T(8,128)S(1)}, f32[96,9280]{1,0:T(8,128)}, u32[]{:S(2)}) copy-start(f32[96,9280]{1,0:T(8,128)} %refs_11_.1) | copy-start | bytes 10690564
  164.0 5.1 %copy-start.5 = (f32[96,9280]{1,0:T(8,128)S(1)}, f32[96,9280]{1,0:T(8,128)}, u32[]{:S(2)}) copy-start(f32[96,9280]{1,0:T(8,128)} %refs_12_.1) | copy-start | bytes 10690564
  164.7 12.5 %copy-start.18 = (f32[96,13]{0,1:T(8,128)S(1)}, f32[96,13]{0,1:T(8,128)}, u32[]{:S(2)}) copy-start(f32[96,13]{0,1:T(8,128)} %param.19) | copy-start | bytes 14980
  164.7 12.5 %copy-start.19 = (f32[96,13]{0,1:T(8,128)S(1)}, f32[96,13]{0,1:T(8,128)}, u32[]{:S(2)}) copy-start(f32[96,13]{0,1:T(8,128)} %param.21) | copy-start | bytes 14980
  164.7 12.5 %copy-start.20 = (f32[96,13]{0,1:T(8,128)S(1)}, f32[96,13]{0,1:T(8,128)}, u32[]{:S(2)}) copy-start(f32[96,13]{0,1:T(8,128)} %param.23) | copy-start | bytes 14980
  164.7 12.5 %copy-start.21 = (f32[96,13]{0,1:T(8,128)S(1)}, f32[96,13]{0,1:T(8,128)}, u32[]{:S(2)}) copy-start(f32[96,13]{0,1:T(8,128)} %param.25) | copy-start | bytes 14980
  164.7 12.4 %collective-permute-start.31 = (bf16[2,96,384]{2,1,0:T(8,128)(2,1)S(1)}, bf16[2,96,384]{2,1,0:T(8,128)(2,1)S(1)}, u32[]{:S(2)}, u32[]{:S(2)}) collective-permute-start(bf16[2,96,384]{2,1,0:T(8,128)(2,1)S(1)} %get-tuple-element.384.refs_0_), channel_id=1, source_target_pairs={{0,24},{8,16},{16,8},{24,0},{1,25},{9,17},{17,9},{25,1},{2,26},{10... | collective-permute-start | bytes 442376 | tf_op jit(solution)/shard_map/ppermute | solution.py:584
  166.2 11.0 %collective-permute-start.30 = (bf16[2,96,384]{2,1,0:T(8,128)(2,1)S(1)}, bf16[2,96,384]{2,1,0:T(8,128)(2,1)S(1)}, u32[]{:S(2)}, u32[]{:S(2)}) collective-permute-start(bf16[2,96,384]{2,1,0:T(8,128)(2,1)S(1)} %get-tuple-element.384.refs_0_), channel_id=1, source_target_pairs={{0,16},{8,24},{16,0},{24,8},{1,17},{9,25},{17,1},{25,9},{2,18},{10... | collective-permute-start | bytes 442376 | tf_op jit(solution)/shard_map/ppermute | solution.py:584
  166.8 10.4 %collective-permute-start.29 = (bf16[2,96,384]{2,1,0:T(8,128)(2,1)S(1)}, bf16[2,96,384]{2,1,0:T(8,128)(2,1)S(1)}, u32[]{:S(2)}, u32[]{:S(2)}) collective-permute-start(bf16[2,96,384]{2,1,0:T(8,128)(2,1)S(1)} %get-tuple-element.384.refs_0_), channel_id=1, source_target_pairs={{0,8},{8,0},{16,24},{24,16},{1,9},{9,1},{17,25},{25,17},{2,10},{10... | collective-permute-start | bytes 442376 | tf_op jit(solution)/shard_map/ppermute | solution.py:584

commit v4 on v3

--- a/solution.py
+++ b/solution.py
@@ -13,7 +13,7 @@
 FF = 3072
 QUAD = 4
 N_QUAD = HEADS // QUAD
-AUG = 80
+AUG = 72
 
 norm_eps = 1e-05
 adam_eps = 1e-08
@@ -468,7 +468,7 @@
                         for at, z in enumerate((3, 1, 2, 0)):
                             ref[4 * (at // 2) + 2 * x_last + at % 2, rows, :] = part(z)
             else:
-                base = y_last + 4 * x_last
+                base = 4 * y_last + 1 * x_last
                 for ref, order in ((send, (3, 1)), (keep, (2, 0))):
                     for at, z in enumerate(order):
                         ref[2 * at + base, rows, :] = part(z)
@@ -514,9 +514,14 @@
     return jnp.where(i < 2, i + 2, i - 2)
 
 
+def pick_rows(ref, half, count):
+    rows = [ref[pl.ds(pl.multiple_of(z * 2 * count + half * count, 8), count), :] for z in range(4)]
+    return jnp.concatenate(rows, axis=0)
+
+
 def tail_grads_body(scal, *refs):
     h1, ob, dqk, dvo = refs[0:2], refs[2:4], refs[4:6], refs[6:8]
-    small_own, small_other, send_a, keep_a, send_b, keep_b, small_ref = refs[8:]
+    small_own, small_other, send_a, keep_a, send_b, keep_b, small_ref, sum_ref = refs[8:]
     step = pl.program_id(0)
     wq = send_a.shape[1]
     qb = jnp.bitwise_xor(order_b(step), scal[S_SEQ])
@@ -546,9 +551,10 @@
 
     @pl.when(step == 0)
     def _():
-        small = pack_rows(small_own[0] + small_other[0].astype(f32), 128)
-        small_ref[...] = small
-        send_a[2 * wq :, :] = small.astype(bf16)
+        sum_ref[...] = small_own[0] + small_other[0]
+        x_abs = jnp.bitwise_and(scal[S_SEQ], 1)
+        small_ref[...] = pack_rows(pick_rows(sum_ref, x_abs, 48), 64)
+        send_a[2 * wq :, :] = pack_rows(pick_rows(sum_ref, 1 - x_abs, 48), 64).astype(bf16)
 
 
 def tail_grads(line, sels, dp, small):
@@ -560,8 +566,8 @@
         return pl.BlockSpec((1, depth, rows), lambda i, s: (slot, 0, 0))
 
     outs = [
-        sds((2 * wq + 128, wq), bf16), sds((2 * wq, wq), bf16),
-        sds((2 * wq, wq), bf16), sds((2 * wq, wq), bf16), sds((128, wq), f32),
+        sds((2 * wq + 64, wq), bf16), sds((2 * wq, wq), bf16),
+        sds((2 * wq, wq), bf16), sds((2 * wq, wq), bf16), sds((64, wq), f32),
     ]
     return line.call(
         tail_grads_body,
@@ -574,6 +580,7 @@
         outs,
         [whole(o.shape) for o in outs],
         grid=(4,),
+        scratch=[pltpu.VMEM((depth, 2 * HD), f32)],
         vmem=10,
         hold=4,
         name="tail_grads",
@@ -618,61 +625,63 @@
         final_body, [v for p in pieces for v in (p.keep, p.recv)], [whole((1,) + shape[1:])] * 4,
         [sds(shape, bf16)], [whole(shape)], vmem=4, name="final",
     )
-    return mine.reshape(4, D // 8, shape[2])
-
-
-def tail_one_body(scal, keep_a, recv_a, keep_b, recv_b, small_ref, send_a, send_b):
+    return mine.reshape(4 * (D // 8), shape[2])
+
+
+def tail_one_body(scal, keep_a, recv_a, keep_b, recv_b, small_ref, send_a, send_b, half_ref):
     wq = send_b.shape[0]
     send_a[:wq, :] = (keep_a[wq : 2 * wq].astype(f32) + recv_a[wq : 2 * wq].astype(f32)).astype(bf16)
-    send_a[wq:, :] = (small_ref[...] + recv_a[2 * wq :].astype(f32)).astype(bf16)
+    half_ref[...] = unpack_rows(small_ref[...] + recv_a[2 * wq :].astype(f32))
+    y_abs = jnp.right_shift(scal[S_SEQ], 1)
+    send_a[wq:, :] = pack_rows(pick_rows(half_ref, 1 - y_abs, 24), 32).astype(bf16)
     send_b[...] = (keep_b[wq:].astype(f32) + recv_b[wq:].astype(f32)).astype(bf16)
 
 
-def tail_two_body(scal, keep_a, recv_a, keep_b, recv_b, small_ref, far_a, far_b, own_ref, *out_refs):
+def tail_two_body(scal, keep_a, recv_a, keep_b, recv_b, small_ref, far_a, far_b, own_ref, *refs):
+    out_refs, half_ref = refs[:-1], refs[-1]
     wq = far_b.shape[0]
     block = D // 8
-    small = small_ref[...] + recv_a[2 * wq :].astype(f32) + far_a[wq:].astype(f32)
-    small = unpack_rows(small)
+    half_ref[...] = unpack_rows(small_ref[...] + recv_a[2 * wq :].astype(f32))
+    small = pick_rows(half_ref, jnp.right_shift(scal[S_SEQ], 1), 24) + unpack_rows(far_a[wq:].astype(f32))
     first = keep_a[:wq].astype(f32) + recv_a[:wq].astype(f32) + far_a[:wq].astype(f32)
     second = keep_b[:wq].astype(f32) + recv_b[:wq].astype(f32) + far_b[...].astype(f32)
     for z, ref in enumerate((own_ref, *out_refs)):
         rows = slice(z * block, (z + 1) * block)
         ref[:block, :] = first[rows].astype(ref.dtype)
         ref[block : 2 * block, :] = second[rows].astype(ref.dtype)
-        ref[2 * block :, :] = pack_rows(small[rows], block // 3).astype(ref.dtype)
+        packed = pack_rows(small[z * 24 : (z + 1) * 24], 8)
+        packed = jnp.concatenate([packed, jnp.zeros_like(packed)], axis=0)
+        ref[2 * block :, :] = packed.astype(ref.dtype)
 
 
 def tail_final_body(scal, *refs):
-    mine_ref, small_ref = refs[-2:]
-    block = mine_ref.shape[1]
     total = refs[0][...]
-    for ref in refs[1:-2]:
+    for ref in refs[1:-1]:
         total = total + ref[...].astype(f32)
-    mine_ref[0] = total[:block].astype(bf16)
-    mine_ref[1] = total[block : 2 * block].astype(bf16)
-    small_ref[...] = unpack_rows(total[2 * block :])
+    refs[-1][...] = total.astype(bf16)
 
 
 def tail_one(line, tail):
     send_a, keep_a, send_b, keep_b, small = tail
     wq = D // 2
     recv_a, recv_b = swap(send_a, "seq", 4, 1), swap(send_b, "seq", 4, 2)
-    shapes = [sds((wq + 128, wq), bf16), sds((wq, wq), bf16)]
+    shapes = [sds((wq + 32, wq), bf16), sds((wq, wq), bf16)]
+    halves = [pltpu.VMEM((D // 4, 2 * HD), f32)]
 
     def first():
         args = [keep_a, recv_a, keep_b, recv_b, small]
         next_a, next_b = line.call(
             tail_one_body, args, [whole(v.shape) for v in args], shapes, [whole(v.shape) for v in shapes],
-            vmem=12, name="tail_one",
+            scratch=halves, vmem=12, name="tail_one",
         )
         return swap(next_a, "seq", 4, 2), swap(next_b, "seq", 4, 1)
 
     def second(far_a, far_b):
         args = [keep_a, recv_a, keep_b, recv_b, small, far_a, far_b]
-        shape = (2 * (D // 8) + D // 24, wq)
+        shape = (2 * (D // 8) + 16, wq)
         own, *sends = line.call(
             tail_two_body, args, [whole(v.shape) for v in args], [sds(shape, f32)] + [sds(shape, bf16)] * 3,
-            [whole(shape)] * 4, vmem=10, hold=5, name="tail_two",
+            [whole(shape)] * 4, scratch=halves, vmem=10, hold=5, name="tail_two",
         )
         return [own, *(swap(v, "grp", 8, 2 * (k + 1)) for k, v in enumerate(sends))]
 
@@ -680,12 +689,11 @@
 
 
 def tail_final(line, args):
-    wq = D // 2
-    shapes = [sds((2, D // 8, wq), bf16), sds((D // 8, 2 * HD), f32)]
-    return line.call(
-        tail_final_body, args, [whole(v.shape) for v in args], shapes, [whole(v.shape) for v in shapes],
-        vmem=6, hold=5, name="tail_final",
-    )
+    (mine,) = line.call(
+        tail_final_body, args, [whole(v.shape) for v in args], [sds(args[0].shape, bf16)],
+        [whole(args[0].shape)], vmem=6, hold=5, name="tail_final",
+    )
+    return mine
 
 
 def gather_parts(mine):
@@ -705,11 +713,12 @@
 def adam_body(n_alias, has_small, scal, *refs):
     parts, refs = refs[:4], refs[4:]
     if has_small:
-        small, vec_in, refs = refs[0], refs[1:5], refs[5:]
+        vec_in, refs = refs[:4], refs[4:]
     states, refs = refs[:4], refs[4 + n_alias :]
-    outs, vec_outs = refs[:6], refs[6:]
+    outs, refs = refs[:6], refs[6:]
     grad_ref = outs[0]
-    count, _, wq = parts[0].shape
+    block = D // 8
+    count, wq = parts[0].shape[0] // block, parts[0].shape[1]
     step = pl.program_id(0)
     path, half = jnp.right_shift(step, 1), jnp.bitwise_and(step, 1)
     for k, ref in enumerate(parts):
@@ -718,15 +727,24 @@
         @pl.when((jnp.right_shift(quarter, 1) == half) & (step < 2 * count))
         def _(ref=ref, quarter=quarter):
             at = pl.multiple_of(jnp.bitwise_and(quarter, 1) * wq, 128)
-            grad_ref[:, pl.ds(at, wq)] = ref[jnp.minimum(path, count - 1)].astype(f32)
+            rows = pl.ds(pl.multiple_of(jnp.minimum(path, count - 1) * block, block), block)
+            grad_ref[:, pl.ds(at, wq)] = ref[rows, :].astype(f32)
 
     if has_small:
+        vec_outs, small_ref = refs[:6], refs[6]
 
         @pl.when(step == 2 * count)
         def _():
+            for k, ref in enumerate(parts):
+                quarter = jnp.bitwise_xor(scal[S_SEQ], k)
+                first = jnp.bitwise_and(quarter, 1) * 48 + jnp.right_shift(quarter, 1) * 24
+                packed = ref[2 * block :].astype(f32)
+                for b in range(3):
+                    small_ref[pl.ds(pl.multiple_of(first + 8 * b, 8), 8), :] = packed[:8, b * 128 : (b + 1) * 128]
+            small = small_ref[...]
             grad_ref[...] = jnp.zeros_like(grad_ref)
-            grad_ref[:, : 2 * HD] = small[...]
-            grad = small[...].T[HD : HD + vec_in[0].shape[0]]
+            grad_ref[:, : 2 * HD] = small
+            grad = small.T[HD : HD + vec_in[0].shape[0]]
             results = adam_math(grad, *[v[...] for v in vec_in], vector_rate)
             for ref, value in zip(vec_outs, (grad, *results, results[0])):
                 ref[...] = value.astype(ref.dtype)
@@ -736,14 +754,15 @@
         ref[...] = value.astype(ref.dtype)
 
 
-def adam_piece(line, parts, states, outs, block_of, small=(), vecs=()):
-    count, block, _ = parts[0].shape
+def adam_piece(line, parts, states, outs, block_of, vecs=()):
+    block = D // 8
+    count = parts[0].shape[0] // block
     rows, wide = states[0].shape
     spec = pl.BlockSpec((block, D), lambda i, s: (0, block_of(i)))
     anywhere = pl.BlockSpec(memory_space=pl.ANY)
     n_alias = 0 if outs is None else 6
     shapes = [sds((rows, wide), f32)] * 5 + [sds((rows, wide), bf16)]
-    args = [*parts, *small, *vecs, *states]
+    args = [*parts, *vecs, *states]
     n_before = len(args)
     out_specs = [spec] * 6
     if vecs:
@@ -752,10 +771,11 @@
     return line.call(
         partial(adam_body, n_alias, bool(vecs)),
         [*args, *(outs or [])],
-        [whole(v.shape) for v in [*parts, *small, *vecs]] + [spec] * 4 + [anywhere] * n_alias,
+        [whole(v.shape) for v in [*parts, *vecs]] + [spec] * 4 + [anywhere] * n_alias,
         shapes,
         out_specs,
         grid=(2 * count + (1 if vecs else 0),),
+        scratch=[pltpu.VMEM((rows, 2 * HD), f32)] if vecs else [],
         aliases={1 + n_before + i: i for i in range(n_alias)},
         vmem=16,
         name="adam",
@@ -928,7 +948,7 @@
     if fast:
         first = Halves(
             line, *mlp_grads(line, False, sels, acts[0], out_far=(1,)),
-            [("grp", 8, 2), ("seq", 4, 1), ("grp", 8, 4), ("seq", 4, 2)],
+            [("grp", 8, 2), ("seq", 4, 2), ("grp", 8, 4), ("seq", 4, 1)],
         )
         (acts[1],) = line.wait(acts[1])
     block_output, d_resid, d_attn, rho, ds_own, sums = line.call(
@@ -1026,9 +1046,10 @@
         second.step()
         mine = final_both(line, [first, second])
         part_x, part_y = swap(mine, "seq", 4, 1), swap(mine, "seq", 4, 2)
+        last = tail_second(*far)
+        (part_y,) = line.wait(part_y)
         both_mine = [mine, part_x, part_y, swap(part_x, "seq", 4, 2)]
-        last = tail_second(*far)
-        last_mine, small_own = tail_final(line, last)
+        last_mine = tail_final(line, last)
         outs = adam_piece(
             line, both_mine, states_m, None,
             lambda i: jnp.where(jnp.bitwise_and(i, 2) == 0, 8, 4) + 2 * (i // 4) + jnp.bitwise_and(i, 1),
@@ -1036,7 +1057,7 @@
         last_parts = gather_parts(last_mine)
         outs = adam_piece(
             line, last_parts, states_m, outs, lambda i: jnp.where(i < 4, i, (4 * D + 2 * FF) // D),
-            small=[small_own], vecs=states_v,
+            vecs=states_v,
         )
         mats, vecs = outs[:6], [v.T for v in outs[6:]]
     else:

time: 183 us -> 178 us (0.973)
  waiting for transfers between devices: 35.7 us -> 27.9 us
    ppermute x32, waiting for transfers between devices: 35.7 us -> 27.9 us  [swap(): return lax.ppermute(value, axis, [(i, i ^ bit) for i in range(size)])]
  transfers between devices with their start and end apart: 32 -> 32, of which waited for: 12 -> 7; matrix products, arithmetic and copies ran while one was open for 0% -> 0% of each run, Pallas kernels for 48% -> 50%
where the time goes in v4:
time: 178 us
  Pallas kernels  105 us (59%)
  starting transfers between devices  41 us (23%)
  waiting for transfers between devices  27.9 us (16%)
  between operations  2.02 us (1%)
    pallas_call x24, Pallas kernels, call(): pl.pallas_call(body, out_shape=tuple((pltpu.HBM(o.shape, o.dtype) if k in...  105 us
    ppermute x32, starting transfers between devices, swap(): return lax.ppermute(value, axis, [(i, i ^ bit) for i in range(size)])  41 us
    ppermute x32, waiting for transfers between devices, swap(): return lax.ppermute(value, axis, [(i, i ^ bit) for i in range(size)])  27.9 us
  transfers between devices with their start and end apart: 32, of which 7 were waited for; matrix products, arithmetic and copies ran while one was open for 0% of the time, Pallas kernels for 50%

profile of v4, /device:TPU:0, one launch (start us, length us, event | category | flops | bytes accessed | tf_op | source)
XLA Modules:
  0.0 177.7 jit_solution(8643751001710989497)
XLA Ops:
  1.3 0.1 compare_select_fusion.2.scal
  1.5 0.7 copy-done.12
  2.2 6.6 %keys.1 = (bf16[512,768]{1,0:T(8,128)(2,1)S(1)}, bf16[768,512]{1,0:T(8,128)(2,1)S(1)}, bf16[1536,512]{1,0:T(8,128)(2,1)S(1)}, bf16[768,512]{1,0:T(8,128)(2,1)S(1)}, bf16[864,128]{1,0:T(8,128)(2,1)S(1)}) custom-call(s32[16]{0:T(128)S(1)} %compare_select_fusion.2.scal, bf16[512,768]{1,0:T(8,128)(2,1)} %x_ref.3, bf16[9280,768]{1,0:T(8,128)(2,1)} %bitcast.44, ...), custom_call_target="tpu_custom_call" | custom-call | bytes 1024 | tf_op jit(solution)/shard_map/keys/pallas_call | solution.py:74
  8.8 4.0 %collective-permute-start.2 = (bf16[864,128]{1,0:T(8,128)(2,1)S(1)}, bf16[864,128]{1,0:T(8,128)(2,1)S(1)}, u32[]{:S(2)}, u32[]{:S(2)}) collective-permute-start(bf16[864,128]{1,0:T(8,128)(2,1)S(1)} %get-tuple-element.230), channel_id=1, source_target_pairs={{0,24},{8,16},{16,8},{24,0},{1,25},{9,17},{17,9},{25,1},{2,26},{10... | collective-permute-start | bytes 663560 | tf_op jit(solution)/shard_map/ppermute | solution.py:591
  12.8 0.5 collective-permute-start.1
  13.3 0.1 collective-permute-start
  13.4 5.7 %queries.1 = (bf16[4,384,512]{2,1,0:T(8,128)(2,1)S(1)}, bf16[4,384,512]{2,1,0:T(8,128)(2,1)S(1)}, bf16[768,512]{1,0:T(8,128)(2,1)S(1)}, bf16[1536,512]{1,0:T(8,128)(2,1)S(1)}) custom-call(s32[16]{0:T(128)S(1)} %compare_select_fusion.2.scal, bf16[512,768]{1,0:T(8,128)(2,1)S(1)} %get-tuple-element.220.h1_ref, bf16[512,768]{1,0:T(8,128)(2,1)} %g_ref.7, ...), custom_call_target="tpu_custom_call" | custom-call | bytes 1024 | tf_op jit(solution)/shard_map/queries/pallas_call | solution.py:74
  19.1 4.0 %local.1.refs_3_ = f32[864,512]{1,0:T(8,128)S(1)} custom-call(s32[16]{0:T(128)S(1)} %compare_select_fusion.2.scal, bf16[1536,512]{1,0:T(8,128)(2,1)S(1)} %get-tuple-element.226.fq_ref.refs_4_.refs_3_, bf16[1536,512]{1,0:T(8,128)(2,1)S(1)} %get-tuple-element.227.fk_ref.refs_4_, bf16[768,512]{1,0:T(8,128)(2,1)S(1)} %get-tuple-element.228.vt_ref.refs_5_), custom_call_target="tpu_custom_call" | custom-call | bytes 1024 | tf_op jit(solution)/shard_map/local/pallas_call | solution.py:74
  23.2 4.5 %after.1 = (f32[768,512]{1,0:T(8,128)S(1)}, f32[16,512]{1,0:T(8,128)S(1)}, f32[512,768]{1,0:T(8,128)S(1)}, bf16[512,768]{1,0:T(8,128)(2,1)S(1)}, bf16[864,128]{1...) custom-call(s32[16]{0:T(128)S(1)} %compare_select_fusion.2.scal, ...), custom_call_target="tpu_custom_call", output_to_operand_aliasing={{5}: (9, {}), {6}: (10, {})} | custom-call | bytes 1024 | tf_op jit(solution)/shard_map/after/pallas_call | solution.py:74
  27.9 8.9 %mlp.2 = (f32[512,768]{1,0:T(8,128)S(1)}, f32[512,768]{1,0:T(8,128)S(1)}, bf16[2,2,512,768]{3,2,1,0:T(8,128)(2,1)S(1)}, f32[1,1536]{1,0:T(1,128)S(1)}) custom-call(s32[16]{0:T(128)S(1)} %compare_select_fusion.2.scal, bf16[512,768]{1,0:T(8,128)(2,1)S(1)} %get-tuple-element.242.h2_ref, bf16[512,768]{1,0:T(8,128)(2,1)} %g_ref.7, bf16[9280,768]{1,0:T(8,128)(2,1)} %bitcast.50, ...), custom_call_target="tpu_custom_call" | custom-call | bytes 1024 | tf_op jit(solution)/shard_map/mlp/pallas_call | solution.py:74
  36.8 0.6 collective-permute-start.4
  37.3 9.1 %mlp.3 = (f32[512,768]{1,0:T(8,128)S(1)}, f32[512,768]{1,0:T(8,128)S(1)}, bf16[2,2,512,768]{3,2,1,0:T(8,128)(2,1)S(1)}, f32[1,1536]{1,0:T(1,128)S(1)}) custom-call(s32[16]{0:T(128)S(1)} %compare_select_fusion.2.scal, bf16[512,768]{1,0:T(8,128)(2,1)S(1)} %get-tuple-element.242.h2_ref, bf16[512,768]{1,0:T(8,128)(2,1)} %g_ref.7, bf16[9280,768]{1,0:T(8,128)(2,1)} %bitcast.52, ...), custom_call_target="tpu_custom_call" | custom-call | bytes 1024 | tf_op jit(solution)/shard_map/mlp/pallas_call | solution.py:74
  46.5 0.1 collective-permute-start.5
  46.6 4.7 %mlp_grads.2 = (bf16[8,192,384]{2,1,0:T(8,128)(2,1)}, bf16[8,192,384]{2,1,0:T(8,128)(2,1)}) custom-call(s32[16]{0:T(128)S(1)} %compare_select_fusion.2.scal, bf16[4,384,512]{2,1,0:T(8,128)(2,1)S(1)} %get-tuple-element.258.refs_0_.refs_6_.refs_2_, bf16[4,384,512]{2,1,0:T(8,128)(2,1)S(1)} %collective-permute-done.3.refs_1_.refs_7_.refs_3_, ...), custom_call_target="tpu_custom_call" | custom-call | bytes 1024 | tf_op jit(solution)/shard_map/mlp_grads/pallas_call | solution.py:74
  51.3 2.0 %collective-permute-start.9 = (bf16[8,192,384]{2,1,0:T(8,128)(2,1)}, bf16[8,192,384]{2,1,0:T(8,128)(2,1)}, u32[]{:S(2)}, u32[]{:S(2)}) collective-permute-start(bf16[8,192,384]{2,1,0:T(8,128)(2,1)} %get-tuple-element.311), channel_id=1, source_target_pairs={{0,2},{1,3},{2,0},{3,1},{4,6},{5,7},{6,4},{7,5},{8,10},{9,11},{10,... | collective-permute-start | bytes 3538952 | tf_op jit(solution)/shard_map/ppermute | solution.py:591
  53.3 6.7 %back.1 = (bf16[512,768]{1,0:T(8,128)(2,1)}, f32[512,768]{1,0:T(8,128)}, bf16[768,512]{1,0:T(8,128)(2,1)}, bf16[864,512]{1,0:T(8,128)(2,1)}, bf16[864,128]{1,0:T(8,128)(2,1)}, /*index=5*/f32[4,768]{1,0:T(4,128)S(1)}) custom-call(s32[16]{0:T(128)S(1)} %compare_select_fusion.2.scal, f32[512,768]{1,0:T(8,128)S(1)} %get-tuple-element.266.out_ref, ...), custom_call_target="tpu_custom_call" | custom-call | bytes 1024 | tf_op jit(solution)/shard_map/back/pallas_call | solution.py:74
  60.0 2.5 %collective-permute-start.8 = (bf16[864,128]{1,0:T(8,128)(2,1)}, bf16[864,128]{1,0:T(8,128)(2,1)}, u32[]{:S(2)}, u32[]{:S(2)}) collective-permute-start(bf16[864,128]{1,0:T(8,128)(2,1)} %get-tuple-element.284), channel_id=1, source_target_pairs={{0,24},{8,16},{16,8},{24,0},{1,25},{9,17},{17,9},{25,1},{2,26},{10... | collective-permute-start | bytes 663560 | tf_op jit(solution)/shard_map/ppermute | solution.py:591
  62.5 0.5 collective-permute-start.7
  63.0 0.5 collective-permute-start.6
  63.6 5.8 %mlp_grads.3 = (bf16[8,192,384]{2,1,0:T(8,128)(2,1)S(1)}, bf16[8,192,384]{2,1,0:T(8,128)(2,1)S(1)}) custom-call(s32[16]{0:T(128)S(1)} %compare_select_fusion.2.scal, bf16[4,384,512]{2,1,0:T(8,128)(2,1)S(1)} %get-tuple-element.258.refs_0_.refs_6_.refs_2_, bf16[4,384,512]{2,1,0:T(8,128)(2,1)S(1)} %collective-permute-done.3.refs_1_.refs_7_.refs_3_, ...), custom_call_target="tpu_custom_call" | custom-call | bytes 1024 | tf_op jit(solution)/shard_map/mlp_grads/pallas_call | solution.py:74
  69.4 1.6 collective-permute-start.10
  71.0 2.6 %collective-permute-done.7.refs_1_ = bf16[864,128]{1,0:T(8,128)(2,1)} collective-permute-done((bf16[864,128]{1,0:T(8,128)(2,1)}, bf16[864,128]{1,0:T(8,128)(2,1)}, u32[]{:S(2)}, u32[]{:S(2)}) %collective-permute-start.7) | collective-permute-done | bytes 221216 | tf_op jit(solution)/shard_map/ppermute | solution.py:591
  73.6 13.4 %attend_back.1 = (bf16[4,768,512]{2,1,0:T(8,128)(2,1)S(1)}, f32[768,64]{1,0:T(8,128)S(1)}, f32[768,3]{1,0:T(8,128)S(1)}) custom-call(s32[16]{0:T(128)S(1)} %compare_select_fusion.2.scal, bf16[864,128]{1,0:T(8,128)(2,1)} %collective-permute-done.6.refs_0_, bf16[864,128]{1,0:T(8,128)(2,1)} %collective-permute-done.7.refs_1_, ...), custom_call_target="tpu_custom_call" | custom-call | flops 1000000000 | bytes 1024 | tf_op jit(solution)/shard_map/attend_back/pallas_call | solution.py:74
  87.0 0.1 collective-permute-start.11
  87.1 7.8 %input.1 = (bf16[512,768]{1,0:T(8,128)(2,1)}, f32[1,384,128]{2,1,0:T(8,128)S(1)}, f32[1,384,128]{2,1,0:T(8,128)S(1)}) custom-call(s32[16]{0:T(128)S(1)} %compare_select_fusion.2.scal, bf16[4,768,512]{2,1,0:T(8,128)(2,1)S(1)} %get-tuple-element.298.dp_ref, bf16[9280,768]{1,0:T(8,128)(2,1)} %bitcast.56, bf16[512,768]{1,0:T(8,128)(2,1)} %x_ref.3, ...), custom_call_target="tpu_custom_call" | custom-call | bytes 1024 | tf_op jit(solution)/shard_map/input/pallas_call | solution.py:74
  95.0 0.5 collective-permute-start.12
  95.4 2.1 %halve.6 = (bf16[4,192,384]{2,1,0:T(8,128)(2,1)S(1)}, bf16[4,192,384]{2,1,0:T(8,128)(2,1)S(1)}) custom-call(s32[16]{0:T(128)S(1)} %compare_select_fusion.2.scal, bf16[8,192,384]{2,1,0:T(8,128)(2,1)S(1)} %copy-done.22, bf16[8,192,384]{2,1,0:T(8,128)(2,1)} %collective-permute-done.9.recv_ref), custom_call_target="tpu_custom_call" | custom-call | flops 14000000000 | bytes 1024 | tf_op jit(solution)/shard_map/halve/pallas_call | solution.py:74
  97.5 1.6 collective-permute-start.13
  99.1 0.8 halve.7
  100.0 0.9 collective-permute-start.14
  100.9 5.7 %tail_grads.1 = (bf16[832,384]{1,0:T(8,128)(2,1)S(1)}, bf16[768,384]{1,0:T(8,128)(2,1)S(1)}, bf16[768,384]{1,0:T(8,128)(2,1)S(1)}, bf16[768,384]{1,0:T(8,128)(2,1)S(1)}, f32[64,384]{1,0:T(8,128)S(1)}) custom-call(s32[16]{0:T(128)S(1)} %compare_select_fusion.2.scal, bf16[4,384,512]{2,1,0:T(8,128)(2,1)S(1)} %get-tuple-element.258.refs_0_.refs_6_.refs_2_, ...), custom_call_target="tpu_custom_call" | custom-call | flops 4000000000 | bytes 1024 | tf_op jit(solution)/shard_map/tail_grads/pallas_call | solution.py:74
  106.5 1.6 collective-permute-start.15
  108.1 0.5 collective-permute-start.16
  108.6 5.2 %collective-permute-done.13.recv_ref = bf16[4,192,384]{2,1,0:T(8,128)(2,1)S(1)} collective-permute-done((bf16[4,192,384]{2,1,0:T(8,128)(2,1)S(1)}, bf16[4,192,384]{2,1,0:T(8,128)(2,1)S(1)}, u32[]{:S(2)}, u32[]{:S(2)}) %collective-permute-start.13) | collective-permute-done | bytes 589856 | tf_op jit(solution)/shard_map/ppermute | solution.py:591
  113.8 0.7 halve.8
  114.5 2.7 %collective-permute-start.17 = (bf16[2,192,384]{2,1,0:T(8,128)(2,1)S(1)}, bf16[2,192,384]{2,1,0:T(8,128)(2,1)S(1)}, u32[]{:S(2)}, u32[]{:S(2)}) collective-permute-start(bf16[2,192,384]{2,1,0:T(8,128)(2,1)S(1)} %get-tuple-element.347), channel_id=1, source_target_pairs={{0,4},{1,5},{2,6},{3,7},{4,0},{5,1},{6,2},{7,3},{8,12},{9,13},{10,... | collective-permute-start | bytes 884744 | tf_op jit(solution)/shard_map/ppermute | solution.py:591
  117.2 0.7 halve.9
  117.8 1.5 collective-permute-start.18
  119.4 6.1 %collective-permute-done.16.recv_b = bf16[768,384]{1,0:T(8,128)(2,1)S(1)} collective-permute-done((bf16[768,384]{1,0:T(8,128)(2,1)S(1)}, bf16[768,384]{1,0:T(8,128)(2,1)S(1)}, u32[]{:S(2)}, u32[]{:S(2)}) %collective-permute-start.16) | collective-permute-done | bytes 589856 | tf_op jit(solution)/shard_map/ppermute | solution.py:591
  125.5 0.8 tail_one.1
  126.3 1.6 collective-permute-start.21
  127.9 1.5 collective-permute-start.22
  129.4 0.6 halve.10
  130.0 0.6 halve.11
  130.7 2.6 %collective-permute-start.20 = (bf16[1,192,384]{2,1,0:T(8,128)(2,1)S(1)}, bf16[1,192,384]{2,1,0:T(8,128)(2,1)S(1)}, u32[]{:S(2)}, u32[]{:S(2)}) collective-permute-start(bf16[1,192,384]{2,1,0:T(8,128)(2,1)S(1)} %get-tuple-element.359), channel_id=1, source_target_pairs={{0,4},{1,5},{2,6},{3,7},{4,0},{5,1},{6,2},{7,3},{8,12},{9,13},{10,... | collective-permute-start | bytes 442376 | tf_op jit(solution)/shard_map/ppermute | solution.py:591
  133.3 0.5 collective-permute-start.19
  133.8 5.4 %collective-permute-done.20.refs_3_ = bf16[1,192,384]{2,1,0:T(8,128)(2,1)S(1)} collective-permute-done((bf16[1,192,384]{2,1,0:T(8,128)(2,1)S(1)}, bf16[1,192,384]{2,1,0:T(8,128)(2,1)S(1)}, u32[]{:S(2)}, u32[]{:S(2)}) %collective-permute-start.20) | collective-permute-done | bytes 147488 | tf_op jit(solution)/shard_map/ppermute | solution.py:591
  139.3 0.6 final.1
  139.9 1.6 collective-permute-start.27
  141.5 1.8 %collective-permute-start.23 = (bf16[384,384]{1,0:T(8,128)(2,1)S(1)}, bf16[384,384]{1,0:T(8,128)(2,1)S(1)}, u32[]{:S(2)}, u32[]{:S(2)}) collective-permute-start(bf16[384,384]{1,0:T(8,128)(2,1)S(1)} %bitcast.29), channel_id=1, source_target_pairs={{0,16},{8,24},{16,0},{24,8},{1,17},{9,25},{17,1},{25,9},{2,18},{10... | collective-permute-start | bytes 884744 | tf_op jit(solution)/shard_map/ppermute | solution.py:591
  143.3 0.9 tail_two.1
  144.3 2.0 %collective-permute-start.25 = (bf16[208,384]{1,0:T(8,128)(2,1)S(1)}, bf16[208,384]{1,0:T(8,128)(2,1)S(1)}, u32[]{:S(2)}, u32[]{:S(2)}) collective-permute-start(bf16[208,384]{1,0:T(8,128)(2,1)S(1)} %get-tuple-element.372), channel_id=1, source_target_pairs={{0,4},{1,5},{2,6},{3,7},{4,0},{5,1},{6,2},{7,3},{8,12},{9,13},{10,... | collective-permute-start | bytes 479240 | tf_op jit(solution)/shard_map/ppermute | solution.py:591
  146.3 2.4 %collective-permute-start.26 = (bf16[208,384]{1,0:T(8,128)(2,1)S(1)}, bf16[208,384]{1,0:T(8,128)(2,1)S(1)}, u32[]{:S(2)}, u32[]{:S(2)}) collective-permute-start(bf16[208,384]{1,0:T(8,128)(2,1)S(1)} %get-tuple-element.373), channel_id=1, source_target_pairs={{0,6},{1,7},{2,4},{3,5},{4,2},{5,3},{6,0},{7,1},{8,14},{9,15},{10,... | collective-permute-start | bytes 479240 | tf_op jit(solution)/shard_map/ppermute | solution.py:591
  148.6 1.5 collective-permute-done.23.refs_2_
  150.2 1.7 collective-permute-start.28
  151.9 0.3 collective-permute-done.24.refs_1_
  152.2 6.7 %collective-permute-done.25.refs_2_ = bf16[208,384]{1,0:T(8,128)(2,1)S(1)} collective-permute-done((bf16[208,384]{1,0:T(8,128)(2,1)S(1)}, bf16[208,384]{1,0:T(8,128)(2,1)S(1)}, u32[]{:S(2)}, u32[]{:S(2)}) %collective-permute-start.25) | collective-permute-done | bytes 159776 | tf_op jit(solution)/shard_map/ppermute | solution.py:591
  159.0 0.6 tail_final.1.refs_0_
  159.6 0.4 collective-permute-start.31
  160.0 1.5 collective-permute-start.30
  161.5 1.7 collective-permute-start.29
  163.2 0.9 copy-done.5
  164.1 8.0 %adam.2 = (f32[96,9280]{1,0:T(8,128)}, f32[96,9280]{1,0:T(8,128)}, f32[96,9280]{1,0:T(8,128)}, f32[96,9280]{1,0:T(8,128)}, f32[96,9280]{1,0:T(8,128)}, /*index=5*/bf16[96,9280]{1,0:T(8,128)(2,1)}) custom-call(s32[16]{0:T(128)S(1)} %compare_select_fusion.2.scal, bf16[384,384]{1,0:T(8,128)(2,1)S(1)} %bitcast.30, ...), custom_call_target="tpu_custom_call" | custom-call | bytes 1024 | tf_op jit(solution)/shard_map/adam/pallas_call | solution.py:74
  172.2 5.4 %adam.3 = (f32[96,9280]{1,0:T(8,128)}, f32[96,9280]{1,0:T(8,128)}, f32[96,9280]{1,0:T(8,128)}, f32[96,9280]{1,0:T(8,128)}, f32[96,9280]{1,0:T(8,128)}, /*index=5...) custom-call(s32[16]{0:T(128)S(1)} %compare_select_fusion.2.scal, ...), custom_call_target="tpu_custom_call", output_to_operand_aliasing={{0}: (13, {}), {1}: (14, {}), {2}: (15, {}), {3}: (16, {}),... | custom-call | bytes 1024 | tf_op jit(solution)/shard_map/adam/pallas_call | solution.py:74
  (77 shorter events, 0.4 us)
Async XLA Ops:
  1.5 0.7 copy-start.12
  8.8 10.3 %copy-start.14 = (bf16[768,512]{1,0:T(8,128)(2,1)}, bf16[768,512]{1,0:T(8,128)(2,1)S(1)}, u32[]{:S(2)}) copy-start(bf16[768,512]{1,0:T(8,128)(2,1)S(1)} %get-tuple-element.292.refs_9_) | copy-start | bytes 2359300
  8.8 10.3 %copy-start.7 = (bf16[1536,512]{1,0:T(8,128)(2,1)}, bf16[1536,512]{1,0:T(8,128)(2,1)S(1)}, u32[]{:S(2)}) copy-start(bf16[1536,512]{1,0:T(8,128)(2,1)S(1)} %get-tuple-element.227.fk_ref.refs_4_) | copy-start | bytes 4718596
  8.8 10.3 %copy-start.9 = (bf16[768,512]{1,0:T(8,128)(2,1)}, bf16[768,512]{1,0:T(8,128)(2,1)S(1)}, u32[]{:S(2)}) copy-start(bf16[768,512]{1,0:T(8,128)(2,1)S(1)} %get-tuple-element.228.vt_ref.refs_5_) | copy-start | bytes 2359300
  8.8 14.4 %collective-permute-start.2 = (bf16[864,128]{1,0:T(8,128)(2,1)S(1)}, bf16[864,128]{1,0:T(8,128)(2,1)S(1)}, u32[]{:S(2)}, u32[]{:S(2)}) collective-permute-start(bf16[864,128]{1,0:T(8,128)(2,1)S(1)} %get-tuple-element.230), channel_id=1, source_target_pairs={{0,24},{8,16},{16,8},{24,0},{1,25},{9,17},{17,9},{25,1},{2,26},{10... | collective-permute-start | bytes 663560 | tf_op jit(solution)/shard_map/ppermute | solution.py:591
  12.8 10.4 %collective-permute-start.1 = (bf16[864,128]{1,0:T(8,128)(2,1)S(1)}, bf16[864,128]{1,0:T(8,128)(2,1)S(1)}, u32[]{:S(2)}, u32[]{:S(2)}) collective-permute-start(bf16[864,128]{1,0:T(8,128)(2,1)S(1)} %get-tuple-element.230), channel_id=1, source_target_pairs={{0,16},{8,24},{16,0},{24,8},{1,17},{9,25},{17,1},{25,9},{2,18},{10... | collective-permute-start | bytes 663560 | tf_op jit(solution)/shard_map/ppermute | solution.py:591
  13.3 9.9 %collective-permute-start = (bf16[864,128]{1,0:T(8,128)(2,1)S(1)}, bf16[864,128]{1,0:T(8,128)(2,1)S(1)}, u32[]{:S(2)}, u32[]{:S(2)}) collective-permute-start(bf16[864,128]{1,0:T(8,128)(2,1)S(1)} %get-tuple-element.230), channel_id=1, source_target_pairs={{0,8},{8,0},{16,24},{24,16},{1,9},{9,1},{17,25},{25,17},{2,10},{10... | collective-permute-start | bytes 663560 | tf_op jit(solution)/shard_map/ppermute | solution.py:591
  19.1 4.1 %copy-start.16 = (bf16[768,512]{1,0:T(8,128)(2,1)}, bf16[768,512]{1,0:T(8,128)(2,1)S(1)}, u32[]{:S(2)}) copy-start(bf16[768,512]{1,0:T(8,128)(2,1)S(1)} %get-tuple-element.291.refs_8_) | copy-start | bytes 2359300
  19.1 34.2 %copy-start = (bf16[1536,512]{1,0:T(8,128)(2,1)}, bf16[1536,512]{1,0:T(8,128)(2,1)S(1)}, u32[]{:S(2)}) copy-start(bf16[1536,512]{1,0:T(8,128)(2,1)S(1)} %get-tuple-element.226.fq_ref.refs_4_.refs_3_) | copy-start | bytes 4718596
  27.8 9.6 %collective-permute-start.3 = (bf16[4,384,512]{2,1,0:T(8,128)(2,1)S(1)}, bf16[4,384,512]{2,1,0:T(8,128)(2,1)S(1)}, u32[]{:S(2)}, u32[]{:S(2)}) collective-permute-start(bf16[4,384,512]{2,1,0:T(8,128)(2,1)S(1)} %get-tuple-element.249), channel_id=1, source_target_pairs={{0,1},{1,0},{2,3},{3,2},{4,5},{5,4},{6,7},{7,6},{8,9},{9,8},{10,11... | collective-permute-start | bytes 4718600 | tf_op jit(solution)/shard_map/ppermute | solution.py:591
  36.8 9.8 %collective-permute-start.4 = (bf16[2,2,512,768]{3,2,1,0:T(8,128)(2,1)S(1)}, bf16[2,2,512,768]{3,2,1,0:T(8,128)(2,1)S(1)}, u32[]{:S(2)}, u32[]{:S(2)}) collective-permute-start(bf16[2,2,512,768]{3,2,1,0:T(8,128)(2,1)S(1)} %get-tuple-element.260.refs_2_.refs_4_), channel_id=1, source_target_pairs={{0,1},{1,0},{2,3},{3,2},{4,5},{5,4},{6,7},{7,6},{8,9},{9,8},{10,11... | collective-permute-start | bytes 9437192 | tf_op jit(solution)/shard_map/ppermute | solution.py:591
  46.5 4.9 %copy-start.6 = (bf16[2,2,512,768]{3,2,1,0:T(8,128)(2,1)}, bf16[2,2,512,768]{3,2,1,0:T(8,128)(2,1)S(1)}, u32[]{:S(2)}) copy-start(bf16[2,2,512,768]{3,2,1,0:T(8,128)(2,1)S(1)} %get-tuple-element.279.refs_2_.refs_4_) | copy-start | bytes 9437188
  46.5 6.8 %copy-start.13 = (bf16[768,13]{0,1:T(8,128)(2,1)S(1)}, bf16[768,13]{0,1:T(8,128)(2,1)}, u32[]{:S(2)}) copy-start(bf16[768,13]{0,1:T(8,128)(2,1)} %param.17) | copy-start | bytes 59908
  46.5 6.8 %collective-permute-start.5 = (bf16[2,2,512,768]{3,2,1,0:T(8,128)(2,1)S(1)}, bf16[2,2,512,768]{3,2,1,0:T(8,128)(2,1)S(1)}, u32[]{:S(2)}, u32[]{:S(2)}) collective-permute-start(bf16[2,2,512,768]{3,2,1,0:T(8,128)(2,1)S(1)} %get-tuple-element.279.refs_2_.refs_4_), channel_id=1, source_target_pairs={{0,1},{1,0},{2,3},{3,2},{4,5},{5,4},{6,7},{7,6},{8,9},{9,8},{10,11... | collective-permute-start | bytes 9437192 | tf_op jit(solution)/shard_map/ppermute | solution.py:591
  51.3 44.1 %collective-permute-start.9 = (bf16[8,192,384]{2,1,0:T(8,128)(2,1)}, bf16[8,192,384]{2,1,0:T(8,128)(2,1)}, u32[]{:S(2)}, u32[]{:S(2)}) collective-permute-start(bf16[8,192,384]{2,1,0:T(8,128)(2,1)} %get-tuple-element.311), channel_id=1, source_target_pairs={{0,2},{1,3},{2,0},{3,1},{4,6},{5,7},{6,4},{7,5},{8,10},{9,11},{10,... | collective-permute-start | bytes 3538952 | tf_op jit(solution)/shard_map/ppermute | solution.py:591
  53.3 6.7 %copy-start.23 = (bf16[2,2,512,768]{3,2,1,0:T(8,128)(2,1)}, bf16[2,2,512,768]{3,2,1,0:T(8,128)(2,1)S(1)}, u32[]{:S(2)}) copy-start(bf16[2,2,512,768]{3,2,1,0:T(8,128)(2,1)S(1)} %collective-permute-done.5.refs_3_.refs_5_) | copy-start | bytes 9437188
  60.0 11.0 %collective-permute-start.8 = (bf16[864,128]{1,0:T(8,128)(2,1)}, bf16[864,128]{1,0:T(8,128)(2,1)}, u32[]{:S(2)}, u32[]{:S(2)}) collective-permute-start(bf16[864,128]{1,0:T(8,128)(2,1)} %get-tuple-element.284), channel_id=1, source_target_pairs={{0,24},{8,16},{16,8},{24,0},{1,25},{9,17},{17,9},{25,1},{2,26},{10... | collective-permute-start | bytes 663560 | tf_op jit(solution)/shard_map/ppermute | solution.py:591
  62.5 11.1 %collective-permute-start.7 = (bf16[864,128]{1,0:T(8,128)(2,1)}, bf16[864,128]{1,0:T(8,128)(2,1)}, u32[]{:S(2)}, u32[]{:S(2)}) collective-permute-start(bf16[864,128]{1,0:T(8,128)(2,1)} %get-tuple-element.284), channel_id=1, source_target_pairs={{0,16},{8,24},{16,0},{24,8},{1,17},{9,25},{17,1},{25,9},{2,18},{10... | collective-permute-start | bytes 663560 | tf_op jit(solution)/shard_map/ppermute | solution.py:591
  63.0 10.6 %collective-permute-start.6 = (bf16[864,128]{1,0:T(8,128)(2,1)}, bf16[864,128]{1,0:T(8,128)(2,1)}, u32[]{:S(2)}, u32[]{:S(2)}) collective-permute-start(bf16[864,128]{1,0:T(8,128)(2,1)} %get-tuple-element.284), channel_id=1, source_target_pairs={{0,8},{8,0},{16,24},{24,16},{1,9},{9,1},{17,25},{25,17},{2,10},{10... | collective-permute-start | bytes 663560 | tf_op jit(solution)/shard_map/ppermute | solution.py:591
  63.5 10.1 %copy-start.1 = (bf16[1536,512]{1,0:T(8,128)(2,1)S(1)}, bf16[1536,512]{1,0:T(8,128)(2,1)}, u32[]{:S(2)}) copy-start(bf16[1536,512]{1,0:T(8,128)(2,1)} %copy-done) | copy-start | bytes 4718596
  63.6 10.0 %copy-start.8 = (bf16[1536,512]{1,0:T(8,128)(2,1)S(1)}, bf16[1536,512]{1,0:T(8,128)(2,1)}, u32[]{:S(2)}) copy-start(bf16[1536,512]{1,0:T(8,128)(2,1)} %copy-done.7) | copy-start | bytes 4718596
  63.6 10.0 %copy-start.10 = (bf16[768,512]{1,0:T(8,128)(2,1)S(1)}, bf16[768,512]{1,0:T(8,128)(2,1)}, u32[]{:S(2)}) copy-start(bf16[768,512]{1,0:T(8,128)(2,1)} %copy-done.9) | copy-start | bytes 2359300
  63.6 10.0 %copy-start.15 = (bf16[768,512]{1,0:T(8,128)(2,1)S(1)}, bf16[768,512]{1,0:T(8,128)(2,1)}, u32[]{:S(2)}) copy-start(bf16[768,512]{1,0:T(8,128)(2,1)} %copy-done.14) | copy-start | bytes 2359300
  63.6 10.0 %copy-start.17 = (bf16[768,512]{1,0:T(8,128)(2,1)S(1)}, bf16[768,512]{1,0:T(8,128)(2,1)}, u32[]{:S(2)}) copy-start(bf16[768,512]{1,0:T(8,128)(2,1)} %copy-done.16) | copy-start | bytes 2359300
  69.4 17.7 %copy-start.11 = (f32[512,768]{1,0:T(8,128)S(1)}, f32[512,768]{1,0:T(8,128)}, u32[]{:S(2)}) copy-start(f32[512,768]{1,0:T(8,128)} %get-tuple-element.299.dr_ref) | copy-start | bytes 4718596
  69.4 29.7 %collective-permute-start.10 = (bf16[8,192,384]{2,1,0:T(8,128)(2,1)S(1)}, bf16[8,192,384]{2,1,0:T(8,128)(2,1)S(1)}, u32[]{:S(2)}, u32[]{:S(2)}) collective-permute-start(bf16[8,192,384]{2,1,0:T(8,128)(2,1)S(1)} %get-tuple-element.316), channel_id=1, source_target_pairs={{0,16},{8,24},{16,0},{24,8},{1,17},{9,25},{17,1},{25,9},{2,18},{10... | collective-permute-start | bytes 3538952 | tf_op jit(solution)/shard_map/ppermute | solution.py:591
  87.0 8.4 %copy-start.22 = (bf16[8,192,384]{2,1,0:T(8,128)(2,1)S(1)}, bf16[8,192,384]{2,1,0:T(8,128)(2,1)}, u32[]{:S(2)}) copy-start(bf16[8,192,384]{2,1,0:T(8,128)(2,1)} %get-tuple-element.310.keep_ref) | copy-start | bytes 3538948
  87.0 13.8 %collective-permute-start.11 = (bf16[4,768,512]{2,1,0:T(8,128)(2,1)S(1)}, bf16[4,768,512]{2,1,0:T(8,128)(2,1)S(1)}, u32[]{:S(2)}, u32[]{:S(2)}) collective-permute-start(bf16[4,768,512]{2,1,0:T(8,128)(2,1)S(1)} %get-tuple-element.298.dp_ref), channel_id=1, source_target_pairs={{0,1},{1,0},{2,3},{3,2},{4,5},{5,4},{6,7},{7,6},{8,9},{9,8},{10,11... | collective-permute-start | bytes 9437192 | tf_op jit(solution)/shard_map/ppermute | solution.py:591
  95.0 5.9 %collective-permute-start.12 = (f32[1,384,128]{2,1,0:T(8,128)S(1)}, f32[1,384,128]{2,1,0:T(8,128)S(1)}, u32[]{:S(2)}, u32[]{:S(2)}) collective-permute-start(f32[1,384,128]{2,1,0:T(8,128)S(1)} %get-tuple-element.321), channel_id=1, source_target_pairs={{0,1},{1,0},{2,3},{3,2},{4,5},{5,4},{6,7},{7,6},{8,9},{9,8},{10,11... | collective-permute-start | bytes 589832 | tf_op jit(solution)/shard_map/ppermute | solution.py:591
  97.5 16.3 %collective-permute-start.13 = (bf16[4,192,384]{2,1,0:T(8,128)(2,1)S(1)}, bf16[4,192,384]{2,1,0:T(8,128)(2,1)S(1)}, u32[]{:S(2)}, u32[]{:S(2)}) collective-permute-start(bf16[4,192,384]{2,1,0:T(8,128)(2,1)S(1)} %get-tuple-element.329), channel_id=1, source_target_pairs={{0,16},{8,24},{16,0},{24,8},{1,17},{9,25},{17,1},{25,9},{2,18},{10... | collective-permute-start | bytes 1769480 | tf_op jit(solution)/shard_map/ppermute | solution.py:591
  100.0 17.2 %collective-permute-start.14 = (bf16[4,192,384]{2,1,0:T(8,128)(2,1)S(1)}, bf16[4,192,384]{2,1,0:T(8,128)(2,1)S(1)}, u32[]{:S(2)}, u32[]{:S(2)}) collective-permute-start(bf16[4,192,384]{2,1,0:T(8,128)(2,1)S(1)} %get-tuple-element.334), channel_id=1, source_target_pairs={{0,2},{1,3},{2,0},{3,1},{4,6},{5,7},{6,4},{7,5},{8,10},{9,11},{10,... | collective-permute-start | bytes 1769480 | tf_op jit(solution)/shard_map/ppermute | solution.py:591
  106.5 19.0 %collective-permute-start.15 = (bf16[832,384]{1,0:T(8,128)(2,1)S(1)}, bf16[832,384]{1,0:T(8,128)(2,1)S(1)}, u32[]{:S(2)}, u32[]{:S(2)}) collective-permute-start(bf16[832,384]{1,0:T(8,128)(2,1)S(1)} %get-tuple-element.339), channel_id=1, source_target_pairs={{0,8},{8,0},{16,24},{24,16},{1,9},{9,1},{17,25},{25,17},{2,10},{10... | collective-permute-start | bytes 1916936 | tf_op jit(solution)/shard_map/ppermute | solution.py:591
  108.1 17.4 %collective-permute-start.16 = (bf16[768,384]{1,0:T(8,128)(2,1)S(1)}, bf16[768,384]{1,0:T(8,128)(2,1)S(1)}, u32[]{:S(2)}, u32[]{:S(2)}) collective-permute-start(bf16[768,384]{1,0:T(8,128)(2,1)S(1)} %get-tuple-element.341), channel_id=1, source_target_pairs={{0,16},{8,24},{16,0},{24,8},{1,17},{9,25},{17,1},{25,9},{2,18},{10... | collective-permute-start | bytes 1769480 | tf_op jit(solution)/shard_map/ppermute | solution.py:591
  114.5 14.9 %collective-permute-start.17 = (bf16[2,192,384]{2,1,0:T(8,128)(2,1)S(1)}, bf16[2,192,384]{2,1,0:T(8,128)(2,1)S(1)}, u32[]{:S(2)}, u32[]{:S(2)}) collective-permute-start(bf16[2,192,384]{2,1,0:T(8,128)(2,1)S(1)} %get-tuple-element.347), channel_id=1, source_target_pairs={{0,4},{1,5},{2,6},{3,7},{4,0},{5,1},{6,2},{7,3},{8,12},{9,13},{10,... | collective-permute-start | bytes 884744 | tf_op jit(solution)/shard_map/ppermute | solution.py:591
  117.8 12.2 %collective-permute-start.18 = (bf16[2,192,384]{2,1,0:T(8,128)(2,1)S(1)}, bf16[2,192,384]{2,1,0:T(8,128)(2,1)S(1)}, u32[]{:S(2)}, u32[]{:S(2)}) collective-permute-start(bf16[2,192,384]{2,1,0:T(8,128)(2,1)S(1)} %get-tuple-element.352), channel_id=1, source_target_pairs={{0,8},{8,0},{16,24},{24,16},{1,9},{9,1},{17,25},{25,17},{2,10},{10... | collective-permute-start | bytes 884744 | tf_op jit(solution)/shard_map/ppermute | solution.py:591
  126.3 17.0 %collective-permute-start.21 = (bf16[416,384]{1,0:T(8,128)(2,1)S(1)}, bf16[416,384]{1,0:T(8,128)(2,1)S(1)}, u32[]{:S(2)}, u32[]{:S(2)}) collective-permute-start(bf16[416,384]{1,0:T(8,128)(2,1)S(1)} %get-tuple-element.361), channel_id=1, source_target_pairs={{0,16},{8,24},{16,0},{24,8},{1,17},{9,25},{17,1},{25,9},{2,18},{10... | collective-permute-start | bytes 958472 | tf_op jit(solution)/shard_map/ppermute | solution.py:591
  127.9 15.4 %collective-permute-start.22 = (bf16[384,384]{1,0:T(8,128)(2,1)S(1)}, bf16[384,384]{1,0:T(8,128)(2,1)S(1)}, u32[]{:S(2)}, u32[]{:S(2)}) collective-permute-start(bf16[384,384]{1,0:T(8,128)(2,1)S(1)} %get-tuple-element.362), channel_id=1, source_target_pairs={{0,8},{8,0},{16,24},{24,16},{1,9},{9,1},{17,25},{25,17},{2,10},{10... | collective-permute-start | bytes 884744 | tf_op jit(solution)/shard_map/ppermute | solution.py:591
  130.7 8.6 %collective-permute-start.20 = (bf16[1,192,384]{2,1,0:T(8,128)(2,1)S(1)}, bf16[1,192,384]{2,1,0:T(8,128)(2,1)S(1)}, u32[]{:S(2)}, u32[]{:S(2)}) collective-permute-start(bf16[1,192,384]{2,1,0:T(8,128)(2,1)S(1)} %get-tuple-element.359), channel_id=1, source_target_pairs={{0,4},{1,5},{2,6},{3,7},{4,0},{5,1},{6,2},{7,3},{8,12},{9,13},{10,... | collective-permute-start | bytes 442376 | tf_op jit(solution)/shard_map/ppermute | solution.py:591
  133.3 6.0 %collective-permute-start.19 = (bf16[1,192,384]{2,1,0:T(8,128)(2,1)S(1)}, bf16[1,192,384]{2,1,0:T(8,128)(2,1)S(1)}, u32[]{:S(2)}, u32[]{:S(2)}) collective-permute-start(bf16[1,192,384]{2,1,0:T(8,128)(2,1)S(1)} %get-tuple-element.357), channel_id=1, source_target_pairs={{0,8},{8,0},{16,24},{24,16},{1,9},{9,1},{17,25},{25,17},{2,10},{10... | collective-permute-start | bytes 442376 | tf_op jit(solution)/shard_map/ppermute | solution.py:591
  139.9 10.3 %collective-permute-start.27 = (bf16[384,384]{1,0:T(8,128)(2,1)S(1)}, bf16[384,384]{1,0:T(8,128)(2,1)S(1)}, u32[]{:S(2)}, u32[]{:S(2)}) collective-permute-start(bf16[384,384]{1,0:T(8,128)(2,1)S(1)} %bitcast.28), channel_id=1, source_target_pairs={{0,8},{8,0},{16,24},{24,16},{1,9},{9,1},{17,25},{25,17},{2,10},{10... | collective-permute-start | bytes 884744 | tf_op jit(solution)/shard_map/ppermute | solution.py:591
  141.5 8.7 %collective-permute-start.23 = (bf16[384,384]{1,0:T(8,128)(2,1)S(1)}, bf16[384,384]{1,0:T(8,128)(2,1)S(1)}, u32[]{:S(2)}, u32[]{:S(2)}) collective-permute-start(bf16[384,384]{1,0:T(8,128)(2,1)S(1)} %bitcast.29), channel_id=1, source_target_pairs={{0,16},{8,24},{16,0},{24,8},{1,17},{9,25},{17,1},{25,9},{2,18},{10... | collective-permute-start | bytes 884744 | tf_op jit(solution)/shard_map/ppermute | solution.py:591
  144.2 8.0 %collective-permute-start.24 = (bf16[208,384]{1,0:T(8,128)(2,1)S(1)}, bf16[208,384]{1,0:T(8,128)(2,1)S(1)}, u32[]{:S(2)}, u32[]{:S(2)}) collective-permute-start(bf16[208,384]{1,0:T(8,128)(2,1)S(1)} %get-tuple-element.371), channel_id=1, source_target_pairs={{0,2},{1,3},{2,0},{3,1},{4,6},{5,7},{6,4},{7,5},{8,10},{9,11},{10,... | collective-permute-start | bytes 479240 | tf_op jit(solution)/shard_map/ppermute | solution.py:591
  144.3 14.7 %collective-permute-start.25 = (bf16[208,384]{1,0:T(8,128)(2,1)S(1)}, bf16[208,384]{1,0:T(8,128)(2,1)S(1)}, u32[]{:S(2)}, u32[]{:S(2)}) collective-permute-start(bf16[208,384]{1,0:T(8,128)(2,1)S(1)} %get-tuple-element.372), channel_id=1, source_target_pairs={{0,4},{1,5},{2,6},{3,7},{4,0},{5,1},{6,2},{7,3},{8,12},{9,13},{10,... | collective-permute-start | bytes 479240 | tf_op jit(solution)/shard_map/ppermute | solution.py:591
  146.3 12.6 %collective-permute-start.26 = (bf16[208,384]{1,0:T(8,128)(2,1)S(1)}, bf16[208,384]{1,0:T(8,128)(2,1)S(1)}, u32[]{:S(2)}, u32[]{:S(2)}) collective-permute-start(bf16[208,384]{1,0:T(8,128)(2,1)S(1)} %get-tuple-element.373), channel_id=1, source_target_pairs={{0,6},{1,7},{2,4},{3,5},{4,2},{5,3},{6,0},{7,1},{8,14},{9,15},{10,... | collective-permute-start | bytes 479240 | tf_op jit(solution)/shard_map/ppermute | solution.py:591
  150.2 13.0 %collective-permute-start.28 = (bf16[384,384]{1,0:T(8,128)(2,1)S(1)}, bf16[384,384]{1,0:T(8,128)(2,1)S(1)}, u32[]{:S(2)}, u32[]{:S(2)}) collective-permute-start(bf16[384,384]{1,0:T(8,128)(2,1)S(1)} %collective-permute-done.27.refs_1_), channel_id=1, source_target_pairs={{0,16},{8,24},{16,0},{24,8},{1,17},{9,25},{17,1},{25,9},{2,18},{10... | collective-permute-start | bytes 884744 | tf_op jit(solution)/shard_map/ppermute | solution.py:591
  158.9 4.3 %copy-start.2 = (f32[96,9280]{1,0:T(8,128)S(1)}, f32[96,9280]{1,0:T(8,128)}, u32[]{:S(2)}) copy-start(f32[96,9280]{1,0:T(8,128)} %refs_8_.1) | copy-start | bytes 10690564
  158.9 4.3 %copy-start.3 = (f32[96,9280]{1,0:T(8,128)S(1)}, f32[96,9280]{1,0:T(8,128)}, u32[]{:S(2)}) copy-start(f32[96,9280]{1,0:T(8,128)} %refs_9_.1) | copy-start | bytes 10690564
  158.9 4.3 %copy-start.4 = (f32[96,9280]{1,0:T(8,128)S(1)}, f32[96,9280]{1,0:T(8,128)}, u32[]{:S(2)}) copy-start(f32[96,9280]{1,0:T(8,128)} %refs_10_.1) | copy-start | bytes 10690564
  158.9 5.1 %copy-start.5 = (f32[96,9280]{1,0:T(8,128)S(1)}, f32[96,9280]{1,0:T(8,128)}, u32[]{:S(2)}) copy-start(f32[96,9280]{1,0:T(8,128)} %refs_11_.1) | copy-start | bytes 10690564
  159.6 12.5 %copy-start.18 = (f32[96,13]{0,1:T(8,128)S(1)}, f32[96,13]{0,1:T(8,128)}, u32[]{:S(2)}) copy-start(f32[96,13]{0,1:T(8,128)} %param.19) | copy-start | bytes 14980
  159.6 12.5 %copy-start.19 = (f32[96,13]{0,1:T(8,128)S(1)}, f32[96,13]{0,1:T(8,128)}, u32[]{:S(2)}) copy-start(f32[96,13]{0,1:T(8,128)} %param.21) | copy-start | bytes 14980
  159.6 12.5 %copy-start.20 = (f32[96,13]{0,1:T(8,128)S(1)}, f32[96,13]{0,1:T(8,128)}, u32[]{:S(2)}) copy-start(f32[96,13]{0,1:T(8,128)} %param.23) | copy-start | bytes 14980
  159.6 12.5 %copy-start.21 = (f32[96,13]{0,1:T(8,128)S(1)}, f32[96,13]{0,1:T(8,128)}, u32[]{:S(2)}) copy-start(f32[96,13]{0,1:T(8,128)} %param.25) | copy-start | bytes 14980
  159.6 12.5 %collective-permute-start.31 = (bf16[208,384]{1,0:T(8,128)(2,1)S(1)}, bf16[208,384]{1,0:T(8,128)(2,1)S(1)}, u32[]{:S(2)}, u32[]{:S(2)}) collective-permute-start(bf16[208,384]{1,0:T(8,128)(2,1)S(1)} %tail_final.1.refs_0_), channel_id=1, source_target_pairs={{0,24},{8,16},{16,8},{24,0},{1,25},{9,17},{17,9},{25,1},{2,26},{10... | collective-permute-start | bytes 479240 | tf_op jit(solution)/shard_map/ppermute | solution.py:591
  160.0 12.1 %collective-permute-start.30 = (bf16[208,384]{1,0:T(8,128)(2,1)S(1)}, bf16[208,384]{1,0:T(8,128)(2,1)S(1)}, u32[]{:S(2)}, u32[]{:S(2)}) collective-permute-start(bf16[208,384]{1,0:T(8,128)(2,1)S(1)} %tail_final.1.refs_0_), channel_id=1, source_target_pairs={{0,16},{8,24},{16,0},{24,8},{1,17},{9,25},{17,1},{25,9},{2,18},{10... | collective-permute-start | bytes 479240 | tf_op jit(solution)/shard_map/ppermute | solution.py:591
  161.5 10.6 %collective-permute-start.29 = (bf16[208,384]{1,0:T(8,128)(2,1)S(1)}, bf16[208,384]{1,0:T(8,128)(2,1)S(1)}, u32[]{:S(2)}, u32[]{:S(2)}) collective-permute-start(bf16[208,384]{1,0:T(8,128)(2,1)S(1)} %tail_final.1.refs_0_), channel_id=1, source_target_pairs={{0,8},{8,0},{16,24},{24,16},{1,9},{9,1},{17,25},{25,17},{2,10},{10... | collective-permute-start | bytes 479240 | tf_op jit(solution)/shard_map/ppermute | solution.py:591

commit v5 on v4

--- a/solution.py
+++ b/solution.py
@@ -387,10 +387,14 @@
         dsk = feature_back(fk, dfk).astype(bf16)
         ds_q.append(dsq)
         ds_k.append(dsk)
-        dm_ref[head, :] = dot_nt(qt_ref[head, :], dsq) + dot_nt(kt_ref[head, :], dsk)
     maps = quad_maps(hedge_ref[...]).T.astype(bf16)
-    dq = dot_nn(maps, jnp.concatenate(ds_q, axis=0)).astype(bf16)
-    dk = dot_nn(maps, jnp.concatenate(ds_k, axis=0)).astype(bf16)
+    ds_q, ds_k = jnp.concatenate(ds_q, axis=0), jnp.concatenate(ds_k, axis=0)
+    dm = dot_nt(qt_ref[...], ds_q) + dot_nt(kt_ref[...], ds_k)
+    for h in range(QUAD):
+        head = slice(h * HD, (h + 1) * HD)
+        dm_ref[head, :] = dm[head, head]
+    dq = dot_nn(maps, ds_q).astype(bf16)
+    dk = dot_nn(maps, ds_k).astype(bf16)
     dp_ref[0] = dq
     dp_ref[1] = dk
     db_ref[...] = jnp.concatenate(

time: 178 us -> 177 us (level)
  transfers between devices with their start and end apart: 32 -> 32, of which waited for: 7 -> 8; matrix products, arithmetic and copies ran while one was open for 0% -> 0% of each run, Pallas kernels for 50% -> 49%
where the time goes in v5:
time: 177 us
  Pallas kernels  104 us (59%)
  starting transfers between devices  42 us (24%)
  waiting for transfers between devices  27 us (15%)
  between operations  2.02 us (1%)
    pallas_call x24, Pallas kernels, call(): pl.pallas_call(body, out_shape=tuple((pltpu.HBM(o.shape, o.dtype) if k in...  104 us
    ppermute x32, starting transfers between devices, swap(): return lax.ppermute(value, axis, [(i, i ^ bit) for i in range(size)])  42 us
    ppermute x32, waiting for transfers between devices, swap(): return lax.ppermute(value, axis, [(i, i ^ bit) for i in range(size)])  27 us
  transfers between devices with their start and end apart: 32, of which 8 were waited for; matrix products, arithmetic and copies ran while one was open for 0% of the time, Pallas kernels for 49%

profile of v5, /device:TPU:0, one launch (start us, length us, event | category | flops | bytes accessed | tf_op | source)
XLA Modules:
  0.0 176.7 jit_solution(11608505551914382800)
XLA Ops:
  1.3 0.1 compare_select_fusion.2.scal
  1.5 0.7 copy-done.12
  2.2 6.6 %keys.1 = (bf16[512,768]{1,0:T(8,128)(2,1)S(1)}, bf16[768,512]{1,0:T(8,128)(2,1)S(1)}, bf16[1536,512]{1,0:T(8,128)(2,1)S(1)}, bf16[768,512]{1,0:T(8,128)(2,1)S(1)}, bf16[864,128]{1,0:T(8,128)(2,1)S(1)}) custom-call(s32[16]{0:T(128)S(1)} %compare_select_fusion.2.scal, bf16[512,768]{1,0:T(8,128)(2,1)} %x_ref.3, bf16[9280,768]{1,0:T(8,128)(2,1)} %bitcast.44, ...), custom_call_target="tpu_custom_call" | custom-call | bytes 1024 | tf_op jit(solution)/shard_map/keys/pallas_call | solution.py:74
  8.8 4.0 %collective-permute-start.2 = (bf16[864,128]{1,0:T(8,128)(2,1)S(1)}, bf16[864,128]{1,0:T(8,128)(2,1)S(1)}, u32[]{:S(2)}, u32[]{:S(2)}) collective-permute-start(bf16[864,128]{1,0:T(8,128)(2,1)S(1)} %get-tuple-element.230), channel_id=1, source_target_pairs={{0,24},{8,16},{16,8},{24,0},{1,25},{9,17},{17,9},{25,1},{2,26},{10... | collective-permute-start | bytes 663560 | tf_op jit(solution)/shard_map/ppermute | solution.py:595
  12.8 0.5 collective-permute-start.1
  13.3 0.1 collective-permute-start
  13.4 5.7 %queries.1 = (bf16[4,384,512]{2,1,0:T(8,128)(2,1)S(1)}, bf16[4,384,512]{2,1,0:T(8,128)(2,1)S(1)}, bf16[768,512]{1,0:T(8,128)(2,1)S(1)}, bf16[1536,512]{1,0:T(8,128)(2,1)S(1)}) custom-call(s32[16]{0:T(128)S(1)} %compare_select_fusion.2.scal, bf16[512,768]{1,0:T(8,128)(2,1)S(1)} %get-tuple-element.220.h1_ref, bf16[512,768]{1,0:T(8,128)(2,1)} %g_ref.7, ...), custom_call_target="tpu_custom_call" | custom-call | bytes 1024 | tf_op jit(solution)/shard_map/queries/pallas_call | solution.py:74
  19.1 4.0 %local.1.refs_3_ = f32[864,512]{1,0:T(8,128)S(1)} custom-call(s32[16]{0:T(128)S(1)} %compare_select_fusion.2.scal, bf16[1536,512]{1,0:T(8,128)(2,1)S(1)} %get-tuple-element.226.fq_ref.refs_4_.refs_3_, bf16[1536,512]{1,0:T(8,128)(2,1)S(1)} %get-tuple-element.227.fk_ref.refs_4_, bf16[768,512]{1,0:T(8,128)(2,1)S(1)} %get-tuple-element.228.vt_ref.refs_5_), custom_call_target="tpu_custom_call" | custom-call | bytes 1024 | tf_op jit(solution)/shard_map/local/pallas_call | solution.py:74
  23.2 4.5 %after.1 = (f32[768,512]{1,0:T(8,128)S(1)}, f32[16,512]{1,0:T(8,128)S(1)}, f32[512,768]{1,0:T(8,128)S(1)}, bf16[512,768]{1,0:T(8,128)(2,1)S(1)}, bf16[864,128]{1...) custom-call(s32[16]{0:T(128)S(1)} %compare_select_fusion.2.scal, ...), custom_call_target="tpu_custom_call", output_to_operand_aliasing={{5}: (9, {}), {6}: (10, {})} | custom-call | bytes 1024 | tf_op jit(solution)/shard_map/after/pallas_call | solution.py:74
  27.9 8.9 %mlp.2 = (f32[512,768]{1,0:T(8,128)S(1)}, f32[512,768]{1,0:T(8,128)S(1)}, bf16[2,2,512,768]{3,2,1,0:T(8,128)(2,1)S(1)}, f32[1,1536]{1,0:T(1,128)S(1)}) custom-call(s32[16]{0:T(128)S(1)} %compare_select_fusion.2.scal, bf16[512,768]{1,0:T(8,128)(2,1)S(1)} %get-tuple-element.242.h2_ref, bf16[512,768]{1,0:T(8,128)(2,1)} %g_ref.7, bf16[9280,768]{1,0:T(8,128)(2,1)} %bitcast.50, ...), custom_call_target="tpu_custom_call" | custom-call | bytes 1024 | tf_op jit(solution)/shard_map/mlp/pallas_call | solution.py:74
  36.8 0.6 collective-permute-start.4
  37.3 9.1 %mlp.3 = (f32[512,768]{1,0:T(8,128)S(1)}, f32[512,768]{1,0:T(8,128)S(1)}, bf16[2,2,512,768]{3,2,1,0:T(8,128)(2,1)S(1)}, f32[1,1536]{1,0:T(1,128)S(1)}) custom-call(s32[16]{0:T(128)S(1)} %compare_select_fusion.2.scal, bf16[512,768]{1,0:T(8,128)(2,1)S(1)} %get-tuple-element.242.h2_ref, bf16[512,768]{1,0:T(8,128)(2,1)} %g_ref.7, bf16[9280,768]{1,0:T(8,128)(2,1)} %bitcast.52, ...), custom_call_target="tpu_custom_call" | custom-call | bytes 1024 | tf_op jit(solution)/shard_map/mlp/pallas_call | solution.py:74
  46.5 0.1 collective-permute-start.5
  46.6 4.7 %mlp_grads.2 = (bf16[8,192,384]{2,1,0:T(8,128)(2,1)}, bf16[8,192,384]{2,1,0:T(8,128)(2,1)}) custom-call(s32[16]{0:T(128)S(1)} %compare_select_fusion.2.scal, bf16[4,384,512]{2,1,0:T(8,128)(2,1)S(1)} %get-tuple-element.258.refs_0_.refs_6_.refs_2_, bf16[4,384,512]{2,1,0:T(8,128)(2,1)S(1)} %collective-permute-done.3.refs_1_.refs_7_.refs_3_, ...), custom_call_target="tpu_custom_call" | custom-call | bytes 1024 | tf_op jit(solution)/shard_map/mlp_grads/pallas_call | solution.py:74
  51.3 2.0 %collective-permute-start.9 = (bf16[8,192,384]{2,1,0:T(8,128)(2,1)}, bf16[8,192,384]{2,1,0:T(8,128)(2,1)}, u32[]{:S(2)}, u32[]{:S(2)}) collective-permute-start(bf16[8,192,384]{2,1,0:T(8,128)(2,1)} %get-tuple-element.311), channel_id=1, source_target_pairs={{0,2},{1,3},{2,0},{3,1},{4,6},{5,7},{6,4},{7,5},{8,10},{9,11},{10,... | collective-permute-start | bytes 3538952 | tf_op jit(solution)/shard_map/ppermute | solution.py:595
  53.3 6.7 %back.1 = (bf16[512,768]{1,0:T(8,128)(2,1)}, f32[512,768]{1,0:T(8,128)}, bf16[768,512]{1,0:T(8,128)(2,1)}, bf16[864,512]{1,0:T(8,128)(2,1)}, bf16[864,128]{1,0:T(8,128)(2,1)}, /*index=5*/f32[4,768]{1,0:T(4,128)S(1)}) custom-call(s32[16]{0:T(128)S(1)} %compare_select_fusion.2.scal, f32[512,768]{1,0:T(8,128)S(1)} %get-tuple-element.266.out_ref, ...), custom_call_target="tpu_custom_call" | custom-call | bytes 1024 | tf_op jit(solution)/shard_map/back/pallas_call | solution.py:74
  60.0 2.5 %collective-permute-start.8 = (bf16[864,128]{1,0:T(8,128)(2,1)}, bf16[864,128]{1,0:T(8,128)(2,1)}, u32[]{:S(2)}, u32[]{:S(2)}) collective-permute-start(bf16[864,128]{1,0:T(8,128)(2,1)} %get-tuple-element.284), channel_id=1, source_target_pairs={{0,24},{8,16},{16,8},{24,0},{1,25},{9,17},{17,9},{25,1},{2,26},{10... | collective-permute-start | bytes 663560 | tf_op jit(solution)/shard_map/ppermute | solution.py:595
  62.5 0.5 collective-permute-start.7
  63.0 0.5 collective-permute-start.6
  63.6 5.8 %mlp_grads.3 = (bf16[8,192,384]{2,1,0:T(8,128)(2,1)S(1)}, bf16[8,192,384]{2,1,0:T(8,128)(2,1)S(1)}) custom-call(s32[16]{0:T(128)S(1)} %compare_select_fusion.2.scal, bf16[4,384,512]{2,1,0:T(8,128)(2,1)S(1)} %get-tuple-element.258.refs_0_.refs_6_.refs_2_, bf16[4,384,512]{2,1,0:T(8,128)(2,1)S(1)} %collective-permute-done.3.refs_1_.refs_7_.refs_3_, ...), custom_call_target="tpu_custom_call" | custom-call | bytes 1024 | tf_op jit(solution)/shard_map/mlp_grads/pallas_call | solution.py:74
  69.4 1.6 collective-permute-start.10
  71.0 2.6 %collective-permute-done.7.refs_1_ = bf16[864,128]{1,0:T(8,128)(2,1)} collective-permute-done((bf16[864,128]{1,0:T(8,128)(2,1)}, bf16[864,128]{1,0:T(8,128)(2,1)}, u32[]{:S(2)}, u32[]{:S(2)}) %collective-permute-start.7) | collective-permute-done | bytes 221216 | tf_op jit(solution)/shard_map/ppermute | solution.py:595
  73.6 12.3 %attend_back.1 = (bf16[4,768,512]{2,1,0:T(8,128)(2,1)S(1)}, f32[768,64]{1,0:T(8,128)S(1)}, f32[768,3]{1,0:T(8,128)S(1)}) custom-call(s32[16]{0:T(128)S(1)} %compare_select_fusion.2.scal, bf16[864,128]{1,0:T(8,128)(2,1)} %collective-permute-done.6.refs_0_, bf16[864,128]{1,0:T(8,128)(2,1)} %collective-permute-done.7.refs_1_, ...), custom_call_target="tpu_custom_call" | custom-call | flops 1000000000 | bytes 1024 | tf_op jit(solution)/shard_map/attend_back/pallas_call | solution.py:74
  86.1 7.8 %input.1 = (bf16[512,768]{1,0:T(8,128)(2,1)}, f32[1,384,128]{2,1,0:T(8,128)S(1)}, f32[1,384,128]{2,1,0:T(8,128)S(1)}) custom-call(s32[16]{0:T(128)S(1)} %compare_select_fusion.2.scal, bf16[4,768,512]{2,1,0:T(8,128)(2,1)S(1)} %get-tuple-element.298.dp_ref, bf16[9280,768]{1,0:T(8,128)(2,1)} %bitcast.56, bf16[512,768]{1,0:T(8,128)(2,1)} %x_ref.3, ...), custom_call_target="tpu_custom_call" | custom-call | bytes 1024 | tf_op jit(solution)/shard_map/input/pallas_call | solution.py:74
  93.9 0.5 collective-permute-start.12
  94.4 2.1 %halve.6 = (bf16[4,192,384]{2,1,0:T(8,128)(2,1)S(1)}, bf16[4,192,384]{2,1,0:T(8,128)(2,1)S(1)}) custom-call(s32[16]{0:T(128)S(1)} %compare_select_fusion.2.scal, bf16[8,192,384]{2,1,0:T(8,128)(2,1)S(1)} %copy-done.22, bf16[8,192,384]{2,1,0:T(8,128)(2,1)} %collective-permute-done.9.recv_ref), custom_call_target="tpu_custom_call" | custom-call | flops 14000000000 | bytes 1024 | tf_op jit(solution)/shard_map/halve/pallas_call | solution.py:74
  96.5 1.6 collective-permute-start.13
  98.0 0.6 collective-permute-done.10.recv_ref
  98.7 0.8 halve.7
  99.5 0.9 collective-permute-start.14
  100.4 5.7 %tail_grads.1 = (bf16[832,384]{1,0:T(8,128)(2,1)S(1)}, bf16[768,384]{1,0:T(8,128)(2,1)S(1)}, bf16[768,384]{1,0:T(8,128)(2,1)S(1)}, bf16[768,384]{1,0:T(8,128)(2,1)S(1)}, f32[64,384]{1,0:T(8,128)S(1)}) custom-call(s32[16]{0:T(128)S(1)} %compare_select_fusion.2.scal, bf16[4,384,512]{2,1,0:T(8,128)(2,1)S(1)} %get-tuple-element.258.refs_0_.refs_6_.refs_2_, ...), custom_call_target="tpu_custom_call" | custom-call | flops 4000000000 | bytes 1024 | tf_op jit(solution)/shard_map/tail_grads/pallas_call | solution.py:74
  106.1 1.6 collective-permute-start.15
  107.6 0.8 collective-permute-start.16
  108.4 4.3 %collective-permute-done.13.recv_ref = bf16[4,192,384]{2,1,0:T(8,128)(2,1)S(1)} collective-permute-done((bf16[4,192,384]{2,1,0:T(8,128)(2,1)S(1)}, bf16[4,192,384]{2,1,0:T(8,128)(2,1)S(1)}, u32[]{:S(2)}, u32[]{:S(2)}) %collective-permute-start.13) | collective-permute-done | bytes 589856 | tf_op jit(solution)/shard_map/ppermute | solution.py:595
  112.7 0.7 halve.8
  113.4 2.7 %collective-permute-start.17 = (bf16[2,192,384]{2,1,0:T(8,128)(2,1)S(1)}, bf16[2,192,384]{2,1,0:T(8,128)(2,1)S(1)}, u32[]{:S(2)}, u32[]{:S(2)}) collective-permute-start(bf16[2,192,384]{2,1,0:T(8,128)(2,1)S(1)} %get-tuple-element.347), channel_id=1, source_target_pairs={{0,4},{1,5},{2,6},{3,7},{4,0},{5,1},{6,2},{7,3},{8,12},{9,13},{10,... | collective-permute-start | bytes 884744 | tf_op jit(solution)/shard_map/ppermute | solution.py:595
  116.1 0.7 halve.9
  116.8 1.5 collective-permute-start.18
  118.3 6.1 %collective-permute-done.16.recv_b = bf16[768,384]{1,0:T(8,128)(2,1)S(1)} collective-permute-done((bf16[768,384]{1,0:T(8,128)(2,1)S(1)}, bf16[768,384]{1,0:T(8,128)(2,1)S(1)}, u32[]{:S(2)}, u32[]{:S(2)}) %collective-permute-start.16) | collective-permute-done | bytes 589856 | tf_op jit(solution)/shard_map/ppermute | solution.py:595
  124.4 0.8 tail_one.1
  125.2 1.6 collective-permute-start.21
  126.8 1.5 collective-permute-start.22
  128.4 0.6 halve.10
  129.0 0.6 halve.11
  129.6 2.6 %collective-permute-start.20 = (bf16[1,192,384]{2,1,0:T(8,128)(2,1)S(1)}, bf16[1,192,384]{2,1,0:T(8,128)(2,1)S(1)}, u32[]{:S(2)}, u32[]{:S(2)}) collective-permute-start(bf16[1,192,384]{2,1,0:T(8,128)(2,1)S(1)} %get-tuple-element.359), channel_id=1, source_target_pairs={{0,4},{1,5},{2,6},{3,7},{4,0},{5,1},{6,2},{7,3},{8,12},{9,13},{10,... | collective-permute-start | bytes 442376 | tf_op jit(solution)/shard_map/ppermute | solution.py:595
  132.2 1.1 collective-permute-start.19
  133.3 4.8 %collective-permute-done.20.refs_3_ = bf16[1,192,384]{2,1,0:T(8,128)(2,1)S(1)} collective-permute-done((bf16[1,192,384]{2,1,0:T(8,128)(2,1)S(1)}, bf16[1,192,384]{2,1,0:T(8,128)(2,1)S(1)}, u32[]{:S(2)}, u32[]{:S(2)}) %collective-permute-start.20) | collective-permute-done | bytes 147488 | tf_op jit(solution)/shard_map/ppermute | solution.py:595
  138.1 0.6 final.1
  138.7 1.4 collective-permute-start.27
  140.1 2.1 %collective-permute-start.23 = (bf16[384,384]{1,0:T(8,128)(2,1)S(1)}, bf16[384,384]{1,0:T(8,128)(2,1)S(1)}, u32[]{:S(2)}, u32[]{:S(2)}) collective-permute-start(bf16[384,384]{1,0:T(8,128)(2,1)S(1)} %bitcast.29), channel_id=1, source_target_pairs={{0,16},{8,24},{16,0},{24,8},{1,17},{9,25},{17,1},{25,9},{2,18},{10... | collective-permute-start | bytes 884744 | tf_op jit(solution)/shard_map/ppermute | solution.py:595
  142.3 0.9 tail_two.1
  143.2 2.0 %collective-permute-start.25 = (bf16[208,384]{1,0:T(8,128)(2,1)S(1)}, bf16[208,384]{1,0:T(8,128)(2,1)S(1)}, u32[]{:S(2)}, u32[]{:S(2)}) collective-permute-start(bf16[208,384]{1,0:T(8,128)(2,1)S(1)} %get-tuple-element.372), channel_id=1, source_target_pairs={{0,4},{1,5},{2,6},{3,7},{4,0},{5,1},{6,2},{7,3},{8,12},{9,13},{10,... | collective-permute-start | bytes 479240 | tf_op jit(solution)/shard_map/ppermute | solution.py:595
  145.2 2.4 %collective-permute-start.26 = (bf16[208,384]{1,0:T(8,128)(2,1)S(1)}, bf16[208,384]{1,0:T(8,128)(2,1)S(1)}, u32[]{:S(2)}, u32[]{:S(2)}) collective-permute-start(bf16[208,384]{1,0:T(8,128)(2,1)S(1)} %get-tuple-element.373), channel_id=1, source_target_pairs={{0,6},{1,7},{2,4},{3,5},{4,2},{5,3},{6,0},{7,1},{8,14},{9,15},{10,... | collective-permute-start | bytes 479240 | tf_op jit(solution)/shard_map/ppermute | solution.py:595
  147.6 1.5 collective-permute-done.23.refs_2_
  149.2 1.7 collective-permute-start.28
  150.9 0.3 collective-permute-done.24.refs_1_
  151.2 6.7 %collective-permute-done.25.refs_2_ = bf16[208,384]{1,0:T(8,128)(2,1)S(1)} collective-permute-done((bf16[208,384]{1,0:T(8,128)(2,1)S(1)}, bf16[208,384]{1,0:T(8,128)(2,1)S(1)}, u32[]{:S(2)}, u32[]{:S(2)}) %collective-permute-start.25) | collective-permute-done | bytes 159776 | tf_op jit(solution)/shard_map/ppermute | solution.py:595
  157.9 0.6 tail_final.1.refs_0_
  158.6 0.3 collective-permute-start.31
  158.9 1.8 collective-permute-start.30
  160.6 1.5 collective-permute-start.29
  162.2 0.9 copy-done.5
  163.0 8.0 %adam.2 = (f32[96,9280]{1,0:T(8,128)}, f32[96,9280]{1,0:T(8,128)}, f32[96,9280]{1,0:T(8,128)}, f32[96,9280]{1,0:T(8,128)}, f32[96,9280]{1,0:T(8,128)}, /*index=5*/bf16[96,9280]{1,0:T(8,128)(2,1)}) custom-call(s32[16]{0:T(128)S(1)} %compare_select_fusion.2.scal, bf16[384,384]{1,0:T(8,128)(2,1)S(1)} %bitcast.30, ...), custom_call_target="tpu_custom_call" | custom-call | bytes 1024 | tf_op jit(solution)/shard_map/adam/pallas_call | solution.py:74
  171.1 5.4 %adam.3 = (f32[96,9280]{1,0:T(8,128)}, f32[96,9280]{1,0:T(8,128)}, f32[96,9280]{1,0:T(8,128)}, f32[96,9280]{1,0:T(8,128)}, f32[96,9280]{1,0:T(8,128)}, /*index=5...) custom-call(s32[16]{0:T(128)S(1)} %compare_select_fusion.2.scal, ...), custom_call_target="tpu_custom_call", output_to_operand_aliasing={{0}: (13, {}), {1}: (14, {}), {2}: (15, {}), {3}: (16, {}),... | custom-call | bytes 1024 | tf_op jit(solution)/shard_map/adam/pallas_call | solution.py:74
  (77 shorter events, 0.5 us)
Async XLA Ops:
  1.5 0.7 copy-start.12
  8.8 10.3 %copy-start.14 = (bf16[768,512]{1,0:T(8,128)(2,1)}, bf16[768,512]{1,0:T(8,128)(2,1)S(1)}, u32[]{:S(2)}) copy-start(bf16[768,512]{1,0:T(8,128)(2,1)S(1)} %get-tuple-element.292.refs_9_) | copy-start | bytes 2359300
  8.8 10.3 %copy-start.7 = (bf16[1536,512]{1,0:T(8,128)(2,1)}, bf16[1536,512]{1,0:T(8,128)(2,1)S(1)}, u32[]{:S(2)}) copy-start(bf16[1536,512]{1,0:T(8,128)(2,1)S(1)} %get-tuple-element.227.fk_ref.refs_4_) | copy-start | bytes 4718596
  8.8 10.3 %copy-start.9 = (bf16[768,512]{1,0:T(8,128)(2,1)}, bf16[768,512]{1,0:T(8,128)(2,1)S(1)}, u32[]{:S(2)}) copy-start(bf16[768,512]{1,0:T(8,128)(2,1)S(1)} %get-tuple-element.228.vt_ref.refs_5_) | copy-start | bytes 2359300
  8.8 14.4 %collective-permute-start.2 = (bf16[864,128]{1,0:T(8,128)(2,1)S(1)}, bf16[864,128]{1,0:T(8,128)(2,1)S(1)}, u32[]{:S(2)}, u32[]{:S(2)}) collective-permute-start(bf16[864,128]{1,0:T(8,128)(2,1)S(1)} %get-tuple-element.230), channel_id=1, source_target_pairs={{0,24},{8,16},{16,8},{24,0},{1,25},{9,17},{17,9},{25,1},{2,26},{10... | collective-permute-start | bytes 663560 | tf_op jit(solution)/shard_map/ppermute | solution.py:595
  12.8 10.4 %collective-permute-start.1 = (bf16[864,128]{1,0:T(8,128)(2,1)S(1)}, bf16[864,128]{1,0:T(8,128)(2,1)S(1)}, u32[]{:S(2)}, u32[]{:S(2)}) collective-permute-start(bf16[864,128]{1,0:T(8,128)(2,1)S(1)} %get-tuple-element.230), channel_id=1, source_target_pairs={{0,16},{8,24},{16,0},{24,8},{1,17},{9,25},{17,1},{25,9},{2,18},{10... | collective-permute-start | bytes 663560 | tf_op jit(solution)/shard_map/ppermute | solution.py:595
  13.3 9.9 %collective-permute-start = (bf16[864,128]{1,0:T(8,128)(2,1)S(1)}, bf16[864,128]{1,0:T(8,128)(2,1)S(1)}, u32[]{:S(2)}, u32[]{:S(2)}) collective-permute-start(bf16[864,128]{1,0:T(8,128)(2,1)S(1)} %get-tuple-element.230), channel_id=1, source_target_pairs={{0,8},{8,0},{16,24},{24,16},{1,9},{9,1},{17,25},{25,17},{2,10},{10... | collective-permute-start | bytes 663560 | tf_op jit(solution)/shard_map/ppermute | solution.py:595
  19.1 4.1 %copy-start.16 = (bf16[768,512]{1,0:T(8,128)(2,1)}, bf16[768,512]{1,0:T(8,128)(2,1)S(1)}, u32[]{:S(2)}) copy-start(bf16[768,512]{1,0:T(8,128)(2,1)S(1)} %get-tuple-element.291.refs_8_) | copy-start | bytes 2359300
  19.1 34.2 %copy-start = (bf16[1536,512]{1,0:T(8,128)(2,1)}, bf16[1536,512]{1,0:T(8,128)(2,1)S(1)}, u32[]{:S(2)}) copy-start(bf16[1536,512]{1,0:T(8,128)(2,1)S(1)} %get-tuple-element.226.fq_ref.refs_4_.refs_3_) | copy-start | bytes 4718596
  27.8 9.6 %collective-permute-start.3 = (bf16[4,384,512]{2,1,0:T(8,128)(2,1)S(1)}, bf16[4,384,512]{2,1,0:T(8,128)(2,1)S(1)}, u32[]{:S(2)}, u32[]{:S(2)}) collective-permute-start(bf16[4,384,512]{2,1,0:T(8,128)(2,1)S(1)} %get-tuple-element.249), channel_id=1, source_target_pairs={{0,1},{1,0},{2,3},{3,2},{4,5},{5,4},{6,7},{7,6},{8,9},{9,8},{10,11... | collective-permute-start | bytes 4718600 | tf_op jit(solution)/shard_map/ppermute | solution.py:595
  36.8 9.8 %collective-permute-start.4 = (bf16[2,2,512,768]{3,2,1,0:T(8,128)(2,1)S(1)}, bf16[2,2,512,768]{3,2,1,0:T(8,128)(2,1)S(1)}, u32[]{:S(2)}, u32[]{:S(2)}) collective-permute-start(bf16[2,2,512,768]{3,2,1,0:T(8,128)(2,1)S(1)} %get-tuple-element.260.refs_2_.refs_4_), channel_id=1, source_target_pairs={{0,1},{1,0},{2,3},{3,2},{4,5},{5,4},{6,7},{7,6},{8,9},{9,8},{10,11... | collective-permute-start | bytes 9437192 | tf_op jit(solution)/shard_map/ppermute | solution.py:595
  46.5 4.9 %copy-start.6 = (bf16[2,2,512,768]{3,2,1,0:T(8,128)(2,1)}, bf16[2,2,512,768]{3,2,1,0:T(8,128)(2,1)S(1)}, u32[]{:S(2)}) copy-start(bf16[2,2,512,768]{3,2,1,0:T(8,128)(2,1)S(1)} %get-tuple-element.279.refs_2_.refs_4_) | copy-start | bytes 9437188
  46.5 6.8 %copy-start.13 = (bf16[768,13]{0,1:T(8,128)(2,1)S(1)}, bf16[768,13]{0,1:T(8,128)(2,1)}, u32[]{:S(2)}) copy-start(bf16[768,13]{0,1:T(8,128)(2,1)} %param.17) | copy-start | bytes 59908
  46.5 6.8 %collective-permute-start.5 = (bf16[2,2,512,768]{3,2,1,0:T(8,128)(2,1)S(1)}, bf16[2,2,512,768]{3,2,1,0:T(8,128)(2,1)S(1)}, u32[]{:S(2)}, u32[]{:S(2)}) collective-permute-start(bf16[2,2,512,768]{3,2,1,0:T(8,128)(2,1)S(1)} %get-tuple-element.279.refs_2_.refs_4_), channel_id=1, source_target_pairs={{0,1},{1,0},{2,3},{3,2},{4,5},{5,4},{6,7},{7,6},{8,9},{9,8},{10,11... | collective-permute-start | bytes 9437192 | tf_op jit(solution)/shard_map/ppermute | solution.py:595
  51.3 43.0 %collective-permute-start.9 = (bf16[8,192,384]{2,1,0:T(8,128)(2,1)}, bf16[8,192,384]{2,1,0:T(8,128)(2,1)}, u32[]{:S(2)}, u32[]{:S(2)}) collective-permute-start(bf16[8,192,384]{2,1,0:T(8,128)(2,1)} %get-tuple-element.311), channel_id=1, source_target_pairs={{0,2},{1,3},{2,0},{3,1},{4,6},{5,7},{6,4},{7,5},{8,10},{9,11},{10,... | collective-permute-start | bytes 3538952 | tf_op jit(solution)/shard_map/ppermute | solution.py:595
  53.3 6.7 %copy-start.23 = (bf16[2,2,512,768]{3,2,1,0:T(8,128)(2,1)}, bf16[2,2,512,768]{3,2,1,0:T(8,128)(2,1)S(1)}, u32[]{:S(2)}) copy-start(bf16[2,2,512,768]{3,2,1,0:T(8,128)(2,1)S(1)} %collective-permute-done.5.refs_3_.refs_5_) | copy-start | bytes 9437188
  60.0 11.0 %collective-permute-start.8 = (bf16[864,128]{1,0:T(8,128)(2,1)}, bf16[864,128]{1,0:T(8,128)(2,1)}, u32[]{:S(2)}, u32[]{:S(2)}) collective-permute-start(bf16[864,128]{1,0:T(8,128)(2,1)} %get-tuple-element.284), channel_id=1, source_target_pairs={{0,24},{8,16},{16,8},{24,0},{1,25},{9,17},{17,9},{25,1},{2,26},{10... | collective-permute-start | bytes 663560 | tf_op jit(solution)/shard_map/ppermute | solution.py:595
  62.5 11.1 %collective-permute-start.7 = (bf16[864,128]{1,0:T(8,128)(2,1)}, bf16[864,128]{1,0:T(8,128)(2,1)}, u32[]{:S(2)}, u32[]{:S(2)}) collective-permute-start(bf16[864,128]{1,0:T(8,128)(2,1)} %get-tuple-element.284), channel_id=1, source_target_pairs={{0,16},{8,24},{16,0},{24,8},{1,17},{9,25},{17,1},{25,9},{2,18},{10... | collective-permute-start | bytes 663560 | tf_op jit(solution)/shard_map/ppermute | solution.py:595
  63.0 10.6 %collective-permute-start.6 = (bf16[864,128]{1,0:T(8,128)(2,1)}, bf16[864,128]{1,0:T(8,128)(2,1)}, u32[]{:S(2)}, u32[]{:S(2)}) collective-permute-start(bf16[864,128]{1,0:T(8,128)(2,1)} %get-tuple-element.284), channel_id=1, source_target_pairs={{0,8},{8,0},{16,24},{24,16},{1,9},{9,1},{17,25},{25,17},{2,10},{10... | collective-permute-start | bytes 663560 | tf_op jit(solution)/shard_map/ppermute | solution.py:595
  63.5 10.1 %copy-start.1 = (bf16[1536,512]{1,0:T(8,128)(2,1)S(1)}, bf16[1536,512]{1,0:T(8,128)(2,1)}, u32[]{:S(2)}) copy-start(bf16[1536,512]{1,0:T(8,128)(2,1)} %copy-done) | copy-start | bytes 4718596
  63.6 10.0 %copy-start.8 = (bf16[1536,512]{1,0:T(8,128)(2,1)S(1)}, bf16[1536,512]{1,0:T(8,128)(2,1)}, u32[]{:S(2)}) copy-start(bf16[1536,512]{1,0:T(8,128)(2,1)} %copy-done.7) | copy-start | bytes 4718596
  63.6 10.0 %copy-start.10 = (bf16[768,512]{1,0:T(8,128)(2,1)S(1)}, bf16[768,512]{1,0:T(8,128)(2,1)}, u32[]{:S(2)}) copy-start(bf16[768,512]{1,0:T(8,128)(2,1)} %copy-done.9) | copy-start | bytes 2359300
  63.6 10.0 %copy-start.15 = (bf16[768,512]{1,0:T(8,128)(2,1)S(1)}, bf16[768,512]{1,0:T(8,128)(2,1)}, u32[]{:S(2)}) copy-start(bf16[768,512]{1,0:T(8,128)(2,1)} %copy-done.14) | copy-start | bytes 2359300
  63.6 10.0 %copy-start.17 = (bf16[768,512]{1,0:T(8,128)(2,1)S(1)}, bf16[768,512]{1,0:T(8,128)(2,1)}, u32[]{:S(2)}) copy-start(bf16[768,512]{1,0:T(8,128)(2,1)} %copy-done.16) | copy-start | bytes 2359300
  69.4 16.6 %copy-start.11 = (f32[512,768]{1,0:T(8,128)S(1)}, f32[512,768]{1,0:T(8,128)}, u32[]{:S(2)}) copy-start(f32[512,768]{1,0:T(8,128)} %get-tuple-element.299.dr_ref) | copy-start | bytes 4718596
  69.4 29.2 %collective-permute-start.10 = (bf16[8,192,384]{2,1,0:T(8,128)(2,1)S(1)}, bf16[8,192,384]{2,1,0:T(8,128)(2,1)S(1)}, u32[]{:S(2)}, u32[]{:S(2)}) collective-permute-start(bf16[8,192,384]{2,1,0:T(8,128)(2,1)S(1)} %get-tuple-element.316), channel_id=1, source_target_pairs={{0,16},{8,24},{16,0},{24,8},{1,17},{9,25},{17,1},{25,9},{2,18},{10... | collective-permute-start | bytes 3538952 | tf_op jit(solution)/shard_map/ppermute | solution.py:595
  86.0 8.4 %copy-start.22 = (bf16[8,192,384]{2,1,0:T(8,128)(2,1)S(1)}, bf16[8,192,384]{2,1,0:T(8,128)(2,1)}, u32[]{:S(2)}) copy-start(bf16[8,192,384]{2,1,0:T(8,128)(2,1)} %get-tuple-element.310.keep_ref) | copy-start | bytes 3538948
  86.0 14.4 %collective-permute-start.11 = (bf16[4,768,512]{2,1,0:T(8,128)(2,1)S(1)}, bf16[4,768,512]{2,1,0:T(8,128)(2,1)S(1)}, u32[]{:S(2)}, u32[]{:S(2)}) collective-permute-start(bf16[4,768,512]{2,1,0:T(8,128)(2,1)S(1)} %get-tuple-element.298.dp_ref), channel_id=1, source_target_pairs={{0,1},{1,0},{2,3},{3,2},{4,5},{5,4},{6,7},{7,6},{8,9},{9,8},{10,11... | collective-permute-start | bytes 9437192 | tf_op jit(solution)/shard_map/ppermute | solution.py:595
  93.9 6.5 %collective-permute-start.12 = (f32[1,384,128]{2,1,0:T(8,128)S(1)}, f32[1,384,128]{2,1,0:T(8,128)S(1)}, u32[]{:S(2)}, u32[]{:S(2)}) collective-permute-start(f32[1,384,128]{2,1,0:T(8,128)S(1)} %get-tuple-element.321), channel_id=1, source_target_pairs={{0,1},{1,0},{2,3},{3,2},{4,5},{5,4},{6,7},{7,6},{8,9},{9,8},{10,11... | collective-permute-start | bytes 589832 | tf_op jit(solution)/shard_map/ppermute | solution.py:595
  96.5 16.3 %collective-permute-start.13 = (bf16[4,192,384]{2,1,0:T(8,128)(2,1)S(1)}, bf16[4,192,384]{2,1,0:T(8,128)(2,1)S(1)}, u32[]{:S(2)}, u32[]{:S(2)}) collective-permute-start(bf16[4,192,384]{2,1,0:T(8,128)(2,1)S(1)} %get-tuple-element.329), channel_id=1, source_target_pairs={{0,16},{8,24},{16,0},{24,8},{1,17},{9,25},{17,1},{25,9},{2,18},{10... | collective-permute-start | bytes 1769480 | tf_op jit(solution)/shard_map/ppermute | solution.py:595
  99.5 16.6 %collective-permute-start.14 = (bf16[4,192,384]{2,1,0:T(8,128)(2,1)S(1)}, bf16[4,192,384]{2,1,0:T(8,128)(2,1)S(1)}, u32[]{:S(2)}, u32[]{:S(2)}) collective-permute-start(bf16[4,192,384]{2,1,0:T(8,128)(2,1)S(1)} %get-tuple-element.334), channel_id=1, source_target_pairs={{0,2},{1,3},{2,0},{3,1},{4,6},{5,7},{6,4},{7,5},{8,10},{9,11},{10,... | collective-permute-start | bytes 1769480 | tf_op jit(solution)/shard_map/ppermute | solution.py:595
  106.1 18.4 %collective-permute-start.15 = (bf16[832,384]{1,0:T(8,128)(2,1)S(1)}, bf16[832,384]{1,0:T(8,128)(2,1)S(1)}, u32[]{:S(2)}, u32[]{:S(2)}) collective-permute-start(bf16[832,384]{1,0:T(8,128)(2,1)S(1)} %get-tuple-element.339), channel_id=1, source_target_pairs={{0,8},{8,0},{16,24},{24,16},{1,9},{9,1},{17,25},{25,17},{2,10},{10... | collective-permute-start | bytes 1916936 | tf_op jit(solution)/shard_map/ppermute | solution.py:595
  107.6 16.8 %collective-permute-start.16 = (bf16[768,384]{1,0:T(8,128)(2,1)S(1)}, bf16[768,384]{1,0:T(8,128)(2,1)S(1)}, u32[]{:S(2)}, u32[]{:S(2)}) collective-permute-start(bf16[768,384]{1,0:T(8,128)(2,1)S(1)} %get-tuple-element.341), channel_id=1, source_target_pairs={{0,16},{8,24},{16,0},{24,8},{1,17},{9,25},{17,1},{25,9},{2,18},{10... | collective-permute-start | bytes 1769480 | tf_op jit(solution)/shard_map/ppermute | solution.py:595
  113.4 14.9 %collective-permute-start.17 = (bf16[2,192,384]{2,1,0:T(8,128)(2,1)S(1)}, bf16[2,192,384]{2,1,0:T(8,128)(2,1)S(1)}, u32[]{:S(2)}, u32[]{:S(2)}) collective-permute-start(bf16[2,192,384]{2,1,0:T(8,128)(2,1)S(1)} %get-tuple-element.347), channel_id=1, source_target_pairs={{0,4},{1,5},{2,6},{3,7},{4,0},{5,1},{6,2},{7,3},{8,12},{9,13},{10,... | collective-permute-start | bytes 884744 | tf_op jit(solution)/shard_map/ppermute | solution.py:595
  116.8 12.2 %collective-permute-start.18 = (bf16[2,192,384]{2,1,0:T(8,128)(2,1)S(1)}, bf16[2,192,384]{2,1,0:T(8,128)(2,1)S(1)}, u32[]{:S(2)}, u32[]{:S(2)}) collective-permute-start(bf16[2,192,384]{2,1,0:T(8,128)(2,1)S(1)} %get-tuple-element.352), channel_id=1, source_target_pairs={{0,8},{8,0},{16,24},{24,16},{1,9},{9,1},{17,25},{25,17},{2,10},{10... | collective-permute-start | bytes 884744 | tf_op jit(solution)/shard_map/ppermute | solution.py:595
  125.2 17.0 %collective-permute-start.21 = (bf16[416,384]{1,0:T(8,128)(2,1)S(1)}, bf16[416,384]{1,0:T(8,128)(2,1)S(1)}, u32[]{:S(2)}, u32[]{:S(2)}) collective-permute-start(bf16[416,384]{1,0:T(8,128)(2,1)S(1)} %get-tuple-element.361), channel_id=1, source_target_pairs={{0,16},{8,24},{16,0},{24,8},{1,17},{9,25},{17,1},{25,9},{2,18},{10... | collective-permute-start | bytes 958472 | tf_op jit(solution)/shard_map/ppermute | solution.py:595
  126.8 15.4 %collective-permute-start.22 = (bf16[384,384]{1,0:T(8,128)(2,1)S(1)}, bf16[384,384]{1,0:T(8,128)(2,1)S(1)}, u32[]{:S(2)}, u32[]{:S(2)}) collective-permute-start(bf16[384,384]{1,0:T(8,128)(2,1)S(1)} %get-tuple-element.362), channel_id=1, source_target_pairs={{0,8},{8,0},{16,24},{24,16},{1,9},{9,1},{17,25},{25,17},{2,10},{10... | collective-permute-start | bytes 884744 | tf_op jit(solution)/shard_map/ppermute | solution.py:595
  129.6 8.5 %collective-permute-start.20 = (bf16[1,192,384]{2,1,0:T(8,128)(2,1)S(1)}, bf16[1,192,384]{2,1,0:T(8,128)(2,1)S(1)}, u32[]{:S(2)}, u32[]{:S(2)}) collective-permute-start(bf16[1,192,384]{2,1,0:T(8,128)(2,1)S(1)} %get-tuple-element.359), channel_id=1, source_target_pairs={{0,4},{1,5},{2,6},{3,7},{4,0},{5,1},{6,2},{7,3},{8,12},{9,13},{10,... | collective-permute-start | bytes 442376 | tf_op jit(solution)/shard_map/ppermute | solution.py:595
  132.2 5.9 %collective-permute-start.19 = (bf16[1,192,384]{2,1,0:T(8,128)(2,1)S(1)}, bf16[1,192,384]{2,1,0:T(8,128)(2,1)S(1)}, u32[]{:S(2)}, u32[]{:S(2)}) collective-permute-start(bf16[1,192,384]{2,1,0:T(8,128)(2,1)S(1)} %get-tuple-element.357), channel_id=1, source_target_pairs={{0,8},{8,0},{16,24},{24,16},{1,9},{9,1},{17,25},{25,17},{2,10},{10... | collective-permute-start | bytes 442376 | tf_op jit(solution)/shard_map/ppermute | solution.py:595
  138.7 10.4 %collective-permute-start.27 = (bf16[384,384]{1,0:T(8,128)(2,1)S(1)}, bf16[384,384]{1,0:T(8,128)(2,1)S(1)}, u32[]{:S(2)}, u32[]{:S(2)}) collective-permute-start(bf16[384,384]{1,0:T(8,128)(2,1)S(1)} %bitcast.28), channel_id=1, source_target_pairs={{0,8},{8,0},{16,24},{24,16},{1,9},{9,1},{17,25},{25,17},{2,10},{10... | collective-permute-start | bytes 884744 | tf_op jit(solution)/shard_map/ppermute | solution.py:595
  140.1 9.0 %collective-permute-start.23 = (bf16[384,384]{1,0:T(8,128)(2,1)S(1)}, bf16[384,384]{1,0:T(8,128)(2,1)S(1)}, u32[]{:S(2)}, u32[]{:S(2)}) collective-permute-start(bf16[384,384]{1,0:T(8,128)(2,1)S(1)} %bitcast.29), channel_id=1, source_target_pairs={{0,16},{8,24},{16,0},{24,8},{1,17},{9,25},{17,1},{25,9},{2,18},{10... | collective-permute-start | bytes 884744 | tf_op jit(solution)/shard_map/ppermute | solution.py:595
  143.2 8.0 %collective-permute-start.24 = (bf16[208,384]{1,0:T(8,128)(2,1)S(1)}, bf16[208,384]{1,0:T(8,128)(2,1)S(1)}, u32[]{:S(2)}, u32[]{:S(2)}) collective-permute-start(bf16[208,384]{1,0:T(8,128)(2,1)S(1)} %get-tuple-element.371), channel_id=1, source_target_pairs={{0,2},{1,3},{2,0},{3,1},{4,6},{5,7},{6,4},{7,5},{8,10},{9,11},{10,... | collective-permute-start | bytes 479240 | tf_op jit(solution)/shard_map/ppermute | solution.py:595
  143.2 14.7 %collective-permute-start.25 = (bf16[208,384]{1,0:T(8,128)(2,1)S(1)}, bf16[208,384]{1,0:T(8,128)(2,1)S(1)}, u32[]{:S(2)}, u32[]{:S(2)}) collective-permute-start(bf16[208,384]{1,0:T(8,128)(2,1)S(1)} %get-tuple-element.372), channel_id=1, source_target_pairs={{0,4},{1,5},{2,6},{3,7},{4,0},{5,1},{6,2},{7,3},{8,12},{9,13},{10,... | collective-permute-start | bytes 479240 | tf_op jit(solution)/shard_map/ppermute | solution.py:595
  145.2 12.6 %collective-permute-start.26 = (bf16[208,384]{1,0:T(8,128)(2,1)S(1)}, bf16[208,384]{1,0:T(8,128)(2,1)S(1)}, u32[]{:S(2)}, u32[]{:S(2)}) collective-permute-start(bf16[208,384]{1,0:T(8,128)(2,1)S(1)} %get-tuple-element.373), channel_id=1, source_target_pairs={{0,6},{1,7},{2,4},{3,5},{4,2},{5,3},{6,0},{7,1},{8,14},{9,15},{10,... | collective-permute-start | bytes 479240 | tf_op jit(solution)/shard_map/ppermute | solution.py:595
  149.2 13.0 %collective-permute-start.28 = (bf16[384,384]{1,0:T(8,128)(2,1)S(1)}, bf16[384,384]{1,0:T(8,128)(2,1)S(1)}, u32[]{:S(2)}, u32[]{:S(2)}) collective-permute-start(bf16[384,384]{1,0:T(8,128)(2,1)S(1)} %collective-permute-done.27.refs_1_), channel_id=1, source_target_pairs={{0,16},{8,24},{16,0},{24,8},{1,17},{9,25},{17,1},{25,9},{2,18},{10... | collective-permute-start | bytes 884744 | tf_op jit(solution)/shard_map/ppermute | solution.py:595
  157.9 4.3 %copy-start.2 = (f32[96,9280]{1,0:T(8,128)S(1)}, f32[96,9280]{1,0:T(8,128)}, u32[]{:S(2)}) copy-start(f32[96,9280]{1,0:T(8,128)} %refs_8_.1) | copy-start | bytes 10690564
  157.9 4.3 %copy-start.3 = (f32[96,9280]{1,0:T(8,128)S(1)}, f32[96,9280]{1,0:T(8,128)}, u32[]{:S(2)}) copy-start(f32[96,9280]{1,0:T(8,128)} %refs_9_.1) | copy-start | bytes 10690564
  157.9 4.3 %copy-start.4 = (f32[96,9280]{1,0:T(8,128)S(1)}, f32[96,9280]{1,0:T(8,128)}, u32[]{:S(2)}) copy-start(f32[96,9280]{1,0:T(8,128)} %refs_10_.1) | copy-start | bytes 10690564
  157.9 5.1 %copy-start.5 = (f32[96,9280]{1,0:T(8,128)S(1)}, f32[96,9280]{1,0:T(8,128)}, u32[]{:S(2)}) copy-start(f32[96,9280]{1,0:T(8,128)} %refs_11_.1) | copy-start | bytes 10690564
  158.5 12.5 %copy-start.18 = (f32[96,13]{0,1:T(8,128)S(1)}, f32[96,13]{0,1:T(8,128)}, u32[]{:S(2)}) copy-start(f32[96,13]{0,1:T(8,128)} %param.19) | copy-start | bytes 14980
  158.6 12.5 %copy-start.19 = (f32[96,13]{0,1:T(8,128)S(1)}, f32[96,13]{0,1:T(8,128)}, u32[]{:S(2)}) copy-start(f32[96,13]{0,1:T(8,128)} %param.21) | copy-start | bytes 14980
  158.6 12.5 %copy-start.20 = (f32[96,13]{0,1:T(8,128)S(1)}, f32[96,13]{0,1:T(8,128)}, u32[]{:S(2)}) copy-start(f32[96,13]{0,1:T(8,128)} %param.23) | copy-start | bytes 14980
  158.6 12.5 %copy-start.21 = (f32[96,13]{0,1:T(8,128)S(1)}, f32[96,13]{0,1:T(8,128)}, u32[]{:S(2)}) copy-start(f32[96,13]{0,1:T(8,128)} %param.25) | copy-start | bytes 14980
  158.6 12.5 %collective-permute-start.31 = (bf16[208,384]{1,0:T(8,128)(2,1)S(1)}, bf16[208,384]{1,0:T(8,128)(2,1)S(1)}, u32[]{:S(2)}, u32[]{:S(2)}) collective-permute-start(bf16[208,384]{1,0:T(8,128)(2,1)S(1)} %tail_final.1.refs_0_), channel_id=1, source_target_pairs={{0,24},{8,16},{16,8},{24,0},{1,25},{9,17},{17,9},{25,1},{2,26},{10... | collective-permute-start | bytes 479240 | tf_op jit(solution)/shard_map/ppermute | solution.py:595
  158.9 12.2 %collective-permute-start.30 = (bf16[208,384]{1,0:T(8,128)(2,1)S(1)}, bf16[208,384]{1,0:T(8,128)(2,1)S(1)}, u32[]{:S(2)}, u32[]{:S(2)}) collective-permute-start(bf16[208,384]{1,0:T(8,128)(2,1)S(1)} %tail_final.1.refs_0_), channel_id=1, source_target_pairs={{0,16},{8,24},{16,0},{24,8},{1,17},{9,25},{17,1},{25,9},{2,18},{10... | collective-permute-start | bytes 479240 | tf_op jit(solution)/shard_map/ppermute | solution.py:595
  160.6 10.4 %collective-permute-start.29 = (bf16[208,384]{1,0:T(8,128)(2,1)S(1)}, bf16[208,384]{1,0:T(8,128)(2,1)S(1)}, u32[]{:S(2)}, u32[]{:S(2)}) collective-permute-start(bf16[208,384]{1,0:T(8,128)(2,1)S(1)} %tail_final.1.refs_0_), channel_id=1, source_target_pairs={{0,8},{8,0},{16,24},{24,16},{1,9},{9,1},{17,25},{25,17},{2,10},{10... | collective-permute-start | bytes 479240 | tf_op jit(solution)/shard_map/ppermute | solution.py:595

commit v6 on v5

--- a/solution.py
+++ b/solution.py
@@ -586,7 +586,7 @@
         grid=(4,),
         scratch=[pltpu.VMEM((depth, 2 * HD), f32)],
         vmem=10,
-        hold=4,
+        hold=9,
         name="tail_grads",
     )
 
@@ -951,7 +951,7 @@
 
     if fast:
         first = Halves(
-            line, *mlp_grads(line, False, sels, acts[0], out_far=(1,)),
+            line, *mlp_grads(line, False, sels, acts[0]),
             [("grp", 8, 2), ("seq", 4, 2), ("grp", 8, 4), ("seq", 4, 1)],
         )
         (acts[1],) = line.wait(acts[1])

time: 177 us -> 175 us (0.989)
  starting transfers between devices: 42 us -> 39.4 us
    ppermute x32, starting transfers between devices: 42 us -> 39.4 us  [swap(): return lax.ppermute(value, axis, [(i, i ^ bit) for i in range(size)])]
  transfers between devices with their start and end apart: 32 -> 32, of which waited for: 8 -> 9; matrix products, arithmetic and copies ran while one was open for 0% -> 0% of each run, Pallas kernels for 49% -> 50%
where the time goes in v6:
time: 175 us; the launch traced here: 174 us
  Pallas kernels  103 us (59%)
  starting transfers between devices  39.4 us (23%)
  waiting for transfers between devices  26.4 us (15%)
  local copies, waits for them, and re-layouts  3.16 us (2%)
  between operations  1.98 us (1%)
    pallas_call x24, Pallas kernels, call(): pl.pallas_call(body, out_shape=tuple((pltpu.HBM(o.shape, o.dtype) if k in...  103 us
    ppermute x32, starting transfers between devices, swap(): return lax.ppermute(value, axis, [(i, i ^ bit) for i in range(size)])  39.4 us
    ppermute x32, waiting for transfers between devices, swap(): return lax.ppermute(value, axis, [(i, i ^ bit) for i in range(size)])  26.4 us
  transfers between devices with their start and end apart: 32, of which 9 were waited for; matrix products, arithmetic and copies ran while one was open for 0% of the time, Pallas kernels for 50%

profile of v6, /device:TPU:0, one launch (start us, length us, event | category | flops | bytes accessed | tf_op | source)
XLA Modules:
  0.0 174.4 jit_solution(4196232262784266442)
XLA Ops:
  1.5 0.7 copy-done.13
  2.2 6.6 %keys.1 = (bf16[512,768]{1,0:T(8,128)(2,1)S(1)}, bf16[768,512]{1,0:T(8,128)(2,1)S(1)}, bf16[1536,512]{1,0:T(8,128)(2,1)S(1)}, bf16[768,512]{1,0:T(8,128)(2,1)S(1)}, bf16[864,128]{1,0:T(8,128)(2,1)S(1)}) custom-call(s32[16]{0:T(128)S(1)} %compare_select_fusion.2.scal, bf16[512,768]{1,0:T(8,128)(2,1)} %x_ref.3, bf16[9280,768]{1,0:T(8,128)(2,1)} %bitcast.44, ...), custom_call_target="tpu_custom_call" | custom-call | bytes 1024 | tf_op jit(solution)/shard_map/keys/pallas_call | solution.py:74
  8.8 4.0 %collective-permute-start.2 = (bf16[864,128]{1,0:T(8,128)(2,1)S(1)}, bf16[864,128]{1,0:T(8,128)(2,1)S(1)}, u32[]{:S(2)}, u32[]{:S(2)}) collective-permute-start(bf16[864,128]{1,0:T(8,128)(2,1)S(1)} %get-tuple-element.230), channel_id=1, source_target_pairs={{0,24},{8,16},{16,8},{24,0},{1,25},{9,17},{17,9},{25,1},{2,26},{10... | collective-permute-start | bytes 663560 | tf_op jit(solution)/shard_map/ppermute | solution.py:595
  12.8 0.5 collective-permute-start.1
  13.4 5.7 %queries.1 = (bf16[4,384,512]{2,1,0:T(8,128)(2,1)S(1)}, bf16[4,384,512]{2,1,0:T(8,128)(2,1)S(1)}, bf16[768,512]{1,0:T(8,128)(2,1)S(1)}, bf16[1536,512]{1,0:T(8,128)(2,1)S(1)}) custom-call(s32[16]{0:T(128)S(1)} %compare_select_fusion.2.scal, bf16[512,768]{1,0:T(8,128)(2,1)S(1)} %get-tuple-element.220.h1_ref, bf16[512,768]{1,0:T(8,128)(2,1)} %g_ref.7, ...), custom_call_target="tpu_custom_call" | custom-call | bytes 1024 | tf_op jit(solution)/shard_map/queries/pallas_call | solution.py:74
  19.1 4.0 %local.1.refs_3_ = f32[864,512]{1,0:T(8,128)S(1)} custom-call(s32[16]{0:T(128)S(1)} %compare_select_fusion.2.scal, bf16[1536,512]{1,0:T(8,128)(2,1)S(1)} %get-tuple-element.226.fq_ref.refs_4_.refs_3_, bf16[1536,512]{1,0:T(8,128)(2,1)S(1)} %get-tuple-element.227.fk_ref.refs_4_, bf16[768,512]{1,0:T(8,128)(2,1)S(1)} %get-tuple-element.228.vt_ref.refs_5_), custom_call_target="tpu_custom_call" | custom-call | bytes 1024 | tf_op jit(solution)/shard_map/local/pallas_call | solution.py:74
  23.2 4.3 %after.1 = (f32[768,512]{1,0:T(8,128)S(1)}, f32[16,512]{1,0:T(8,128)S(1)}, f32[512,768]{1,0:T(8,128)S(1)}, bf16[512,768]{1,0:T(8,128)(2,1)S(1)}, bf16[864,128]{1...) custom-call(s32[16]{0:T(128)S(1)} %compare_select_fusion.2.scal, ...), custom_call_target="tpu_custom_call", output_to_operand_aliasing={{5}: (9, {}), {6}: (10, {})} | custom-call | bytes 1024 | tf_op jit(solution)/shard_map/after/pallas_call | solution.py:74
  27.7 9.1 %mlp.2 = (f32[512,768]{1,0:T(8,128)S(1)}, f32[512,768]{1,0:T(8,128)S(1)}, bf16[2,2,512,768]{3,2,1,0:T(8,128)(2,1)S(1)}, f32[1,1536]{1,0:T(1,128)S(1)}) custom-call(s32[16]{0:T(128)S(1)} %compare_select_fusion.2.scal, bf16[512,768]{1,0:T(8,128)(2,1)S(1)} %get-tuple-element.242.h2_ref, bf16[512,768]{1,0:T(8,128)(2,1)} %g_ref.7, bf16[9280,768]{1,0:T(8,128)(2,1)} %bitcast.50, ...), custom_call_target="tpu_custom_call" | custom-call | bytes 1024 | tf_op jit(solution)/shard_map/mlp/pallas_call | solution.py:74
  36.8 0.6 collective-permute-start.4
  37.4 9.1 %mlp.3 = (f32[512,768]{1,0:T(8,128)S(1)}, f32[512,768]{1,0:T(8,128)S(1)}, bf16[2,2,512,768]{3,2,1,0:T(8,128)(2,1)S(1)}, f32[1,1536]{1,0:T(1,128)S(1)}) custom-call(s32[16]{0:T(128)S(1)} %compare_select_fusion.2.scal, bf16[512,768]{1,0:T(8,128)(2,1)S(1)} %get-tuple-element.242.h2_ref, bf16[512,768]{1,0:T(8,128)(2,1)} %g_ref.7, bf16[9280,768]{1,0:T(8,128)(2,1)} %bitcast.52, ...), custom_call_target="tpu_custom_call" | custom-call | bytes 1024 | tf_op jit(solution)/shard_map/mlp/pallas_call | solution.py:74
  46.6 4.4 %mlp_grads.2 = (bf16[8,192,384]{2,1,0:T(8,128)(2,1)}, bf16[8,192,384]{2,1,0:T(8,128)(2,1)S(1)}) custom-call(s32[16]{0:T(128)S(1)} %compare_select_fusion.2.scal, bf16[4,384,512]{2,1,0:T(8,128)(2,1)S(1)} %get-tuple-element.258.refs_0_.refs_6_.refs_2_, bf16[4,384,512]{2,1,0:T(8,128)(2,1)S(1)} %collective-permute-done.3.refs_1_.refs_7_.refs_3_, ...), custom_call_target="tpu_custom_call" | custom-call | bytes 1024 | tf_op jit(solution)/shard_map/mlp_grads/pallas_call | solution.py:74
  51.0 2.0 %collective-permute-start.9 = (bf16[8,192,384]{2,1,0:T(8,128)(2,1)}, bf16[8,192,384]{2,1,0:T(8,128)(2,1)}, u32[]{:S(2)}, u32[]{:S(2)}) collective-permute-start(bf16[8,192,384]{2,1,0:T(8,128)(2,1)} %get-tuple-element.311), channel_id=1, source_target_pairs={{0,2},{1,3},{2,0},{3,1},{4,6},{5,7},{6,4},{7,5},{8,10},{9,11},{10,... | collective-permute-start | bytes 3538952 | tf_op jit(solution)/shard_map/ppermute | solution.py:595
  53.0 6.6 %back.1 = (bf16[512,768]{1,0:T(8,128)(2,1)}, f32[512,768]{1,0:T(8,128)}, bf16[768,512]{1,0:T(8,128)(2,1)}, bf16[864,512]{1,0:T(8,128)(2,1)}, bf16[864,128]{1,0:T(8,128)(2,1)}, /*index=5*/f32[4,768]{1,0:T(4,128)S(1)}) custom-call(s32[16]{0:T(128)S(1)} %compare_select_fusion.2.scal, f32[512,768]{1,0:T(8,128)S(1)} %get-tuple-element.266.out_ref, ...), custom_call_target="tpu_custom_call" | custom-call | bytes 1024 | tf_op jit(solution)/shard_map/back/pallas_call | solution.py:74
  59.6 2.5 %collective-permute-start.8 = (bf16[864,128]{1,0:T(8,128)(2,1)}, bf16[864,128]{1,0:T(8,128)(2,1)}, u32[]{:S(2)}, u32[]{:S(2)}) collective-permute-start(bf16[864,128]{1,0:T(8,128)(2,1)} %get-tuple-element.284), channel_id=1, source_target_pairs={{0,24},{8,16},{16,8},{24,0},{1,25},{9,17},{17,9},{25,1},{2,26},{10... | collective-permute-start | bytes 663560 | tf_op jit(solution)/shard_map/ppermute | solution.py:595
  62.1 0.5 collective-permute-start.7
  62.7 0.5 collective-permute-start.6
  63.2 1.4 copy-done.1
  64.6 5.8 %mlp_grads.3 = (bf16[8,192,384]{2,1,0:T(8,128)(2,1)S(1)}, bf16[8,192,384]{2,1,0:T(8,128)(2,1)S(1)}) custom-call(s32[16]{0:T(128)S(1)} %compare_select_fusion.2.scal, bf16[4,384,512]{2,1,0:T(8,128)(2,1)S(1)} %get-tuple-element.258.refs_0_.refs_6_.refs_2_, bf16[4,384,512]{2,1,0:T(8,128)(2,1)S(1)} %copy-done.1, bf16[2,2,512,768]{3,2,1,0:T(8,128)(2,1)} %copy-done.7, ...), custom_call_target="tpu_custom_call" | custom-call | bytes 1024 | tf_op jit(solution)/shard_map/mlp_grads/pallas_call | solution.py:74
  70.5 1.6 collective-permute-start.10
  72.1 1.2 collective-permute-done.7.refs_1_
  73.3 12.3 %attend_back.1 = (bf16[4,768,512]{2,1,0:T(8,128)(2,1)S(1)}, f32[768,64]{1,0:T(8,128)S(1)}, f32[768,3]{1,0:T(8,128)S(1)}) custom-call(s32[16]{0:T(128)S(1)} %compare_select_fusion.2.scal, bf16[864,128]{1,0:T(8,128)(2,1)} %collective-permute-done.6.refs_0_, bf16[864,128]{1,0:T(8,128)(2,1)} %collective-permute-done.7.refs_1_, ...), custom_call_target="tpu_custom_call" | custom-call | flops 1000000000 | bytes 1024 | tf_op jit(solution)/shard_map/attend_back/pallas_call | solution.py:74
  85.7 7.8 %input.1 = (bf16[512,768]{1,0:T(8,128)(2,1)}, f32[1,384,128]{2,1,0:T(8,128)S(1)}, f32[1,384,128]{2,1,0:T(8,128)S(1)}) custom-call(s32[16]{0:T(128)S(1)} %compare_select_fusion.2.scal, bf16[4,768,512]{2,1,0:T(8,128)(2,1)S(1)} %get-tuple-element.298.dp_ref, bf16[9280,768]{1,0:T(8,128)(2,1)} %bitcast.56, bf16[512,768]{1,0:T(8,128)(2,1)} %x_ref.3, ...), custom_call_target="tpu_custom_call" | custom-call | bytes 1024 | tf_op jit(solution)/shard_map/input/pallas_call | solution.py:74
  93.5 0.5 collective-permute-start.12
  94.0 2.1 %halve.6 = (bf16[4,192,384]{2,1,0:T(8,128)(2,1)S(1)}, bf16[4,192,384]{2,1,0:T(8,128)(2,1)S(1)}) custom-call(s32[16]{0:T(128)S(1)} %compare_select_fusion.2.scal, bf16[8,192,384]{2,1,0:T(8,128)(2,1)S(1)} %copy-done.24, bf16[8,192,384]{2,1,0:T(8,128)(2,1)} %collective-permute-done.9.recv_ref), custom_call_target="tpu_custom_call" | custom-call | flops 14000000000 | bytes 1024 | tf_op jit(solution)/shard_map/halve/pallas_call | solution.py:74
  96.1 1.6 collective-permute-start.13
  97.7 0.6 collective-permute-done.10.recv_ref
  98.3 0.8 halve.7
  99.2 1.2 collective-permute-start.14
  100.4 5.7 %tail_grads.1 = (bf16[832,384]{1,0:T(8,128)(2,1)S(1)}, bf16[768,384]{1,0:T(8,128)(2,1)S(1)}, bf16[768,384]{1,0:T(8,128)(2,1)S(1)}, bf16[768,384]{1,0:T(8,128)(2,1)S(1)}, f32[64,384]{1,0:T(8,128)S(1)}) custom-call(s32[16]{0:T(128)S(1)} %compare_select_fusion.2.scal, bf16[4,384,512]{2,1,0:T(8,128)(2,1)S(1)} %get-tuple-element.258.refs_0_.refs_6_.refs_2_, ...), custom_call_target="tpu_custom_call" | custom-call | flops 8999999488 | bytes 1024 | tf_op jit(solution)/shard_map/tail_grads/pallas_call | solution.py:74
  106.1 1.6 collective-permute-start.15
  107.6 0.9 collective-permute-start.16
  108.6 3.8 %collective-permute-done.13.recv_ref = bf16[4,192,384]{2,1,0:T(8,128)(2,1)S(1)} collective-permute-done((bf16[4,192,384]{2,1,0:T(8,128)(2,1)S(1)}, bf16[4,192,384]{2,1,0:T(8,128)(2,1)S(1)}, u32[]{:S(2)}, u32[]{:S(2)}) %collective-permute-start.13) | collective-permute-done | bytes 589856 | tf_op jit(solution)/shard_map/ppermute | solution.py:595
  112.4 0.7 halve.8
  113.1 2.7 %collective-permute-start.17 = (bf16[2,192,384]{2,1,0:T(8,128)(2,1)S(1)}, bf16[2,192,384]{2,1,0:T(8,128)(2,1)S(1)}, u32[]{:S(2)}, u32[]{:S(2)}) collective-permute-start(bf16[2,192,384]{2,1,0:T(8,128)(2,1)S(1)} %get-tuple-element.347), channel_id=1, source_target_pairs={{0,4},{1,5},{2,6},{3,7},{4,0},{5,1},{6,2},{7,3},{8,12},{9,13},{10,... | collective-permute-start | bytes 884744 | tf_op jit(solution)/shard_map/ppermute | solution.py:595
  115.7 0.7 halve.9
  116.4 1.5 collective-permute-start.18
  118.0 6.1 %collective-permute-done.16.recv_b = bf16[768,384]{1,0:T(8,128)(2,1)S(1)} collective-permute-done((bf16[768,384]{1,0:T(8,128)(2,1)S(1)}, bf16[768,384]{1,0:T(8,128)(2,1)S(1)}, u32[]{:S(2)}, u32[]{:S(2)}) %collective-permute-start.16) | collective-permute-done | bytes 589856 | tf_op jit(solution)/shard_map/ppermute | solution.py:595
  124.1 0.8 tail_one.1
  124.9 1.6 collective-permute-start.21
  126.5 0.7 collective-permute-start.22
  127.2 0.3 collective-permute-done.17.recv_ref
  127.5 0.6 halve.10
  128.1 0.6 halve.11
  128.8 2.3 %collective-permute-start.20 = (bf16[1,192,384]{2,1,0:T(8,128)(2,1)S(1)}, bf16[1,192,384]{2,1,0:T(8,128)(2,1)S(1)}, u32[]{:S(2)}, u32[]{:S(2)}) collective-permute-start(bf16[1,192,384]{2,1,0:T(8,128)(2,1)S(1)} %get-tuple-element.359), channel_id=1, source_target_pairs={{0,4},{1,5},{2,6},{3,7},{4,0},{5,1},{6,2},{7,3},{8,12},{9,13},{10,... | collective-permute-start | bytes 442376 | tf_op jit(solution)/shard_map/ppermute | solution.py:595
  131.1 1.3 collective-permute-start.19
  132.4 5.4 %collective-permute-done.20.refs_3_ = bf16[1,192,384]{2,1,0:T(8,128)(2,1)S(1)} collective-permute-done((bf16[1,192,384]{2,1,0:T(8,128)(2,1)S(1)}, bf16[1,192,384]{2,1,0:T(8,128)(2,1)S(1)}, u32[]{:S(2)}, u32[]{:S(2)}) %collective-permute-start.20) | collective-permute-done | bytes 147488 | tf_op jit(solution)/shard_map/ppermute | solution.py:595
  137.9 0.6 final.1
  138.5 1.7 collective-permute-start.27
  140.2 0.7 collective-permute-start.23
  140.9 0.9 tail_two.1
  141.8 0.5 collective-permute-start.24
  142.3 2.6 %collective-permute-start.25 = (bf16[208,384]{1,0:T(8,128)(2,1)S(1)}, bf16[208,384]{1,0:T(8,128)(2,1)S(1)}, u32[]{:S(2)}, u32[]{:S(2)}) collective-permute-start(bf16[208,384]{1,0:T(8,128)(2,1)S(1)} %get-tuple-element.372), channel_id=1, source_target_pairs={{0,4},{1,5},{2,6},{3,7},{4,0},{5,1},{6,2},{7,3},{8,12},{9,13},{10,... | collective-permute-start | bytes 479240 | tf_op jit(solution)/shard_map/ppermute | solution.py:595
  144.9 1.4 collective-permute-start.26
  146.2 1.7 collective-permute-done.23.refs_2_
  147.9 0.6 collective-permute-start.28
  148.5 2.0 %collective-permute-done.24.refs_1_ = bf16[208,384]{1,0:T(8,128)(2,1)S(1)} collective-permute-done((bf16[208,384]{1,0:T(8,128)(2,1)S(1)}, bf16[208,384]{1,0:T(8,128)(2,1)S(1)}, u32[]{:S(2)}, u32[]{:S(2)}) %collective-permute-start.24) | collective-permute-done | bytes 159776 | tf_op jit(solution)/shard_map/ppermute | solution.py:595
  150.5 5.1 %collective-permute-done.25.refs_2_ = bf16[208,384]{1,0:T(8,128)(2,1)S(1)} collective-permute-done((bf16[208,384]{1,0:T(8,128)(2,1)S(1)}, bf16[208,384]{1,0:T(8,128)(2,1)S(1)}, u32[]{:S(2)}, u32[]{:S(2)}) %collective-permute-start.25) | collective-permute-done | bytes 159776 | tf_op jit(solution)/shard_map/ppermute | solution.py:595
  155.6 0.6 tail_final.1.refs_0_
  156.3 1.7 collective-permute-start.31
  158.0 1.1 collective-permute-start.30
  159.1 0.7 collective-permute-start.29
  159.9 0.9 copy-done.6
  160.8 8.0 %adam.2 = (f32[96,9280]{1,0:T(8,128)}, f32[96,9280]{1,0:T(8,128)}, f32[96,9280]{1,0:T(8,128)}, f32[96,9280]{1,0:T(8,128)}, f32[96,9280]{1,0:T(8,128)}, /*index=5*/bf16[96,9280]{1,0:T(8,128)(2,1)}) custom-call(s32[16]{0:T(128)S(1)} %compare_select_fusion.2.scal, bf16[384,384]{1,0:T(8,128)(2,1)S(1)} %bitcast.28, ...), custom_call_target="tpu_custom_call" | custom-call | bytes 1024 | tf_op jit(solution)/shard_map/adam/pallas_call | solution.py:74
  168.8 5.4 %adam.3 = (f32[96,9280]{1,0:T(8,128)}, f32[96,9280]{1,0:T(8,128)}, f32[96,9280]{1,0:T(8,128)}, f32[96,9280]{1,0:T(8,128)}, f32[96,9280]{1,0:T(8,128)}, /*index=5...) custom-call(s32[16]{0:T(128)S(1)} %compare_select_fusion.2.scal, ...), custom_call_target="tpu_custom_call", output_to_operand_aliasing={{0}: (13, {}), {1}: (14, {}), {2}: (15, {}), {3}: (16, {}),... | custom-call | bytes 1024 | tf_op jit(solution)/shard_map/adam/pallas_call | solution.py:74
  (81 shorter events, 0.8 us)
Async XLA Ops:
  1.5 0.7 copy-start.13
  8.8 10.3 %copy-start.15 = (bf16[768,512]{1,0:T(8,128)(2,1)}, bf16[768,512]{1,0:T(8,128)(2,1)S(1)}, u32[]{:S(2)}) copy-start(bf16[768,512]{1,0:T(8,128)(2,1)S(1)} %get-tuple-element.292.refs_9_) | copy-start | bytes 2359300
  8.8 10.3 %copy-start.8 = (bf16[1536,512]{1,0:T(8,128)(2,1)}, bf16[1536,512]{1,0:T(8,128)(2,1)S(1)}, u32[]{:S(2)}) copy-start(bf16[1536,512]{1,0:T(8,128)(2,1)S(1)} %get-tuple-element.227.fk_ref.refs_4_) | copy-start | bytes 4718596
  8.8 10.3 %copy-start.10 = (bf16[768,512]{1,0:T(8,128)(2,1)}, bf16[768,512]{1,0:T(8,128)(2,1)S(1)}, u32[]{:S(2)}) copy-start(bf16[768,512]{1,0:T(8,128)(2,1)S(1)} %get-tuple-element.228.vt_ref.refs_5_) | copy-start | bytes 2359300
  8.8 14.4 %collective-permute-start.2 = (bf16[864,128]{1,0:T(8,128)(2,1)S(1)}, bf16[864,128]{1,0:T(8,128)(2,1)S(1)}, u32[]{:S(2)}, u32[]{:S(2)}) collective-permute-start(bf16[864,128]{1,0:T(8,128)(2,1)S(1)} %get-tuple-element.230), channel_id=1, source_target_pairs={{0,24},{8,16},{16,8},{24,0},{1,25},{9,17},{17,9},{25,1},{2,26},{10... | collective-permute-start | bytes 663560 | tf_op jit(solution)/shard_map/ppermute | solution.py:595
  12.8 10.4 %collective-permute-start.1 = (bf16[864,128]{1,0:T(8,128)(2,1)S(1)}, bf16[864,128]{1,0:T(8,128)(2,1)S(1)}, u32[]{:S(2)}, u32[]{:S(2)}) collective-permute-start(bf16[864,128]{1,0:T(8,128)(2,1)S(1)} %get-tuple-element.230), channel_id=1, source_target_pairs={{0,16},{8,24},{16,0},{24,8},{1,17},{9,25},{17,1},{25,9},{2,18},{10... | collective-permute-start | bytes 663560 | tf_op jit(solution)/shard_map/ppermute | solution.py:595
  13.3 9.9 %collective-permute-start = (bf16[864,128]{1,0:T(8,128)(2,1)S(1)}, bf16[864,128]{1,0:T(8,128)(2,1)S(1)}, u32[]{:S(2)}, u32[]{:S(2)}) collective-permute-start(bf16[864,128]{1,0:T(8,128)(2,1)S(1)} %get-tuple-element.230), channel_id=1, source_target_pairs={{0,8},{8,0},{16,24},{24,16},{1,9},{9,1},{17,25},{25,17},{2,10},{10... | collective-permute-start | bytes 663560 | tf_op jit(solution)/shard_map/ppermute | solution.py:595
  19.1 4.1 %copy-start.17 = (bf16[768,512]{1,0:T(8,128)(2,1)}, bf16[768,512]{1,0:T(8,128)(2,1)S(1)}, u32[]{:S(2)}) copy-start(bf16[768,512]{1,0:T(8,128)(2,1)S(1)} %get-tuple-element.291.refs_8_) | copy-start | bytes 2359300
  27.6 9.8 %collective-permute-start.3 = (bf16[4,384,512]{2,1,0:T(8,128)(2,1)S(1)}, bf16[4,384,512]{2,1,0:T(8,128)(2,1)S(1)}, u32[]{:S(2)}, u32[]{:S(2)}) collective-permute-start(bf16[4,384,512]{2,1,0:T(8,128)(2,1)S(1)} %get-tuple-element.249), channel_id=1, source_target_pairs={{0,1},{1,0},{2,3},{3,2},{4,5},{5,4},{6,7},{7,6},{8,9},{9,8},{10,11... | collective-permute-start | bytes 4718600 | tf_op jit(solution)/shard_map/ppermute | solution.py:595
  36.8 9.8 %collective-permute-start.4 = (bf16[2,2,512,768]{3,2,1,0:T(8,128)(2,1)S(1)}, bf16[2,2,512,768]{3,2,1,0:T(8,128)(2,1)S(1)}, u32[]{:S(2)}, u32[]{:S(2)}) collective-permute-start(bf16[2,2,512,768]{3,2,1,0:T(8,128)(2,1)S(1)} %get-tuple-element.260.refs_2_.refs_4_), channel_id=1, source_target_pairs={{0,1},{1,0},{2,3},{3,2},{4,5},{5,4},{6,7},{7,6},{8,9},{9,8},{10,11... | collective-permute-start | bytes 9437192 | tf_op jit(solution)/shard_map/ppermute | solution.py:595
  37.4 9.3 %copy-start = (bf16[4,384,512]{2,1,0:T(8,128)(2,1)}, bf16[4,384,512]{2,1,0:T(8,128)(2,1)S(1)}, u32[]{:S(2)}) copy-start(bf16[4,384,512]{2,1,0:T(8,128)(2,1)S(1)} %collective-permute-done.3.refs_1_.refs_7_.refs_3_) | copy-start | bytes 4718596
  46.5 4.5 %copy-start.7 = (bf16[2,2,512,768]{3,2,1,0:T(8,128)(2,1)}, bf16[2,2,512,768]{3,2,1,0:T(8,128)(2,1)S(1)}, u32[]{:S(2)}) copy-start(bf16[2,2,512,768]{3,2,1,0:T(8,128)(2,1)S(1)} %get-tuple-element.279.refs_2_.refs_4_) | copy-start | bytes 9437188
  46.5 6.5 %copy-start.14 = (bf16[768,13]{0,1:T(8,128)(2,1)S(1)}, bf16[768,13]{0,1:T(8,128)(2,1)}, u32[]{:S(2)}) copy-start(bf16[768,13]{0,1:T(8,128)(2,1)} %param.17) | copy-start | bytes 59908
  46.5 6.5 %collective-permute-start.5 = (bf16[2,2,512,768]{3,2,1,0:T(8,128)(2,1)S(1)}, bf16[2,2,512,768]{3,2,1,0:T(8,128)(2,1)S(1)}, u32[]{:S(2)}, u32[]{:S(2)}) collective-permute-start(bf16[2,2,512,768]{3,2,1,0:T(8,128)(2,1)S(1)} %get-tuple-element.279.refs_2_.refs_4_), channel_id=1, source_target_pairs={{0,1},{1,0},{2,3},{3,2},{4,5},{5,4},{6,7},{7,6},{8,9},{9,8},{10,11... | collective-permute-start | bytes 9437192 | tf_op jit(solution)/shard_map/ppermute | solution.py:595
  51.0 8.6 %copy-start.23 = (bf16[8,192,384]{2,1,0:T(8,128)(2,1)}, bf16[8,192,384]{2,1,0:T(8,128)(2,1)S(1)}, u32[]{:S(2)}) copy-start(bf16[8,192,384]{2,1,0:T(8,128)(2,1)S(1)} %get-tuple-element.310.keep_ref) | copy-start | bytes 3538948
  51.0 43.0 %collective-permute-start.9 = (bf16[8,192,384]{2,1,0:T(8,128)(2,1)}, bf16[8,192,384]{2,1,0:T(8,128)(2,1)}, u32[]{:S(2)}, u32[]{:S(2)}) collective-permute-start(bf16[8,192,384]{2,1,0:T(8,128)(2,1)} %get-tuple-element.311), channel_id=1, source_target_pairs={{0,2},{1,3},{2,0},{3,1},{4,6},{5,7},{6,4},{7,5},{8,10},{9,11},{10,... | collective-permute-start | bytes 3538952 | tf_op jit(solution)/shard_map/ppermute | solution.py:595
  53.0 6.7 %copy-start.25 = (bf16[2,2,512,768]{3,2,1,0:T(8,128)(2,1)}, bf16[2,2,512,768]{3,2,1,0:T(8,128)(2,1)S(1)}, u32[]{:S(2)}) copy-start(bf16[2,2,512,768]{3,2,1,0:T(8,128)(2,1)S(1)} %collective-permute-done.5.refs_3_.refs_5_) | copy-start | bytes 9437188
  59.6 12.4 %collective-permute-start.8 = (bf16[864,128]{1,0:T(8,128)(2,1)}, bf16[864,128]{1,0:T(8,128)(2,1)}, u32[]{:S(2)}, u32[]{:S(2)}) collective-permute-start(bf16[864,128]{1,0:T(8,128)(2,1)} %get-tuple-element.284), channel_id=1, source_target_pairs={{0,24},{8,16},{16,8},{24,0},{1,25},{9,17},{17,9},{25,1},{2,26},{10... | collective-permute-start | bytes 663560 | tf_op jit(solution)/shard_map/ppermute | solution.py:595
  62.1 11.1 %collective-permute-start.7 = (bf16[864,128]{1,0:T(8,128)(2,1)}, bf16[864,128]{1,0:T(8,128)(2,1)}, u32[]{:S(2)}, u32[]{:S(2)}) collective-permute-start(bf16[864,128]{1,0:T(8,128)(2,1)} %get-tuple-element.284), channel_id=1, source_target_pairs={{0,16},{8,24},{16,0},{24,8},{1,17},{9,25},{17,1},{25,9},{2,18},{10... | collective-permute-start | bytes 663560 | tf_op jit(solution)/shard_map/ppermute | solution.py:595
  62.7 10.6 %collective-permute-start.6 = (bf16[864,128]{1,0:T(8,128)(2,1)}, bf16[864,128]{1,0:T(8,128)(2,1)}, u32[]{:S(2)}, u32[]{:S(2)}) collective-permute-start(bf16[864,128]{1,0:T(8,128)(2,1)} %get-tuple-element.284), channel_id=1, source_target_pairs={{0,8},{8,0},{16,24},{24,16},{1,9},{9,1},{17,25},{25,17},{2,10},{10... | collective-permute-start | bytes 663560 | tf_op jit(solution)/shard_map/ppermute | solution.py:595
  63.2 1.4 copy-start.1
  64.6 8.6 %copy-start.9 = (bf16[1536,512]{1,0:T(8,128)(2,1)S(1)}, bf16[1536,512]{1,0:T(8,128)(2,1)}, u32[]{:S(2)}) copy-start(bf16[1536,512]{1,0:T(8,128)(2,1)} %copy-done.8) | copy-start | bytes 4718596
  64.6 8.6 %copy-start.11 = (bf16[768,512]{1,0:T(8,128)(2,1)S(1)}, bf16[768,512]{1,0:T(8,128)(2,1)}, u32[]{:S(2)}) copy-start(bf16[768,512]{1,0:T(8,128)(2,1)} %copy-done.10) | copy-start | bytes 2359300
  64.6 8.6 %copy-start.16 = (bf16[768,512]{1,0:T(8,128)(2,1)S(1)}, bf16[768,512]{1,0:T(8,128)(2,1)}, u32[]{:S(2)}) copy-start(bf16[768,512]{1,0:T(8,128)(2,1)} %copy-done.15) | copy-start | bytes 2359300
  64.6 8.6 %copy-start.18 = (bf16[768,512]{1,0:T(8,128)(2,1)S(1)}, bf16[768,512]{1,0:T(8,128)(2,1)}, u32[]{:S(2)}) copy-start(bf16[768,512]{1,0:T(8,128)(2,1)} %copy-done.17) | copy-start | bytes 2359300
  70.5 15.2 %copy-start.12 = (f32[512,768]{1,0:T(8,128)S(1)}, f32[512,768]{1,0:T(8,128)}, u32[]{:S(2)}) copy-start(f32[512,768]{1,0:T(8,128)} %get-tuple-element.299.dr_ref) | copy-start | bytes 4718596
  70.5 27.9 %collective-permute-start.10 = (bf16[8,192,384]{2,1,0:T(8,128)(2,1)S(1)}, bf16[8,192,384]{2,1,0:T(8,128)(2,1)S(1)}, u32[]{:S(2)}, u32[]{:S(2)}) collective-permute-start(bf16[8,192,384]{2,1,0:T(8,128)(2,1)S(1)} %get-tuple-element.316), channel_id=1, source_target_pairs={{0,16},{8,24},{16,0},{24,8},{1,17},{9,25},{17,1},{25,9},{2,18},{10... | collective-permute-start | bytes 3538952 | tf_op jit(solution)/shard_map/ppermute | solution.py:595
  85.6 8.4 %copy-start.24 = (bf16[8,192,384]{2,1,0:T(8,128)(2,1)S(1)}, bf16[8,192,384]{2,1,0:T(8,128)(2,1)}, u32[]{:S(2)}) copy-start(bf16[8,192,384]{2,1,0:T(8,128)(2,1)} %copy-done.23) | copy-start | bytes 3538948
  85.6 14.8 %collective-permute-start.11 = (bf16[4,768,512]{2,1,0:T(8,128)(2,1)S(1)}, bf16[4,768,512]{2,1,0:T(8,128)(2,1)S(1)}, u32[]{:S(2)}, u32[]{:S(2)}) collective-permute-start(bf16[4,768,512]{2,1,0:T(8,128)(2,1)S(1)} %get-tuple-element.298.dp_ref), channel_id=1, source_target_pairs={{0,1},{1,0},{2,3},{3,2},{4,5},{5,4},{6,7},{7,6},{8,9},{9,8},{10,11... | collective-permute-start | bytes 9437192 | tf_op jit(solution)/shard_map/ppermute | solution.py:595
  93.5 6.9 %collective-permute-start.12 = (f32[1,384,128]{2,1,0:T(8,128)S(1)}, f32[1,384,128]{2,1,0:T(8,128)S(1)}, u32[]{:S(2)}, u32[]{:S(2)}) collective-permute-start(f32[1,384,128]{2,1,0:T(8,128)S(1)} %get-tuple-element.321), channel_id=1, source_target_pairs={{0,1},{1,0},{2,3},{3,2},{4,5},{5,4},{6,7},{7,6},{8,9},{9,8},{10,11... | collective-permute-start | bytes 589832 | tf_op jit(solution)/shard_map/ppermute | solution.py:595
  96.1 4.3 %copy-start.2 = (bf16[4,384,512]{2,1,0:T(8,128)(2,1)S(1)}, bf16[4,384,512]{2,1,0:T(8,128)(2,1)}, u32[]{:S(2)}) copy-start(bf16[4,384,512]{2,1,0:T(8,128)(2,1)} %copy-done) | copy-start | bytes 4718596
  96.1 16.3 %collective-permute-start.13 = (bf16[4,192,384]{2,1,0:T(8,128)(2,1)S(1)}, bf16[4,192,384]{2,1,0:T(8,128)(2,1)S(1)}, u32[]{:S(2)}, u32[]{:S(2)}) collective-permute-start(bf16[4,192,384]{2,1,0:T(8,128)(2,1)S(1)} %get-tuple-element.329), channel_id=1, source_target_pairs={{0,16},{8,24},{16,0},{24,8},{1,17},{9,25},{17,1},{25,9},{2,18},{10... | collective-permute-start | bytes 1769480 | tf_op jit(solution)/shard_map/ppermute | solution.py:595
  99.2 16.6 %collective-permute-start.14 = (bf16[4,192,384]{2,1,0:T(8,128)(2,1)S(1)}, bf16[4,192,384]{2,1,0:T(8,128)(2,1)S(1)}, u32[]{:S(2)}, u32[]{:S(2)}) collective-permute-start(bf16[4,192,384]{2,1,0:T(8,128)(2,1)S(1)} %get-tuple-element.334), channel_id=1, source_target_pairs={{0,2},{1,3},{2,0},{3,1},{4,6},{5,7},{6,4},{7,5},{8,10},{9,11},{10,... | collective-permute-start | bytes 1769480 | tf_op jit(solution)/shard_map/ppermute | solution.py:595
  106.1 18.0 %collective-permute-start.15 = (bf16[832,384]{1,0:T(8,128)(2,1)S(1)}, bf16[832,384]{1,0:T(8,128)(2,1)S(1)}, u32[]{:S(2)}, u32[]{:S(2)}) collective-permute-start(bf16[832,384]{1,0:T(8,128)(2,1)S(1)} %get-tuple-element.339), channel_id=1, source_target_pairs={{0,8},{8,0},{16,24},{24,16},{1,9},{9,1},{17,25},{25,17},{2,10},{10... | collective-permute-start | bytes 1916936 | tf_op jit(solution)/shard_map/ppermute | solution.py:595
  107.6 16.4 %collective-permute-start.16 = (bf16[768,384]{1,0:T(8,128)(2,1)S(1)}, bf16[768,384]{1,0:T(8,128)(2,1)S(1)}, u32[]{:S(2)}, u32[]{:S(2)}) collective-permute-start(bf16[768,384]{1,0:T(8,128)(2,1)S(1)} %get-tuple-element.341), channel_id=1, source_target_pairs={{0,16},{8,24},{16,0},{24,8},{1,17},{9,25},{17,1},{25,9},{2,18},{10... | collective-permute-start | bytes 1769480 | tf_op jit(solution)/shard_map/ppermute | solution.py:595
  113.1 14.5 %collective-permute-start.17 = (bf16[2,192,384]{2,1,0:T(8,128)(2,1)S(1)}, bf16[2,192,384]{2,1,0:T(8,128)(2,1)S(1)}, u32[]{:S(2)}, u32[]{:S(2)}) collective-permute-start(bf16[2,192,384]{2,1,0:T(8,128)(2,1)S(1)} %get-tuple-element.347), channel_id=1, source_target_pairs={{0,4},{1,5},{2,6},{3,7},{4,0},{5,1},{6,2},{7,3},{8,12},{9,13},{10,... | collective-permute-start | bytes 884744 | tf_op jit(solution)/shard_map/ppermute | solution.py:595
  116.4 11.7 %collective-permute-start.18 = (bf16[2,192,384]{2,1,0:T(8,128)(2,1)S(1)}, bf16[2,192,384]{2,1,0:T(8,128)(2,1)S(1)}, u32[]{:S(2)}, u32[]{:S(2)}) collective-permute-start(bf16[2,192,384]{2,1,0:T(8,128)(2,1)S(1)} %get-tuple-element.352), channel_id=1, source_target_pairs={{0,8},{8,0},{16,24},{24,16},{1,9},{9,1},{17,25},{25,17},{2,10},{10... | collective-permute-start | bytes 884744 | tf_op jit(solution)/shard_map/ppermute | solution.py:595
  124.9 16.0 %collective-permute-start.21 = (bf16[416,384]{1,0:T(8,128)(2,1)S(1)}, bf16[416,384]{1,0:T(8,128)(2,1)S(1)}, u32[]{:S(2)}, u32[]{:S(2)}) collective-permute-start(bf16[416,384]{1,0:T(8,128)(2,1)S(1)} %get-tuple-element.361), channel_id=1, source_target_pairs={{0,16},{8,24},{16,0},{24,8},{1,17},{9,25},{17,1},{25,9},{2,18},{10... | collective-permute-start | bytes 958472 | tf_op jit(solution)/shard_map/ppermute | solution.py:595
  126.5 14.4 %collective-permute-start.22 = (bf16[384,384]{1,0:T(8,128)(2,1)S(1)}, bf16[384,384]{1,0:T(8,128)(2,1)S(1)}, u32[]{:S(2)}, u32[]{:S(2)}) collective-permute-start(bf16[384,384]{1,0:T(8,128)(2,1)S(1)} %get-tuple-element.362), channel_id=1, source_target_pairs={{0,8},{8,0},{16,24},{24,16},{1,9},{9,1},{17,25},{25,17},{2,10},{10... | collective-permute-start | bytes 884744 | tf_op jit(solution)/shard_map/ppermute | solution.py:595
  128.8 9.1 %collective-permute-start.20 = (bf16[1,192,384]{2,1,0:T(8,128)(2,1)S(1)}, bf16[1,192,384]{2,1,0:T(8,128)(2,1)S(1)}, u32[]{:S(2)}, u32[]{:S(2)}) collective-permute-start(bf16[1,192,384]{2,1,0:T(8,128)(2,1)S(1)} %get-tuple-element.359), channel_id=1, source_target_pairs={{0,4},{1,5},{2,6},{3,7},{4,0},{5,1},{6,2},{7,3},{8,12},{9,13},{10,... | collective-permute-start | bytes 442376 | tf_op jit(solution)/shard_map/ppermute | solution.py:595
  131.1 6.8 %collective-permute-start.19 = (bf16[1,192,384]{2,1,0:T(8,128)(2,1)S(1)}, bf16[1,192,384]{2,1,0:T(8,128)(2,1)S(1)}, u32[]{:S(2)}, u32[]{:S(2)}) collective-permute-start(bf16[1,192,384]{2,1,0:T(8,128)(2,1)S(1)} %get-tuple-element.357), channel_id=1, source_target_pairs={{0,8},{8,0},{16,24},{24,16},{1,9},{9,1},{17,25},{25,17},{2,10},{10... | collective-permute-start | bytes 442376 | tf_op jit(solution)/shard_map/ppermute | solution.py:595
  138.5 9.4 %collective-permute-start.27 = (bf16[384,384]{1,0:T(8,128)(2,1)S(1)}, bf16[384,384]{1,0:T(8,128)(2,1)S(1)}, u32[]{:S(2)}, u32[]{:S(2)}) collective-permute-start(bf16[384,384]{1,0:T(8,128)(2,1)S(1)} %bitcast.26), channel_id=1, source_target_pairs={{0,8},{8,0},{16,24},{24,16},{1,9},{9,1},{17,25},{25,17},{2,10},{10... | collective-permute-start | bytes 884744 | tf_op jit(solution)/shard_map/ppermute | solution.py:595
  140.2 7.7 %collective-permute-start.23 = (bf16[384,384]{1,0:T(8,128)(2,1)S(1)}, bf16[384,384]{1,0:T(8,128)(2,1)S(1)}, u32[]{:S(2)}, u32[]{:S(2)}) collective-permute-start(bf16[384,384]{1,0:T(8,128)(2,1)S(1)} %bitcast.27), channel_id=1, source_target_pairs={{0,16},{8,24},{16,0},{24,8},{1,17},{9,25},{17,1},{25,9},{2,18},{10... | collective-permute-start | bytes 884744 | tf_op jit(solution)/shard_map/ppermute | solution.py:595
  141.8 8.7 %collective-permute-start.24 = (bf16[208,384]{1,0:T(8,128)(2,1)S(1)}, bf16[208,384]{1,0:T(8,128)(2,1)S(1)}, u32[]{:S(2)}, u32[]{:S(2)}) collective-permute-start(bf16[208,384]{1,0:T(8,128)(2,1)S(1)} %get-tuple-element.371), channel_id=1, source_target_pairs={{0,2},{1,3},{2,0},{3,1},{4,6},{5,7},{6,4},{7,5},{8,10},{9,11},{10,... | collective-permute-start | bytes 479240 | tf_op jit(solution)/shard_map/ppermute | solution.py:595
  142.3 13.3 %collective-permute-start.25 = (bf16[208,384]{1,0:T(8,128)(2,1)S(1)}, bf16[208,384]{1,0:T(8,128)(2,1)S(1)}, u32[]{:S(2)}, u32[]{:S(2)}) collective-permute-start(bf16[208,384]{1,0:T(8,128)(2,1)S(1)} %get-tuple-element.372), channel_id=1, source_target_pairs={{0,4},{1,5},{2,6},{3,7},{4,0},{5,1},{6,2},{7,3},{8,12},{9,13},{10,... | collective-permute-start | bytes 479240 | tf_op jit(solution)/shard_map/ppermute | solution.py:595
  144.9 10.7 %collective-permute-start.26 = (bf16[208,384]{1,0:T(8,128)(2,1)S(1)}, bf16[208,384]{1,0:T(8,128)(2,1)S(1)}, u32[]{:S(2)}, u32[]{:S(2)}) collective-permute-start(bf16[208,384]{1,0:T(8,128)(2,1)S(1)} %get-tuple-element.373), channel_id=1, source_target_pairs={{0,6},{1,7},{2,4},{3,5},{4,2},{5,3},{6,0},{7,1},{8,14},{9,15},{10,... | collective-permute-start | bytes 479240 | tf_op jit(solution)/shard_map/ppermute | solution.py:595
  147.9 12.0 %collective-permute-start.28 = (bf16[384,384]{1,0:T(8,128)(2,1)S(1)}, bf16[384,384]{1,0:T(8,128)(2,1)S(1)}, u32[]{:S(2)}, u32[]{:S(2)}) collective-permute-start(bf16[384,384]{1,0:T(8,128)(2,1)S(1)} %collective-permute-done.27.refs_1_), channel_id=1, source_target_pairs={{0,16},{8,24},{16,0},{24,8},{1,17},{9,25},{17,1},{25,9},{2,18},{10... | collective-permute-start | bytes 884744 | tf_op jit(solution)/shard_map/ppermute | solution.py:595
  155.6 4.3 %copy-start.3 = (f32[96,9280]{1,0:T(8,128)S(1)}, f32[96,9280]{1,0:T(8,128)}, u32[]{:S(2)}) copy-start(f32[96,9280]{1,0:T(8,128)} %refs_8_.1) | copy-start | bytes 10690564
  155.6 4.3 %copy-start.4 = (f32[96,9280]{1,0:T(8,128)S(1)}, f32[96,9280]{1,0:T(8,128)}, u32[]{:S(2)}) copy-start(f32[96,9280]{1,0:T(8,128)} %refs_9_.1) | copy-start | bytes 10690564
  155.6 4.3 %copy-start.5 = (f32[96,9280]{1,0:T(8,128)S(1)}, f32[96,9280]{1,0:T(8,128)}, u32[]{:S(2)}) copy-start(f32[96,9280]{1,0:T(8,128)} %refs_10_.1) | copy-start | bytes 10690564
  155.6 5.1 %copy-start.6 = (f32[96,9280]{1,0:T(8,128)S(1)}, f32[96,9280]{1,0:T(8,128)}, u32[]{:S(2)}) copy-start(f32[96,9280]{1,0:T(8,128)} %refs_11_.1) | copy-start | bytes 10690564
  156.3 12.5 %copy-start.19 = (f32[96,13]{0,1:T(8,128)S(1)}, f32[96,13]{0,1:T(8,128)}, u32[]{:S(2)}) copy-start(f32[96,13]{0,1:T(8,128)} %param.19) | copy-start | bytes 14980
  156.3 12.5 %copy-start.20 = (f32[96,13]{0,1:T(8,128)S(1)}, f32[96,13]{0,1:T(8,128)}, u32[]{:S(2)}) copy-start(f32[96,13]{0,1:T(8,128)} %param.21) | copy-start | bytes 14980
  156.3 12.5 %copy-start.21 = (f32[96,13]{0,1:T(8,128)S(1)}, f32[96,13]{0,1:T(8,128)}, u32[]{:S(2)}) copy-start(f32[96,13]{0,1:T(8,128)} %param.23) | copy-start | bytes 14980
  156.3 12.5 %copy-start.22 = (f32[96,13]{0,1:T(8,128)S(1)}, f32[96,13]{0,1:T(8,128)}, u32[]{:S(2)}) copy-start(f32[96,13]{0,1:T(8,128)} %param.25) | copy-start | bytes 14980
  156.3 12.5 %collective-permute-start.31 = (bf16[208,384]{1,0:T(8,128)(2,1)S(1)}, bf16[208,384]{1,0:T(8,128)(2,1)S(1)}, u32[]{:S(2)}, u32[]{:S(2)}) collective-permute-start(bf16[208,384]{1,0:T(8,128)(2,1)S(1)} %tail_final.1.refs_0_), channel_id=1, source_target_pairs={{0,24},{8,16},{16,8},{24,0},{1,25},{9,17},{17,9},{25,1},{2,26},{10... | collective-permute-start | bytes 479240 | tf_op jit(solution)/shard_map/ppermute | solution.py:595
  158.0 10.8 %collective-permute-start.30 = (bf16[208,384]{1,0:T(8,128)(2,1)S(1)}, bf16[208,384]{1,0:T(8,128)(2,1)S(1)}, u32[]{:S(2)}, u32[]{:S(2)}) collective-permute-start(bf16[208,384]{1,0:T(8,128)(2,1)S(1)} %tail_final.1.refs_0_), channel_id=1, source_target_pairs={{0,16},{8,24},{16,0},{24,8},{1,17},{9,25},{17,1},{25,9},{2,18},{10... | collective-permute-start | bytes 479240 | tf_op jit(solution)/shard_map/ppermute | solution.py:595
  159.1 9.7 %collective-permute-start.29 = (bf16[208,384]{1,0:T(8,128)(2,1)S(1)}, bf16[208,384]{1,0:T(8,128)(2,1)S(1)}, u32[]{:S(2)}, u32[]{:S(2)}) collective-permute-start(bf16[208,384]{1,0:T(8,128)(2,1)S(1)} %tail_final.1.refs_0_), channel_id=1, source_target_pairs={{0,8},{8,0},{16,24},{24,16},{1,9},{9,1},{17,25},{25,17},{2,10},{10... | collective-permute-start | bytes 479240 | tf_op jit(solution)/shard_map/ppermute | solution.py:595

commit v7 on v6

--- a/solution.py
+++ b/solution.py
@@ -724,20 +724,19 @@
     block = D // 8
     count, wq = parts[0].shape[0] // block, parts[0].shape[1]
     step = pl.program_id(0)
-    path, half = jnp.right_shift(step, 1), jnp.bitwise_and(step, 1)
     for k, ref in enumerate(parts):
         quarter = jnp.bitwise_xor(scal[S_SEQ], k)
 
-        @pl.when((jnp.right_shift(quarter, 1) == half) & (step < 2 * count))
+        @pl.when(step < count)
         def _(ref=ref, quarter=quarter):
-            at = pl.multiple_of(jnp.bitwise_and(quarter, 1) * wq, 128)
-            rows = pl.ds(pl.multiple_of(jnp.minimum(path, count - 1) * block, block), block)
+            at = pl.multiple_of(quarter * wq, 128)
+            rows = pl.ds(pl.multiple_of(jnp.minimum(step, count - 1) * block, block), block)
             grad_ref[:, pl.ds(at, wq)] = ref[rows, :].astype(f32)
 
     if has_small:
         vec_outs, small_ref = refs[:6], refs[6]
 
-        @pl.when(step == 2 * count)
+        @pl.when(step == count)
         def _():
             for k, ref in enumerate(parts):
                 quarter = jnp.bitwise_xor(scal[S_SEQ], k)
@@ -762,7 +761,7 @@
     block = D // 8
     count = parts[0].shape[0] // block
     rows, wide = states[0].shape
-    spec = pl.BlockSpec((block, D), lambda i, s: (0, block_of(i)))
+    spec = pl.BlockSpec((block, 2 * D), lambda i, s: (0, block_of(i)))
     anywhere = pl.BlockSpec(memory_space=pl.ANY)
     n_alias = 0 if outs is None else 6
     shapes = [sds((rows, wide), f32)] * 5 + [sds((rows, wide), bf16)]
@@ -778,10 +777,10 @@
         [whole(v.shape) for v in [*parts, *vecs]] + [spec] * 4 + [anywhere] * n_alias,
         shapes,
         out_specs,
-        grid=(2 * count + (1 if vecs else 0),),
+        grid=(count + (1 if vecs else 0),),
         scratch=[pltpu.VMEM((rows, 2 * HD), f32)] if vecs else [],
         aliases={1 + n_before + i: i for i in range(n_alias)},
-        vmem=16,
+        vmem=24,
         name="adam",
     )
 
@@ -1056,11 +1055,11 @@
         last_mine = tail_final(line, last)
         outs = adam_piece(
             line, both_mine, states_m, None,
-            lambda i: jnp.where(jnp.bitwise_and(i, 2) == 0, 8, 4) + 2 * (i // 4) + jnp.bitwise_and(i, 1),
+            lambda i: jnp.where(jnp.bitwise_and(i, 1) == 0, 4, 2) + i // 2,
         )
         last_parts = gather_parts(last_mine)
         outs = adam_piece(
-            line, last_parts, states_m, outs, lambda i: jnp.where(i < 4, i, (4 * D + 2 * FF) // D),
+            line, last_parts, states_m, outs, lambda i: jnp.where(i < 2, i, (4 * D + 2 * FF) // (2 * D)),
             vecs=states_v,
         )
         mats, vecs = outs[:6], [v.T for v in outs[6:]]

time: 175 us -> 173 us (0.989)
  no operation moved by 1% of the time
where the time goes in v7:
time: 173 us
  Pallas kernels  102 us (59%)
  starting transfers between devices  39.4 us (23%)
  waiting for transfers between devices  26.4 us (15%)
  local copies, waits for them, and re-layouts  3.15 us (2%)
  between operations  1.98 us (1%)
    pallas_call x24, Pallas kernels, call(): pl.pallas_call(body, out_shape=tuple((pltpu.HBM(o.shape, o.dtype) if k in...  102 us
    ppermute x32, starting transfers between devices, swap(): return lax.ppermute(value, axis, [(i, i ^ bit) for i in range(size)])  39.4 us
    ppermute x32, waiting for transfers between devices, swap(): return lax.ppermute(value, axis, [(i, i ^ bit) for i in range(size)])  26.4 us
  transfers between devices with their start and end apart: 32, of which 9 were waited for; matrix products, arithmetic and copies ran while one was open for 0% of the time, Pallas kernels for 50%

profile of v7, /device:TPU:0, one launch (start us, length us, event | category | flops | bytes accessed | tf_op | source)
XLA Modules:
  0.0 172.8 jit_solution(18011137094428474643)
XLA Ops:
  1.5 0.7 copy-done.13
  2.2 6.6 %keys.1 = (bf16[512,768]{1,0:T(8,128)(2,1)S(1)}, bf16[768,512]{1,0:T(8,128)(2,1)S(1)}, bf16[1536,512]{1,0:T(8,128)(2,1)S(1)}, bf16[768,512]{1,0:T(8,128)(2,1)S(1)}, bf16[864,128]{1,0:T(8,128)(2,1)S(1)}) custom-call(s32[16]{0:T(128)S(1)} %compare_select_fusion.2.scal, bf16[512,768]{1,0:T(8,128)(2,1)} %x_ref.3, bf16[9280,768]{1,0:T(8,128)(2,1)} %bitcast.44, ...), custom_call_target="tpu_custom_call" | custom-call | bytes 1024 | tf_op jit(solution)/shard_map/keys/pallas_call | solution.py:74
  8.8 4.0 %collective-permute-start.2 = (bf16[864,128]{1,0:T(8,128)(2,1)S(1)}, bf16[864,128]{1,0:T(8,128)(2,1)S(1)}, u32[]{:S(2)}, u32[]{:S(2)}) collective-permute-start(bf16[864,128]{1,0:T(8,128)(2,1)S(1)} %get-tuple-element.230), channel_id=1, source_target_pairs={{0,24},{8,16},{16,8},{24,0},{1,25},{9,17},{17,9},{25,1},{2,26},{10... | collective-permute-start | bytes 663560 | tf_op jit(solution)/shard_map/ppermute | solution.py:595
  12.8 0.5 collective-permute-start.1
  13.4 5.7 %queries.1 = (bf16[4,384,512]{2,1,0:T(8,128)(2,1)S(1)}, bf16[4,384,512]{2,1,0:T(8,128)(2,1)S(1)}, bf16[768,512]{1,0:T(8,128)(2,1)S(1)}, bf16[1536,512]{1,0:T(8,128)(2,1)S(1)}) custom-call(s32[16]{0:T(128)S(1)} %compare_select_fusion.2.scal, bf16[512,768]{1,0:T(8,128)(2,1)S(1)} %get-tuple-element.220.h1_ref, bf16[512,768]{1,0:T(8,128)(2,1)} %g_ref.7, ...), custom_call_target="tpu_custom_call" | custom-call | bytes 1024 | tf_op jit(solution)/shard_map/queries/pallas_call | solution.py:74
  19.1 4.0 %local.1.refs_3_ = f32[864,512]{1,0:T(8,128)S(1)} custom-call(s32[16]{0:T(128)S(1)} %compare_select_fusion.2.scal, bf16[1536,512]{1,0:T(8,128)(2,1)S(1)} %get-tuple-element.226.fq_ref.refs_4_.refs_3_, bf16[1536,512]{1,0:T(8,128)(2,1)S(1)} %get-tuple-element.227.fk_ref.refs_4_, bf16[768,512]{1,0:T(8,128)(2,1)S(1)} %get-tuple-element.228.vt_ref.refs_5_), custom_call_target="tpu_custom_call" | custom-call | bytes 1024 | tf_op jit(solution)/shard_map/local/pallas_call | solution.py:74
  23.2 4.3 %after.1 = (f32[768,512]{1,0:T(8,128)S(1)}, f32[16,512]{1,0:T(8,128)S(1)}, f32[512,768]{1,0:T(8,128)S(1)}, bf16[512,768]{1,0:T(8,128)(2,1)S(1)}, bf16[864,128]{1...) custom-call(s32[16]{0:T(128)S(1)} %compare_select_fusion.2.scal, ...), custom_call_target="tpu_custom_call", output_to_operand_aliasing={{5}: (9, {}), {6}: (10, {})} | custom-call | bytes 1024 | tf_op jit(solution)/shard_map/after/pallas_call | solution.py:74
  27.7 9.1 %mlp.2 = (f32[512,768]{1,0:T(8,128)S(1)}, f32[512,768]{1,0:T(8,128)S(1)}, bf16[2,2,512,768]{3,2,1,0:T(8,128)(2,1)S(1)}, f32[1,1536]{1,0:T(1,128)S(1)}) custom-call(s32[16]{0:T(128)S(1)} %compare_select_fusion.2.scal, bf16[512,768]{1,0:T(8,128)(2,1)S(1)} %get-tuple-element.242.h2_ref, bf16[512,768]{1,0:T(8,128)(2,1)} %g_ref.7, bf16[9280,768]{1,0:T(8,128)(2,1)} %bitcast.50, ...), custom_call_target="tpu_custom_call" | custom-call | bytes 1024 | tf_op jit(solution)/shard_map/mlp/pallas_call | solution.py:74
  36.8 0.6 collective-permute-start.4
  37.4 9.1 %mlp.3 = (f32[512,768]{1,0:T(8,128)S(1)}, f32[512,768]{1,0:T(8,128)S(1)}, bf16[2,2,512,768]{3,2,1,0:T(8,128)(2,1)S(1)}, f32[1,1536]{1,0:T(1,128)S(1)}) custom-call(s32[16]{0:T(128)S(1)} %compare_select_fusion.2.scal, bf16[512,768]{1,0:T(8,128)(2,1)S(1)} %get-tuple-element.242.h2_ref, bf16[512,768]{1,0:T(8,128)(2,1)} %g_ref.7, bf16[9280,768]{1,0:T(8,128)(2,1)} %bitcast.52, ...), custom_call_target="tpu_custom_call" | custom-call | bytes 1024 | tf_op jit(solution)/shard_map/mlp/pallas_call | solution.py:74
  46.6 4.4 %mlp_grads.2 = (bf16[8,192,384]{2,1,0:T(8,128)(2,1)}, bf16[8,192,384]{2,1,0:T(8,128)(2,1)S(1)}) custom-call(s32[16]{0:T(128)S(1)} %compare_select_fusion.2.scal, bf16[4,384,512]{2,1,0:T(8,128)(2,1)S(1)} %get-tuple-element.258.refs_0_.refs_6_.refs_2_, bf16[4,384,512]{2,1,0:T(8,128)(2,1)S(1)} %collective-permute-done.3.refs_1_.refs_7_.refs_3_, ...), custom_call_target="tpu_custom_call" | custom-call | bytes 1024 | tf_op jit(solution)/shard_map/mlp_grads/pallas_call | solution.py:74
  51.0 2.0 %collective-permute-start.9 = (bf16[8,192,384]{2,1,0:T(8,128)(2,1)}, bf16[8,192,384]{2,1,0:T(8,128)(2,1)}, u32[]{:S(2)}, u32[]{:S(2)}) collective-permute-start(bf16[8,192,384]{2,1,0:T(8,128)(2,1)} %get-tuple-element.311), channel_id=1, source_target_pairs={{0,2},{1,3},{2,0},{3,1},{4,6},{5,7},{6,4},{7,5},{8,10},{9,11},{10,... | collective-permute-start | bytes 3538952 | tf_op jit(solution)/shard_map/ppermute | solution.py:595
  53.0 6.6 %back.1 = (bf16[512,768]{1,0:T(8,128)(2,1)}, f32[512,768]{1,0:T(8,128)}, bf16[768,512]{1,0:T(8,128)(2,1)}, bf16[864,512]{1,0:T(8,128)(2,1)}, bf16[864,128]{1,0:T(8,128)(2,1)}, /*index=5*/f32[4,768]{1,0:T(4,128)S(1)}) custom-call(s32[16]{0:T(128)S(1)} %compare_select_fusion.2.scal, f32[512,768]{1,0:T(8,128)S(1)} %get-tuple-element.266.out_ref, ...), custom_call_target="tpu_custom_call" | custom-call | bytes 1024 | tf_op jit(solution)/shard_map/back/pallas_call | solution.py:74
  59.6 2.5 %collective-permute-start.8 = (bf16[864,128]{1,0:T(8,128)(2,1)}, bf16[864,128]{1,0:T(8,128)(2,1)}, u32[]{:S(2)}, u32[]{:S(2)}) collective-permute-start(bf16[864,128]{1,0:T(8,128)(2,1)} %get-tuple-element.284), channel_id=1, source_target_pairs={{0,24},{8,16},{16,8},{24,0},{1,25},{9,17},{17,9},{25,1},{2,26},{10... | collective-permute-start | bytes 663560 | tf_op jit(solution)/shard_map/ppermute | solution.py:595
  62.1 0.5 collective-permute-start.7
  62.7 0.5 collective-permute-start.6
  63.2 1.4 copy-done.1
  64.6 5.8 %mlp_grads.3 = (bf16[8,192,384]{2,1,0:T(8,128)(2,1)S(1)}, bf16[8,192,384]{2,1,0:T(8,128)(2,1)S(1)}) custom-call(s32[16]{0:T(128)S(1)} %compare_select_fusion.2.scal, bf16[4,384,512]{2,1,0:T(8,128)(2,1)S(1)} %get-tuple-element.258.refs_0_.refs_6_.refs_2_, bf16[4,384,512]{2,1,0:T(8,128)(2,1)S(1)} %copy-done.1, bf16[2,2,512,768]{3,2,1,0:T(8,128)(2,1)} %copy-done.7, ...), custom_call_target="tpu_custom_call" | custom-call | bytes 1024 | tf_op jit(solution)/shard_map/mlp_grads/pallas_call | solution.py:74
  70.5 1.6 collective-permute-start.10
  72.1 1.2 collective-permute-done.7.refs_1_
  73.3 12.3 %attend_back.1 = (bf16[4,768,512]{2,1,0:T(8,128)(2,1)S(1)}, f32[768,64]{1,0:T(8,128)S(1)}, f32[768,3]{1,0:T(8,128)S(1)}) custom-call(s32[16]{0:T(128)S(1)} %compare_select_fusion.2.scal, bf16[864,128]{1,0:T(8,128)(2,1)} %collective-permute-done.6.refs_0_, bf16[864,128]{1,0:T(8,128)(2,1)} %collective-permute-done.7.refs_1_, ...), custom_call_target="tpu_custom_call" | custom-call | flops 1000000000 | bytes 1024 | tf_op jit(solution)/shard_map/attend_back/pallas_call | solution.py:74
  85.7 7.8 %input.1 = (bf16[512,768]{1,0:T(8,128)(2,1)}, f32[1,384,128]{2,1,0:T(8,128)S(1)}, f32[1,384,128]{2,1,0:T(8,128)S(1)}) custom-call(s32[16]{0:T(128)S(1)} %compare_select_fusion.2.scal, bf16[4,768,512]{2,1,0:T(8,128)(2,1)S(1)} %get-tuple-element.298.dp_ref, bf16[9280,768]{1,0:T(8,128)(2,1)} %bitcast.56, bf16[512,768]{1,0:T(8,128)(2,1)} %x_ref.3, ...), custom_call_target="tpu_custom_call" | custom-call | bytes 1024 | tf_op jit(solution)/shard_map/input/pallas_call | solution.py:74
  93.5 0.5 collective-permute-start.12
  94.0 2.1 %halve.6 = (bf16[4,192,384]{2,1,0:T(8,128)(2,1)S(1)}, bf16[4,192,384]{2,1,0:T(8,128)(2,1)S(1)}) custom-call(s32[16]{0:T(128)S(1)} %compare_select_fusion.2.scal, bf16[8,192,384]{2,1,0:T(8,128)(2,1)S(1)} %copy-done.24, bf16[8,192,384]{2,1,0:T(8,128)(2,1)} %collective-permute-done.9.recv_ref), custom_call_target="tpu_custom_call" | custom-call | flops 14000000000 | bytes 1024 | tf_op jit(solution)/shard_map/halve/pallas_call | solution.py:74
  96.1 1.6 collective-permute-start.13
  97.7 0.6 collective-permute-done.10.recv_ref
  98.3 0.8 halve.7
  99.2 1.2 collective-permute-start.14
  100.4 5.7 %tail_grads.1 = (bf16[832,384]{1,0:T(8,128)(2,1)S(1)}, bf16[768,384]{1,0:T(8,128)(2,1)S(1)}, bf16[768,384]{1,0:T(8,128)(2,1)S(1)}, bf16[768,384]{1,0:T(8,128)(2,1)S(1)}, f32[64,384]{1,0:T(8,128)S(1)}) custom-call(s32[16]{0:T(128)S(1)} %compare_select_fusion.2.scal, bf16[4,384,512]{2,1,0:T(8,128)(2,1)S(1)} %get-tuple-element.258.refs_0_.refs_6_.refs_2_, ...), custom_call_target="tpu_custom_call" | custom-call | flops 8999999488 | bytes 1024 | tf_op jit(solution)/shard_map/tail_grads/pallas_call | solution.py:74
  106.1 1.6 collective-permute-start.15
  107.6 0.9 collective-permute-start.16
  108.6 3.8 %collective-permute-done.13.recv_ref = bf16[4,192,384]{2,1,0:T(8,128)(2,1)S(1)} collective-permute-done((bf16[4,192,384]{2,1,0:T(8,128)(2,1)S(1)}, bf16[4,192,384]{2,1,0:T(8,128)(2,1)S(1)}, u32[]{:S(2)}, u32[]{:S(2)}) %collective-permute-start.13) | collective-permute-done | bytes 589856 | tf_op jit(solution)/shard_map/ppermute | solution.py:595
  112.4 0.7 halve.8
  113.1 2.7 %collective-permute-start.17 = (bf16[2,192,384]{2,1,0:T(8,128)(2,1)S(1)}, bf16[2,192,384]{2,1,0:T(8,128)(2,1)S(1)}, u32[]{:S(2)}, u32[]{:S(2)}) collective-permute-start(bf16[2,192,384]{2,1,0:T(8,128)(2,1)S(1)} %get-tuple-element.347), channel_id=1, source_target_pairs={{0,4},{1,5},{2,6},{3,7},{4,0},{5,1},{6,2},{7,3},{8,12},{9,13},{10,... | collective-permute-start | bytes 884744 | tf_op jit(solution)/shard_map/ppermute | solution.py:595
  115.7 0.7 halve.9
  116.4 1.5 collective-permute-start.18
  118.0 6.1 %collective-permute-done.16.recv_b = bf16[768,384]{1,0:T(8,128)(2,1)S(1)} collective-permute-done((bf16[768,384]{1,0:T(8,128)(2,1)S(1)}, bf16[768,384]{1,0:T(8,128)(2,1)S(1)}, u32[]{:S(2)}, u32[]{:S(2)}) %collective-permute-start.16) | collective-permute-done | bytes 589856 | tf_op jit(solution)/shard_map/ppermute | solution.py:595
  124.1 0.8 tail_one.1
  124.9 1.6 collective-permute-start.21
  126.5 0.7 collective-permute-start.22
  127.2 0.3 collective-permute-done.17.recv_ref
  127.5 0.6 halve.10
  128.1 0.6 halve.11
  128.8 2.3 %collective-permute-start.20 = (bf16[1,192,384]{2,1,0:T(8,128)(2,1)S(1)}, bf16[1,192,384]{2,1,0:T(8,128)(2,1)S(1)}, u32[]{:S(2)}, u32[]{:S(2)}) collective-permute-start(bf16[1,192,384]{2,1,0:T(8,128)(2,1)S(1)} %get-tuple-element.359), channel_id=1, source_target_pairs={{0,4},{1,5},{2,6},{3,7},{4,0},{5,1},{6,2},{7,3},{8,12},{9,13},{10,... | collective-permute-start | bytes 442376 | tf_op jit(solution)/shard_map/ppermute | solution.py:595
  131.1 1.3 collective-permute-start.19
  132.4 5.4 %collective-permute-done.20.refs_3_ = bf16[1,192,384]{2,1,0:T(8,128)(2,1)S(1)} collective-permute-done((bf16[1,192,384]{2,1,0:T(8,128)(2,1)S(1)}, bf16[1,192,384]{2,1,0:T(8,128)(2,1)S(1)}, u32[]{:S(2)}, u32[]{:S(2)}) %collective-permute-start.20) | collective-permute-done | bytes 147488 | tf_op jit(solution)/shard_map/ppermute | solution.py:595
  137.9 0.6 final.1
  138.5 1.7 collective-permute-start.27
  140.2 0.7 collective-permute-start.23
  140.9 0.9 tail_two.1
  141.8 0.5 collective-permute-start.24
  142.3 2.6 %collective-permute-start.25 = (bf16[208,384]{1,0:T(8,128)(2,1)S(1)}, bf16[208,384]{1,0:T(8,128)(2,1)S(1)}, u32[]{:S(2)}, u32[]{:S(2)}) collective-permute-start(bf16[208,384]{1,0:T(8,128)(2,1)S(1)} %get-tuple-element.372), channel_id=1, source_target_pairs={{0,4},{1,5},{2,6},{3,7},{4,0},{5,1},{6,2},{7,3},{8,12},{9,13},{10,... | collective-permute-start | bytes 479240 | tf_op jit(solution)/shard_map/ppermute | solution.py:595
  144.9 1.4 collective-permute-start.26
  146.2 1.7 collective-permute-done.23.refs_2_
  147.9 0.6 collective-permute-start.28
  148.5 2.0 %collective-permute-done.24.refs_1_ = bf16[208,384]{1,0:T(8,128)(2,1)S(1)} collective-permute-done((bf16[208,384]{1,0:T(8,128)(2,1)S(1)}, bf16[208,384]{1,0:T(8,128)(2,1)S(1)}, u32[]{:S(2)}, u32[]{:S(2)}) %collective-permute-start.24) | collective-permute-done | bytes 159776 | tf_op jit(solution)/shard_map/ppermute | solution.py:595
  150.5 5.1 %collective-permute-done.25.refs_2_ = bf16[208,384]{1,0:T(8,128)(2,1)S(1)} collective-permute-done((bf16[208,384]{1,0:T(8,128)(2,1)S(1)}, bf16[208,384]{1,0:T(8,128)(2,1)S(1)}, u32[]{:S(2)}, u32[]{:S(2)}) %collective-permute-start.25) | collective-permute-done | bytes 159776 | tf_op jit(solution)/shard_map/ppermute | solution.py:595
  155.6 0.6 tail_final.1.refs_0_
  156.3 1.7 collective-permute-start.31
  158.0 1.1 collective-permute-start.30
  159.1 0.7 collective-permute-start.29
  159.9 0.9 copy-done.6
  160.8 6.9 %adam.2 = (f32[96,9280]{1,0:T(8,128)}, f32[96,9280]{1,0:T(8,128)}, f32[96,9280]{1,0:T(8,128)}, f32[96,9280]{1,0:T(8,128)}, f32[96,9280]{1,0:T(8,128)}, /*index=5*/bf16[96,9280]{1,0:T(8,128)(2,1)}) custom-call(s32[16]{0:T(128)S(1)} %compare_select_fusion.2.scal, bf16[384,384]{1,0:T(8,128)(2,1)S(1)} %bitcast.28, ...), custom_call_target="tpu_custom_call" | custom-call | bytes 1024 | tf_op jit(solution)/shard_map/adam/pallas_call | solution.py:74
  167.7 4.9 %adam.3 = (f32[96,9280]{1,0:T(8,128)}, f32[96,9280]{1,0:T(8,128)}, f32[96,9280]{1,0:T(8,128)}, f32[96,9280]{1,0:T(8,128)}, f32[96,9280]{1,0:T(8,128)}, /*index=5...) custom-call(s32[16]{0:T(128)S(1)} %compare_select_fusion.2.scal, ...), custom_call_target="tpu_custom_call", output_to_operand_aliasing={{0}: (13, {}), {1}: (14, {}), {2}: (15, {}), {3}: (16, {}),... | custom-call | bytes 1024 | tf_op jit(solution)/shard_map/adam/pallas_call | solution.py:74
  (81 shorter events, 0.8 us)
Async XLA Ops:
  1.5 0.7 copy-start.13
  8.8 10.3 %copy-start.15 = (bf16[768,512]{1,0:T(8,128)(2,1)}, bf16[768,512]{1,0:T(8,128)(2,1)S(1)}, u32[]{:S(2)}) copy-start(bf16[768,512]{1,0:T(8,128)(2,1)S(1)} %get-tuple-element.292.refs_9_) | copy-start | bytes 2359300
  8.8 10.3 %copy-start.8 = (bf16[1536,512]{1,0:T(8,128)(2,1)}, bf16[1536,512]{1,0:T(8,128)(2,1)S(1)}, u32[]{:S(2)}) copy-start(bf16[1536,512]{1,0:T(8,128)(2,1)S(1)} %get-tuple-element.227.fk_ref.refs_4_) | copy-start | bytes 4718596
  8.8 10.3 %copy-start.10 = (bf16[768,512]{1,0:T(8,128)(2,1)}, bf16[768,512]{1,0:T(8,128)(2,1)S(1)}, u32[]{:S(2)}) copy-start(bf16[768,512]{1,0:T(8,128)(2,1)S(1)} %get-tuple-element.228.vt_ref.refs_5_) | copy-start | bytes 2359300
  8.8 14.4 %collective-permute-start.2 = (bf16[864,128]{1,0:T(8,128)(2,1)S(1)}, bf16[864,128]{1,0:T(8,128)(2,1)S(1)}, u32[]{:S(2)}, u32[]{:S(2)}) collective-permute-start(bf16[864,128]{1,0:T(8,128)(2,1)S(1)} %get-tuple-element.230), channel_id=1, source_target_pairs={{0,24},{8,16},{16,8},{24,0},{1,25},{9,17},{17,9},{25,1},{2,26},{10... | collective-permute-start | bytes 663560 | tf_op jit(solution)/shard_map/ppermute | solution.py:595
  12.8 10.4 %collective-permute-start.1 = (bf16[864,128]{1,0:T(8,128)(2,1)S(1)}, bf16[864,128]{1,0:T(8,128)(2,1)S(1)}, u32[]{:S(2)}, u32[]{:S(2)}) collective-permute-start(bf16[864,128]{1,0:T(8,128)(2,1)S(1)} %get-tuple-element.230), channel_id=1, source_target_pairs={{0,16},{8,24},{16,0},{24,8},{1,17},{9,25},{17,1},{25,9},{2,18},{10... | collective-permute-start | bytes 663560 | tf_op jit(solution)/shard_map/ppermute | solution.py:595
  13.3 9.9 %collective-permute-start = (bf16[864,128]{1,0:T(8,128)(2,1)S(1)}, bf16[864,128]{1,0:T(8,128)(2,1)S(1)}, u32[]{:S(2)}, u32[]{:S(2)}) collective-permute-start(bf16[864,128]{1,0:T(8,128)(2,1)S(1)} %get-tuple-element.230), channel_id=1, source_target_pairs={{0,8},{8,0},{16,24},{24,16},{1,9},{9,1},{17,25},{25,17},{2,10},{10... | collective-permute-start | bytes 663560 | tf_op jit(solution)/shard_map/ppermute | solution.py:595
  19.1 4.1 %copy-start.17 = (bf16[768,512]{1,0:T(8,128)(2,1)}, bf16[768,512]{1,0:T(8,128)(2,1)S(1)}, u32[]{:S(2)}) copy-start(bf16[768,512]{1,0:T(8,128)(2,1)S(1)} %get-tuple-element.291.refs_8_) | copy-start | bytes 2359300
  27.6 9.8 %collective-permute-start.3 = (bf16[4,384,512]{2,1,0:T(8,128)(2,1)S(1)}, bf16[4,384,512]{2,1,0:T(8,128)(2,1)S(1)}, u32[]{:S(2)}, u32[]{:S(2)}) collective-permute-start(bf16[4,384,512]{2,1,0:T(8,128)(2,1)S(1)} %get-tuple-element.249), channel_id=1, source_target_pairs={{0,1},{1,0},{2,3},{3,2},{4,5},{5,4},{6,7},{7,6},{8,9},{9,8},{10,11... | collective-permute-start | bytes 4718600 | tf_op jit(solution)/shard_map/ppermute | solution.py:595
  36.8 9.8 %collective-permute-start.4 = (bf16[2,2,512,768]{3,2,1,0:T(8,128)(2,1)S(1)}, bf16[2,2,512,768]{3,2,1,0:T(8,128)(2,1)S(1)}, u32[]{:S(2)}, u32[]{:S(2)}) collective-permute-start(bf16[2,2,512,768]{3,2,1,0:T(8,128)(2,1)S(1)} %get-tuple-element.260.refs_2_.refs_4_), channel_id=1, source_target_pairs={{0,1},{1,0},{2,3},{3,2},{4,5},{5,4},{6,7},{7,6},{8,9},{9,8},{10,11... | collective-permute-start | bytes 9437192 | tf_op jit(solution)/shard_map/ppermute | solution.py:595
  37.4 9.3 %copy-start = (bf16[4,384,512]{2,1,0:T(8,128)(2,1)}, bf16[4,384,512]{2,1,0:T(8,128)(2,1)S(1)}, u32[]{:S(2)}) copy-start(bf16[4,384,512]{2,1,0:T(8,128)(2,1)S(1)} %collective-permute-done.3.refs_1_.refs_7_.refs_3_) | copy-start | bytes 4718596
  46.5 4.5 %copy-start.7 = (bf16[2,2,512,768]{3,2,1,0:T(8,128)(2,1)}, bf16[2,2,512,768]{3,2,1,0:T(8,128)(2,1)S(1)}, u32[]{:S(2)}) copy-start(bf16[2,2,512,768]{3,2,1,0:T(8,128)(2,1)S(1)} %get-tuple-element.279.refs_2_.refs_4_) | copy-start | bytes 9437188
  46.5 6.5 %copy-start.14 = (bf16[768,13]{0,1:T(8,128)(2,1)S(1)}, bf16[768,13]{0,1:T(8,128)(2,1)}, u32[]{:S(2)}) copy-start(bf16[768,13]{0,1:T(8,128)(2,1)} %param.17) | copy-start | bytes 59908
  46.5 6.5 %collective-permute-start.5 = (bf16[2,2,512,768]{3,2,1,0:T(8,128)(2,1)S(1)}, bf16[2,2,512,768]{3,2,1,0:T(8,128)(2,1)S(1)}, u32[]{:S(2)}, u32[]{:S(2)}) collective-permute-start(bf16[2,2,512,768]{3,2,1,0:T(8,128)(2,1)S(1)} %get-tuple-element.279.refs_2_.refs_4_), channel_id=1, source_target_pairs={{0,1},{1,0},{2,3},{3,2},{4,5},{5,4},{6,7},{7,6},{8,9},{9,8},{10,11... | collective-permute-start | bytes 9437192 | tf_op jit(solution)/shard_map/ppermute | solution.py:595
  51.0 8.6 %copy-start.23 = (bf16[8,192,384]{2,1,0:T(8,128)(2,1)}, bf16[8,192,384]{2,1,0:T(8,128)(2,1)S(1)}, u32[]{:S(2)}) copy-start(bf16[8,192,384]{2,1,0:T(8,128)(2,1)S(1)} %get-tuple-element.310.keep_ref) | copy-start | bytes 3538948
  51.0 43.0 %collective-permute-start.9 = (bf16[8,192,384]{2,1,0:T(8,128)(2,1)}, bf16[8,192,384]{2,1,0:T(8,128)(2,1)}, u32[]{:S(2)}, u32[]{:S(2)}) collective-permute-start(bf16[8,192,384]{2,1,0:T(8,128)(2,1)} %get-tuple-element.311), channel_id=1, source_target_pairs={{0,2},{1,3},{2,0},{3,1},{4,6},{5,7},{6,4},{7,5},{8,10},{9,11},{10,... | collective-permute-start | bytes 3538952 | tf_op jit(solution)/shard_map/ppermute | solution.py:595
  53.0 6.7 %copy-start.25 = (bf16[2,2,512,768]{3,2,1,0:T(8,128)(2,1)}, bf16[2,2,512,768]{3,2,1,0:T(8,128)(2,1)S(1)}, u32[]{:S(2)}) copy-start(bf16[2,2,512,768]{3,2,1,0:T(8,128)(2,1)S(1)} %collective-permute-done.5.refs_3_.refs_5_) | copy-start | bytes 9437188
  59.6 12.4 %collective-permute-start.8 = (bf16[864,128]{1,0:T(8,128)(2,1)}, bf16[864,128]{1,0:T(8,128)(2,1)}, u32[]{:S(2)}, u32[]{:S(2)}) collective-permute-start(bf16[864,128]{1,0:T(8,128)(2,1)} %get-tuple-element.284), channel_id=1, source_target_pairs={{0,24},{8,16},{16,8},{24,0},{1,25},{9,17},{17,9},{25,1},{2,26},{10... | collective-permute-start | bytes 663560 | tf_op jit(solution)/shard_map/ppermute | solution.py:595
  62.1 11.1 %collective-permute-start.7 = (bf16[864,128]{1,0:T(8,128)(2,1)}, bf16[864,128]{1,0:T(8,128)(2,1)}, u32[]{:S(2)}, u32[]{:S(2)}) collective-permute-start(bf16[864,128]{1,0:T(8,128)(2,1)} %get-tuple-element.284), channel_id=1, source_target_pairs={{0,16},{8,24},{16,0},{24,8},{1,17},{9,25},{17,1},{25,9},{2,18},{10... | collective-permute-start | bytes 663560 | tf_op jit(solution)/shard_map/ppermute | solution.py:595
  62.7 10.6 %collective-permute-start.6 = (bf16[864,128]{1,0:T(8,128)(2,1)}, bf16[864,128]{1,0:T(8,128)(2,1)}, u32[]{:S(2)}, u32[]{:S(2)}) collective-permute-start(bf16[864,128]{1,0:T(8,128)(2,1)} %get-tuple-element.284), channel_id=1, source_target_pairs={{0,8},{8,0},{16,24},{24,16},{1,9},{9,1},{17,25},{25,17},{2,10},{10... | collective-permute-start | bytes 663560 | tf_op jit(solution)/shard_map/ppermute | solution.py:595
  63.2 1.4 copy-start.1
  64.6 8.6 %copy-start.9 = (bf16[1536,512]{1,0:T(8,128)(2,1)S(1)}, bf16[1536,512]{1,0:T(8,128)(2,1)}, u32[]{:S(2)}) copy-start(bf16[1536,512]{1,0:T(8,128)(2,1)} %copy-done.8) | copy-start | bytes 4718596
  64.6 8.6 %copy-start.11 = (bf16[768,512]{1,0:T(8,128)(2,1)S(1)}, bf16[768,512]{1,0:T(8,128)(2,1)}, u32[]{:S(2)}) copy-start(bf16[768,512]{1,0:T(8,128)(2,1)} %copy-done.10) | copy-start | bytes 2359300
  64.6 8.6 %copy-start.16 = (bf16[768,512]{1,0:T(8,128)(2,1)S(1)}, bf16[768,512]{1,0:T(8,128)(2,1)}, u32[]{:S(2)}) copy-start(bf16[768,512]{1,0:T(8,128)(2,1)} %copy-done.15) | copy-start | bytes 2359300
  64.6 8.6 %copy-start.18 = (bf16[768,512]{1,0:T(8,128)(2,1)S(1)}, bf16[768,512]{1,0:T(8,128)(2,1)}, u32[]{:S(2)}) copy-start(bf16[768,512]{1,0:T(8,128)(2,1)} %copy-done.17) | copy-start | bytes 2359300
  70.5 15.2 %copy-start.12 = (f32[512,768]{1,0:T(8,128)S(1)}, f32[512,768]{1,0:T(8,128)}, u32[]{:S(2)}) copy-start(f32[512,768]{1,0:T(8,128)} %get-tuple-element.299.dr_ref) | copy-start | bytes 4718596
  70.5 27.9 %collective-permute-start.10 = (bf16[8,192,384]{2,1,0:T(8,128)(2,1)S(1)}, bf16[8,192,384]{2,1,0:T(8,128)(2,1)S(1)}, u32[]{:S(2)}, u32[]{:S(2)}) collective-permute-start(bf16[8,192,384]{2,1,0:T(8,128)(2,1)S(1)} %get-tuple-element.316), channel_id=1, source_target_pairs={{0,16},{8,24},{16,0},{24,8},{1,17},{9,25},{17,1},{25,9},{2,18},{10... | collective-permute-start | bytes 3538952 | tf_op jit(solution)/shard_map/ppermute | solution.py:595
  85.6 8.4 %copy-start.24 = (bf16[8,192,384]{2,1,0:T(8,128)(2,1)S(1)}, bf16[8,192,384]{2,1,0:T(8,128)(2,1)}, u32[]{:S(2)}) copy-start(bf16[8,192,384]{2,1,0:T(8,128)(2,1)} %copy-done.23) | copy-start | bytes 3538948
  85.6 14.8 %collective-permute-start.11 = (bf16[4,768,512]{2,1,0:T(8,128)(2,1)S(1)}, bf16[4,768,512]{2,1,0:T(8,128)(2,1)S(1)}, u32[]{:S(2)}, u32[]{:S(2)}) collective-permute-start(bf16[4,768,512]{2,1,0:T(8,128)(2,1)S(1)} %get-tuple-element.298.dp_ref), channel_id=1, source_target_pairs={{0,1},{1,0},{2,3},{3,2},{4,5},{5,4},{6,7},{7,6},{8,9},{9,8},{10,11... | collective-permute-start | bytes 9437192 | tf_op jit(solution)/shard_map/ppermute | solution.py:595
  93.5 6.9 %collective-permute-start.12 = (f32[1,384,128]{2,1,0:T(8,128)S(1)}, f32[1,384,128]{2,1,0:T(8,128)S(1)}, u32[]{:S(2)}, u32[]{:S(2)}) collective-permute-start(f32[1,384,128]{2,1,0:T(8,128)S(1)} %get-tuple-element.321), channel_id=1, source_target_pairs={{0,1},{1,0},{2,3},{3,2},{4,5},{5,4},{6,7},{7,6},{8,9},{9,8},{10,11... | collective-permute-start | bytes 589832 | tf_op jit(solution)/shard_map/ppermute | solution.py:595
  96.1 4.3 %copy-start.2 = (bf16[4,384,512]{2,1,0:T(8,128)(2,1)S(1)}, bf16[4,384,512]{2,1,0:T(8,128)(2,1)}, u32[]{:S(2)}) copy-start(bf16[4,384,512]{2,1,0:T(8,128)(2,1)} %copy-done) | copy-start | bytes 4718596
  96.1 16.3 %collective-permute-start.13 = (bf16[4,192,384]{2,1,0:T(8,128)(2,1)S(1)}, bf16[4,192,384]{2,1,0:T(8,128)(2,1)S(1)}, u32[]{:S(2)}, u32[]{:S(2)}) collective-permute-start(bf16[4,192,384]{2,1,0:T(8,128)(2,1)S(1)} %get-tuple-element.329), channel_id=1, source_target_pairs={{0,16},{8,24},{16,0},{24,8},{1,17},{9,25},{17,1},{25,9},{2,18},{10... | collective-permute-start | bytes 1769480 | tf_op jit(solution)/shard_map/ppermute | solution.py:595
  99.2 16.6 %collective-permute-start.14 = (bf16[4,192,384]{2,1,0:T(8,128)(2,1)S(1)}, bf16[4,192,384]{2,1,0:T(8,128)(2,1)S(1)}, u32[]{:S(2)}, u32[]{:S(2)}) collective-permute-start(bf16[4,192,384]{2,1,0:T(8,128)(2,1)S(1)} %get-tuple-element.334), channel_id=1, source_target_pairs={{0,2},{1,3},{2,0},{3,1},{4,6},{5,7},{6,4},{7,5},{8,10},{9,11},{10,... | collective-permute-start | bytes 1769480 | tf_op jit(solution)/shard_map/ppermute | solution.py:595
  106.1 18.0 %collective-permute-start.15 = (bf16[832,384]{1,0:T(8,128)(2,1)S(1)}, bf16[832,384]{1,0:T(8,128)(2,1)S(1)}, u32[]{:S(2)}, u32[]{:S(2)}) collective-permute-start(bf16[832,384]{1,0:T(8,128)(2,1)S(1)} %get-tuple-element.339), channel_id=1, source_target_pairs={{0,8},{8,0},{16,24},{24,16},{1,9},{9,1},{17,25},{25,17},{2,10},{10... | collective-permute-start | bytes 1916936 | tf_op jit(solution)/shard_map/ppermute | solution.py:595
  107.6 16.4 %collective-permute-start.16 = (bf16[768,384]{1,0:T(8,128)(2,1)S(1)}, bf16[768,384]{1,0:T(8,128)(2,1)S(1)}, u32[]{:S(2)}, u32[]{:S(2)}) collective-permute-start(bf16[768,384]{1,0:T(8,128)(2,1)S(1)} %get-tuple-element.341), channel_id=1, source_target_pairs={{0,16},{8,24},{16,0},{24,8},{1,17},{9,25},{17,1},{25,9},{2,18},{10... | collective-permute-start | bytes 1769480 | tf_op jit(solution)/shard_map/ppermute | solution.py:595
  113.1 14.5 %collective-permute-start.17 = (bf16[2,192,384]{2,1,0:T(8,128)(2,1)S(1)}, bf16[2,192,384]{2,1,0:T(8,128)(2,1)S(1)}, u32[]{:S(2)}, u32[]{:S(2)}) collective-permute-start(bf16[2,192,384]{2,1,0:T(8,128)(2,1)S(1)} %get-tuple-element.347), channel_id=1, source_target_pairs={{0,4},{1,5},{2,6},{3,7},{4,0},{5,1},{6,2},{7,3},{8,12},{9,13},{10,... | collective-permute-start | bytes 884744 | tf_op jit(solution)/shard_map/ppermute | solution.py:595
  116.4 11.7 %collective-permute-start.18 = (bf16[2,192,384]{2,1,0:T(8,128)(2,1)S(1)}, bf16[2,192,384]{2,1,0:T(8,128)(2,1)S(1)}, u32[]{:S(2)}, u32[]{:S(2)}) collective-permute-start(bf16[2,192,384]{2,1,0:T(8,128)(2,1)S(1)} %get-tuple-element.352), channel_id=1, source_target_pairs={{0,8},{8,0},{16,24},{24,16},{1,9},{9,1},{17,25},{25,17},{2,10},{10... | collective-permute-start | bytes 884744 | tf_op jit(solution)/shard_map/ppermute | solution.py:595
  124.9 16.0 %collective-permute-start.21 = (bf16[416,384]{1,0:T(8,128)(2,1)S(1)}, bf16[416,384]{1,0:T(8,128)(2,1)S(1)}, u32[]{:S(2)}, u32[]{:S(2)}) collective-permute-start(bf16[416,384]{1,0:T(8,128)(2,1)S(1)} %get-tuple-element.361), channel_id=1, source_target_pairs={{0,16},{8,24},{16,0},{24,8},{1,17},{9,25},{17,1},{25,9},{2,18},{10... | collective-permute-start | bytes 958472 | tf_op jit(solution)/shard_map/ppermute | solution.py:595
  126.5 14.4 %collective-permute-start.22 = (bf16[384,384]{1,0:T(8,128)(2,1)S(1)}, bf16[384,384]{1,0:T(8,128)(2,1)S(1)}, u32[]{:S(2)}, u32[]{:S(2)}) collective-permute-start(bf16[384,384]{1,0:T(8,128)(2,1)S(1)} %get-tuple-element.362), channel_id=1, source_target_pairs={{0,8},{8,0},{16,24},{24,16},{1,9},{9,1},{17,25},{25,17},{2,10},{10... | collective-permute-start | bytes 884744 | tf_op jit(solution)/shard_map/ppermute | solution.py:595
  128.8 9.1 %collective-permute-start.20 = (bf16[1,192,384]{2,1,0:T(8,128)(2,1)S(1)}, bf16[1,192,384]{2,1,0:T(8,128)(2,1)S(1)}, u32[]{:S(2)}, u32[]{:S(2)}) collective-permute-start(bf16[1,192,384]{2,1,0:T(8,128)(2,1)S(1)} %get-tuple-element.359), channel_id=1, source_target_pairs={{0,4},{1,5},{2,6},{3,7},{4,0},{5,1},{6,2},{7,3},{8,12},{9,13},{10,... | collective-permute-start | bytes 442376 | tf_op jit(solution)/shard_map/ppermute | solution.py:595
  131.1 6.8 %collective-permute-start.19 = (bf16[1,192,384]{2,1,0:T(8,128)(2,1)S(1)}, bf16[1,192,384]{2,1,0:T(8,128)(2,1)S(1)}, u32[]{:S(2)}, u32[]{:S(2)}) collective-permute-start(bf16[1,192,384]{2,1,0:T(8,128)(2,1)S(1)} %get-tuple-element.357), channel_id=1, source_target_pairs={{0,8},{8,0},{16,24},{24,16},{1,9},{9,1},{17,25},{25,17},{2,10},{10... | collective-permute-start | bytes 442376 | tf_op jit(solution)/shard_map/ppermute | solution.py:595
  138.5 9.4 %collective-permute-start.27 = (bf16[384,384]{1,0:T(8,128)(2,1)S(1)}, bf16[384,384]{1,0:T(8,128)(2,1)S(1)}, u32[]{:S(2)}, u32[]{:S(2)}) collective-permute-start(bf16[384,384]{1,0:T(8,128)(2,1)S(1)} %bitcast.26), channel_id=1, source_target_pairs={{0,8},{8,0},{16,24},{24,16},{1,9},{9,1},{17,25},{25,17},{2,10},{10... | collective-permute-start | bytes 884744 | tf_op jit(solution)/shard_map/ppermute | solution.py:595
  140.2 7.7 %collective-permute-start.23 = (bf16[384,384]{1,0:T(8,128)(2,1)S(1)}, bf16[384,384]{1,0:T(8,128)(2,1)S(1)}, u32[]{:S(2)}, u32[]{:S(2)}) collective-permute-start(bf16[384,384]{1,0:T(8,128)(2,1)S(1)} %bitcast.27), channel_id=1, source_target_pairs={{0,16},{8,24},{16,0},{24,8},{1,17},{9,25},{17,1},{25,9},{2,18},{10... | collective-permute-start | bytes 884744 | tf_op jit(solution)/shard_map/ppermute | solution.py:595
  141.8 8.7 %collective-permute-start.24 = (bf16[208,384]{1,0:T(8,128)(2,1)S(1)}, bf16[208,384]{1,0:T(8,128)(2,1)S(1)}, u32[]{:S(2)}, u32[]{:S(2)}) collective-permute-start(bf16[208,384]{1,0:T(8,128)(2,1)S(1)} %get-tuple-element.371), channel_id=1, source_target_pairs={{0,2},{1,3},{2,0},{3,1},{4,6},{5,7},{6,4},{7,5},{8,10},{9,11},{10,... | collective-permute-start | bytes 479240 | tf_op jit(solution)/shard_map/ppermute | solution.py:595
  142.3 13.3 %collective-permute-start.25 = (bf16[208,384]{1,0:T(8,128)(2,1)S(1)}, bf16[208,384]{1,0:T(8,128)(2,1)S(1)}, u32[]{:S(2)}, u32[]{:S(2)}) collective-permute-start(bf16[208,384]{1,0:T(8,128)(2,1)S(1)} %get-tuple-element.372), channel_id=1, source_target_pairs={{0,4},{1,5},{2,6},{3,7},{4,0},{5,1},{6,2},{7,3},{8,12},{9,13},{10,... | collective-permute-start | bytes 479240 | tf_op jit(solution)/shard_map/ppermute | solution.py:595
  144.9 10.7 %collective-permute-start.26 = (bf16[208,384]{1,0:T(8,128)(2,1)S(1)}, bf16[208,384]{1,0:T(8,128)(2,1)S(1)}, u32[]{:S(2)}, u32[]{:S(2)}) collective-permute-start(bf16[208,384]{1,0:T(8,128)(2,1)S(1)} %get-tuple-element.373), channel_id=1, source_target_pairs={{0,6},{1,7},{2,4},{3,5},{4,2},{5,3},{6,0},{7,1},{8,14},{9,15},{10,... | collective-permute-start | bytes 479240 | tf_op jit(solution)/shard_map/ppermute | solution.py:595
  147.9 12.0 %collective-permute-start.28 = (bf16[384,384]{1,0:T(8,128)(2,1)S(1)}, bf16[384,384]{1,0:T(8,128)(2,1)S(1)}, u32[]{:S(2)}, u32[]{:S(2)}) collective-permute-start(bf16[384,384]{1,0:T(8,128)(2,1)S(1)} %collective-permute-done.27.refs_1_), channel_id=1, source_target_pairs={{0,16},{8,24},{16,0},{24,8},{1,17},{9,25},{17,1},{25,9},{2,18},{10... | collective-permute-start | bytes 884744 | tf_op jit(solution)/shard_map/ppermute | solution.py:595
  155.6 4.3 %copy-start.3 = (f32[96,9280]{1,0:T(8,128)S(1)}, f32[96,9280]{1,0:T(8,128)}, u32[]{:S(2)}) copy-start(f32[96,9280]{1,0:T(8,128)} %refs_8_.1) | copy-start | bytes 10690564
  155.6 4.3 %copy-start.4 = (f32[96,9280]{1,0:T(8,128)S(1)}, f32[96,9280]{1,0:T(8,128)}, u32[]{:S(2)}) copy-start(f32[96,9280]{1,0:T(8,128)} %refs_9_.1) | copy-start | bytes 10690564
  155.6 4.3 %copy-start.5 = (f32[96,9280]{1,0:T(8,128)S(1)}, f32[96,9280]{1,0:T(8,128)}, u32[]{:S(2)}) copy-start(f32[96,9280]{1,0:T(8,128)} %refs_10_.1) | copy-start | bytes 10690564
  155.6 5.1 %copy-start.6 = (f32[96,9280]{1,0:T(8,128)S(1)}, f32[96,9280]{1,0:T(8,128)}, u32[]{:S(2)}) copy-start(f32[96,9280]{1,0:T(8,128)} %refs_11_.1) | copy-start | bytes 10690564
  156.3 11.4 %copy-start.19 = (f32[96,13]{0,1:T(8,128)S(1)}, f32[96,13]{0,1:T(8,128)}, u32[]{:S(2)}) copy-start(f32[96,13]{0,1:T(8,128)} %param.19) | copy-start | bytes 14980
  156.3 11.4 %copy-start.20 = (f32[96,13]{0,1:T(8,128)S(1)}, f32[96,13]{0,1:T(8,128)}, u32[]{:S(2)}) copy-start(f32[96,13]{0,1:T(8,128)} %param.21) | copy-start | bytes 14980
  156.3 11.4 %copy-start.21 = (f32[96,13]{0,1:T(8,128)S(1)}, f32[96,13]{0,1:T(8,128)}, u32[]{:S(2)}) copy-start(f32[96,13]{0,1:T(8,128)} %param.23) | copy-start | bytes 14980
  156.3 11.4 %copy-start.22 = (f32[96,13]{0,1:T(8,128)S(1)}, f32[96,13]{0,1:T(8,128)}, u32[]{:S(2)}) copy-start(f32[96,13]{0,1:T(8,128)} %param.25) | copy-start | bytes 14980
  156.3 11.4 %collective-permute-start.31 = (bf16[208,384]{1,0:T(8,128)(2,1)S(1)}, bf16[208,384]{1,0:T(8,128)(2,1)S(1)}, u32[]{:S(2)}, u32[]{:S(2)}) collective-permute-start(bf16[208,384]{1,0:T(8,128)(2,1)S(1)} %tail_final.1.refs_0_), channel_id=1, source_target_pairs={{0,24},{8,16},{16,8},{24,0},{1,25},{9,17},{17,9},{25,1},{2,26},{10... | collective-permute-start | bytes 479240 | tf_op jit(solution)/shard_map/ppermute | solution.py:595
  158.0 9.7 %collective-permute-start.30 = (bf16[208,384]{1,0:T(8,128)(2,1)S(1)}, bf16[208,384]{1,0:T(8,128)(2,1)S(1)}, u32[]{:S(2)}, u32[]{:S(2)}) collective-permute-start(bf16[208,384]{1,0:T(8,128)(2,1)S(1)} %tail_final.1.refs_0_), channel_id=1, source_target_pairs={{0,16},{8,24},{16,0},{24,8},{1,17},{9,25},{17,1},{25,9},{2,18},{10... | collective-permute-start | bytes 479240 | tf_op jit(solution)/shard_map/ppermute | solution.py:595
  159.1 8.5 %collective-permute-start.29 = (bf16[208,384]{1,0:T(8,128)(2,1)S(1)}, bf16[208,384]{1,0:T(8,128)(2,1)S(1)}, u32[]{:S(2)}, u32[]{:S(2)}) collective-permute-start(bf16[208,384]{1,0:T(8,128)(2,1)S(1)} %tail_final.1.refs_0_), channel_id=1, source_target_pairs={{0,8},{8,0},{16,24},{24,16},{1,9},{9,1},{17,25},{25,17},{2,10},{10... | collective-permute-start | bytes 479240 | tf_op jit(solution)/shard_map/ppermute | solution.py:595

commit v8 on v7

--- a/solution.py
+++ b/solution.py
@@ -941,7 +941,7 @@
                 pl.BlockSpec((1, D), lambda i, s: (0, jnp.bitwise_xor(i, jnp.right_shift(s[S_SEQ], 1)))),
             ],
             grid=(2,),
-            vmem=14,
+            vmem=20,
             name="mlp",
         )
         acc = [out_y, out_dh]

time: 173 us -> 173 us (level)
  no operation moved by 1% of the time
where the time goes in v8:
time: 173 us
  Pallas kernels  102 us (59%)
  starting transfers between devices  39.4 us (23%)
  waiting for transfers between devices  26.4 us (15%)
  local copies, waits for them, and re-layouts  3.15 us (2%)
  between operations  1.98 us (1%)
    pallas_call x24, Pallas kernels, call(): pl.pallas_call(body, out_shape=tuple((pltpu.HBM(o.shape, o.dtype) if k in...  102 us
    ppermute x32, starting transfers between devices, swap(): return lax.ppermute(value, axis, [(i, i ^ bit) for i in range(size)])  39.4 us
    ppermute x32, waiting for transfers between devices, swap(): return lax.ppermute(value, axis, [(i, i ^ bit) for i in range(size)])  26.4 us
  transfers between devices with their start and end apart: 32, of which 9 were waited for; matrix products, arithmetic and copies ran while one was open for 0% of the time, Pallas kernels for 50%

profile of v8, /device:TPU:0, one launch (start us, length us, event | category | flops | bytes accessed | tf_op | source)
XLA Modules:
  0.0 172.7 jit_solution(7334820264987084053)
XLA Ops:
  1.5 0.7 copy-done.13
  2.2 6.6 %keys.1 = (bf16[512,768]{1,0:T(8,128)(2,1)S(1)}, bf16[768,512]{1,0:T(8,128)(2,1)S(1)}, bf16[1536,512]{1,0:T(8,128)(2,1)S(1)}, bf16[768,512]{1,0:T(8,128)(2,1)S(1)}, bf16[864,128]{1,0:T(8,128)(2,1)S(1)}) custom-call(s32[16]{0:T(128)S(1)} %compare_select_fusion.2.scal, bf16[512,768]{1,0:T(8,128)(2,1)} %x_ref.3, bf16[9280,768]{1,0:T(8,128)(2,1)} %bitcast.44, ...), custom_call_target="tpu_custom_call" | custom-call | bytes 1024 | tf_op jit(solution)/shard_map/keys/pallas_call | solution.py:74
  8.8 4.0 %collective-permute-start.2 = (bf16[864,128]{1,0:T(8,128)(2,1)S(1)}, bf16[864,128]{1,0:T(8,128)(2,1)S(1)}, u32[]{:S(2)}, u32[]{:S(2)}) collective-permute-start(bf16[864,128]{1,0:T(8,128)(2,1)S(1)} %get-tuple-element.230), channel_id=1, source_target_pairs={{0,24},{8,16},{16,8},{24,0},{1,25},{9,17},{17,9},{25,1},{2,26},{10... | collective-permute-start | bytes 663560 | tf_op jit(solution)/shard_map/ppermute | solution.py:595
  12.8 0.5 collective-permute-start.1
  13.4 5.7 %queries.1 = (bf16[4,384,512]{2,1,0:T(8,128)(2,1)S(1)}, bf16[4,384,512]{2,1,0:T(8,128)(2,1)S(1)}, bf16[768,512]{1,0:T(8,128)(2,1)S(1)}, bf16[1536,512]{1,0:T(8,128)(2,1)S(1)}) custom-call(s32[16]{0:T(128)S(1)} %compare_select_fusion.2.scal, bf16[512,768]{1,0:T(8,128)(2,1)S(1)} %get-tuple-element.220.h1_ref, bf16[512,768]{1,0:T(8,128)(2,1)} %g_ref.7, ...), custom_call_target="tpu_custom_call" | custom-call | bytes 1024 | tf_op jit(solution)/shard_map/queries/pallas_call | solution.py:74
  19.1 4.0 %local.1.refs_3_ = f32[864,512]{1,0:T(8,128)S(1)} custom-call(s32[16]{0:T(128)S(1)} %compare_select_fusion.2.scal, bf16[1536,512]{1,0:T(8,128)(2,1)S(1)} %get-tuple-element.226.fq_ref.refs_4_.refs_3_, bf16[1536,512]{1,0:T(8,128)(2,1)S(1)} %get-tuple-element.227.fk_ref.refs_4_, bf16[768,512]{1,0:T(8,128)(2,1)S(1)} %get-tuple-element.228.vt_ref.refs_5_), custom_call_target="tpu_custom_call" | custom-call | bytes 1024 | tf_op jit(solution)/shard_map/local/pallas_call | solution.py:74
  23.2 4.4 %after.1 = (f32[768,512]{1,0:T(8,128)S(1)}, f32[16,512]{1,0:T(8,128)S(1)}, f32[512,768]{1,0:T(8,128)S(1)}, bf16[512,768]{1,0:T(8,128)(2,1)S(1)}, bf16[864,128]{1...) custom-call(s32[16]{0:T(128)S(1)} %compare_select_fusion.2.scal, ...), custom_call_target="tpu_custom_call", output_to_operand_aliasing={{5}: (9, {}), {6}: (10, {})} | custom-call | bytes 1024 | tf_op jit(solution)/shard_map/after/pallas_call | solution.py:74
  27.7 9.0 %mlp.2 = (f32[512,768]{1,0:T(8,128)S(1)}, f32[512,768]{1,0:T(8,128)S(1)}, bf16[2,2,512,768]{3,2,1,0:T(8,128)(2,1)S(1)}, f32[1,1536]{1,0:T(1,128)S(1)}) custom-call(s32[16]{0:T(128)S(1)} %compare_select_fusion.2.scal, bf16[512,768]{1,0:T(8,128)(2,1)S(1)} %get-tuple-element.242.h2_ref, bf16[512,768]{1,0:T(8,128)(2,1)} %g_ref.7, bf16[9280,768]{1,0:T(8,128)(2,1)} %bitcast.50, ...), custom_call_target="tpu_custom_call" | custom-call | bytes 1024 | tf_op jit(solution)/shard_map/mlp/pallas_call | solution.py:74
  36.8 0.6 collective-permute-start.4
  37.3 9.1 %mlp.3 = (f32[512,768]{1,0:T(8,128)S(1)}, f32[512,768]{1,0:T(8,128)S(1)}, bf16[2,2,512,768]{3,2,1,0:T(8,128)(2,1)S(1)}, f32[1,1536]{1,0:T(1,128)S(1)}) custom-call(s32[16]{0:T(128)S(1)} %compare_select_fusion.2.scal, bf16[512,768]{1,0:T(8,128)(2,1)S(1)} %get-tuple-element.242.h2_ref, bf16[512,768]{1,0:T(8,128)(2,1)} %g_ref.7, bf16[9280,768]{1,0:T(8,128)(2,1)} %bitcast.52, ...), custom_call_target="tpu_custom_call" | custom-call | bytes 1024 | tf_op jit(solution)/shard_map/mlp/pallas_call | solution.py:74
  46.5 4.4 %mlp_grads.2 = (bf16[8,192,384]{2,1,0:T(8,128)(2,1)}, bf16[8,192,384]{2,1,0:T(8,128)(2,1)S(1)}) custom-call(s32[16]{0:T(128)S(1)} %compare_select_fusion.2.scal, bf16[4,384,512]{2,1,0:T(8,128)(2,1)S(1)} %get-tuple-element.258.refs_0_.refs_6_.refs_2_, bf16[4,384,512]{2,1,0:T(8,128)(2,1)S(1)} %collective-permute-done.3.refs_1_.refs_7_.refs_3_, ...), custom_call_target="tpu_custom_call" | custom-call | bytes 1024 | tf_op jit(solution)/shard_map/mlp_grads/pallas_call | solution.py:74
  50.9 2.0 %collective-permute-start.9 = (bf16[8,192,384]{2,1,0:T(8,128)(2,1)}, bf16[8,192,384]{2,1,0:T(8,128)(2,1)}, u32[]{:S(2)}, u32[]{:S(2)}) collective-permute-start(bf16[8,192,384]{2,1,0:T(8,128)(2,1)} %get-tuple-element.311), channel_id=1, source_target_pairs={{0,2},{1,3},{2,0},{3,1},{4,6},{5,7},{6,4},{7,5},{8,10},{9,11},{10,... | collective-permute-start | bytes 3538952 | tf_op jit(solution)/shard_map/ppermute | solution.py:595
  52.9 6.6 %back.1 = (bf16[512,768]{1,0:T(8,128)(2,1)}, f32[512,768]{1,0:T(8,128)}, bf16[768,512]{1,0:T(8,128)(2,1)}, bf16[864,512]{1,0:T(8,128)(2,1)}, bf16[864,128]{1,0:T(8,128)(2,1)}, /*index=5*/f32[4,768]{1,0:T(4,128)S(1)}) custom-call(s32[16]{0:T(128)S(1)} %compare_select_fusion.2.scal, f32[512,768]{1,0:T(8,128)S(1)} %get-tuple-element.266.out_ref, ...), custom_call_target="tpu_custom_call" | custom-call | bytes 1024 | tf_op jit(solution)/shard_map/back/pallas_call | solution.py:74
  59.5 2.5 %collective-permute-start.8 = (bf16[864,128]{1,0:T(8,128)(2,1)}, bf16[864,128]{1,0:T(8,128)(2,1)}, u32[]{:S(2)}, u32[]{:S(2)}) collective-permute-start(bf16[864,128]{1,0:T(8,128)(2,1)} %get-tuple-element.284), channel_id=1, source_target_pairs={{0,24},{8,16},{16,8},{24,0},{1,25},{9,17},{17,9},{25,1},{2,26},{10... | collective-permute-start | bytes 663560 | tf_op jit(solution)/shard_map/ppermute | solution.py:595
  62.0 0.5 collective-permute-start.7
  62.5 0.5 collective-permute-start.6
  63.1 1.4 copy-done.1
  64.5 5.8 %mlp_grads.3 = (bf16[8,192,384]{2,1,0:T(8,128)(2,1)S(1)}, bf16[8,192,384]{2,1,0:T(8,128)(2,1)S(1)}) custom-call(s32[16]{0:T(128)S(1)} %compare_select_fusion.2.scal, bf16[4,384,512]{2,1,0:T(8,128)(2,1)S(1)} %get-tuple-element.258.refs_0_.refs_6_.refs_2_, bf16[4,384,512]{2,1,0:T(8,128)(2,1)S(1)} %copy-done.1, bf16[2,2,512,768]{3,2,1,0:T(8,128)(2,1)} %copy-done.7, ...), custom_call_target="tpu_custom_call" | custom-call | bytes 1024 | tf_op jit(solution)/shard_map/mlp_grads/pallas_call | solution.py:74
  70.4 1.6 collective-permute-start.10
  72.0 1.2 collective-permute-done.7.refs_1_
  73.2 12.3 %attend_back.1 = (bf16[4,768,512]{2,1,0:T(8,128)(2,1)S(1)}, f32[768,64]{1,0:T(8,128)S(1)}, f32[768,3]{1,0:T(8,128)S(1)}) custom-call(s32[16]{0:T(128)S(1)} %compare_select_fusion.2.scal, bf16[864,128]{1,0:T(8,128)(2,1)} %collective-permute-done.6.refs_0_, bf16[864,128]{1,0:T(8,128)(2,1)} %collective-permute-done.7.refs_1_, ...), custom_call_target="tpu_custom_call" | custom-call | flops 1000000000 | bytes 1024 | tf_op jit(solution)/shard_map/attend_back/pallas_call | solution.py:74
  85.6 7.8 %input.1 = (bf16[512,768]{1,0:T(8,128)(2,1)}, f32[1,384,128]{2,1,0:T(8,128)S(1)}, f32[1,384,128]{2,1,0:T(8,128)S(1)}) custom-call(s32[16]{0:T(128)S(1)} %compare_select_fusion.2.scal, bf16[4,768,512]{2,1,0:T(8,128)(2,1)S(1)} %get-tuple-element.298.dp_ref, bf16[9280,768]{1,0:T(8,128)(2,1)} %bitcast.56, bf16[512,768]{1,0:T(8,128)(2,1)} %x_ref.3, ...), custom_call_target="tpu_custom_call" | custom-call | bytes 1024 | tf_op jit(solution)/shard_map/input/pallas_call | solution.py:74
  93.4 0.5 collective-permute-start.12
  93.9 2.1 %halve.6 = (bf16[4,192,384]{2,1,0:T(8,128)(2,1)S(1)}, bf16[4,192,384]{2,1,0:T(8,128)(2,1)S(1)}) custom-call(s32[16]{0:T(128)S(1)} %compare_select_fusion.2.scal, bf16[8,192,384]{2,1,0:T(8,128)(2,1)S(1)} %copy-done.24, bf16[8,192,384]{2,1,0:T(8,128)(2,1)} %collective-permute-done.9.recv_ref), custom_call_target="tpu_custom_call" | custom-call | flops 14000000000 | bytes 1024 | tf_op jit(solution)/shard_map/halve/pallas_call | solution.py:74
  96.0 1.6 collective-permute-start.13
  97.6 0.6 collective-permute-done.10.recv_ref
  98.2 0.8 halve.7
  99.1 1.2 collective-permute-start.14
  100.3 5.7 %tail_grads.1 = (bf16[832,384]{1,0:T(8,128)(2,1)S(1)}, bf16[768,384]{1,0:T(8,128)(2,1)S(1)}, bf16[768,384]{1,0:T(8,128)(2,1)S(1)}, bf16[768,384]{1,0:T(8,128)(2,1)S(1)}, f32[64,384]{1,0:T(8,128)S(1)}) custom-call(s32[16]{0:T(128)S(1)} %compare_select_fusion.2.scal, bf16[4,384,512]{2,1,0:T(8,128)(2,1)S(1)} %get-tuple-element.258.refs_0_.refs_6_.refs_2_, ...), custom_call_target="tpu_custom_call" | custom-call | flops 8999999488 | bytes 1024 | tf_op jit(solution)/shard_map/tail_grads/pallas_call | solution.py:74
  106.0 1.6 collective-permute-start.15
  107.5 0.9 collective-permute-start.16
  108.5 3.8 %collective-permute-done.13.recv_ref = bf16[4,192,384]{2,1,0:T(8,128)(2,1)S(1)} collective-permute-done((bf16[4,192,384]{2,1,0:T(8,128)(2,1)S(1)}, bf16[4,192,384]{2,1,0:T(8,128)(2,1)S(1)}, u32[]{:S(2)}, u32[]{:S(2)}) %collective-permute-start.13) | collective-permute-done | bytes 589856 | tf_op jit(solution)/shard_map/ppermute | solution.py:595
  112.3 0.7 halve.8
  113.0 2.7 %collective-permute-start.17 = (bf16[2,192,384]{2,1,0:T(8,128)(2,1)S(1)}, bf16[2,192,384]{2,1,0:T(8,128)(2,1)S(1)}, u32[]{:S(2)}, u32[]{:S(2)}) collective-permute-start(bf16[2,192,384]{2,1,0:T(8,128)(2,1)S(1)} %get-tuple-element.347), channel_id=1, source_target_pairs={{0,4},{1,5},{2,6},{3,7},{4,0},{5,1},{6,2},{7,3},{8,12},{9,13},{10,... | collective-permute-start | bytes 884744 | tf_op jit(solution)/shard_map/ppermute | solution.py:595
  115.6 0.7 halve.9
  116.3 1.6 collective-permute-start.18
  117.9 6.1 %collective-permute-done.16.recv_b = bf16[768,384]{1,0:T(8,128)(2,1)S(1)} collective-permute-done((bf16[768,384]{1,0:T(8,128)(2,1)S(1)}, bf16[768,384]{1,0:T(8,128)(2,1)S(1)}, u32[]{:S(2)}, u32[]{:S(2)}) %collective-permute-start.16) | collective-permute-done | bytes 589856 | tf_op jit(solution)/shard_map/ppermute | solution.py:595
  124.0 0.8 tail_one.1
  124.8 1.6 collective-permute-start.21
  126.4 0.7 collective-permute-start.22
  127.1 0.4 collective-permute-done.17.recv_ref
  127.4 0.6 halve.10
  128.1 0.6 halve.11
  128.7 2.3 %collective-permute-start.20 = (bf16[1,192,384]{2,1,0:T(8,128)(2,1)S(1)}, bf16[1,192,384]{2,1,0:T(8,128)(2,1)S(1)}, u32[]{:S(2)}, u32[]{:S(2)}) collective-permute-start(bf16[1,192,384]{2,1,0:T(8,128)(2,1)S(1)} %get-tuple-element.359), channel_id=1, source_target_pairs={{0,4},{1,5},{2,6},{3,7},{4,0},{5,1},{6,2},{7,3},{8,12},{9,13},{10,... | collective-permute-start | bytes 442376 | tf_op jit(solution)/shard_map/ppermute | solution.py:595
  131.0 1.3 collective-permute-start.19
  132.3 5.4 %collective-permute-done.20.refs_3_ = bf16[1,192,384]{2,1,0:T(8,128)(2,1)S(1)} collective-permute-done((bf16[1,192,384]{2,1,0:T(8,128)(2,1)S(1)}, bf16[1,192,384]{2,1,0:T(8,128)(2,1)S(1)}, u32[]{:S(2)}, u32[]{:S(2)}) %collective-permute-start.20) | collective-permute-done | bytes 147488 | tf_op jit(solution)/shard_map/ppermute | solution.py:595
  137.8 0.6 final.1
  138.4 1.7 collective-permute-start.27
  140.1 0.7 collective-permute-start.23
  140.8 0.9 tail_two.1
  141.7 0.5 collective-permute-start.24
  142.2 2.6 %collective-permute-start.25 = (bf16[208,384]{1,0:T(8,128)(2,1)S(1)}, bf16[208,384]{1,0:T(8,128)(2,1)S(1)}, u32[]{:S(2)}, u32[]{:S(2)}) collective-permute-start(bf16[208,384]{1,0:T(8,128)(2,1)S(1)} %get-tuple-element.372), channel_id=1, source_target_pairs={{0,4},{1,5},{2,6},{3,7},{4,0},{5,1},{6,2},{7,3},{8,12},{9,13},{10,... | collective-permute-start | bytes 479240 | tf_op jit(solution)/shard_map/ppermute | solution.py:595
  144.8 1.4 collective-permute-start.26
  146.1 1.7 collective-permute-done.23.refs_2_
  147.8 0.6 collective-permute-start.28
  148.4 2.0 %collective-permute-done.24.refs_1_ = bf16[208,384]{1,0:T(8,128)(2,1)S(1)} collective-permute-done((bf16[208,384]{1,0:T(8,128)(2,1)S(1)}, bf16[208,384]{1,0:T(8,128)(2,1)S(1)}, u32[]{:S(2)}, u32[]{:S(2)}) %collective-permute-start.24) | collective-permute-done | bytes 159776 | tf_op jit(solution)/shard_map/ppermute | solution.py:595
  150.4 5.1 %collective-permute-done.25.refs_2_ = bf16[208,384]{1,0:T(8,128)(2,1)S(1)} collective-permute-done((bf16[208,384]{1,0:T(8,128)(2,1)S(1)}, bf16[208,384]{1,0:T(8,128)(2,1)S(1)}, u32[]{:S(2)}, u32[]{:S(2)}) %collective-permute-start.25) | collective-permute-done | bytes 159776 | tf_op jit(solution)/shard_map/ppermute | solution.py:595
  155.6 0.6 tail_final.1.refs_0_
  156.2 1.7 collective-permute-start.31
  157.9 1.1 collective-permute-start.30
  159.0 0.7 collective-permute-start.29
  159.8 0.9 copy-done.6
  160.7 6.9 %adam.2 = (f32[96,9280]{1,0:T(8,128)}, f32[96,9280]{1,0:T(8,128)}, f32[96,9280]{1,0:T(8,128)}, f32[96,9280]{1,0:T(8,128)}, f32[96,9280]{1,0:T(8,128)}, /*index=5*/bf16[96,9280]{1,0:T(8,128)(2,1)}) custom-call(s32[16]{0:T(128)S(1)} %compare_select_fusion.2.scal, bf16[384,384]{1,0:T(8,128)(2,1)S(1)} %bitcast.28, ...), custom_call_target="tpu_custom_call" | custom-call | bytes 1024 | tf_op jit(solution)/shard_map/adam/pallas_call | solution.py:74
  167.6 4.9 %adam.3 = (f32[96,9280]{1,0:T(8,128)}, f32[96,9280]{1,0:T(8,128)}, f32[96,9280]{1,0:T(8,128)}, f32[96,9280]{1,0:T(8,128)}, f32[96,9280]{1,0:T(8,128)}, /*index=5...) custom-call(s32[16]{0:T(128)S(1)} %compare_select_fusion.2.scal, ...), custom_call_target="tpu_custom_call", output_to_operand_aliasing={{0}: (13, {}), {1}: (14, {}), {2}: (15, {}), {3}: (16, {}),... | custom-call | bytes 1024 | tf_op jit(solution)/shard_map/adam/pallas_call | solution.py:74
  (81 shorter events, 0.8 us)
Async XLA Ops:
  1.5 0.7 copy-start.13
  8.8 10.3 %copy-start.15 = (bf16[768,512]{1,0:T(8,128)(2,1)}, bf16[768,512]{1,0:T(8,128)(2,1)S(1)}, u32[]{:S(2)}) copy-start(bf16[768,512]{1,0:T(8,128)(2,1)S(1)} %get-tuple-element.292.refs_9_) | copy-start | bytes 2359300
  8.8 10.3 %copy-start.8 = (bf16[1536,512]{1,0:T(8,128)(2,1)}, bf16[1536,512]{1,0:T(8,128)(2,1)S(1)}, u32[]{:S(2)}) copy-start(bf16[1536,512]{1,0:T(8,128)(2,1)S(1)} %get-tuple-element.227.fk_ref.refs_4_) | copy-start | bytes 4718596
  8.8 10.3 %copy-start.10 = (bf16[768,512]{1,0:T(8,128)(2,1)}, bf16[768,512]{1,0:T(8,128)(2,1)S(1)}, u32[]{:S(2)}) copy-start(bf16[768,512]{1,0:T(8,128)(2,1)S(1)} %get-tuple-element.228.vt_ref.refs_5_) | copy-start | bytes 2359300
  8.8 14.4 %collective-permute-start.2 = (bf16[864,128]{1,0:T(8,128)(2,1)S(1)}, bf16[864,128]{1,0:T(8,128)(2,1)S(1)}, u32[]{:S(2)}, u32[]{:S(2)}) collective-permute-start(bf16[864,128]{1,0:T(8,128)(2,1)S(1)} %get-tuple-element.230), channel_id=1, source_target_pairs={{0,24},{8,16},{16,8},{24,0},{1,25},{9,17},{17,9},{25,1},{2,26},{10... | collective-permute-start | bytes 663560 | tf_op jit(solution)/shard_map/ppermute | solution.py:595
  12.8 10.4 %collective-permute-start.1 = (bf16[864,128]{1,0:T(8,128)(2,1)S(1)}, bf16[864,128]{1,0:T(8,128)(2,1)S(1)}, u32[]{:S(2)}, u32[]{:S(2)}) collective-permute-start(bf16[864,128]{1,0:T(8,128)(2,1)S(1)} %get-tuple-element.230), channel_id=1, source_target_pairs={{0,16},{8,24},{16,0},{24,8},{1,17},{9,25},{17,1},{25,9},{2,18},{10... | collective-permute-start | bytes 663560 | tf_op jit(solution)/shard_map/ppermute | solution.py:595
  13.3 9.9 %collective-permute-start = (bf16[864,128]{1,0:T(8,128)(2,1)S(1)}, bf16[864,128]{1,0:T(8,128)(2,1)S(1)}, u32[]{:S(2)}, u32[]{:S(2)}) collective-permute-start(bf16[864,128]{1,0:T(8,128)(2,1)S(1)} %get-tuple-element.230), channel_id=1, source_target_pairs={{0,8},{8,0},{16,24},{24,16},{1,9},{9,1},{17,25},{25,17},{2,10},{10... | collective-permute-start | bytes 663560 | tf_op jit(solution)/shard_map/ppermute | solution.py:595
  19.1 4.1 %copy-start.17 = (bf16[768,512]{1,0:T(8,128)(2,1)}, bf16[768,512]{1,0:T(8,128)(2,1)S(1)}, u32[]{:S(2)}) copy-start(bf16[768,512]{1,0:T(8,128)(2,1)S(1)} %get-tuple-element.291.refs_8_) | copy-start | bytes 2359300
  27.6 9.7 %collective-permute-start.3 = (bf16[4,384,512]{2,1,0:T(8,128)(2,1)S(1)}, bf16[4,384,512]{2,1,0:T(8,128)(2,1)S(1)}, u32[]{:S(2)}, u32[]{:S(2)}) collective-permute-start(bf16[4,384,512]{2,1,0:T(8,128)(2,1)S(1)} %get-tuple-element.249), channel_id=1, source_target_pairs={{0,1},{1,0},{2,3},{3,2},{4,5},{5,4},{6,7},{7,6},{8,9},{9,8},{10,11... | collective-permute-start | bytes 4718600 | tf_op jit(solution)/shard_map/ppermute | solution.py:595
  36.8 9.8 %collective-permute-start.4 = (bf16[2,2,512,768]{3,2,1,0:T(8,128)(2,1)S(1)}, bf16[2,2,512,768]{3,2,1,0:T(8,128)(2,1)S(1)}, u32[]{:S(2)}, u32[]{:S(2)}) collective-permute-start(bf16[2,2,512,768]{3,2,1,0:T(8,128)(2,1)S(1)} %get-tuple-element.260.refs_2_.refs_4_), channel_id=1, source_target_pairs={{0,1},{1,0},{2,3},{3,2},{4,5},{5,4},{6,7},{7,6},{8,9},{9,8},{10,11... | collective-permute-start | bytes 9437192 | tf_op jit(solution)/shard_map/ppermute | solution.py:595
  37.3 9.2 %copy-start = (bf16[4,384,512]{2,1,0:T(8,128)(2,1)}, bf16[4,384,512]{2,1,0:T(8,128)(2,1)S(1)}, u32[]{:S(2)}) copy-start(bf16[4,384,512]{2,1,0:T(8,128)(2,1)S(1)} %collective-permute-done.3.refs_1_.refs_7_.refs_3_) | copy-start | bytes 4718596
  46.4 4.5 %copy-start.7 = (bf16[2,2,512,768]{3,2,1,0:T(8,128)(2,1)}, bf16[2,2,512,768]{3,2,1,0:T(8,128)(2,1)S(1)}, u32[]{:S(2)}) copy-start(bf16[2,2,512,768]{3,2,1,0:T(8,128)(2,1)S(1)} %get-tuple-element.279.refs_2_.refs_4_) | copy-start | bytes 9437188
  46.4 6.5 %copy-start.14 = (bf16[768,13]{0,1:T(8,128)(2,1)S(1)}, bf16[768,13]{0,1:T(8,128)(2,1)}, u32[]{:S(2)}) copy-start(bf16[768,13]{0,1:T(8,128)(2,1)} %param.17) | copy-start | bytes 59908
  46.4 6.5 %collective-permute-start.5 = (bf16[2,2,512,768]{3,2,1,0:T(8,128)(2,1)S(1)}, bf16[2,2,512,768]{3,2,1,0:T(8,128)(2,1)S(1)}, u32[]{:S(2)}, u32[]{:S(2)}) collective-permute-start(bf16[2,2,512,768]{3,2,1,0:T(8,128)(2,1)S(1)} %get-tuple-element.279.refs_2_.refs_4_), channel_id=1, source_target_pairs={{0,1},{1,0},{2,3},{3,2},{4,5},{5,4},{6,7},{7,6},{8,9},{9,8},{10,11... | collective-permute-start | bytes 9437192 | tf_op jit(solution)/shard_map/ppermute | solution.py:595
  50.9 8.6 %copy-start.23 = (bf16[8,192,384]{2,1,0:T(8,128)(2,1)}, bf16[8,192,384]{2,1,0:T(8,128)(2,1)S(1)}, u32[]{:S(2)}) copy-start(bf16[8,192,384]{2,1,0:T(8,128)(2,1)S(1)} %get-tuple-element.310.keep_ref) | copy-start | bytes 3538948
  50.9 43.0 %collective-permute-start.9 = (bf16[8,192,384]{2,1,0:T(8,128)(2,1)}, bf16[8,192,384]{2,1,0:T(8,128)(2,1)}, u32[]{:S(2)}, u32[]{:S(2)}) collective-permute-start(bf16[8,192,384]{2,1,0:T(8,128)(2,1)} %get-tuple-element.311), channel_id=1, source_target_pairs={{0,2},{1,3},{2,0},{3,1},{4,6},{5,7},{6,4},{7,5},{8,10},{9,11},{10,... | collective-permute-start | bytes 3538952 | tf_op jit(solution)/shard_map/ppermute | solution.py:595
  52.9 6.6 %copy-start.25 = (bf16[2,2,512,768]{3,2,1,0:T(8,128)(2,1)}, bf16[2,2,512,768]{3,2,1,0:T(8,128)(2,1)S(1)}, u32[]{:S(2)}) copy-start(bf16[2,2,512,768]{3,2,1,0:T(8,128)(2,1)S(1)} %collective-permute-done.5.refs_3_.refs_5_) | copy-start | bytes 9437188
  59.5 12.4 %collective-permute-start.8 = (bf16[864,128]{1,0:T(8,128)(2,1)}, bf16[864,128]{1,0:T(8,128)(2,1)}, u32[]{:S(2)}, u32[]{:S(2)}) collective-permute-start(bf16[864,128]{1,0:T(8,128)(2,1)} %get-tuple-element.284), channel_id=1, source_target_pairs={{0,24},{8,16},{16,8},{24,0},{1,25},{9,17},{17,9},{25,1},{2,26},{10... | collective-permute-start | bytes 663560 | tf_op jit(solution)/shard_map/ppermute | solution.py:595
  62.0 11.1 %collective-permute-start.7 = (bf16[864,128]{1,0:T(8,128)(2,1)}, bf16[864,128]{1,0:T(8,128)(2,1)}, u32[]{:S(2)}, u32[]{:S(2)}) collective-permute-start(bf16[864,128]{1,0:T(8,128)(2,1)} %get-tuple-element.284), channel_id=1, source_target_pairs={{0,16},{8,24},{16,0},{24,8},{1,17},{9,25},{17,1},{25,9},{2,18},{10... | collective-permute-start | bytes 663560 | tf_op jit(solution)/shard_map/ppermute | solution.py:595
  62.5 10.6 %collective-permute-start.6 = (bf16[864,128]{1,0:T(8,128)(2,1)}, bf16[864,128]{1,0:T(8,128)(2,1)}, u32[]{:S(2)}, u32[]{:S(2)}) collective-permute-start(bf16[864,128]{1,0:T(8,128)(2,1)} %get-tuple-element.284), channel_id=1, source_target_pairs={{0,8},{8,0},{16,24},{24,16},{1,9},{9,1},{17,25},{25,17},{2,10},{10... | collective-permute-start | bytes 663560 | tf_op jit(solution)/shard_map/ppermute | solution.py:595
  63.1 1.4 copy-start.1
  64.5 8.6 %copy-start.9 = (bf16[1536,512]{1,0:T(8,128)(2,1)S(1)}, bf16[1536,512]{1,0:T(8,128)(2,1)}, u32[]{:S(2)}) copy-start(bf16[1536,512]{1,0:T(8,128)(2,1)} %copy-done.8) | copy-start | bytes 4718596
  64.5 8.6 %copy-start.11 = (bf16[768,512]{1,0:T(8,128)(2,1)S(1)}, bf16[768,512]{1,0:T(8,128)(2,1)}, u32[]{:S(2)}) copy-start(bf16[768,512]{1,0:T(8,128)(2,1)} %copy-done.10) | copy-start | bytes 2359300
  64.5 8.6 %copy-start.16 = (bf16[768,512]{1,0:T(8,128)(2,1)S(1)}, bf16[768,512]{1,0:T(8,128)(2,1)}, u32[]{:S(2)}) copy-start(bf16[768,512]{1,0:T(8,128)(2,1)} %copy-done.15) | copy-start | bytes 2359300
  64.5 8.6 %copy-start.18 = (bf16[768,512]{1,0:T(8,128)(2,1)S(1)}, bf16[768,512]{1,0:T(8,128)(2,1)}, u32[]{:S(2)}) copy-start(bf16[768,512]{1,0:T(8,128)(2,1)} %copy-done.17) | copy-start | bytes 2359300
  70.3 15.3 %copy-start.12 = (f32[512,768]{1,0:T(8,128)S(1)}, f32[512,768]{1,0:T(8,128)}, u32[]{:S(2)}) copy-start(f32[512,768]{1,0:T(8,128)} %get-tuple-element.299.dr_ref) | copy-start | bytes 4718596
  70.4 27.9 %collective-permute-start.10 = (bf16[8,192,384]{2,1,0:T(8,128)(2,1)S(1)}, bf16[8,192,384]{2,1,0:T(8,128)(2,1)S(1)}, u32[]{:S(2)}, u32[]{:S(2)}) collective-permute-start(bf16[8,192,384]{2,1,0:T(8,128)(2,1)S(1)} %get-tuple-element.316), channel_id=1, source_target_pairs={{0,16},{8,24},{16,0},{24,8},{1,17},{9,25},{17,1},{25,9},{2,18},{10... | collective-permute-start | bytes 3538952 | tf_op jit(solution)/shard_map/ppermute | solution.py:595
  85.5 8.4 %copy-start.24 = (bf16[8,192,384]{2,1,0:T(8,128)(2,1)S(1)}, bf16[8,192,384]{2,1,0:T(8,128)(2,1)}, u32[]{:S(2)}) copy-start(bf16[8,192,384]{2,1,0:T(8,128)(2,1)} %copy-done.23) | copy-start | bytes 3538948
  85.5 14.8 %collective-permute-start.11 = (bf16[4,768,512]{2,1,0:T(8,128)(2,1)S(1)}, bf16[4,768,512]{2,1,0:T(8,128)(2,1)S(1)}, u32[]{:S(2)}, u32[]{:S(2)}) collective-permute-start(bf16[4,768,512]{2,1,0:T(8,128)(2,1)S(1)} %get-tuple-element.298.dp_ref), channel_id=1, source_target_pairs={{0,1},{1,0},{2,3},{3,2},{4,5},{5,4},{6,7},{7,6},{8,9},{9,8},{10,11... | collective-permute-start | bytes 9437192 | tf_op jit(solution)/shard_map/ppermute | solution.py:595
  93.4 6.9 %collective-permute-start.12 = (f32[1,384,128]{2,1,0:T(8,128)S(1)}, f32[1,384,128]{2,1,0:T(8,128)S(1)}, u32[]{:S(2)}, u32[]{:S(2)}) collective-permute-start(f32[1,384,128]{2,1,0:T(8,128)S(1)} %get-tuple-element.321), channel_id=1, source_target_pairs={{0,1},{1,0},{2,3},{3,2},{4,5},{5,4},{6,7},{7,6},{8,9},{9,8},{10,11... | collective-permute-start | bytes 589832 | tf_op jit(solution)/shard_map/ppermute | solution.py:595
  96.0 4.3 %copy-start.2 = (bf16[4,384,512]{2,1,0:T(8,128)(2,1)S(1)}, bf16[4,384,512]{2,1,0:T(8,128)(2,1)}, u32[]{:S(2)}) copy-start(bf16[4,384,512]{2,1,0:T(8,128)(2,1)} %copy-done) | copy-start | bytes 4718596
  96.0 16.3 %collective-permute-start.13 = (bf16[4,192,384]{2,1,0:T(8,128)(2,1)S(1)}, bf16[4,192,384]{2,1,0:T(8,128)(2,1)S(1)}, u32[]{:S(2)}, u32[]{:S(2)}) collective-permute-start(bf16[4,192,384]{2,1,0:T(8,128)(2,1)S(1)} %get-tuple-element.329), channel_id=1, source_target_pairs={{0,16},{8,24},{16,0},{24,8},{1,17},{9,25},{17,1},{25,9},{2,18},{10... | collective-permute-start | bytes 1769480 | tf_op jit(solution)/shard_map/ppermute | solution.py:595
  99.1 16.6 %collective-permute-start.14 = (bf16[4,192,384]{2,1,0:T(8,128)(2,1)S(1)}, bf16[4,192,384]{2,1,0:T(8,128)(2,1)S(1)}, u32[]{:S(2)}, u32[]{:S(2)}) collective-permute-start(bf16[4,192,384]{2,1,0:T(8,128)(2,1)S(1)} %get-tuple-element.334), channel_id=1, source_target_pairs={{0,2},{1,3},{2,0},{3,1},{4,6},{5,7},{6,4},{7,5},{8,10},{9,11},{10,... | collective-permute-start | bytes 1769480 | tf_op jit(solution)/shard_map/ppermute | solution.py:595
  106.0 18.0 %collective-permute-start.15 = (bf16[832,384]{1,0:T(8,128)(2,1)S(1)}, bf16[832,384]{1,0:T(8,128)(2,1)S(1)}, u32[]{:S(2)}, u32[]{:S(2)}) collective-permute-start(bf16[832,384]{1,0:T(8,128)(2,1)S(1)} %get-tuple-element.339), channel_id=1, source_target_pairs={{0,8},{8,0},{16,24},{24,16},{1,9},{9,1},{17,25},{25,17},{2,10},{10... | collective-permute-start | bytes 1916936 | tf_op jit(solution)/shard_map/ppermute | solution.py:595
  107.5 16.5 %collective-permute-start.16 = (bf16[768,384]{1,0:T(8,128)(2,1)S(1)}, bf16[768,384]{1,0:T(8,128)(2,1)S(1)}, u32[]{:S(2)}, u32[]{:S(2)}) collective-permute-start(bf16[768,384]{1,0:T(8,128)(2,1)S(1)} %get-tuple-element.341), channel_id=1, source_target_pairs={{0,16},{8,24},{16,0},{24,8},{1,17},{9,25},{17,1},{25,9},{2,18},{10... | collective-permute-start | bytes 1769480 | tf_op jit(solution)/shard_map/ppermute | solution.py:595
  113.0 14.5 %collective-permute-start.17 = (bf16[2,192,384]{2,1,0:T(8,128)(2,1)S(1)}, bf16[2,192,384]{2,1,0:T(8,128)(2,1)S(1)}, u32[]{:S(2)}, u32[]{:S(2)}) collective-permute-start(bf16[2,192,384]{2,1,0:T(8,128)(2,1)S(1)} %get-tuple-element.347), channel_id=1, source_target_pairs={{0,4},{1,5},{2,6},{3,7},{4,0},{5,1},{6,2},{7,3},{8,12},{9,13},{10,... | collective-permute-start | bytes 884744 | tf_op jit(solution)/shard_map/ppermute | solution.py:595
  116.3 11.7 %collective-permute-start.18 = (bf16[2,192,384]{2,1,0:T(8,128)(2,1)S(1)}, bf16[2,192,384]{2,1,0:T(8,128)(2,1)S(1)}, u32[]{:S(2)}, u32[]{:S(2)}) collective-permute-start(bf16[2,192,384]{2,1,0:T(8,128)(2,1)S(1)} %get-tuple-element.352), channel_id=1, source_target_pairs={{0,8},{8,0},{16,24},{24,16},{1,9},{9,1},{17,25},{25,17},{2,10},{10... | collective-permute-start | bytes 884744 | tf_op jit(solution)/shard_map/ppermute | solution.py:595
  124.8 16.0 %collective-permute-start.21 = (bf16[416,384]{1,0:T(8,128)(2,1)S(1)}, bf16[416,384]{1,0:T(8,128)(2,1)S(1)}, u32[]{:S(2)}, u32[]{:S(2)}) collective-permute-start(bf16[416,384]{1,0:T(8,128)(2,1)S(1)} %get-tuple-element.361), channel_id=1, source_target_pairs={{0,16},{8,24},{16,0},{24,8},{1,17},{9,25},{17,1},{25,9},{2,18},{10... | collective-permute-start | bytes 958472 | tf_op jit(solution)/shard_map/ppermute | solution.py:595
  126.4 14.4 %collective-permute-start.22 = (bf16[384,384]{1,0:T(8,128)(2,1)S(1)}, bf16[384,384]{1,0:T(8,128)(2,1)S(1)}, u32[]{:S(2)}, u32[]{:S(2)}) collective-permute-start(bf16[384,384]{1,0:T(8,128)(2,1)S(1)} %get-tuple-element.362), channel_id=1, source_target_pairs={{0,8},{8,0},{16,24},{24,16},{1,9},{9,1},{17,25},{25,17},{2,10},{10... | collective-permute-start | bytes 884744 | tf_op jit(solution)/shard_map/ppermute | solution.py:595
  128.7 9.1 %collective-permute-start.20 = (bf16[1,192,384]{2,1,0:T(8,128)(2,1)S(1)}, bf16[1,192,384]{2,1,0:T(8,128)(2,1)S(1)}, u32[]{:S(2)}, u32[]{:S(2)}) collective-permute-start(bf16[1,192,384]{2,1,0:T(8,128)(2,1)S(1)} %get-tuple-element.359), channel_id=1, source_target_pairs={{0,4},{1,5},{2,6},{3,7},{4,0},{5,1},{6,2},{7,3},{8,12},{9,13},{10,... | collective-permute-start | bytes 442376 | tf_op jit(solution)/shard_map/ppermute | solution.py:595
  131.0 6.8 %collective-permute-start.19 = (bf16[1,192,384]{2,1,0:T(8,128)(2,1)S(1)}, bf16[1,192,384]{2,1,0:T(8,128)(2,1)S(1)}, u32[]{:S(2)}, u32[]{:S(2)}) collective-permute-start(bf16[1,192,384]{2,1,0:T(8,128)(2,1)S(1)} %get-tuple-element.357), channel_id=1, source_target_pairs={{0,8},{8,0},{16,24},{24,16},{1,9},{9,1},{17,25},{25,17},{2,10},{10... | collective-permute-start | bytes 442376 | tf_op jit(solution)/shard_map/ppermute | solution.py:595
  138.4 9.4 %collective-permute-start.27 = (bf16[384,384]{1,0:T(8,128)(2,1)S(1)}, bf16[384,384]{1,0:T(8,128)(2,1)S(1)}, u32[]{:S(2)}, u32[]{:S(2)}) collective-permute-start(bf16[384,384]{1,0:T(8,128)(2,1)S(1)} %bitcast.26), channel_id=1, source_target_pairs={{0,8},{8,0},{16,24},{24,16},{1,9},{9,1},{17,25},{25,17},{2,10},{10... | collective-permute-start | bytes 884744 | tf_op jit(solution)/shard_map/ppermute | solution.py:595
  140.1 7.7 %collective-permute-start.23 = (bf16[384,384]{1,0:T(8,128)(2,1)S(1)}, bf16[384,384]{1,0:T(8,128)(2,1)S(1)}, u32[]{:S(2)}, u32[]{:S(2)}) collective-permute-start(bf16[384,384]{1,0:T(8,128)(2,1)S(1)} %bitcast.27), channel_id=1, source_target_pairs={{0,16},{8,24},{16,0},{24,8},{1,17},{9,25},{17,1},{25,9},{2,18},{10... | collective-permute-start | bytes 884744 | tf_op jit(solution)/shard_map/ppermute | solution.py:595
  141.7 8.7 %collective-permute-start.24 = (bf16[208,384]{1,0:T(8,128)(2,1)S(1)}, bf16[208,384]{1,0:T(8,128)(2,1)S(1)}, u32[]{:S(2)}, u32[]{:S(2)}) collective-permute-start(bf16[208,384]{1,0:T(8,128)(2,1)S(1)} %get-tuple-element.371), channel_id=1, source_target_pairs={{0,2},{1,3},{2,0},{3,1},{4,6},{5,7},{6,4},{7,5},{8,10},{9,11},{10,... | collective-permute-start | bytes 479240 | tf_op jit(solution)/shard_map/ppermute | solution.py:595
  142.2 13.3 %collective-permute-start.25 = (bf16[208,384]{1,0:T(8,128)(2,1)S(1)}, bf16[208,384]{1,0:T(8,128)(2,1)S(1)}, u32[]{:S(2)}, u32[]{:S(2)}) collective-permute-start(bf16[208,384]{1,0:T(8,128)(2,1)S(1)} %get-tuple-element.372), channel_id=1, source_target_pairs={{0,4},{1,5},{2,6},{3,7},{4,0},{5,1},{6,2},{7,3},{8,12},{9,13},{10,... | collective-permute-start | bytes 479240 | tf_op jit(solution)/shard_map/ppermute | solution.py:595
  144.8 10.7 %collective-permute-start.26 = (bf16[208,384]{1,0:T(8,128)(2,1)S(1)}, bf16[208,384]{1,0:T(8,128)(2,1)S(1)}, u32[]{:S(2)}, u32[]{:S(2)}) collective-permute-start(bf16[208,384]{1,0:T(8,128)(2,1)S(1)} %get-tuple-element.373), channel_id=1, source_target_pairs={{0,6},{1,7},{2,4},{3,5},{4,2},{5,3},{6,0},{7,1},{8,14},{9,15},{10,... | collective-permute-start | bytes 479240 | tf_op jit(solution)/shard_map/ppermute | solution.py:595
  147.8 12.0 %collective-permute-start.28 = (bf16[384,384]{1,0:T(8,128)(2,1)S(1)}, bf16[384,384]{1,0:T(8,128)(2,1)S(1)}, u32[]{:S(2)}, u32[]{:S(2)}) collective-permute-start(bf16[384,384]{1,0:T(8,128)(2,1)S(1)} %collective-permute-done.27.refs_1_), channel_id=1, source_target_pairs={{0,16},{8,24},{16,0},{24,8},{1,17},{9,25},{17,1},{25,9},{2,18},{10... | collective-permute-start | bytes 884744 | tf_op jit(solution)/shard_map/ppermute | solution.py:595
  155.5 4.3 %copy-start.3 = (f32[96,9280]{1,0:T(8,128)S(1)}, f32[96,9280]{1,0:T(8,128)}, u32[]{:S(2)}) copy-start(f32[96,9280]{1,0:T(8,128)} %refs_8_.1) | copy-start | bytes 10690564
  155.5 4.3 %copy-start.4 = (f32[96,9280]{1,0:T(8,128)S(1)}, f32[96,9280]{1,0:T(8,128)}, u32[]{:S(2)}) copy-start(f32[96,9280]{1,0:T(8,128)} %refs_9_.1) | copy-start | bytes 10690564
  155.5 4.3 %copy-start.5 = (f32[96,9280]{1,0:T(8,128)S(1)}, f32[96,9280]{1,0:T(8,128)}, u32[]{:S(2)}) copy-start(f32[96,9280]{1,0:T(8,128)} %refs_10_.1) | copy-start | bytes 10690564
  155.5 5.1 %copy-start.6 = (f32[96,9280]{1,0:T(8,128)S(1)}, f32[96,9280]{1,0:T(8,128)}, u32[]{:S(2)}) copy-start(f32[96,9280]{1,0:T(8,128)} %refs_11_.1) | copy-start | bytes 10690564
  156.2 11.4 %copy-start.19 = (f32[96,13]{0,1:T(8,128)S(1)}, f32[96,13]{0,1:T(8,128)}, u32[]{:S(2)}) copy-start(f32[96,13]{0,1:T(8,128)} %param.19) | copy-start | bytes 14980
  156.2 11.4 %copy-start.20 = (f32[96,13]{0,1:T(8,128)S(1)}, f32[96,13]{0,1:T(8,128)}, u32[]{:S(2)}) copy-start(f32[96,13]{0,1:T(8,128)} %param.21) | copy-start | bytes 14980
  156.2 11.4 %copy-start.21 = (f32[96,13]{0,1:T(8,128)S(1)}, f32[96,13]{0,1:T(8,128)}, u32[]{:S(2)}) copy-start(f32[96,13]{0,1:T(8,128)} %param.23) | copy-start | bytes 14980
  156.2 11.4 %copy-start.22 = (f32[96,13]{0,1:T(8,128)S(1)}, f32[96,13]{0,1:T(8,128)}, u32[]{:S(2)}) copy-start(f32[96,13]{0,1:T(8,128)} %param.25) | copy-start | bytes 14980
  156.2 11.4 %collective-permute-start.31 = (bf16[208,384]{1,0:T(8,128)(2,1)S(1)}, bf16[208,384]{1,0:T(8,128)(2,1)S(1)}, u32[]{:S(2)}, u32[]{:S(2)}) collective-permute-start(bf16[208,384]{1,0:T(8,128)(2,1)S(1)} %tail_final.1.refs_0_), channel_id=1, source_target_pairs={{0,24},{8,16},{16,8},{24,0},{1,25},{9,17},{17,9},{25,1},{2,26},{10... | collective-permute-start | bytes 479240 | tf_op jit(solution)/shard_map/ppermute | solution.py:595
  157.9 9.6 %collective-permute-start.30 = (bf16[208,384]{1,0:T(8,128)(2,1)S(1)}, bf16[208,384]{1,0:T(8,128)(2,1)S(1)}, u32[]{:S(2)}, u32[]{:S(2)}) collective-permute-start(bf16[208,384]{1,0:T(8,128)(2,1)S(1)} %tail_final.1.refs_0_), channel_id=1, source_target_pairs={{0,16},{8,24},{16,0},{24,8},{1,17},{9,25},{17,1},{25,9},{2,18},{10... | collective-permute-start | bytes 479240 | tf_op jit(solution)/shard_map/ppermute | solution.py:595
  159.0 8.6 %collective-permute-start.29 = (bf16[208,384]{1,0:T(8,128)(2,1)S(1)}, bf16[208,384]{1,0:T(8,128)(2,1)S(1)}, u32[]{:S(2)}, u32[]{:S(2)}) collective-permute-start(bf16[208,384]{1,0:T(8,128)(2,1)S(1)} %tail_final.1.refs_0_), channel_id=1, source_target_pairs={{0,8},{8,0},{16,24},{24,16},{1,9},{9,1},{17,25},{25,17},{2,10},{10... | collective-permute-start | bytes 479240 | tf_op jit(solution)/shard_map/ppermute | solution.py:595
